TPU v7x, 256 devices: a whole 4x4x8 slice. The times are simulated.
256 devices in a mesh: px: 8 (over y, core), py: 8 (over z), case: 4 (over x).
Axes of the slice: x: 4, y: 4, z: 8, core: 2. Of those that a mesh axis runs over, the one named last changes fastest.
Arguments:
- comp_type: int32 [8192], P(('px', 'py')), may hold values from 0 to 7
- stiffness: float32 [8192], P(('px', 'py')), may hold values from 0.3 to 3
- near_port: int32 [8192], P(('px', 'py')), may hold values from 0 to 127
- far_owner: int32 [8192, 1], P(('px', 'py')), may hold values from 0 to 63; in each aligned block of 128 rows (0 to 127, 128 to 255, ...) at most 3 rows name the same one
- far_port: int32 [8192], P(('px', 'py')), may hold values from 0 to 127
- bubble_load: float32 [64, 32, 8192], P(None, 'case', ('px', 'py')), may hold values from -6 to 6
- port_load: float32 [48, 32, 8192], P(None, 'case', ('px', 'py')), may hold values from -3 to 3
- bubble_inverse: float32 [8, 64, 64], replicated, may hold values from -1.5 to 2, as said below
- coupling: float32 [8, 96, 64], replicated, may hold values from -0.1 to 0.1
- port_block: float32 [8, 96, 96], replicated, may hold values from -3 to 8, as said below
Outputs:
- port_solution: float32 [48, 32, 8192], P(None, 'case', ('px', 'py'))
- port_residual: float32 [48, 32, 8192], P(None, 'case', ('px', 'py'))
- bubble_solution: float32 [64, 32, 8192], P(None, 'case', ('px', 'py'))
Inputs may be any that keep to these rules, and one draw needn't show every extreme that they name: `far_owner`: among the 128 components of one partition, at most 3 name the same owner, a bound that some block reaches. `bubble_inverse`: each matrix is symmetric positive definite. `port_block`: each matrix is symmetric positive definite.
All inputs are finite; a program needn't handle non-finite values.
Results may differ from a plain program's by a relative error of at most 0.00016.
Values sent between devices are 32-bit elements; how exact they have to be, the bound alone decides.
No kernel may reach another device: no remote copies, remote signals or barrier semaphores. Data moves between devices by JAX's collectives and lax.ppermute only.
A program may use at most 64 MiB of HBM per device.

v0:
```python
import functools

import jax
import jax.numpy as jnp
from jax import lax
from jax.experimental import pallas as pl
from jax.experimental.pallas import tpu as pltpu
from jax.sharding import PartitionSpec as P

HIGH = lax.Precision.HIGHEST
PLANE = ("px", "py")
F32 = jnp.float32
BF16 = jnp.bfloat16
KINDS = 8
LANES = 128
CASES = 8
SLOTS = 3
NN = (((1,), (0,)), ((), ()))
NT = (((1,), (1,)), ((), ()))
TN = (((0,), (0,)), ((), ()))


def dot(lhs, rhs, dims=NN):
    return lax.dot_general(lhs, rhs, dims, preferred_element_type=F32)


def dot_high(lhs, rhs, dims=NN):
    return lax.dot_general(lhs, rhs, dims, precision=HIGH, preferred_element_type=F32)


def split2(x):
    high = x.astype(BF16)
    return high, (x - high.astype(F32)).astype(BF16)


def split3(x):
    high = x.astype(BF16)
    rest = x - high.astype(F32)
    middle = rest.astype(BF16)
    return high, middle, (rest - middle.astype(F32)).astype(BF16)


def pick_left(onehot, x, dims):
    a, b, c = split3(x)
    return dot(onehot, a, dims) + dot(onehot, b, dims) + dot(onehot, c, dims)


def pick_right(x, onehot, dims):
    a, b, c = split3(x)
    return dot(a, onehot, dims) + dot(b, onehot, dims) + dot(c, onehot, dims)


def iota(shape, dim):
    return lax.broadcasted_iota(jnp.int32, shape, dim)


def column(row):
    return jnp.transpose(jnp.broadcast_to(row, (8, row.shape[1])))[:, :1]


def onehot(mask):
    return mask.astype(F32).astype(BF16)


def owner_slots(owner, parts):
    count = owner.shape[1]
    owner_f = owner.astype(F32)
    same = (column(owner_f) == owner_f) & (iota((count, count), 0) < iota((count, count), 1))
    rank = jnp.sum(same.astype(F32), axis=0, keepdims=True).astype(jnp.int32)
    to = iota((parts, count), 0) == owner
    return [to & (rank == s) for s in range(SLOTS)]


def near_onehot(near):
    count = near.shape[1]
    return onehot(column(near.astype(F32)) == iota((count, LANES), 1).astype(F32))


def stacked_rows(meta, lanes):
    turned = jnp.transpose(meta)
    return jnp.concatenate([turned[lanes + s : lanes + s + 1, :] for s in range(SLOTS)], axis=1)


def port_onehot(meta):
    parts = meta.shape[0]
    ports = (iota((parts, LANES), 1) + 1).astype(F32)
    return onehot(jnp.concatenate([meta[:, s : s + 1] == ports for s in range(SLOTS)], axis=0))


def pad_lanes(x, spare):
    if not spare:
        return x
    return jnp.concatenate([x, jnp.zeros((x.shape[0], spare), x.dtype)], axis=1)


def put(pay_ref, rows, first, pitch):
    parts = pay_ref.shape[0] // pitch
    tiles = rows.shape[1] // LANES
    for g in range(rows.shape[0] // parts):
        for t in range(tiles):
            pay_ref[pl.ds(first + g * tiles + t, parts, stride=pitch), :] = rows[
                g * parts : (g + 1) * parts, t * LANES : (t + 1) * LANES
            ]


def get(pay_ref, first, pitch, tiles):
    parts = pay_ref.shape[0] // pitch
    return jnp.concatenate(
        [
            jnp.concatenate(
                [pay_ref[pl.ds(first + s * tiles + t, parts, stride=pitch), :] for t in range(tiles)],
                axis=1,
            )
            for s in range(SLOTS)
        ],
        axis=0,
    )


def by_kind(products, kind, rows):
    chosen = products[:rows]
    for t in range(1, KINDS):
        chosen = jnp.where(kind == t, products[t * rows : (t + 1) * rows], chosen)
    return chosen


def table_product(high, low, x):
    a, b = split2(x)
    return dot(high, a) + (dot(high, b) + dot(low, a))


def condense_kernel(
    parts, kind_ref, stiff_ref, near_ref, owner_ref, far_ref, load_ref, inverse_ref, coupling_ref,
    pay_ref, near_sum_ref, meta_ref, near_part, far_part,
):
    modes = load_ref.shape[0] // CASES
    dofs = near_sum_ref.shape[0] // CASES
    table = jnp.concatenate(
        [dot_high(coupling_ref[t], inverse_ref[t]) for t in range(KINDS)], axis=0
    )
    high, low = split2(table)
    left = jnp.concatenate([high, high, low], axis=1)
    kind = kind_ref[...]
    kind2 = jnp.concatenate([kind, kind], axis=1)
    for k in range(0, CASES, 2):
        loads = jnp.concatenate(
            [load_ref[pl.ds(k + i, modes, stride=CASES), :] for i in range(2)], axis=1
        )
        a, b = split2(loads)
        condensed = -by_kind(dot(left, jnp.concatenate([a, b, a], axis=0)), kind2, 2 * dofs)
        for i in range(2):
            lanes = slice(i * LANES, (i + 1) * LANES)
            near_part[pl.ds(k + i, dofs, stride=CASES), :] = condensed[:dofs, lanes]
            far_part[pl.ds(k + i, dofs, stride=CASES), :] = condensed[dofs:, lanes]
    near = near_ref[...]
    slots = owner_slots(owner_ref[...], parts)
    near_sum_ref[...] = pick_right(near_part[...], near_onehot(near), NN)
    chosen = onehot(jnp.concatenate(slots, axis=0))
    put(pay_ref, pick_left(chosen, far_part[...], NT), 0, 10)
    lane = iota((parts, LANES), 1)
    far_row = (far_ref[...] + 1).astype(F32)
    near_row = (near + 1).astype(F32)
    message = jnp.zeros((parts, LANES), F32)
    own = jnp.zeros((parts, LANES), F32)
    for s in range(SLOTS):
        for at, row in ((0, far_row), (SLOTS, kind.astype(F32)), (2 * SLOTS, stiff_ref[...])):
            value = jnp.sum(jnp.where(slots[s], row, 0.0), axis=1, keepdims=True)
            message = jnp.where(lane == at + s, value, message)
        value = jnp.sum(jnp.where(slots[s], near_row, 0.0), axis=1, keepdims=True)
        own = jnp.where(lane == s, value, own)
    pay_ref[pl.ds(9, parts, stride=10), :] = message
    meta_ref[...] = own


def tables_kernel(
    kind_ref, stiff_ref, load_ref, inverse_ref, coupling_ref, block_ref,
    near_high, near_low, far_high, far_low, turned_high, turned_low, base_ref,
):
    dofs = block_ref.shape[1] // 2
    modes = inverse_ref.shape[1]
    inverses = []
    for t in range(KINDS):
        reduced = dot_high(coupling_ref[t], inverse_ref[t])
        schur = block_ref[t] - dot_high(reduced, coupling_ref[t], NT)
        near_high[t * dofs : (t + 1) * dofs, :], near_low[t * dofs : (t + 1) * dofs, :] = split2(schur[:dofs])
        far_high[t * dofs : (t + 1) * dofs, :], far_low[t * dofs : (t + 1) * dofs, :] = split2(schur[dofs:])
        turned = jnp.transpose(reduced)
        turned_high[t * modes : (t + 1) * modes, :], turned_low[t * modes : (t + 1) * modes, :] = split2(turned)
        inverses.append(inverse_ref[t])
    high, low = split2(jnp.concatenate(inverses, axis=0))
    kind = kind_ref[...]
    stiff = stiff_ref[...]
    for k in range(CASES):
        loads = load_ref[pl.ds(k, modes, stride=CASES), :]
        base_ref[pl.ds(k, modes, stride=CASES), :] = by_kind(table_product(high, low, loads), kind, modes) / stiff


def send_ports(field, asked, own, pay_ref):
    put(pay_ref, pick_left(jnp.concatenate([asked, own], axis=0), field, NT), 0, 18)


def rhs_kernel(parts, arrived_ref, near_sum_ref, load_ref, meta_ref, field_ref, pay_ref, asked_ref):
    asked = arrived_ref[pl.ds(9, parts, stride=10), :]
    asked_ref[...] = asked
    asked_hot = port_onehot(asked)
    arrived = get(arrived_ref, 0, 10, 3)
    field = load_ref[...] + (near_sum_ref[...] + pick_right(arrived, asked_hot, TN))
    field_ref[...] = field
    send_ports(field, asked_hot, port_onehot(meta_ref[...]), pay_ref)


def apply_kernel(
    parts, last, arrived_ref, field_ref, meta_ref, asked_ref, kind_ref, stiff_ref, near_ref, owner_ref,
    near_high, near_low, far_high, far_low, *rest,
):
    if last:
        image_ref, spread_ref, slot_ref, near_part, far_part = rest
    else:
        image_ref, spread_ref, pay_ref, slot_ref, near_part, far_part = rest
    rows = field_ref.shape[0]
    dofs = rows // CASES
    field = field_ref[...]
    asked = asked_ref[...]
    asked_hot = port_onehot(asked)
    near_hot = near_onehot(near_ref[...])
    slots = onehot(jnp.concatenate(owner_slots(owner_ref[...], parts), axis=0))
    spread_ref[:rows, :] = pick_right(field, near_hot, NT)
    spread_ref[rows:, :] = pick_right(get(arrived_ref, 0, 18, 3), slots, TN)
    groups = slot_ref.shape[0]
    spare = groups * LANES - SLOTS * parts
    wide_hot = asked_hot
    if spare:
        wide_hot = jnp.concatenate([asked_hot, jnp.zeros((spare, LANES), BF16)], axis=0)
    from_near = pad_lanes(jnp.transpose(get(arrived_ref, 9, 18, 3)), spare)
    from_far = pick_right(field, wide_hot, NT)
    for g in range(groups):
        lanes = slice(g * LANES, (g + 1) * LANES)
        slot_ref[g, :rows, :] = from_near[:, lanes]
        slot_ref[g, rows:, :] = from_far[:, lanes]
    kind = kind_ref[...]
    stiff = stiff_ref[...]
    kind2 = jnp.concatenate([kind, kind], axis=1)
    stiff2 = jnp.concatenate([stiff, stiff], axis=1)
    asked_kind = pad_lanes(stacked_rows(asked, SLOTS), spare).astype(jnp.int32)
    asked_stiff = pad_lanes(stacked_rows(asked, 2 * SLOTS), spare)
    for k in range(0, CASES, 2):
        values = jnp.concatenate(
            [spread_ref[pl.ds(k + i, 2 * dofs, stride=CASES), :] for i in range(2)], axis=1
        )
        result = by_kind(table_product(near_high[...], near_low[...], values), kind2, dofs) * stiff2
        for i in range(2):
            near_part[pl.ds(k + i, dofs, stride=CASES), :] = result[:, i * LANES : (i + 1) * LANES]
    for k in range(CASES):
        values = jnp.concatenate(
            [slot_ref[g, pl.ds(k, 2 * dofs, stride=CASES), :] for g in range(groups)], axis=1
        )
        result = by_kind(table_product(far_high[...], far_low[...], values), asked_kind, dofs) * asked_stiff
        for g in range(groups):
            far_part[g, pl.ds(k, dofs, stride=CASES), :] = result[:, g * LANES : (g + 1) * LANES]
    image = pick_right(near_part[...], near_hot, NN)
    for g in range(groups):
        image = image + pick_right(far_part[g], wide_hot[g * LANES : (g + 1) * LANES], NN)
    image_ref[...] = image
    if not last:
        send_ports(image, asked_hot, port_onehot(meta_ref[...]), pay_ref)


def turned_kernel(spread_ref, kind_ref, high_ref, low_ref, out_ref):
    dofs2 = spread_ref.shape[0] // CASES
    modes = out_ref.shape[0] // CASES
    kind = kind_ref[...]
    kind2 = jnp.concatenate([kind, kind], axis=1)
    for k in range(0, CASES, 2):
        values = jnp.concatenate(
            [spread_ref[pl.ds(k + i, dofs2, stride=CASES), :] for i in range(2)], axis=1
        )
        result = by_kind(table_product(high_ref[...], low_ref[...], values), kind2, modes)
        for i in range(2):
            out_ref[pl.ds(k + i, modes, stride=CASES), :] = result[:, i * LANES : (i + 1) * LANES]


def gram_kernel(base_all, image_all, base_ref, image_ref, second_ref, out_ref):
    groups, dofs = base_all.shape[:2]
    total = groups * CASES
    lane = iota((CASES, LANES), 1)
    out = jnp.zeros((CASES, LANES), F32)
    for j0 in range(0, total, 8):
        def step(d, sums):
            own = pl.ds(pl.multiple_of(d * CASES, CASES), CASES)
            base, image, second = base_ref[own, :], image_ref[own, :], second_ref[own, :]
            new = []
            for j in range(8):
                q, i = divmod(j0 + j, CASES)
                bj = base_all[q, d, i : i + 1, :]
                aj = image_all[q, d, i : i + 1, :]
                s = sums[j]
                new.append((s[0] + bj * base, s[1] + bj * image, s[2] + aj * image, s[3] + aj * second))
            return tuple(new)

        zero = jnp.zeros((CASES, LANES), F32)
        sums = lax.fori_loop(0, dofs, step, tuple((zero,) * 4 for _ in range(8)))
        for j in range(8):
            for g in range(4):
                value = jnp.sum(sums[j][g], axis=1, keepdims=True)
                out = jnp.where(lane == g * total + j0 + j, value, out)
    for p in range(out_ref.shape[0]):
        out_ref[p] = out


def sum_kernel(in_ref, out_ref):
    total = in_ref[0]
    for p in range(1, in_ref.shape[0]):
        total = total + in_ref[p]
    for p in range(out_ref.shape[0]):
        out_ref[p] = total


def spd_solve(pairs):
    n = pairs[0][0].shape[0]
    row_of = iota((n, 2 * n), 0)
    work = [jnp.concatenate(pair, axis=1) for pair in pairs]
    for k in range(n):
        nxt = []
        for a in work:
            pivot = a[k : k + 1, :] / a[k : k + 1, k : k + 1]
            nxt.append(jnp.where(row_of == k, pivot, a - a[:, k : k + 1] * pivot))
        work = nxt
    return [a[:, n:] for a in work]


def symmetric(m):
    return 0.5 * (m + jnp.transpose(m))


def finish_kernel(
    case_ref, gram_ref, base_all, image_all, second_all, turned0_all, turned1_all, base_ref, bubble_ref,
    x_ref, residual_ref, bubble_out, turned_coef, coef,
):
    groups, dofs = base_all.shape[:2]
    modes = turned0_all.shape[1]
    n = groups * CASES
    rows = jnp.concatenate([gram_ref[q] for q in range(groups)], axis=0)
    g00, g01, g11, g12 = [symmetric(rows[:, g * n : (g + 1) * n]) for g in range(4)]
    eye = (iota((n, n), 0) == iota((n, n), 1)).astype(F32)
    step0, inverse00 = spd_solve([(g01, g00), (g00, eye)])
    step0_t = jnp.transpose(step0)
    gram1 = g00 - dot_high(g01, step0)
    gram1 = gram1 + jnp.transpose(dot_high(dot_high(g11, step0) - g01, step0, TN))
    gram1 = symmetric(gram1)
    update = eye + dot_high(inverse00, gram1)
    update_t = jnp.transpose(update)
    left = dot_high(update_t, g01) - dot_high(step0_t, g11)
    right = dot_high(update_t, g11) - dot_high(step0_t, g12)
    curvature = symmetric(dot_high(left, update) - dot_high(right, step0))
    (step1,) = spd_solve([(curvature, gram1)])
    first = step0 + dot_high(update, step1)
    second = -dot_high(step0, step1)
    turned_coef[:n, :n] = jnp.transpose(first)
    turned_coef[n:, :n] = jnp.transpose(second)
    at = pl.multiple_of(case_ref[0] * CASES, CASES)
    for h in range(2):
        mine = turned_coef[pl.ds(h * n + at, CASES), :]
        for j in range(n):
            coef[h * n + j] = jnp.broadcast_to(mine[:, j : j + 1], (CASES, LANES))

    def ports(block, carry):
        d0 = block * 4
        for i in range(4):
            d = d0 + i
            own = pl.ds(pl.multiple_of(d * CASES, CASES), CASES)
            x = jnp.zeros((CASES, LANES), F32)
            r = base_ref[own, :]
            for j in range(n):
                q, c = divmod(j, CASES)
                a = image_all[q, d, c : c + 1, :]
                c0, c1 = coef[j], coef[n + j]
                x = x + (c0 * base_all[q, d, c : c + 1, :] + c1 * a)
                r = r - (c0 * a + c1 * second_all[q, d, c : c + 1, :])
            x_ref[own, :] = x
            residual_ref[own, :] = r
        return carry

    lax.fori_loop(0, dofs // 4, ports, 0)

    def bubbles(block, carry):
        for i in range(4):
            d = block * 4 + i
            own = pl.ds(pl.multiple_of(d * CASES, CASES), CASES)
            w = bubble_ref[own, :]
            for j in range(n):
                q, c = divmod(j, CASES)
                w = w - (coef[j] * turned0_all[q, d, c : c + 1, :] + coef[n + j] * turned1_all[q, d, c : c + 1, :])
            bubble_out[own, :] = w
        return carry

    lax.fori_loop(0, modes // 4, bubbles, 0)


def call(kernel, outs, scratch=(), name=None, flops=0, smem=0):
    outs = [jax.ShapeDtypeStruct(shape, dtype) for shape, dtype in outs]
    vmem = pl.BlockSpec(memory_space=pltpu.VMEM)

    def run(*args):
        specs = [pl.BlockSpec(memory_space=pltpu.SMEM)] * smem + [vmem] * (len(args) - smem)
        moved = sum(a.size * a.dtype.itemsize for a in args) + sum(o.size * o.dtype.itemsize for o in outs)
        return pl.pallas_call(
            kernel,
            out_shape=outs,
            in_specs=specs,
            out_specs=[vmem] * len(outs),
            scratch_shapes=[pltpu.VMEM(shape, F32) for shape in scratch],
            compiler_params=pltpu.CompilerParams(vmem_limit_bytes=40 << 20),
            cost_estimate=pl.CostEstimate(flops=flops, bytes_accessed=moved, transcendentals=0),
            name=name,
        )(*args)

    return run


def exchange(rows, parts):
    moved = lax.all_to_all(rows.reshape(parts, 1, -1), PLANE, split_axis=0, concat_axis=0)
    return moved.reshape(rows.shape)


def local(
    comp_type, stiffness, near_port, far_owner, far_port, bubble_load, port_load,
    bubble_inverse, coupling, port_block,
):
    parts = lax.axis_size("px") * lax.axis_size("py")
    groups = lax.axis_size("case")
    modes, cases, comps = bubble_load.shape
    dofs, _, ports = port_load.shape
    rows, bubbles = dofs * cases, modes * cases
    slot_tiles = -(-SLOTS * parts // LANES)
    kind = comp_type.reshape(1, comps)
    stiff = stiffness.reshape(1, comps)
    near = near_port.reshape(1, comps)
    owner = far_owner.reshape(1, comps)
    far = far_port.reshape(1, comps)
    loads = bubble_load.reshape(bubbles, comps)
    field_of = ((rows, ports), F32)
    meta_of = ((parts, LANES), F32)
    pay, near_sum, meta = call(
        functools.partial(condense_kernel, parts),
        [((parts * 10, LANES), F32), field_of, meta_of],
        [(rows, comps)] * 2,
        "condense",
    )(kind, stiff, near, owner, far, loads, bubble_inverse, coupling)
    tables = call(
        tables_kernel,
        [((KINDS * dofs, 2 * dofs), BF16)] * 4 + [((KINDS * modes, 2 * dofs), BF16)] * 2 + [((bubbles, comps), F32)],
        name="tables",
        flops=10**9,
    )(kind, stiff, loads, bubble_inverse, coupling, port_block)
    schur, turned_tables, bubble_base = tables[:4], tables[4:6], tables[6]
    base, pay, asked = call(
        functools.partial(rhs_kernel, parts),
        [field_of, ((parts * 18, LANES), F32), meta_of],
        name="rhs",
    )(exchange(pay, parts), near_sum, port_load.reshape(rows, ports), meta)

    def operator(field, pay, last):
        spread_of = ((2 * rows, comps), F32)
        return call(
            functools.partial(apply_kernel, parts, last),
            [field_of, spread_of] + ([] if last else [((parts * 18, LANES), F32)]),
            [(slot_tiles, 2 * rows, LANES), (rows, comps), (slot_tiles, rows, LANES)],
            "apply",
        )(exchange(pay, parts), field, meta, asked, kind, stiff, near, owner, *schur)

    def turned(spread):
        return call(turned_kernel, [((bubbles, comps), F32)], name="turned", flops=10**9)(
            spread, kind, *turned_tables
        )[0]

    def all_cases(field):
        return lax.all_gather(field.reshape(-1, cases, LANES), "case")

    base_all = all_cases(base)
    image, spread, pay = operator(base, pay, False)
    image_all = all_cases(image)
    turned0_all = all_cases(turned(spread))
    second, spread = operator(image, pay, True)
    second_all = all_cases(second)
    turned1_all = all_cases(turned(spread))
    (copies,) = call(gram_kernel, [((parts, cases, LANES), F32)], name="gram")(
        base_all, image_all, base, image, second
    )
    (copies,) = call(sum_kernel, [((groups, cases, LANES), F32)], name="sum")(
        lax.all_to_all(copies, PLANE, split_axis=0, concat_axis=0)
    )
    gram = lax.all_to_all(copies, "case", split_axis=0, concat_axis=0)
    x, residual, bubble = call(
        finish_kernel,
        [field_of, field_of, ((bubbles, comps), F32)],
        [(2 * groups * cases, LANES), (2 * groups * cases, cases, LANES)],
        "finish",
        smem=1,
    )(
        lax.axis_index("case").reshape(1), gram, base_all, image_all, second_all,
        turned0_all, turned1_all, base, bubble_base,
    )
    return (
        x.reshape(port_load.shape),
        residual.reshape(port_load.shape),
        bubble.reshape(bubble_load.shape),
    )


def solution(mesh):
    placed = (
        P(PLANE),
        P(PLANE),
        P(PLANE),
        P(PLANE, None),
        P(PLANE),
        P(None, "case", PLANE),
        P(None, "case", PLANE),
        P(),
        P(),
        P(),
    )
    out = P(None, "case", PLANE)
    return jax.shard_map(
        local, mesh=mesh, in_specs=placed, out_specs=(out, out, out), check_vma=False
    )
```

profile of v0, /device:TPU:1, one launch (start us, length us, event | category | flops | bytes accessed | tf_op | source)
XLA Modules:
  0.0 192.3 jit_solution(9903284538952168657)
XLA Ops:
  7.2 0.0 copy-start.3
  7.2 0.0 copy-start.2
  7.2 1.2 copy.15.coupling_ref
  8.4 0.0 copy-start.8
  8.4 0.0 copy-start.9
  8.4 0.0 copy-start.5
  8.4 0.0 copy-start.6
  8.4 0.0 copy-start.7
  8.4 0.0 copy-done.3
  8.4 0.0 copy-done.2
  8.4 0.6 copy-done.8
  9.0 0.0 copy-done.9
  9.0 0.0 copy-done.5
  9.1 0.0 copy-done.6
  9.1 0.0 copy-done.7
  9.1 1.5 condense.1
  10.5 0.0 copy-start.4
  10.6 26.4 %all_to_all.25 = f32[64,1,1280]{2,1,0:T(1,128)S(1)} all-to-all(f32[64,1,1280]{2,1,0:T(1,128)S(1)} %bitcast.29), channel_id=1, replica_groups=mesh['px'=8,'py'=8,'case'=4] {'px','py'}, dimensions={0} | all-to-all | bytes 655360 | tf_op jit(solution)/shard_map/all_to_all | solution.py:421
  36.9 0.0 copy-done.4
  36.9 1.7 rhs.1
  38.6 6.3 %all-to-all-start.1 = ((f32[64,1,2304]{2,1,0:T(1,128)}), f32[64,1,2304]{2,1,0:T(1,128)S(1)}, u32[]{:S(2)}, u32[]{:S(2)}) async-start(f32[64,1,2304]{2,1,0:T(1,128)} %bitcast.11), calls=%async_computation.1 | async-start | bytes 1179648 | tf_op jit(solution)/shard_map/all_to_all | solution.py:421
  44.9 0.0 all-gather.3.cloned.1.call-start
  45.0 2.5 %tables.1 = (bf16[384,96]{1,0:T(8,128)(2,1)S(1)}, bf16[384,96]{1,0:T(8,128)(2,1)S(1)}, bf16[384,96]{1,0:T(8,128)(2,1)S(1)}, bf16[384,96]{1,0:T(8,128)(2,1)S(1)},...) custom-call(s32[1,128]{1,0:T(1,128)S(1)} %bitcast.44, f32[1,128]{1,0:T(1,128)S(1)} %bitcast.34, ...), custom_call_target="tpu_custom_call" | custom-call | flops 1000000000 | bytes 1639424 | tf_op jit(solution)/shard_map/tables/pallas_call | solution.py:406
  47.5 0.0 copy-start.11
  47.5 16.0 %all-to-all-done.1 = f32[64,1,2304]{2,1,0:T(1,128)S(1)} async-done(((f32[64,1,2304]{2,1,0:T(1,128)}), f32[64,1,2304]{2,1,0:T(1,128)S(1)}, u32[]{:S(2)}, u32[]{:S(2)}) %all-to-all-start.1) | async-done | bytes 589856 | tf_op jit(solution)/shard_map/all_to_all | solution.py:421
  63.5 3.7 %apply.2 = (f32[384,128]{1,0:T(8,128)S(1)}, f32[768,128]{1,0:T(8,128)S(1)}, f32[1152,128]{1,0:T(8,128)S(1)}) custom-call(f32[1152,128]{1,0:T(8,128)S(1)} %bitcast.23, f32[384,128]{1,0:T(8,128)S(1)} %get-tuple-element.27.field_ref.base_ref, f32[64,128]{1,0:T(8,128)S(1)} %get-tuple-element.26.meta_ref, f32[64,128]{1,0:T(8,128)S(1)} %get-tuple-element.29.asked_ref, ...), custom_call_target="tpu_custom_call" | custom-call | bytes 2328576 | tf_op jit(solution)/shard_map/apply/pallas_call | solution.py:406
  67.2 0.0 copy-done.11
  67.3 1.7 turned.2
  68.9 0.0 all-gather.3.cloned.1.call-update
  69.0 0.0 all-gather.5.cloned.1.call-start
  69.0 24.9 %all_to_all.26 = f32[64,1,2304]{2,1,0:T(1,128)S(1)} all-to-all(f32[64,1,2304]{2,1,0:T(1,128)S(1)} %bitcast.28), channel_id=1, replica_groups=mesh['px'=8,'py'=8,'case'=4] {'px','py'}, dimensions={0} | all-to-all | bytes 1179648 | tf_op jit(solution)/shard_map/all_to_all | solution.py:421
  93.9 3.2 %apply.3 = (f32[384,128]{1,0:T(8,128)S(1)}, f32[768,128]{1,0:T(8,128)S(1)}) custom-call(f32[1152,128]{1,0:T(8,128)S(1)} %bitcast.24, f32[384,128]{1,0:T(8,128)S(1)} %get-tuple-element.34.field_ref.image_ref, f32[64,128]{1,0:T(8,128)S(1)} %get-tuple-element.26.meta_ref, f32[64,128]{1,0:T(8,128)S(1)} %get-tuple-element.29.asked_ref, s32[1,128]{1,0:T(1,128)S(1)} %bitcast.47, ...), custom_call_target="tpu_custom_call" | custom-call | bytes 1738752 | tf_op jit(solution)/shard_map/apply/pallas_call | solution.py:406
  97.1 0.0 copy-done.12
  97.2 1.7 turned.3
  98.8 0.0 all-gather.5.cloned.1.call-update
  98.9 12.5 %all_gather.15.base_all = f32[4,48,8,128]{3,2,1,0:T(8,128)S(1)} all-gather(f32[1,48,8,128]{3,2,1,0:T(8,128)S(1)} %bitcast.22), channel_id=1, replica_groups=mesh['px'=8,'py'=8,'case'=4] {'case'}, dimensions={0}, use_global_device_ids=true | all-gather | bytes 983040 | tf_op jit(solution)/shard_map/all_gather | solution.py:477
  111.4 15.3 %all_gather.16.image_all = f32[4,48,8,128]{3,2,1,0:T(8,128)S(1)} all-gather(f32[1,48,8,128]{3,2,1,0:T(8,128)S(1)} %bitcast.25), channel_id=1, replica_groups=mesh['px'=8,'py'=8,'case'=4] {'case'}, dimensions={0}, use_global_device_ids=true | all-gather | bytes 983040 | tf_op jit(solution)/shard_map/all_gather | solution.py:477
  126.7 4.9 %gram.1 = f32[64,8,128]{2,1,0:T(8,128)} custom-call(f32[4,48,8,128]{3,2,1,0:T(8,128)S(1)} %all_gather.15.base_all, f32[4,48,8,128]{3,2,1,0:T(8,128)S(1)} %all_gather.16.image_all, f32[384,128]{1,0:T(8,128)S(1)} %get-tuple-element.27.field_ref.base_ref, f32[384,128]{1,0:T(8,128)S(1)} %get-tuple-element.34.field_ref.image_ref, ...), custom_call_target="tpu_custom_call" | custom-call | bytes 2424832 | tf_op jit(solution)/shard_map/gram/pallas_call | solution.py:406
  131.6 10.9 %all-to-all-start.3 = ((f32[64,8,128]{2,1,0:T(8,128)}), f32[64,8,128]{2,1,0:T(8,128)S(1)}, u32[]{:S(2)}, u32[]{:S(2)}) async-start(f32[64,8,128]{2,1,0:T(8,128)} %gram.1), calls=%async_computation.3 | async-start | bytes 524288 | tf_op jit(solution)/shard_map/all_to_all | solution.py:490
  142.5 12.0 %all-to-all-done.3.in_ref = f32[64,8,128]{2,1,0:T(8,128)S(1)} async-done(((f32[64,8,128]{2,1,0:T(8,128)}), f32[64,8,128]{2,1,0:T(8,128)S(1)}, u32[]{:S(2)}, u32[]{:S(2)}) %all-to-all-start.3) | async-done | bytes 262176 | tf_op jit(solution)/shard_map/all_to_all | solution.py:490
  154.6 0.7 sum.1
  155.2 3.3 %all-to-all-start.4 = ((f32[4,8,128]{2,1,0:T(8,128)}), f32[4,8,128]{2,1,0:T(8,128)S(1)}, u32[]{:S(2)}, u32[]{:S(2)}) async-start(f32[4,8,128]{2,1,0:T(8,128)} %sum.1), calls=%async_computation.4 | async-start | bytes 32768 | tf_op jit(solution)/shard_map/all_to_all | solution.py:492
  158.5 12.2 %all_gather.17.second_all = f32[4,48,8,128]{3,2,1,0:T(8,128)S(1)} all-gather(f32[1,48,8,128]{3,2,1,0:T(8,128)S(1)} %bitcast.27), channel_id=1, replica_groups=mesh['px'=8,'py'=8,'case'=4] {'case'}, dimensions={0}, use_global_device_ids=true | all-gather | bytes 983040 | tf_op jit(solution)/shard_map/all_gather | solution.py:477
  170.7 0.0 all-to-all-done.4.gram_ref
  170.7 0.0 all-gather.5.cloned.1.call-done.turned1_all
  170.7 1.2 copy-done
  171.9 1.2 copy-done.1
  173.2 12.3 %finish.1 = (f32[384,128]{1,0:T(8,128)}, f32[384,128]{1,0:T(8,128)}, f32[512,128]{1,0:T(8,128)}) custom-call(s32[1]{0:T(128)} %bitcast.case_ref, f32[4,8,128]{2,1,0:T(8,128)S(1)} %all-to-all-done.4.gram_ref, f32[4,48,8,128]{3,2,1,0:T(8,128)S(1)} %all_gather.15.base_all, f32[4,48,8,128]{3,2,1,0:T(8,128)S(1)} %all_gather.16.image_all, ...), custom_call_target="tpu_custom_call" | custom-call | bytes 5586948 | tf_op jit(solution)/shard_map/finish/pallas_call | solution.py:406
  (6 shorter events, 0.0 us)
Async XLA Ops:
  7.2 1.3 copy-start.3
  7.2 1.3 copy-start.2
  8.4 0.7 copy-start.8
  8.4 0.7 copy-start.9
  8.4 0.7 copy-start.5
  8.4 0.7 copy-start.6
  8.4 0.7 copy-start.7
  10.5 26.4 %copy-start.4 = (f32[48,8,128]{2,1,0:T(8,128)S(1)}, f32[48,8,128]{2,1,0:T(8,128)}, u32[]{:S(2)}) copy-start(f32[48,8,128]{2,1,0:T(8,128)} %param.16) | copy-start | bytes 589828
  38.6 6.4 %copy-start.10 = (f32[8,96,96]{2,1,0:T(8,128)S(1)}, f32[8,96,96]{2,1,0:T(8,128)}, u32[]{:S(2)}) copy-start(f32[8,96,96]{2,1,0:T(8,128)} %block_ref.1) | copy-start | bytes 884740
  38.6 24.9 %all-to-all-start.1 = ((f32[64,1,2304]{2,1,0:T(1,128)}), f32[64,1,2304]{2,1,0:T(1,128)S(1)}, u32[]{:S(2)}, u32[]{:S(2)}) async-start(f32[64,1,2304]{2,1,0:T(1,128)} %bitcast.11), calls=%async_computation.1 | async-start | bytes 1179648 | tf_op jit(solution)/shard_map/all_to_all | solution.py:421
  44.9 125.7 %all-gather.3.cloned.1.call-start = ((), (), s32[]{:S(2)}) async-start(), calls=%async_computation.5 | async-start | bytes 1310720 | tf_op jit(solution)/shard_map/all_gather | solution.py:477
  47.5 19.7 %copy-start.11 = (bf16[512,96]{1,0:T(8,128)(2,1)}, bf16[512,96]{1,0:T(8,128)(2,1)S(1)}, u32[]{:S(2)}) copy-start(bf16[512,96]{1,0:T(8,128)(2,1)S(1)} %get-tuple-element.39.low_ref) | copy-start | bytes 294916
  69.0 101.7 %all-gather.5.cloned.1.call-start = ((), (), s32[]{:S(2)}) async-start(), calls=%async_computation.6 | async-start | bytes 1310720 | tf_op jit(solution)/shard_map/all_gather | solution.py:477
  93.9 3.2 %copy-start.12 = (bf16[512,96]{1,0:T(8,128)(2,1)S(1)}, bf16[512,96]{1,0:T(8,128)(2,1)}, u32[]{:S(2)}) copy-start(bf16[512,96]{1,0:T(8,128)(2,1)} %copy-done.11) | copy-start | bytes 294916
  131.6 23.0 %all-to-all-start.3 = ((f32[64,8,128]{2,1,0:T(8,128)}), f32[64,8,128]{2,1,0:T(8,128)S(1)}, u32[]{:S(2)}, u32[]{:S(2)}) async-start(f32[64,8,128]{2,1,0:T(8,128)} %gram.1), calls=%async_computation.3 | async-start | bytes 524288 | tf_op jit(solution)/shard_map/all_to_all | solution.py:490
  155.2 15.5 %all-to-all-start.4 = ((f32[4,8,128]{2,1,0:T(8,128)}), f32[4,8,128]{2,1,0:T(8,128)S(1)}, u32[]{:S(2)}, u32[]{:S(2)}) async-start(f32[4,8,128]{2,1,0:T(8,128)} %sum.1), calls=%async_computation.4 | async-start | bytes 32768 | tf_op jit(solution)/shard_map/all_to_all | solution.py:492
  170.7 1.2 copy-start
  171.9 1.2 copy-start.1
Sparse Core Ops, SparseCore 0:
  69.1 22.7 all-gather.2
  99.0 27.1 all-gather.4
where the time goes:
time: 195 us; the launch traced here: 192 us
  blocking collectives  91.3 us (47%)
  Pallas kernels  33.8 us (17%)
  waiting for transfers between devices  28.1 us (14%)
  starting transfers between devices  20.6 us (11%)
  between operations  14.2 us (7%)
  local copies, waits for them, and re-layouts  4.31 us (2%)
    all_to_all x2, blocking collectives, exchange(): lax.all_to_all(rows.reshape(parts, 1, -1), PLANE, split_axis=0, concat_ax...  51.2 us
    all_gather x3, blocking collectives, all_cases(): return lax.all_gather(field.reshape(-1, cases, LANES), 'case')  40 us
    pallas_call x10, Pallas kernels, run(): pl.pallas_call(kernel, out_shape=outs, in_specs=specs, out_specs=[vmem] *...  33.8 us
    all_to_all x1, waiting for transfers between devices, exchange(): lax.all_to_all(rows.reshape(parts, 1, -1), PLANE, split_axis=0, concat_ax...  16 us
    all_to_all x1, waiting for transfers between devices, local(): lax.all_to_all(copies, PLANE, split_axis=0, concat_axis=0)  12 us
    all_to_all x1, starting transfers between devices, local(): lax.all_to_all(copies, PLANE, split_axis=0, concat_axis=0)  10.9 us
    all_to_all x1, starting transfers between devices, exchange(): lax.all_to_all(rows.reshape(parts, 1, -1), PLANE, split_axis=0, concat_ax...  6.31 us
    unnamed x27, local copies, waits for them, and re-layouts  4.31 us
  transfers between devices with their start and end apart: 5, of which 2 were waited for; matrix products, arithmetic and copies ran while one was open for 0% of the time, Pallas kernels for 7%

commit v1 on v0

--- a/solution.py
+++ b/solution.py
@@ -210,11 +210,12 @@
 
 
 def apply_kernel(
-    parts, last, arrived_ref, field_ref, meta_ref, asked_ref, kind_ref, stiff_ref, near_ref, owner_ref,
-    near_high, near_low, far_high, far_low, *rest,
+    parts, groups, last, arrived_ref, meta_ref, asked_ref, kind_ref, stiff_ref, near_ref, owner_ref,
+    near_high, near_low, far_high, far_low, field_ref, *rest,
 ):
     if last:
-        image_ref, spread_ref, slot_ref, near_part, far_part = rest
+        others, rest = rest[: groups - 1], rest[groups - 1 :]
+        gram_ref, case_ref, image_ref, spread_ref, copies_ref, slot_ref, near_part, far_part = rest
     else:
         image_ref, spread_ref, pay_ref, slot_ref, near_part, far_part = rest
     rows = field_ref.shape[0]
@@ -226,14 +227,14 @@
     slots = onehot(jnp.concatenate(owner_slots(owner_ref[...], parts), axis=0))
     spread_ref[:rows, :] = pick_right(field, near_hot, NT)
     spread_ref[rows:, :] = pick_right(get(arrived_ref, 0, 18, 3), slots, TN)
-    groups = slot_ref.shape[0]
-    spare = groups * LANES - SLOTS * parts
+    tiles = slot_ref.shape[0]
+    spare = tiles * LANES - SLOTS * parts
     wide_hot = asked_hot
     if spare:
         wide_hot = jnp.concatenate([asked_hot, jnp.zeros((spare, LANES), BF16)], axis=0)
     from_near = pad_lanes(jnp.transpose(get(arrived_ref, 9, 18, 3)), spare)
     from_far = pick_right(field, wide_hot, NT)
-    for g in range(groups):
+    for g in range(tiles):
         lanes = slice(g * LANES, (g + 1) * LANES)
         slot_ref[g, :rows, :] = from_near[:, lanes]
         slot_ref[g, rows:, :] = from_far[:, lanes]
@@ -252,16 +253,22 @@
             near_part[pl.ds(k + i, dofs, stride=CASES), :] = result[:, i * LANES : (i + 1) * LANES]
     for k in range(CASES):
         values = jnp.concatenate(
-            [slot_ref[g, pl.ds(k, 2 * dofs, stride=CASES), :] for g in range(groups)], axis=1
+            [slot_ref[g, pl.ds(k, 2 * dofs, stride=CASES), :] for g in range(tiles)], axis=1
         )
         result = by_kind(table_product(far_high[...], far_low[...], values), asked_kind, dofs) * asked_stiff
-        for g in range(groups):
+        for g in range(tiles):
             far_part[g, pl.ds(k, dofs, stride=CASES), :] = result[:, g * LANES : (g + 1) * LANES]
     image = pick_right(near_part[...], near_hot, NN)
-    for g in range(groups):
+    for g in range(tiles):
         image = image + pick_right(far_part[g], wide_hot[g * LANES : (g + 1) * LANES], NN)
     image_ref[...] = image
-    if not last:
+    if last:
+        gram = add_products(
+            LANES, [field_ref, *others], [image_ref], [3 * groups * CASES], case_ref[0], gram_ref[...]
+        )
+        for p in range(parts):
+            copies_ref[p] = gram
+    else:
         send_ports(image, asked_hot, port_onehot(meta_ref[...]), pay_ref)
 
 
@@ -279,40 +286,44 @@
             out_ref[pl.ds(k + i, modes, stride=CASES), :] = result[:, i * LANES : (i + 1) * LANES]
 
 
-def gram_kernel(base_all, image_all, base_ref, image_ref, second_ref, out_ref):
-    groups, dofs = base_all.shape[:2]
+def add_products(lanes, lefts, rights, first, case, out):
+    groups = len(lefts)
     total = groups * CASES
+    dofs = lefts[0].shape[0] // CASES
     lane = iota((CASES, LANES), 1)
-    out = jnp.zeros((CASES, LANES), F32)
-    for j0 in range(0, total, 8):
+    for h in range(groups):
         def step(d, sums):
             own = pl.ds(pl.multiple_of(d * CASES, CASES), CASES)
-            base, image, second = base_ref[own, :], image_ref[own, :], second_ref[own, :]
+            values = [ref[own, :] for ref in rights]
             new = []
-            for j in range(8):
-                q, i = divmod(j0 + j, CASES)
-                bj = base_all[q, d, i : i + 1, :]
-                aj = image_all[q, d, i : i + 1, :]
-                s = sums[j]
-                new.append((s[0] + bj * base, s[1] + bj * image, s[2] + aj * image, s[3] + aj * second))
+            for i in range(CASES):
+                row = lefts[h][pl.ds(d * CASES + i, 1), :]
+                new.append(tuple(s + row * v for s, v in zip(sums[i], values)))
             return tuple(new)
 
         zero = jnp.zeros((CASES, LANES), F32)
-        sums = lax.fori_loop(0, dofs, step, tuple((zero,) * 4 for _ in range(8)))
-        for j in range(8):
-            for g in range(4):
-                value = jnp.sum(sums[j][g], axis=1, keepdims=True)
-                out = jnp.where(lane == g * total + j0 + j, value, out)
-    for p in range(out_ref.shape[0]):
-        out_ref[p] = out
+        sums = lax.fori_loop(0, dofs, step, ((zero,) * len(rights),) * CASES)
+        at = lax.rem(case + h, groups) * CASES
+        for i in range(CASES):
+            for g in range(len(rights)):
+                value = jnp.sum(sums[i][g], axis=1, keepdims=True)
+                out = jnp.where(lane == first[g] + at + i, value, out)
+    return out
+
+
+def gram_kernel(groups, case_ref, *refs):
+    base, image, out_ref = refs[:groups], refs[groups : 2 * groups], refs[2 * groups]
+    total = groups * CASES
+    out = jnp.zeros((CASES, LANES), F32)
+    out = add_products(LANES, base, [base[0], image[0]], [0, total], case_ref[0], out)
+    out_ref[...] = add_products(LANES, image, [image[0]], [2 * total], case_ref[0], out)
 
 
 def sum_kernel(in_ref, out_ref):
     total = in_ref[0]
     for p in range(1, in_ref.shape[0]):
         total = total + in_ref[p]
-    for p in range(out_ref.shape[0]):
-        out_ref[p] = total
+    out_ref[...] = total
 
 
 def spd_solve(pairs):
@@ -332,15 +343,13 @@
     return 0.5 * (m + jnp.transpose(m))
 
 
-def finish_kernel(
-    case_ref, gram_ref, base_all, image_all, second_all, turned0_all, turned1_all, base_ref, bubble_ref,
-    x_ref, residual_ref, bubble_out, turned_coef, coef,
-):
-    groups, dofs = base_all.shape[:2]
-    modes = turned0_all.shape[1]
+def solve_kernel(groups, case_ref, *refs):
+    grams, coef, rows_ref, turned_coef = refs[:groups], refs[groups], refs[groups + 1], refs[groups + 2]
     n = groups * CASES
-    rows = jnp.concatenate([gram_ref[q] for q in range(groups)], axis=0)
-    g00, g01, g11, g12 = [symmetric(rows[:, g * n : (g + 1) * n]) for g in range(4)]
+    for h in range(groups):
+        at = pl.multiple_of(lax.rem(case_ref[0] + h, groups) * CASES, CASES)
+        rows_ref[pl.ds(at, CASES), :] = grams[h][...]
+    g00, g01, g11, g12 = [symmetric(rows_ref[:, g * n : (g + 1) * n]) for g in range(4)]
     eye = (iota((n, n), 0) == iota((n, n), 1)).astype(F32)
     step0, inverse00 = spd_solve([(g01, g00), (g00, eye)])
     step0_t = jnp.transpose(step0)
@@ -353,29 +362,37 @@
     right = dot_high(update_t, g11) - dot_high(step0_t, g12)
     curvature = symmetric(dot_high(left, update) - dot_high(right, step0))
     (step1,) = spd_solve([(curvature, gram1)])
-    first = step0 + dot_high(update, step1)
-    second = -dot_high(step0, step1)
-    turned_coef[:n, :n] = jnp.transpose(first)
-    turned_coef[n:, :n] = jnp.transpose(second)
+    first = jnp.transpose(step0 + dot_high(update, step1))
+    second = jnp.transpose(-dot_high(step0, step1))
+    turned_coef[:n, :] = jnp.concatenate([first] * (LANES // n), axis=1)
+    turned_coef[n:, :] = jnp.concatenate([second] * (LANES // n), axis=1)
     at = pl.multiple_of(case_ref[0] * CASES, CASES)
     for h in range(2):
-        mine = turned_coef[pl.ds(h * n + at, CASES), :]
+        mine = pltpu.roll(turned_coef[pl.ds(h * n + at, CASES), :], LANES - case_ref[0] * CASES, 1)
         for j in range(n):
             coef[h * n + j] = jnp.broadcast_to(mine[:, j : j + 1], (CASES, LANES))
 
+
+def finish_kernel(groups, coef, bubble_ref, *refs):
+    base, image, second, turned0, turned1 = [refs[g * groups : (g + 1) * groups] for g in range(5)]
+    x_ref, residual_ref, bubble_out = refs[5 * groups :]
+    n = groups * CASES
+    dofs = x_ref.shape[0] // CASES
+    modes = bubble_out.shape[0] // CASES
+
     def ports(block, carry):
-        d0 = block * 4
         for i in range(4):
-            d = d0 + i
+            d = block * 4 + i
             own = pl.ds(pl.multiple_of(d * CASES, CASES), CASES)
             x = jnp.zeros((CASES, LANES), F32)
-            r = base_ref[own, :]
+            r = base[0][own, :]
             for j in range(n):
                 q, c = divmod(j, CASES)
-                a = image_all[q, d, c : c + 1, :]
+                row = pl.ds(d * CASES + c, 1)
+                a = image[q][row, :]
                 c0, c1 = coef[j], coef[n + j]
-                x = x + (c0 * base_all[q, d, c : c + 1, :] + c1 * a)
-                r = r - (c0 * a + c1 * second_all[q, d, c : c + 1, :])
+                x = x + (c0 * base[q][row, :] + c1 * a)
+                r = r - (c0 * a + c1 * second[q][row, :])
             x_ref[own, :] = x
             residual_ref[own, :] = r
         return carry
@@ -389,19 +406,20 @@
             w = bubble_ref[own, :]
             for j in range(n):
                 q, c = divmod(j, CASES)
-                w = w - (coef[j] * turned0_all[q, d, c : c + 1, :] + coef[n + j] * turned1_all[q, d, c : c + 1, :])
+                row = pl.ds(d * CASES + c, 1)
+                w = w - (coef[j] * turned0[q][row, :] + coef[n + j] * turned1[q][row, :])
             bubble_out[own, :] = w
         return carry
 
     lax.fori_loop(0, modes // 4, bubbles, 0)
 
 
-def call(kernel, outs, scratch=(), name=None, flops=0, smem=0):
+def call(kernel, outs, scratch=(), name=None, flops=0, smem=()):
     outs = [jax.ShapeDtypeStruct(shape, dtype) for shape, dtype in outs]
     vmem = pl.BlockSpec(memory_space=pltpu.VMEM)
 
     def run(*args):
-        specs = [pl.BlockSpec(memory_space=pltpu.SMEM)] * smem + [vmem] * (len(args) - smem)
+        specs = [pl.BlockSpec(memory_space=pltpu.SMEM) if i in smem else vmem for i in range(len(args))]
         moved = sum(a.size * a.dtype.itemsize for a in args) + sum(o.size * o.dtype.itemsize for o in outs)
         return pl.pallas_call(
             kernel,
@@ -459,14 +477,9 @@
         name="rhs",
     )(exchange(pay, parts), near_sum, port_load.reshape(rows, ports), meta)
 
-    def operator(field, pay, last):
-        spread_of = ((2 * rows, comps), F32)
-        return call(
-            functools.partial(apply_kernel, parts, last),
-            [field_of, spread_of] + ([] if last else [((parts * 18, LANES), F32)]),
-            [(slot_tiles, 2 * rows, LANES), (rows, comps), (slot_tiles, rows, LANES)],
-            "apply",
-        )(exchange(pay, parts), field, meta, asked, kind, stiff, near, owner, *schur)
+    case = lax.axis_index("case").reshape(1)
+    spread_of = ((2 * rows, comps), F32)
+    scratch = [(slot_tiles, 2 * rows, LANES), (rows, comps), (slot_tiles, rows, LANES)]
 
     def turned(spread):
         return call(turned_kernel, [((bubbles, comps), F32)], name="turned", flops=10**9)(
@@ -474,32 +487,53 @@
         )[0]
 
     def all_cases(field):
-        return lax.all_gather(field.reshape(-1, cases, LANES), "case")
-
+        return [field] + [
+            lax.ppermute(field, "case", [((k + h) % groups, k) for k in range(groups)])
+            for h in range(1, groups)
+        ]
+
+    arrived = exchange(pay, parts)
     base_all = all_cases(base)
-    image, spread, pay = operator(base, pay, False)
+    arrived, *base_all = lax.optimization_barrier((arrived, *base_all))
+    shared = (meta, asked, kind, stiff, near, owner, *schur)
+    image, spread, pay = call(
+        functools.partial(apply_kernel, parts, groups, False),
+        [field_of, spread_of, ((parts * 18, LANES), F32)],
+        scratch,
+        "apply",
+    )(arrived, *shared, base_all[0])
+    arrived = exchange(pay, parts)
     image_all = all_cases(image)
     turned0_all = all_cases(turned(spread))
-    second, spread = operator(image, pay, True)
+    (gram,) = call(functools.partial(gram_kernel, groups), [((cases, LANES), F32)], name="gram", smem=(0,))(
+        case, *base_all, *image_all
+    )
+    arrived, *turned0_all = lax.optimization_barrier((arrived, *turned0_all))
+    second, spread, copies = call(
+        functools.partial(apply_kernel, parts, groups, True),
+        [field_of, spread_of, ((parts, cases, LANES), F32)],
+        scratch,
+        "apply_last",
+        smem=(12 + groups,),
+    )(arrived, *shared, *image_all, gram, case)
+    copies = lax.all_to_all(copies, PLANE, split_axis=0, concat_axis=0)
     second_all = all_cases(second)
     turned1_all = all_cases(turned(spread))
-    (copies,) = call(gram_kernel, [((parts, cases, LANES), F32)], name="gram")(
-        base_all, image_all, base, image, second
-    )
-    (copies,) = call(sum_kernel, [((groups, cases, LANES), F32)], name="sum")(
-        lax.all_to_all(copies, PLANE, split_axis=0, concat_axis=0)
-    )
-    gram = lax.all_to_all(copies, "case", split_axis=0, concat_axis=0)
+    copies, *rest = lax.optimization_barrier((copies, *second_all, *turned1_all))
+    second_all, turned1_all = rest[:groups], rest[groups:]
+    (gram,) = call(sum_kernel, [((cases, LANES), F32)], name="sum")(copies)
+    (coef,) = call(
+        functools.partial(solve_kernel, groups),
+        [((2 * groups * cases, cases, LANES), F32)],
+        [(groups * cases, LANES), (2 * groups * cases, LANES)],
+        "solve",
+        smem=(0,),
+    )(case, *all_cases(gram))
     x, residual, bubble = call(
-        finish_kernel,
+        functools.partial(finish_kernel, groups),
         [field_of, field_of, ((bubbles, comps), F32)],
-        [(2 * groups * cases, LANES), (2 * groups * cases, cases, LANES)],
-        "finish",
-        smem=1,
-    )(
-        lax.axis_index("case").reshape(1), gram, base_all, image_all, second_all,
-        turned0_all, turned1_all, base, bubble_base,
-    )
+        name="finish",
+    )(coef, bubble_base, *base_all, *image_all, *second_all, *turned0_all, *turned1_all)
     return (
         x.reshape(port_load.shape),
         residual.reshape(port_load.shape),

time: 195 us -> 173 us (0.89)
  blocking collectives: 91.3 us -> 26.4 us
  starting transfers between devices: 20.6 us -> 50.1 us
  waiting for transfers between devices: 28.1 us -> 43.9 us
  between operations: 14.2 us -> 0.87 us
  local copies, waits for them, and re-layouts: 4.31 us -> 14.9 us
    all_gather x3 -> x0, blocking collectives: 40 us -> none  [all_cases(): return lax.all_gather(field.reshape(-1, cases, LANES), 'case')]
    ppermute x0 -> x18, waiting for transfers between devices: none -> 37.9 us  [all_cases(): lax.ppermute(field, 'case', [((k + h) % groups, k) for k in range(groups)])]
    ppermute x0 -> x18, starting transfers between devices: none -> 25.7 us  [all_cases(): lax.ppermute(field, 'case', [((k + h) % groups, k) for k in range(groups)])]
    all_to_all x2 -> x1, blocking collectives: 51.2 us -> 26.4 us  [exchange(): lax.all_to_all(rows.reshape(parts, 1, -1), PLANE, split_axis=0, concat_ax...]
    all_to_all x2 -> x1, waiting for transfers between devices: 12 us -> 0.01 us  [local(): copies = lax.all_to_all(copies, PLANE, split_axis=0, concat_axis=0)]
    unnamed x27 -> x59, local copies, waits for them, and re-layouts: 4.31 us -> 14.9 us
    all_to_all x1 -> x2, waiting for transfers between devices: 16 us -> 6.06 us  [exchange(): lax.all_to_all(rows.reshape(parts, 1, -1), PLANE, split_axis=0, concat_ax...]
    all_to_all x1 -> x2, starting transfers between devices: 6.31 us -> 12.7 us  [exchange(): lax.all_to_all(rows.reshape(parts, 1, -1), PLANE, split_axis=0, concat_ax...]
  transfers between devices with their start and end apart: 5 -> 21, of which waited for: 2 -> 8; matrix products, arithmetic and copies ran while one was open for 0% -> 0% of each run, Pallas kernels for 7% -> 5%
where the time goes in v1:
time: 173 us; the launch traced here: 172 us
  starting transfers between devices  50.1 us (29%)
  waiting for transfers between devices  43.9 us (25%)
  Pallas kernels  35.6 us (21%)
  blocking collectives  26.4 us (15%)
  local copies, waits for them, and re-layouts  14.9 us (9%)
    ppermute x18, waiting for transfers between devices, all_cases(): lax.ppermute(field, 'case', [((k + h) % groups, k) for k in range(groups)])  37.9 us
    pallas_call x11, Pallas kernels, run(): pl.pallas_call(kernel, out_shape=outs, in_specs=specs, out_specs=[vmem] *...  35.6 us
    all_to_all x1, blocking collectives, exchange(): lax.all_to_all(rows.reshape(parts, 1, -1), PLANE, split_axis=0, concat_ax...  26.4 us
    ppermute x18, starting transfers between devices, all_cases(): lax.ppermute(field, 'case', [((k + h) % groups, k) for k in range(groups)])  25.7 us
    unnamed x59, local copies, waits for them, and re-layouts  14.9 us
    all_to_all x2, starting transfers between devices, exchange(): lax.all_to_all(rows.reshape(parts, 1, -1), PLANE, split_axis=0, concat_ax...  12.7 us
    all_to_all x1, starting transfers between devices, local(): copies = lax.all_to_all(copies, PLANE, split_axis=0, concat_axis=0)  11.7 us
    all_to_all x2, waiting for transfers between devices, exchange(): lax.all_to_all(rows.reshape(parts, 1, -1), PLANE, split_axis=0, concat_ax...  6.06 us
  transfers between devices with their start and end apart: 21, of which 8 were waited for; matrix products, arithmetic and copies ran while one was open for 0% of the time, Pallas kernels for 5%

profile of v1, /device:TPU:1, one launch (start us, length us, event | category | flops | bytes accessed | tf_op | source)
XLA Modules:
  0.0 171.7 jit_solution(8758429026292970444)
XLA Ops:
  0.7 1.2 copy.15.coupling_ref
  2.6 1.5 condense.1
  4.0 26.4 %all_to_all.20 = f32[64,1,1280]{2,1,0:T(1,128)S(1)} all-to-all(f32[64,1,1280]{2,1,0:T(1,128)S(1)} %bitcast.20), channel_id=1, replica_groups=mesh['px'=8,'py'=8,'case'=4] {'px','py'}, dimensions={0} | all-to-all | bytes 655360 | tf_op jit(solution)/shard_map/all_to_all | solution.py:439
  30.4 1.7 rhs.1
  32.1 6.2 %all-to-all-start.1 = ((f32[64,1,2304]{2,1,0:T(1,128)}), f32[64,1,2304]{2,1,0:T(1,128)S(1)}, u32[]{:S(2)}, u32[]{:S(2)}) async-start(f32[64,1,2304]{2,1,0:T(1,128)} %bitcast.10), calls=%async_computation.1 | async-start | bytes 1179648 | tf_op jit(solution)/shard_map/all_to_all | solution.py:439
  38.3 1.3 collective-permute-start.2
  39.6 2.4 %collective-permute-start.1 = (f32[384,128]{1,0:T(8,128)S(1)}, f32[384,128]{1,0:T(8,128)S(1)}, u32[]{:S(2)}, u32[]{:S(2)}) collective-permute-start(f32[384,128]{1,0:T(8,128)S(1)} %get-tuple-element.55.field_ref.refs_0_), channel_id=1, source_target_pairs={{2,0},{3,1},{0,2},{1,3},{6,4},{7,5},{4,6},{5,7},{10,8},{11,9},{8,1... | collective-permute-start | bytes 589832 | tf_op jit(solution)/shard_map/ppermute | solution.py:491
  42.0 1.2 collective-permute-start
  43.2 1.0 copy-done.19
  44.2 2.5 %tables.1 = (bf16[384,96]{1,0:T(8,128)(2,1)S(1)}, bf16[384,96]{1,0:T(8,128)(2,1)S(1)}, bf16[384,96]{1,0:T(8,128)(2,1)S(1)}, bf16[384,96]{1,0:T(8,128)(2,1)S(1)},...) custom-call(s32[1,128]{1,0:T(1,128)S(1)} %bitcast.35, f32[1,128]{1,0:T(1,128)S(1)} %bitcast.25, ...), custom_call_target="tpu_custom_call" | custom-call | flops 1000000000 | bytes 1639424 | tf_op jit(solution)/shard_map/tables/pallas_call | solution.py:424
  47.3 3.5 %collective-permute-done.1.refs_2_ = f32[384,128]{1,0:T(8,128)S(1)} collective-permute-done((f32[384,128]{1,0:T(8,128)S(1)}, f32[384,128]{1,0:T(8,128)S(1)}, u32[]{:S(2)}, u32[]{:S(2)}) %collective-permute-start.1) | collective-permute-done | bytes 196640 | tf_op jit(solution)/shard_map/ppermute | solution.py:491
  50.8 6.1 %all-to-all-done.1 = f32[64,1,2304]{2,1,0:T(1,128)S(1)} async-done(((f32[64,1,2304]{2,1,0:T(1,128)}), f32[64,1,2304]{2,1,0:T(1,128)S(1)}, u32[]{:S(2)}, u32[]{:S(2)}) %all-to-all-start.1) | async-done | bytes 589856 | tf_op jit(solution)/shard_map/all_to_all | solution.py:439
  56.9 4.6 %apply.1 = (f32[384,128]{1,0:T(8,128)S(1)}, f32[768,128]{1,0:T(8,128)S(1)}, f32[1152,128]{1,0:T(8,128)}) custom-call(f32[1152,128]{1,0:T(8,128)S(1)} %bitcast.18, f32[64,128]{1,0:T(8,128)S(1)} %get-tuple-element.46.meta_ref, f32[64,128]{1,0:T(8,128)S(1)} %get-tuple-element.50.asked_ref, s32[1,128]{1,0:T(1,128)S(1)} %bitcast.36, f32[1,128]{1,0:T(1,128)S(1)} %bitcast.26, ...), custom_call_target="tpu_custom_call" | custom-call | bytes 2328576 | tf_op jit(solution)/shard_map/apply/pallas_call | solution.py:424
  61.4 0.8 copy-done.22
  62.2 6.5 %all-to-all-start.2 = ((f32[64,1,2304]{2,1,0:T(1,128)}), f32[64,1,2304]{2,1,0:T(1,128)S(1)}, u32[]{:S(2)}, u32[]{:S(2)}) async-start(f32[64,1,2304]{2,1,0:T(1,128)} %bitcast.12), calls=%async_computation.2 | async-start | bytes 1179648 | tf_op jit(solution)/shard_map/all_to_all | solution.py:439
  68.7 1.5 collective-permute-start.8
  70.2 1.0 copy-done.23
  71.2 0.9 copy-done.25
  72.1 1.0 turned.2.refs_12_
  73.1 1.3 collective-permute-start.5
  74.3 1.4 collective-permute-start.4
  75.8 1.9 %collective-permute-start.3 = (f32[512,128]{1,0:T(8,128)S(1)}, f32[512,128]{1,0:T(8,128)}, u32[]{:S(2)}, u32[]{:S(2)}) collective-permute-start(f32[512,128]{1,0:T(8,128)S(1)} %turned.2.refs_12_), channel_id=1, source_target_pairs={{1,0},{2,1},{3,2},{0,3},{5,4},{6,5},{7,6},{4,7},{9,8},{10,9},{11,1... | collective-permute-start | bytes 786440 | tf_op jit(solution)/shard_map/ppermute | solution.py:491
  78.2 1.5 collective-permute-start.6
  79.6 13.0 %collective-permute-done.7.refs_6_.rest_1_ = f32[384,128]{1,0:T(8,128)S(1)} collective-permute-done((f32[384,128]{1,0:T(8,128)S(1)}, f32[384,128]{1,0:T(8,128)S(1)}, u32[]{:S(2)}, u32[]{:S(2)}) %collective-permute-start.7) | collective-permute-done | bytes 196640 | tf_op jit(solution)/shard_map/ppermute | solution.py:491
  92.6 3.6 %collective-permute-done.6.refs_5_.rest_0_ = f32[384,128]{1,0:T(8,128)S(1)} collective-permute-done((f32[384,128]{1,0:T(8,128)S(1)}, f32[384,128]{1,0:T(8,128)S(1)}, u32[]{:S(2)}, u32[]{:S(2)}) %collective-permute-start.6) | collective-permute-done | bytes 196640 | tf_op jit(solution)/shard_map/ppermute | solution.py:491
  96.2 3.7 %gram.1.rest_3_ = f32[8,128]{1,0:T(8,128)S(1)} custom-call(s32[1]{0:T(128)} %bitcast.case_ref.rest_4_, f32[384,128]{1,0:T(8,128)S(1)} %get-tuple-element.55.field_ref.refs_0_, f32[384,128]{1,0:T(8,128)S(1)} %collective-permute-done.refs_1_, f32[384,128]{1,0:T(8,128)S(1)} %collective-permute-done.1.refs_2_, f32[384,128]{1,0:T(8,128)S(1)} %collective-permute-done.2.refs_3_, ...), custom_call_target="tpu_custom_call" | custom-call | bytes 1576964 | tf_op jit(solution)/shard_map/gram/pallas_call | solution.py:424
  99.9 5.4 %apply_last.1 = (f32[384,128]{1,0:T(8,128)}, f32[768,128]{1,0:T(8,128)S(1)}, f32[64,8,128]{2,1,0:T(8,128)S(1)}) custom-call(f32[1152,128]{1,0:T(8,128)S(1)} %bitcast.17, f32[64,128]{1,0:T(8,128)S(1)} %get-tuple-element.46.meta_ref, f32[64,128]{1,0:T(8,128)S(1)} %get-tuple-element.50.asked_ref, s32[1,128]{1,0:T(1,128)S(1)} %bitcast.38, ...), custom_call_target="tpu_custom_call" | custom-call | bytes 2594820 | tf_op jit(solution)/shard_map/apply_last/pallas_call | solution.py:424
  106.0 0.8 copy-done.20
  106.7 11.7 %all-to-all-start.3 = ((f32[64,8,128]{2,1,0:T(8,128)}), f32[64,8,128]{2,1,0:T(8,128)S(1)}, u32[]{:S(2)}, u32[]{:S(2)}) async-start(f32[64,8,128]{2,1,0:T(8,128)} %copy-done.6), calls=%async_computation.3 | async-start | bytes 524288 | tf_op jit(solution)/shard_map/all_to_all | solution.py:519
  118.4 1.5 collective-permute-start.11
  119.9 1.0 copy-done.21
  120.9 1.0 turned.3.refs_16_
  121.9 0.8 collective-permute-start.14
  122.7 1.7 %collective-permute-start.13 = (f32[512,128]{1,0:T(8,128)S(1)}, f32[512,128]{1,0:T(8,128)S(1)}, u32[]{:S(2)}, u32[]{:S(2)}) collective-permute-start(f32[512,128]{1,0:T(8,128)S(1)} %turned.3.refs_16_), channel_id=1, source_target_pairs={{2,0},{3,1},{0,2},{1,3},{6,4},{7,5},{4,6},{5,7},{10,8},{11,9},{8,1... | collective-permute-start | bytes 786440 | tf_op jit(solution)/shard_map/ppermute | solution.py:491
  124.4 1.7 collective-permute-start.12
  126.1 0.9 collective-permute-start.10
  127.7 1.3 collective-permute-start.9
  129.0 13.2 %collective-permute-done.10.refs_10_ = f32[384,128]{1,0:T(8,128)S(1)} collective-permute-done((f32[384,128]{1,0:T(8,128)}, f32[384,128]{1,0:T(8,128)S(1)}, u32[]{:S(2)}, u32[]{:S(2)}) %collective-permute-start.10) | collective-permute-done | bytes 196640 | tf_op jit(solution)/shard_map/ppermute | solution.py:491
  142.9 2.2 %collective-permute-done.9.refs_9_ = f32[384,128]{1,0:T(8,128)S(1)} collective-permute-done((f32[384,128]{1,0:T(8,128)}, f32[384,128]{1,0:T(8,128)S(1)}, u32[]{:S(2)}, u32[]{:S(2)}) %collective-permute-start.9) | collective-permute-done | bytes 196640 | tf_op jit(solution)/shard_map/ppermute | solution.py:491
  147.3 2.4 %collective-permute-start.17 = (f32[8,128]{1,0:T(8,128)S(1)}, f32[8,128]{1,0:T(8,128)S(1)}, u32[]{:S(2)}, u32[]{:S(2)}) collective-permute-start(f32[8,128]{1,0:T(8,128)S(1)} %sum.1.refs_0_), channel_id=1, source_target_pairs={{3,0},{0,1},{1,2},{2,3},{7,4},{4,5},{5,6},{6,7},{11,8},{8,9},{9,10... | collective-permute-start | bytes 12296 | tf_op jit(solution)/shard_map/ppermute | solution.py:491
  149.7 2.1 %collective-permute-start.16 = (f32[8,128]{1,0:T(8,128)S(1)}, f32[8,128]{1,0:T(8,128)S(1)}, u32[]{:S(2)}, u32[]{:S(2)}) collective-permute-start(f32[8,128]{1,0:T(8,128)S(1)} %sum.1.refs_0_), channel_id=1, source_target_pairs={{2,0},{3,1},{0,2},{1,3},{6,4},{7,5},{4,6},{5,7},{10,8},{11,9},{8,1... | collective-permute-start | bytes 12296 | tf_op jit(solution)/shard_map/ppermute | solution.py:491
  152.2 1.5 collective-permute-done.16.refs_2_
  153.7 0.9 collective-permute-done.15.refs_1_
  154.6 7.9 %solve.1.coef = f32[64,8,128]{2,1,0:T(8,128)S(1)} custom-call(s32[1]{0:T(128)} %bitcast.case_ref.rest_4_, f32[8,128]{1,0:T(8,128)S(1)} %sum.1.refs_0_, f32[8,128]{1,0:T(8,128)S(1)} %collective-permute-done.15.refs_1_, f32[8,128]{1,0:T(8,128)S(1)} %collective-permute-done.16.refs_2_, f32[8,128]{1,0:T(8,128)S(1)} %collective-permute-done.17.refs_3_), custom_call_target="tpu_custom_call" | custom-call | bytes 278532 | tf_op jit(solution)/shard_map/solve/pallas_call | solution.py:424
  162.6 0.9 copy-done.8
  163.5 0.9 copy-done.10
  164.4 0.9 copy-done.12
  165.4 6.3 %finish.1 = (f32[384,128]{1,0:T(8,128)}, f32[384,128]{1,0:T(8,128)}, f32[512,128]{1,0:T(8,128)}) custom-call(f32[64,8,128]{2,1,0:T(8,128)S(1)} %solve.1.coef, f32[512,128]{1,0:T(8,128)S(1)} %get-tuple-element.69.bubble_ref, f32[384,128]{1,0:T(8,128)S(1)} %get-tuple-element.55.field_ref.refs_0_, f32[384,128]{1,0:T(8,128)S(1)} %collective-permute-done.refs_1_, ...), custom_call_target="tpu_custom_call" | custom-call | bytes 5636096 | tf_op jit(solution)/shard_map/finish/pallas_call | solution.py:424
  (65 shorter events, 6.5 us)
Async XLA Ops:
  0.6 1.3 copy-start.1
  0.6 1.3 copy-start
  1.8 0.7 copy-start.18
  1.9 0.7 copy-start.14
  1.9 0.7 copy-start.15
  1.9 0.7 copy-start.16
  4.0 26.4 %copy-start.13 = (f32[48,8,128]{2,1,0:T(8,128)S(1)}, f32[48,8,128]{2,1,0:T(8,128)}, u32[]{:S(2)}) copy-start(f32[48,8,128]{2,1,0:T(8,128)} %param.16) | copy-start | bytes 589828
  32.1 24.8 %all-to-all-start.1 = ((f32[64,1,2304]{2,1,0:T(1,128)}), f32[64,1,2304]{2,1,0:T(1,128)S(1)}, u32[]{:S(2)}, u32[]{:S(2)}) async-start(f32[64,1,2304]{2,1,0:T(1,128)} %bitcast.10), calls=%async_computation.1 | async-start | bytes 1179648 | tf_op jit(solution)/shard_map/all_to_all | solution.py:439
  38.3 9.0 %collective-permute-start.2 = (f32[384,128]{1,0:T(8,128)S(1)}, f32[384,128]{1,0:T(8,128)S(1)}, u32[]{:S(2)}, u32[]{:S(2)}) collective-permute-start(f32[384,128]{1,0:T(8,128)S(1)} %get-tuple-element.55.field_ref.refs_0_), channel_id=1, source_target_pairs={{3,0},{0,1},{1,2},{2,3},{7,4},{4,5},{5,6},{6,7},{11,8},{8,9},{9,10... | collective-permute-start | bytes 589832 | tf_op jit(solution)/shard_map/ppermute | solution.py:491
  39.6 11.2 %collective-permute-start.1 = (f32[384,128]{1,0:T(8,128)S(1)}, f32[384,128]{1,0:T(8,128)S(1)}, u32[]{:S(2)}, u32[]{:S(2)}) collective-permute-start(f32[384,128]{1,0:T(8,128)S(1)} %get-tuple-element.55.field_ref.refs_0_), channel_id=1, source_target_pairs={{2,0},{3,1},{0,2},{1,3},{6,4},{7,5},{4,6},{5,7},{10,8},{11,9},{8,1... | collective-permute-start | bytes 589832 | tf_op jit(solution)/shard_map/ppermute | solution.py:491
  42.0 8.8 %collective-permute-start = (f32[384,128]{1,0:T(8,128)S(1)}, f32[384,128]{1,0:T(8,128)S(1)}, u32[]{:S(2)}, u32[]{:S(2)}) collective-permute-start(f32[384,128]{1,0:T(8,128)S(1)} %get-tuple-element.55.field_ref.refs_0_), channel_id=1, source_target_pairs={{1,0},{2,1},{3,2},{0,3},{5,4},{6,5},{7,6},{4,7},{9,8},{10,9},{11,1... | collective-permute-start | bytes 589832 | tf_op jit(solution)/shard_map/ppermute | solution.py:491
  43.2 1.0 copy-start.19
  47.3 22.8 %copy-start.27 = (bf16[512,96]{1,0:T(8,128)(2,1)}, bf16[512,96]{1,0:T(8,128)(2,1)S(1)}, u32[]{:S(2)}) copy-start(bf16[512,96]{1,0:T(8,128)(2,1)S(1)} %get-tuple-element.59.low_ref) | copy-start | bytes 294916
  61.4 0.8 copy-start.22
  62.2 37.7 %all-to-all-start.2 = ((f32[64,1,2304]{2,1,0:T(1,128)}), f32[64,1,2304]{2,1,0:T(1,128)S(1)}, u32[]{:S(2)}, u32[]{:S(2)}) async-start(f32[64,1,2304]{2,1,0:T(1,128)} %bitcast.12), calls=%async_computation.2 | async-start | bytes 1179648 | tf_op jit(solution)/shard_map/all_to_all | solution.py:439
  68.7 9.5 %collective-permute-start.8 = (f32[384,128]{1,0:T(8,128)S(1)}, f32[384,128]{1,0:T(8,128)S(1)}, u32[]{:S(2)}, u32[]{:S(2)}) collective-permute-start(f32[384,128]{1,0:T(8,128)S(1)} %get-tuple-element.61.refs_4_.field_ref), channel_id=1, source_target_pairs={{3,0},{0,1},{1,2},{2,3},{7,4},{4,5},{5,6},{6,7},{11,8},{8,9},{9,10... | collective-permute-start | bytes 589832 | tf_op jit(solution)/shard_map/ppermute | solution.py:491
  70.2 1.0 copy-start.23
  71.2 0.9 copy-start.25
  73.1 26.8 %collective-permute-start.5 = (f32[512,128]{1,0:T(8,128)S(1)}, f32[512,128]{1,0:T(8,128)S(1)}, u32[]{:S(2)}, u32[]{:S(2)}) collective-permute-start(f32[512,128]{1,0:T(8,128)S(1)} %turned.2.refs_12_), channel_id=1, source_target_pairs={{3,0},{0,1},{1,2},{2,3},{7,4},{4,5},{5,6},{6,7},{11,8},{8,9},{9,10... | collective-permute-start | bytes 786440 | tf_op jit(solution)/shard_map/ppermute | solution.py:491
  74.3 25.5 %collective-permute-start.4 = (f32[512,128]{1,0:T(8,128)S(1)}, f32[512,128]{1,0:T(8,128)}, u32[]{:S(2)}, u32[]{:S(2)}) collective-permute-start(f32[512,128]{1,0:T(8,128)S(1)} %turned.2.refs_12_), channel_id=1, source_target_pairs={{2,0},{3,1},{0,2},{1,3},{6,4},{7,5},{4,6},{5,7},{10,8},{11,9},{8,1... | collective-permute-start | bytes 786440 | tf_op jit(solution)/shard_map/ppermute | solution.py:491
  75.8 24.1 %collective-permute-start.3 = (f32[512,128]{1,0:T(8,128)S(1)}, f32[512,128]{1,0:T(8,128)}, u32[]{:S(2)}, u32[]{:S(2)}) collective-permute-start(f32[512,128]{1,0:T(8,128)S(1)} %turned.2.refs_12_), channel_id=1, source_target_pairs={{1,0},{2,1},{3,2},{0,3},{5,4},{6,5},{7,6},{4,7},{9,8},{10,9},{11,1... | collective-permute-start | bytes 786440 | tf_op jit(solution)/shard_map/ppermute | solution.py:491
  77.6 15.0 %collective-permute-start.7 = (f32[384,128]{1,0:T(8,128)S(1)}, f32[384,128]{1,0:T(8,128)S(1)}, u32[]{:S(2)}, u32[]{:S(2)}) collective-permute-start(f32[384,128]{1,0:T(8,128)S(1)} %get-tuple-element.61.refs_4_.field_ref), channel_id=1, source_target_pairs={{2,0},{3,1},{0,2},{1,3},{6,4},{7,5},{4,6},{5,7},{10,8},{11,9},{8,1... | collective-permute-start | bytes 589832 | tf_op jit(solution)/shard_map/ppermute | solution.py:491
  78.2 18.0 %collective-permute-start.6 = (f32[384,128]{1,0:T(8,128)S(1)}, f32[384,128]{1,0:T(8,128)S(1)}, u32[]{:S(2)}, u32[]{:S(2)}) collective-permute-start(f32[384,128]{1,0:T(8,128)S(1)} %get-tuple-element.61.refs_4_.field_ref), channel_id=1, source_target_pairs={{1,0},{2,1},{3,2},{0,3},{5,4},{6,5},{7,6},{4,7},{9,8},{10,9},{11,1... | collective-permute-start | bytes 589832 | tf_op jit(solution)/shard_map/ppermute | solution.py:491
  105.3 0.7 copy-start.6
  106.0 0.8 copy-start.20
  106.7 13.2 %copy-start.26 = (bf16[512,96]{1,0:T(8,128)(2,1)S(1)}, bf16[512,96]{1,0:T(8,128)(2,1)}, u32[]{:S(2)}) copy-start(bf16[512,96]{1,0:T(8,128)(2,1)} %copy-done.24) | copy-start | bytes 294916
  106.7 13.2 %copy-start.28 = (bf16[512,96]{1,0:T(8,128)(2,1)S(1)}, bf16[512,96]{1,0:T(8,128)(2,1)}, u32[]{:S(2)}) copy-start(bf16[512,96]{1,0:T(8,128)(2,1)} %copy-done.27) | copy-start | bytes 294916
  106.7 40.5 %all-to-all-start.3 = ((f32[64,8,128]{2,1,0:T(8,128)}), f32[64,8,128]{2,1,0:T(8,128)S(1)}, u32[]{:S(2)}, u32[]{:S(2)}) async-start(f32[64,8,128]{2,1,0:T(8,128)} %copy-done.6), calls=%async_computation.3 | async-start | bytes 524288 | tf_op jit(solution)/shard_map/all_to_all | solution.py:519
  118.4 8.6 %collective-permute-start.11 = (f32[384,128]{1,0:T(8,128)}, f32[384,128]{1,0:T(8,128)S(1)}, u32[]{:S(2)}, u32[]{:S(2)}) collective-permute-start(f32[384,128]{1,0:T(8,128)} %get-tuple-element.70.refs_8_), channel_id=1, source_target_pairs={{3,0},{0,1},{1,2},{2,3},{7,4},{4,5},{5,6},{6,7},{11,8},{8,9},{9,10... | collective-permute-start | bytes 589832 | tf_op jit(solution)/shard_map/ppermute | solution.py:491
  119.9 1.0 copy-start.21
  121.9 23.9 %collective-permute-start.14 = (f32[512,128]{1,0:T(8,128)S(1)}, f32[512,128]{1,0:T(8,128)S(1)}, u32[]{:S(2)}, u32[]{:S(2)}) collective-permute-start(f32[512,128]{1,0:T(8,128)S(1)} %turned.3.refs_16_), channel_id=1, source_target_pairs={{3,0},{0,1},{1,2},{2,3},{7,4},{4,5},{5,6},{6,7},{11,8},{8,9},{9,10... | collective-permute-start | bytes 786440 | tf_op jit(solution)/shard_map/ppermute | solution.py:491
  122.7 23.1 %collective-permute-start.13 = (f32[512,128]{1,0:T(8,128)S(1)}, f32[512,128]{1,0:T(8,128)S(1)}, u32[]{:S(2)}, u32[]{:S(2)}) collective-permute-start(f32[512,128]{1,0:T(8,128)S(1)} %turned.3.refs_16_), channel_id=1, source_target_pairs={{2,0},{3,1},{0,2},{1,3},{6,4},{7,5},{4,6},{5,7},{10,8},{11,9},{8,1... | collective-permute-start | bytes 786440 | tf_op jit(solution)/shard_map/ppermute | solution.py:491
  124.4 22.1 %collective-permute-start.12 = (f32[512,128]{1,0:T(8,128)S(1)}, f32[512,128]{1,0:T(8,128)S(1)}, u32[]{:S(2)}, u32[]{:S(2)}) collective-permute-start(f32[512,128]{1,0:T(8,128)S(1)} %turned.3.refs_16_), channel_id=1, source_target_pairs={{1,0},{2,1},{3,2},{0,3},{5,4},{6,5},{7,6},{4,7},{9,8},{10,9},{11,1... | collective-permute-start | bytes 786440 | tf_op jit(solution)/shard_map/ppermute | solution.py:491
  126.1 16.1 %collective-permute-start.10 = (f32[384,128]{1,0:T(8,128)}, f32[384,128]{1,0:T(8,128)S(1)}, u32[]{:S(2)}, u32[]{:S(2)}) collective-permute-start(f32[384,128]{1,0:T(8,128)} %get-tuple-element.70.refs_8_), channel_id=1, source_target_pairs={{2,0},{3,1},{0,2},{1,3},{6,4},{7,5},{4,6},{5,7},{10,8},{11,9},{8,1... | collective-permute-start | bytes 589832 | tf_op jit(solution)/shard_map/ppermute | solution.py:491
  127.0 0.7 copy-start.7
  127.7 17.4 %collective-permute-start.9 = (f32[384,128]{1,0:T(8,128)}, f32[384,128]{1,0:T(8,128)S(1)}, u32[]{:S(2)}, u32[]{:S(2)}) collective-permute-start(f32[384,128]{1,0:T(8,128)} %get-tuple-element.70.refs_8_), channel_id=1, source_target_pairs={{1,0},{2,1},{3,2},{0,3},{5,4},{6,5},{7,6},{4,7},{9,8},{10,9},{11,1... | collective-permute-start | bytes 589832 | tf_op jit(solution)/shard_map/ppermute | solution.py:491
  142.2 0.7 copy-start.9
  145.1 0.7 copy-start.11
  145.8 0.7 copy-start.2
  146.5 0.7 copy-start.4
  147.2 15.3 %copy-start.3 = (f32[512,128]{1,0:T(8,128)S(1)}, f32[512,128]{1,0:T(8,128)}, u32[]{:S(2)}) copy-start(f32[512,128]{1,0:T(8,128)} %copy-done.2) | copy-start | bytes 786436
  147.2 15.3 %copy-start.5 = (f32[512,128]{1,0:T(8,128)S(1)}, f32[512,128]{1,0:T(8,128)}, u32[]{:S(2)}) copy-start(f32[512,128]{1,0:T(8,128)} %copy-done.4) | copy-start | bytes 786436
  147.3 4.9 %collective-permute-start.17 = (f32[8,128]{1,0:T(8,128)S(1)}, f32[8,128]{1,0:T(8,128)S(1)}, u32[]{:S(2)}, u32[]{:S(2)}) collective-permute-start(f32[8,128]{1,0:T(8,128)S(1)} %sum.1.refs_0_), channel_id=1, source_target_pairs={{3,0},{0,1},{1,2},{2,3},{7,4},{4,5},{5,6},{6,7},{11,8},{8,9},{9,10... | collective-permute-start | bytes 12296 | tf_op jit(solution)/shard_map/ppermute | solution.py:491
  149.7 4.0 %collective-permute-start.16 = (f32[8,128]{1,0:T(8,128)S(1)}, f32[8,128]{1,0:T(8,128)S(1)}, u32[]{:S(2)}, u32[]{:S(2)}) collective-permute-start(f32[8,128]{1,0:T(8,128)S(1)} %sum.1.refs_0_), channel_id=1, source_target_pairs={{2,0},{3,1},{0,2},{1,3},{6,4},{7,5},{4,6},{5,7},{10,8},{11,9},{8,1... | collective-permute-start | bytes 12296 | tf_op jit(solution)/shard_map/ppermute | solution.py:491
  151.9 2.8 %collective-permute-start.15 = (f32[8,128]{1,0:T(8,128)S(1)}, f32[8,128]{1,0:T(8,128)S(1)}, u32[]{:S(2)}, u32[]{:S(2)}) collective-permute-start(f32[8,128]{1,0:T(8,128)S(1)} %sum.1.refs_0_), channel_id=1, source_target_pairs={{1,0},{2,1},{3,2},{0,3},{5,4},{6,5},{7,6},{4,7},{9,8},{10,9},{11,1... | collective-permute-start | bytes 12296 | tf_op jit(solution)/shard_map/ppermute | solution.py:491
  162.6 0.9 copy-start.8
  163.5 0.9 copy-start.10
  164.4 0.9 copy-start.12
  (2 other events, 1.3 us)

commit v2 on v1

--- a/solution.py
+++ b/solution.py
@@ -136,7 +136,7 @@
     modes = load_ref.shape[0] // CASES
     dofs = near_sum_ref.shape[0] // CASES
     table = jnp.concatenate(
-        [dot_high(coupling_ref[t], inverse_ref[t]) for t in range(KINDS)], axis=0
+        [jnp.transpose(dot_high(inverse_ref[t], coupling_ref[t], TN)) for t in range(KINDS)], axis=0
     )
     high, low = split2(table)
     left = jnp.concatenate([high, high, low], axis=1)
@@ -180,11 +180,10 @@
     modes = inverse_ref.shape[1]
     inverses = []
     for t in range(KINDS):
-        reduced = dot_high(coupling_ref[t], inverse_ref[t])
-        schur = block_ref[t] - dot_high(reduced, coupling_ref[t], NT)
+        turned = dot_high(inverse_ref[t], coupling_ref[t], TN)
+        schur = block_ref[t] - dot_high(turned, coupling_ref[t], TN)
         near_high[t * dofs : (t + 1) * dofs, :], near_low[t * dofs : (t + 1) * dofs, :] = split2(schur[:dofs])
         far_high[t * dofs : (t + 1) * dofs, :], far_low[t * dofs : (t + 1) * dofs, :] = split2(schur[dofs:])
-        turned = jnp.transpose(reduced)
         turned_high[t * modes : (t + 1) * modes, :], turned_low[t * modes : (t + 1) * modes, :] = split2(turned)
         inverses.append(inverse_ref[t])
     high, low = split2(jnp.concatenate(inverses, axis=0))
@@ -266,15 +265,18 @@
         gram = add_products(
             LANES, [field_ref, *others], [image_ref], [3 * groups * CASES], case_ref[0], gram_ref[...]
         )
-        for p in range(parts):
+        for p in range(copies_ref.shape[0]):
             copies_ref[p] = gram
     else:
         send_ports(image, asked_hot, port_onehot(meta_ref[...]), pay_ref)
 
 
-def turned_kernel(spread_ref, kind_ref, high_ref, low_ref, out_ref):
+def turned_kernel(groups, case_ref, spread_ref, field_ref, kind_ref, high_ref, low_ref, *rest):
+    own_ref, messages, out_ref = rest[0], rest[1:groups], rest[groups]
     dofs2 = spread_ref.shape[0] // CASES
+    rows = field_ref.shape[0]
     modes = out_ref.shape[0] // CASES
+    part = out_ref.shape[0] // groups
     kind = kind_ref[...]
     kind2 = jnp.concatenate([kind, kind], axis=1)
     for k in range(0, CASES, 2):
@@ -284,6 +286,11 @@
         result = by_kind(table_product(high_ref[...], low_ref[...], values), kind2, modes)
         for i in range(2):
             out_ref[pl.ds(k + i, modes, stride=CASES), :] = result[:, i * LANES : (i + 1) * LANES]
+    own_ref[...] = out_ref[pl.ds(pl.multiple_of(case_ref[0] * part, part), part), :]
+    for h in range(1, groups):
+        at = lax.rem(case_ref[0] + h, groups)
+        messages[h - 1][:rows, :] = field_ref[...]
+        messages[h - 1][rows:, :] = out_ref[pl.ds(pl.multiple_of(at * part, part), part), :]
 
 
 def add_products(lanes, lefts, rights, first, case, out):
@@ -320,101 +327,122 @@
 
 
 def sum_kernel(in_ref, out_ref):
-    total = in_ref[0]
-    for p in range(1, in_ref.shape[0]):
-        total = total + in_ref[p]
-    out_ref[...] = total
-
-
-def spd_solve(pairs):
-    n = pairs[0][0].shape[0]
-    row_of = iota((n, 2 * n), 0)
-    work = [jnp.concatenate(pair, axis=1) for pair in pairs]
-    for k in range(n):
-        nxt = []
-        for a in work:
-            pivot = a[k : k + 1, :] / a[k : k + 1, k : k + 1]
-            nxt.append(jnp.where(row_of == k, pivot, a - a[:, k : k + 1] * pivot))
-        work = nxt
-    return [a[:, n:] for a in work]
+    for q in range(in_ref.shape[0]):
+        total = in_ref[q, 0]
+        for p in range(1, in_ref.shape[1]):
+            total = total + in_ref[q, p]
+        for p in range(out_ref.shape[0]):
+            out_ref[p, q * CASES : (q + 1) * CASES, :] = total
+
+
+def spd_solve(matrix, target):
+    n = matrix.shape[0]
+    a = jnp.concatenate([matrix, target], axis=1)
+    row_of = iota(a.shape, 0)
+    for k in range(0, n, 2):
+        r0, r1 = a[k : k + 1, :], a[k + 1 : k + 2, :]
+        c0, c1 = a[:, k : k + 1], a[:, k + 1 : k + 2]
+        p00, p01, p10, p11 = c0[k : k + 1], c1[k : k + 1], c0[k + 1 : k + 2], c1[k + 1 : k + 2]
+        scale = 1.0 / (p00 * p11 - p01 * p10)
+        u0 = (r0 * p11 - r1 * p01) * scale
+        u1 = (r1 * p00 - r0 * p10) * scale
+        a = a - (c0 * u0 + c1 * u1)
+        a = jnp.where(row_of == k, u0, jnp.where(row_of == k + 1, u1, a))
+    return a[:, n:]
 
 
 def symmetric(m):
     return 0.5 * (m + jnp.transpose(m))
 
 
-def solve_kernel(groups, case_ref, *refs):
-    grams, coef, rows_ref, turned_coef = refs[:groups], refs[groups], refs[groups + 1], refs[groups + 2]
+def solve_kernel(groups, case_ref, gram_ref, coef, coef_rows, turned_coef):
     n = groups * CASES
-    for h in range(groups):
-        at = pl.multiple_of(lax.rem(case_ref[0] + h, groups) * CASES, CASES)
-        rows_ref[pl.ds(at, CASES), :] = grams[h][...]
-    g00, g01, g11, g12 = [symmetric(rows_ref[:, g * n : (g + 1) * n]) for g in range(4)]
-    eye = (iota((n, n), 0) == iota((n, n), 1)).astype(F32)
-    step0, inverse00 = spd_solve([(g01, g00), (g00, eye)])
-    step0_t = jnp.transpose(step0)
-    gram1 = g00 - dot_high(g01, step0)
-    gram1 = gram1 + jnp.transpose(dot_high(dot_high(g11, step0) - g01, step0, TN))
-    gram1 = symmetric(gram1)
-    update = eye + dot_high(inverse00, gram1)
-    update_t = jnp.transpose(update)
-    left = dot_high(update_t, g01) - dot_high(step0_t, g11)
-    right = dot_high(update_t, g11) - dot_high(step0_t, g12)
-    curvature = symmetric(dot_high(left, update) - dot_high(right, step0))
-    (step1,) = spd_solve([(curvature, gram1)])
-    first = jnp.transpose(step0 + dot_high(update, step1))
-    second = jnp.transpose(-dot_high(step0, step1))
-    turned_coef[:n, :] = jnp.concatenate([first] * (LANES // n), axis=1)
-    turned_coef[n:, :] = jnp.concatenate([second] * (LANES // n), axis=1)
-    at = pl.multiple_of(case_ref[0] * CASES, CASES)
-    for h in range(2):
-        mine = pltpu.roll(turned_coef[pl.ds(h * n + at, CASES), :], LANES - case_ref[0] * CASES, 1)
-        for j in range(n):
-            coef[h * n + j] = jnp.broadcast_to(mine[:, j : j + 1], (CASES, LANES))
-
-
-def finish_kernel(groups, coef, bubble_ref, *refs):
-    base, image, second, turned0, turned1 = [refs[g * groups : (g + 1) * groups] for g in range(5)]
-    x_ref, residual_ref, bubble_out = refs[5 * groups :]
+    total = gram_ref[0]
+    for p in range(1, gram_ref.shape[0]):
+        total = total + gram_ref[p]
+    g00, g01, g11, g12 = [symmetric(total[:, g * n : (g + 1) * n]) for g in range(4)]
+    steps = spd_solve(g01, jnp.concatenate([g00, g11], axis=1))
+    step0, step1 = steps[:, :n], steps[:, n:]
+    both = dot_high(g11, steps)
+    second = spd_solve(symmetric(g12 - both[:, n:]), g01 - both[:, :n])
+    first = step0 - dot_high(step1, second)
+    first, second = jnp.transpose(first), jnp.transpose(second)
+    turned_coef[0] = jnp.concatenate([first] * (LANES // n), axis=1)
+    turned_coef[1] = jnp.concatenate([second] * (LANES // n), axis=1)
+    shift = LANES - case_ref[0] * CASES
+    for q in range(groups):
+        at = pl.multiple_of(lax.rem(case_ref[0] + q, groups) * CASES, CASES)
+        for h in range(2):
+            mine = pltpu.roll(turned_coef[h, pl.ds(at, CASES), :], shift, 1)
+            coef_rows[q * CASES : (q + 1) * CASES, h * LANES : (h + 1) * LANES] = mine
+            if q == 0:
+                for j in range(n):
+                    coef[h * n + j] = jnp.broadcast_to(mine[:, j : j + 1], (CASES, LANES))
+
+
+def bubble_kernel(groups, rows, coef_ref, *refs):
+    turned0, turned1, outs = refs[:groups], refs[groups : 2 * groups], refs[2 * groups :]
+    n = groups * CASES
+    part = turned0[0].shape[0]
+    coef = jnp.concatenate([coef_ref[:, :n], coef_ref[:, LANES : LANES + n]], axis=1)
+    high, low = split2(coef)
+    left = jnp.concatenate([high, high, low], axis=1)
+    for m in range(0, part // CASES, 2):
+        values = []
+        for i in range(2):
+            at = (m + i) * CASES
+            pieces = [
+                ref[at + (0 if h == 0 else rows) : at + (0 if h == 0 else rows) + CASES, :]
+                for refs_ in (turned0, turned1)
+                for h, ref in enumerate(refs_)
+            ]
+            values.append(jnp.concatenate(pieces, axis=0))
+        a, b = split2(jnp.concatenate(values, axis=1))
+        result = dot(left, jnp.concatenate([a, b, a], axis=0))
+        for i in range(2):
+            for h in range(groups):
+                outs[h][(m + i) * CASES : (m + i + 1) * CASES, :] = result[
+                    h * CASES : (h + 1) * CASES, i * LANES : (i + 1) * LANES
+                ]
+
+
+def ports_kernel(groups, coef, *refs):
+    base, image, second = [refs[g * groups : (g + 1) * groups] for g in range(3)]
+    x_ref, residual_ref = refs[3 * groups :]
     n = groups * CASES
     dofs = x_ref.shape[0] // CASES
-    modes = bubble_out.shape[0] // CASES
+    wide = 4
 
     def ports(block, carry):
-        for i in range(4):
-            d = block * 4 + i
-            own = pl.ds(pl.multiple_of(d * CASES, CASES), CASES)
-            x = jnp.zeros((CASES, LANES), F32)
-            r = base[0][own, :]
-            for j in range(n):
-                q, c = divmod(j, CASES)
-                row = pl.ds(d * CASES + c, 1)
+        d0 = block * wide
+        own = [pl.ds(pl.multiple_of((d0 + i) * CASES, CASES), CASES) for i in range(wide)]
+        x = [jnp.zeros((CASES, LANES), F32)] * wide
+        r = [base[0][own[i], :] for i in range(wide)]
+        for j in range(n):
+            q, c = divmod(j, CASES)
+            c0, c1 = coef[j], coef[n + j]
+            for i in range(wide):
+                row = pl.ds((d0 + i) * CASES + c, 1)
                 a = image[q][row, :]
-                c0, c1 = coef[j], coef[n + j]
-                x = x + (c0 * base[q][row, :] + c1 * a)
-                r = r - (c0 * a + c1 * second[q][row, :])
-            x_ref[own, :] = x
-            residual_ref[own, :] = r
+                x[i] = x[i] + (c0 * base[q][row, :] + c1 * a)
+                r[i] = r[i] - (c0 * a + c1 * second[q][row, :])
+        for i in range(wide):
+            x_ref[own[i], :] = x[i]
+            residual_ref[own[i], :] = r[i]
         return carry
 
-    lax.fori_loop(0, dofs // 4, ports, 0)
-
-    def bubbles(block, carry):
-        for i in range(4):
-            d = block * 4 + i
-            own = pl.ds(pl.multiple_of(d * CASES, CASES), CASES)
-            w = bubble_ref[own, :]
-            for j in range(n):
-                q, c = divmod(j, CASES)
-                row = pl.ds(d * CASES + c, 1)
-                w = w - (coef[j] * turned0[q][row, :] + coef[n + j] * turned1[q][row, :])
-            bubble_out[own, :] = w
-        return carry
-
-    lax.fori_loop(0, modes // 4, bubbles, 0)
-
-
-def call(kernel, outs, scratch=(), name=None, flops=0, smem=()):
+    lax.fori_loop(0, dofs // wide, ports, 0)
+
+
+def join_kernel(groups, case_ref, bubble_ref, *refs):
+    parts, out_ref = refs[:groups], refs[groups]
+    part = parts[0].shape[0]
+    for h in range(groups):
+        at = pl.ds(pl.multiple_of(lax.rem(case_ref[0] + h, groups) * part, part), part)
+        out_ref[at, :] = bubble_ref[at, :] - parts[h][...]
+
+
+def call(kernel, outs, scratch=(), name=None, flops=0, smem=(), limit=12):
     outs = [jax.ShapeDtypeStruct(shape, dtype) for shape, dtype in outs]
     vmem = pl.BlockSpec(memory_space=pltpu.VMEM)
 
@@ -427,7 +455,7 @@
             in_specs=specs,
             out_specs=[vmem] * len(outs),
             scratch_shapes=[pltpu.VMEM(shape, F32) for shape in scratch],
-            compiler_params=pltpu.CompilerParams(vmem_limit_bytes=40 << 20),
+            compiler_params=pltpu.CompilerParams(vmem_limit_bytes=limit << 20),
             cost_estimate=pl.CostEstimate(flops=flops, bytes_accessed=moved, transcendentals=0),
             name=name,
         )(*args)
@@ -450,6 +478,7 @@
     dofs, _, ports = port_load.shape
     rows, bubbles = dofs * cases, modes * cases
     slot_tiles = -(-SLOTS * parts // LANES)
+    coupling = jnp.swapaxes(coupling, 1, 2)
     kind = comp_type.reshape(1, comps)
     stiff = stiffness.reshape(1, comps)
     near = near_port.reshape(1, comps)
@@ -481,19 +510,28 @@
     spread_of = ((2 * rows, comps), F32)
     scratch = [(slot_tiles, 2 * rows, LANES), (rows, comps), (slot_tiles, rows, LANES)]
 
-    def turned(spread):
-        return call(turned_kernel, [((bubbles, comps), F32)], name="turned", flops=10**9)(
-            spread, kind, *turned_tables
-        )[0]
-
-    def all_cases(field):
-        return [field] + [
-            lax.ppermute(field, "case", [((k + h) % groups, k) for k in range(groups)])
-            for h in range(1, groups)
+    part = bubbles // groups
+
+    def turned(spread, field):
+        own, *messages = call(
+            functools.partial(turned_kernel, groups),
+            [((part, comps), F32)] + [((rows + part, comps), F32)] * (groups - 1),
+            [(bubbles, comps)],
+            name="turned",
+            flops=10**9,
+            smem=(0,),
+        )(case, spread, field, kind, *turned_tables)
+        return own, messages
+
+    def to_cases(messages):
+        backward = [
+            lax.ppermute(message, "case", [(k, (k + h) % groups) for k in range(groups)])
+            for h, message in enumerate(messages, 1)
         ]
+        return backward[::-1]
 
     arrived = exchange(pay, parts)
-    base_all = all_cases(base)
+    base_all = [base, *to_cases([base] * (groups - 1))]
     arrived, *base_all = lax.optimization_barrier((arrived, *base_all))
     shared = (meta, asked, kind, stiff, near, owner, *schur)
     image, spread, pay = call(
@@ -503,37 +541,44 @@
         "apply",
     )(arrived, *shared, base_all[0])
     arrived = exchange(pay, parts)
-    image_all = all_cases(image)
-    turned0_all = all_cases(turned(spread))
+    turned0, messages = turned(spread, image)
+    both0 = to_cases(messages)
     (gram,) = call(functools.partial(gram_kernel, groups), [((cases, LANES), F32)], name="gram", smem=(0,))(
-        case, *base_all, *image_all
-    )
-    arrived, *turned0_all = lax.optimization_barrier((arrived, *turned0_all))
+        case, *base_all, image, *both0
+    )
+    minor = lax.axis_size("py")
     second, spread, copies = call(
         functools.partial(apply_kernel, parts, groups, True),
-        [field_of, spread_of, ((parts, cases, LANES), F32)],
+        [field_of, spread_of, ((groups * minor, cases, LANES), F32)],
         scratch,
         "apply_last",
         smem=(12 + groups,),
-    )(arrived, *shared, *image_all, gram, case)
-    copies = lax.all_to_all(copies, PLANE, split_axis=0, concat_axis=0)
-    second_all = all_cases(second)
-    turned1_all = all_cases(turned(spread))
-    copies, *rest = lax.optimization_barrier((copies, *second_all, *turned1_all))
-    second_all, turned1_all = rest[:groups], rest[groups:]
-    (gram,) = call(sum_kernel, [((cases, LANES), F32)], name="sum")(copies)
-    (coef,) = call(
+    )(arrived, *shared, image, *both0, gram, case)
+    copies = lax.all_to_all(copies, ("case", "py"), split_axis=0, concat_axis=0)
+    turned1, messages = turned(spread, second)
+    both1 = to_cases(messages)
+    (copies,) = call(sum_kernel, [((parts // minor, groups * cases, LANES), F32)], name="sum")(
+        copies.reshape(groups, minor, cases, LANES)
+    )
+    copies = lax.all_to_all(copies, "px", split_axis=0, concat_axis=0)
+    copies, *both1 = lax.optimization_barrier((copies, *both1))
+    coef, coef_rows = call(
         functools.partial(solve_kernel, groups),
-        [((2 * groups * cases, cases, LANES), F32)],
-        [(groups * cases, LANES), (2 * groups * cases, LANES)],
+        [((2 * groups * cases, cases, LANES), F32), ((groups * cases, 2 * LANES), F32)],
+        [(2, groups * cases, LANES)],
         "solve",
         smem=(0,),
-    )(case, *all_cases(gram))
-    x, residual, bubble = call(
-        functools.partial(finish_kernel, groups),
-        [field_of, field_of, ((bubbles, comps), F32)],
-        name="finish",
-    )(coef, bubble_base, *base_all, *image_all, *second_all, *turned0_all, *turned1_all)
+    )(case, copies)
+    own, *messages = call(
+        functools.partial(bubble_kernel, groups, rows), [((part, comps), F32)] * groups, name="bubble"
+    )(coef_rows, turned0, *both0, turned1, *both1)
+    back = to_cases(messages)
+    x, residual = call(
+        functools.partial(ports_kernel, groups), [field_of, field_of], name="ports", flops=10**9
+    )(coef, *base_all, image, *both0, second, *both1)
+    (bubble,) = call(functools.partial(join_kernel, groups), [((bubbles, comps), F32)], name="join", smem=(0,))(
+        case, bubble_base, own, *back
+    )
     return (
         x.reshape(port_load.shape),
         residual.reshape(port_load.shape),

time: 173 us -> 145 us (0.84)
  waiting for transfers between devices: 43.9 us -> 34 us
  starting transfers between devices: 50.1 us -> 40.9 us
  local copies, waits for them, and re-layouts: 14.9 us -> 6.28 us
    ppermute x18 -> x12, waiting for transfers between devices: 37.9 us -> 24.7 us  [to_cases(): lax.ppermute(message, 'case', [(k, (k + h) % groups) for k in range(group...]
    ppermute x18 -> x12, starting transfers between devices: 25.7 us -> 14.3 us  [to_cases(): lax.ppermute(message, 'case', [(k, (k + h) % groups) for k in range(group...]
    unnamed x59 -> x38, local copies, waits for them, and re-layouts: 14.9 us -> 6.28 us
    all_to_all x1 -> x2, waiting for transfers between devices: 0.01 us -> 3.21 us  [the longest x1 2.67 us: local(): copies = lax.all_to_all(copies, ('case', 'py'), split_axis=0, concat_axis=0)]
    all_to_all x1 -> x2, starting transfers between devices: 11.7 us -> 13.8 us  [the longest x1 7.33 us: local(): copies = lax.all_to_all(copies, ('case', 'py'), split_axis=0, concat_axis=0)]
    pallas_call x11 -> x13, Pallas kernels: 35.6 us -> 36.2 us  [run(): pl.pallas_call(kernel, out_shape=outs, in_specs=specs, out_specs=[vmem] *...]
  transfers between devices with their start and end apart: 21 -> 16, of which waited for: 8 -> 10; matrix products, arithmetic and copies ran while one was open for 0% -> 0% of each run, Pallas kernels for 5% -> 9%
where the time goes in v2:
time: 145 us
  starting transfers between devices  40.9 us (28%)
  Pallas kernels  36.2 us (25%)
  waiting for transfers between devices  34 us (23%)
  blocking collectives  26.4 us (18%)
  local copies, waits for them, and re-layouts  6.28 us (4%)
    pallas_call x13, Pallas kernels, run(): pl.pallas_call(kernel, out_shape=outs, in_specs=specs, out_specs=[vmem] *...  36.2 us
    all_to_all x1, blocking collectives, exchange(): lax.all_to_all(rows.reshape(parts, 1, -1), PLANE, split_axis=0, concat_ax...  26.4 us
    ppermute x12, waiting for transfers between devices, to_cases(): lax.ppermute(message, 'case', [(k, (k + h) % groups) for k in range(group...  24.7 us
    ppermute x12, starting transfers between devices, to_cases(): lax.ppermute(message, 'case', [(k, (k + h) % groups) for k in range(group...  14.3 us
    all_to_all x2, starting transfers between devices, exchange(): lax.all_to_all(rows.reshape(parts, 1, -1), PLANE, split_axis=0, concat_ax...  12.8 us
    all_to_all x1, starting transfers between devices, local(): copies = lax.all_to_all(copies, ('case', 'py'), split_axis=0, concat_axis=0)  7.33 us
    all_to_all x1, starting transfers between devices, local(): copies = lax.all_to_all(copies, 'px', split_axis=0, concat_axis=0)  6.5 us
    unnamed x38, local copies, waits for them, and re-layouts  6.28 us
  transfers between devices with their start and end apart: 16, of which 10 were waited for; matrix products, arithmetic and copies ran while one was open for 0% of the time, Pallas kernels for 9%

profile of v2, /device:TPU:1, one launch (start us, length us, event | category | flops | bytes accessed | tf_op | source)
XLA Modules:
  0.0 144.6 jit_solution(7083502882411383007)
XLA Ops:
  0.7 0.6 copy-done.10
  1.3 0.0 copy-done.11
  1.3 0.0 copy-done.7
  1.4 0.9 copy-done
  2.3 0.9 copy-done.2
  3.3 0.9 copy-done.4
  4.2 1.9 %condense.1 = (f32[640,128]{1,0:T(8,128)S(1)}, f32[384,128]{1,0:T(8,128)S(1)}, f32[64,128]{1,0:T(8,128)S(1)}) custom-call(s32[1,128]{1,0:T(1,128)S(1)} %bitcast.39, f32[1,128]{1,0:T(1,128)S(1)} %bitcast.29, s32[1,128]{1,0:T(1,128)S(1)} %bitcast.33, s32[1,128]{1,0:T(1,128)S(1)} %bitcast.36, s32[1,128]{1,0:T(1,128)S(1)} %bitcast.45, f32[512,128]{1,0:T(8,128)S(1)} %bitcast.24, ...), custom_call_target="tpu_custom_call" | custom-call | bytes 1149440 | tf_op jit(solution)/shard_map/condense/pallas_call | solution.py:452
  6.1 26.4 %all_to_all.25 = f32[64,1,1280]{2,1,0:T(1,128)S(1)} all-to-all(f32[64,1,1280]{2,1,0:T(1,128)S(1)} %bitcast.23), channel_id=1, replica_groups=mesh['px'=8,'py'=8,'case'=4] {'px','py'}, dimensions={0} | all-to-all | bytes 655360 | tf_op jit(solution)/shard_map/all_to_all | solution.py:467
  32.5 1.7 %rhs.1 = (f32[384,128]{1,0:T(8,128)S(1)}, f32[1152,128]{1,0:T(8,128)}, f32[64,128]{1,0:T(8,128)S(1)}) custom-call(f32[640,128]{1,0:T(8,128)S(1)} %bitcast.21, f32[384,128]{1,0:T(8,128)S(1)} %get-tuple-element.48.near_sum_ref, f32[384,128]{1,0:T(8,128)S(1)} %bitcast.28, f32[64,128]{1,0:T(8,128)S(1)} %get-tuple-element.49.meta_ref), custom_call_target="tpu_custom_call" | custom-call | bytes 1572864 | tf_op jit(solution)/shard_map/rhs/pallas_call | solution.py:452
  34.1 6.3 %all-to-all-start.1 = ((f32[64,1,2304]{2,1,0:T(1,128)}), f32[64,1,2304]{2,1,0:T(1,128)S(1)}, u32[]{:S(2)}, u32[]{:S(2)}) async-start(f32[64,1,2304]{2,1,0:T(1,128)} %bitcast.11), calls=%async_computation.1 | async-start | bytes 1179648 | tf_op jit(solution)/shard_map/all_to_all | solution.py:467
  40.5 1.3 collective-permute-start.2
  41.7 2.4 %collective-permute-start.1 = (f32[384,128]{1,0:T(8,128)S(1)}, f32[384,128]{1,0:T(8,128)S(1)}, u32[]{:S(2)}, u32[]{:S(2)}) collective-permute-start(f32[384,128]{1,0:T(8,128)S(1)} %get-tuple-element.58.field_ref.refs_0_), channel_id=1, source_target_pairs={{0,2},{1,3},{2,0},{3,1},{4,6},{5,7},{6,4},{7,5},{8,10},{9,11},{10,... | collective-permute-start | bytes 589832 | tf_op jit(solution)/shard_map/ppermute | solution.py:528
  44.2 1.2 collective-permute-start
  45.4 1.0 copy-done.12
  46.3 2.3 %tables.1 = (bf16[384,96]{1,0:T(8,128)(2,1)S(1)}, bf16[384,96]{1,0:T(8,128)(2,1)S(1)}, bf16[384,96]{1,0:T(8,128)(2,1)S(1)}, bf16[384,96]{1,0:T(8,128)(2,1)S(1)},...) custom-call(s32[1,128]{1,0:T(1,128)S(1)} %bitcast.40, f32[1,128]{1,0:T(1,128)S(1)} %bitcast.30, ...), custom_call_target="tpu_custom_call" | custom-call | flops 1000000000 | bytes 1639424 | tf_op jit(solution)/shard_map/tables/pallas_call | solution.py:452
  48.7 4.2 %collective-permute-done.1.refs_2_ = f32[384,128]{1,0:T(8,128)S(1)} collective-permute-done((f32[384,128]{1,0:T(8,128)S(1)}, f32[384,128]{1,0:T(8,128)S(1)}, u32[]{:S(2)}, u32[]{:S(2)}) %collective-permute-start.1) | collective-permute-done | bytes 196640 | tf_op jit(solution)/shard_map/ppermute | solution.py:528
  53.0 6.1 %all-to-all-done.1 = f32[64,1,2304]{2,1,0:T(1,128)S(1)} async-done(((f32[64,1,2304]{2,1,0:T(1,128)}), f32[64,1,2304]{2,1,0:T(1,128)S(1)}, u32[]{:S(2)}, u32[]{:S(2)}) %all-to-all-start.1) | async-done | bytes 589856 | tf_op jit(solution)/shard_map/all_to_all | solution.py:467
  59.0 4.6 %apply.1 = (f32[384,128]{1,0:T(8,128)S(1)}, f32[768,128]{1,0:T(8,128)S(1)}, f32[1152,128]{1,0:T(8,128)}) custom-call(f32[1152,128]{1,0:T(8,128)S(1)} %bitcast.19, f32[64,128]{1,0:T(8,128)S(1)} %get-tuple-element.49.meta_ref, f32[64,128]{1,0:T(8,128)S(1)} %get-tuple-element.53.asked_ref, s32[1,128]{1,0:T(1,128)S(1)} %bitcast.41, f32[1,128]{1,0:T(1,128)S(1)} %bitcast.31, ...), custom_call_target="tpu_custom_call" | custom-call | bytes 2328576 | tf_op jit(solution)/shard_map/apply/pallas_call | solution.py:452
  63.6 6.5 %all-to-all-start.2 = ((f32[64,1,2304]{2,1,0:T(1,128)}), f32[64,1,2304]{2,1,0:T(1,128)S(1)}, u32[]{:S(2)}, u32[]{:S(2)}) async-start(f32[64,1,2304]{2,1,0:T(1,128)} %bitcast.13), calls=%async_computation.2 | async-start | bytes 1179648 | tf_op jit(solution)/shard_map/all_to_all | solution.py:467
  70.1 1.0 turned.2
  71.1 2.5 %collective-permute-start.3 = (f32[512,128]{1,0:T(8,128)S(1)}, f32[512,128]{1,0:T(8,128)S(1)}, u32[]{:S(2)}, u32[]{:S(2)}) collective-permute-start(f32[512,128]{1,0:T(8,128)S(1)} %get-tuple-element.64), channel_id=1, source_target_pairs={{0,3},{1,0},{2,1},{3,2},{4,7},{5,4},{6,5},{7,6},{8,11},{9,8},{10,9... | collective-permute-start | bytes 786440 | tf_op jit(solution)/shard_map/ppermute | solution.py:528
  73.7 0.5 collective-permute-start.4
  74.2 0.6 collective-permute-start.5
  74.8 4.7 %collective-permute-done.3.refs_5_.rest_0_.refs_1_ = f32[512,128]{1,0:T(8,128)S(1)} collective-permute-done((f32[512,128]{1,0:T(8,128)S(1)}, f32[512,128]{1,0:T(8,128)S(1)}, u32[]{:S(2)}, u32[]{:S(2)}) %collective-permute-start.3) | collective-permute-done | bytes 262176 | tf_op jit(solution)/shard_map/ppermute | solution.py:528
  79.5 2.6 %collective-permute-done.4.refs_6_.rest_1_.refs_2_ = f32[512,128]{1,0:T(8,128)S(1)} collective-permute-done((f32[512,128]{1,0:T(8,128)S(1)}, f32[512,128]{1,0:T(8,128)S(1)}, u32[]{:S(2)}, u32[]{:S(2)}) %collective-permute-start.4) | collective-permute-done | bytes 262176 | tf_op jit(solution)/shard_map/ppermute | solution.py:528
  82.1 6.9 %collective-permute-done.5.refs_7_.rest_2_.refs_3_ = f32[512,128]{1,0:T(8,128)S(1)} collective-permute-done((f32[512,128]{1,0:T(8,128)S(1)}, f32[512,128]{1,0:T(8,128)S(1)}, u32[]{:S(2)}, u32[]{:S(2)}) %collective-permute-start.5) | collective-permute-done | bytes 262176 | tf_op jit(solution)/shard_map/ppermute | solution.py:528
  89.0 3.7 %gram.1.rest_3_ = f32[8,128]{1,0:T(8,128)S(1)} custom-call(s32[1]{0:T(128)} %bitcast.case_ref.rest_4_, f32[384,128]{1,0:T(8,128)S(1)} %get-tuple-element.58.field_ref.refs_0_, f32[384,128]{1,0:T(8,128)S(1)} %collective-permute-done.refs_1_, f32[384,128]{1,0:T(8,128)S(1)} %collective-permute-done.1.refs_2_, f32[384,128]{1,0:T(8,128)S(1)} %collective-permute-done.2.refs_3_, ...), custom_call_target="tpu_custom_call" | custom-call | bytes 1773572 | tf_op jit(solution)/shard_map/gram/pallas_call | solution.py:452
  92.7 5.5 %apply_last.1 = (f32[384,128]{1,0:T(8,128)S(1)}, f32[768,128]{1,0:T(8,128)S(1)}, f32[32,8,128]{2,1,0:T(8,128)}) custom-call(f32[1152,128]{1,0:T(8,128)S(1)} %bitcast.20, f32[64,128]{1,0:T(8,128)S(1)} %get-tuple-element.49.meta_ref, f32[64,128]{1,0:T(8,128)S(1)} %get-tuple-element.53.asked_ref, s32[1,128]{1,0:T(1,128)S(1)} %bitcast.43, ...), custom_call_target="tpu_custom_call" | custom-call | bytes 2660356 | tf_op jit(solution)/shard_map/apply_last/pallas_call | solution.py:452
  98.2 0.7 copy-done.13
  98.9 7.3 %all-to-all-start.3 = ((f32[32,8,128]{2,1,0:T(8,128)}), f32[32,8,128]{2,1,0:T(8,128)S(1)}, u32[]{:S(2)}, u32[]{:S(2)}) async-start(f32[32,8,128]{2,1,0:T(8,128)} %get-tuple-element.70), calls=%async_computation.3 | async-start | bytes 262144 | tf_op jit(solution)/shard_map/all_to_all | solution.py:557
  106.3 1.0 copy-done.14
  107.3 1.9 %turned.3 = (f32[128,128]{1,0:T(8,128)S(1)}, f32[512,128]{1,0:T(8,128)}, f32[512,128]{1,0:T(8,128)}, f32[512,128]{1,0:T(8,128)}) custom-call(s32[1]{0:T(128)} %bitcast.case_ref.rest_4_, f32[768,128]{1,0:T(8,128)S(1)} %copy-done.14, f32[384,128]{1,0:T(8,128)S(1)} %get-tuple-element.72.field_ref.refs_8_, s32[1,128]{1,0:T(1,128)S(1)} %bitcast.44, ...), custom_call_target="tpu_custom_call" | custom-call | flops 1000000000 | bytes 1638916 | tf_op jit(solution)/shard_map/turned/pallas_call | solution.py:452
  109.2 2.5 %collective-permute-start.6 = (f32[512,128]{1,0:T(8,128)}, f32[512,128]{1,0:T(8,128)S(1)}, u32[]{:S(2)}, u32[]{:S(2)}) collective-permute-start(f32[512,128]{1,0:T(8,128)} %get-tuple-element.73), channel_id=1, source_target_pairs={{0,3},{1,0},{2,1},{3,2},{4,7},{5,4},{6,5},{7,6},{8,11},{9,8},{10,9... | collective-permute-start | bytes 786440 | tf_op jit(solution)/shard_map/ppermute | solution.py:528
  111.7 0.5 collective-permute-start.7
  112.2 0.6 collective-permute-start.8
  112.8 2.7 %all-to-all-done.3 = f32[32,8,128]{2,1,0:T(8,128)S(1)} async-done(((f32[32,8,128]{2,1,0:T(8,128)}), f32[32,8,128]{2,1,0:T(8,128)S(1)}, u32[]{:S(2)}, u32[]{:S(2)}) %all-to-all-start.3) | async-done | bytes 131104 | tf_op jit(solution)/shard_map/all_to_all | solution.py:557
  115.4 0.7 sum.1
  116.1 6.5 %all-to-all-start.4 = ((f32[8,32,128]{2,1,0:T(8,128)}), f32[8,32,128]{2,1,0:T(8,128)S(1)}, u32[]{:S(2)}, u32[]{:S(2)}) async-start(f32[8,32,128]{2,1,0:T(8,128)} %sum.1), calls=%async_computation.4 | async-start | bytes 262144 | tf_op jit(solution)/shard_map/all_to_all | solution.py:563
  122.6 4.7 %collective-permute-done.8.refs_11_.refs_7_ = f32[512,128]{1,0:T(8,128)S(1)} collective-permute-done((f32[512,128]{1,0:T(8,128)}, f32[512,128]{1,0:T(8,128)S(1)}, u32[]{:S(2)}, u32[]{:S(2)}) %collective-permute-start.8) | collective-permute-done | bytes 262176 | tf_op jit(solution)/shard_map/ppermute | solution.py:528
  127.3 0.5 all-to-all-done.4.gram_ref
  127.9 8.8 %solve.1 = (f32[64,8,128]{2,1,0:T(8,128)S(1)}, f32[32,256]{1,0:T(8,128)S(1)}) custom-call(s32[1]{0:T(128)} %bitcast.case_ref.rest_4_, f32[8,32,128]{2,1,0:T(8,128)S(1)} %all-to-all-done.4.gram_ref), custom_call_target="tpu_custom_call" | custom-call | bytes 425988 | tf_op jit(solution)/shard_map/solve/pallas_call | solution.py:452
  136.7 0.4 bubble.1
  137.1 0.8 collective-permute-start.9
  137.9 1.2 collective-permute-start.10
  139.2 3.2 %ports.1 = (f32[384,128]{1,0:T(8,128)}, f32[384,128]{1,0:T(8,128)}) custom-call(f32[64,8,128]{2,1,0:T(8,128)S(1)} %get-tuple-element.77.coef, f32[384,128]{1,0:T(8,128)S(1)} %get-tuple-element.58.field_ref.refs_0_, f32[384,128]{1,0:T(8,128)S(1)} %collective-permute-done.refs_1_, f32[384,128]{1,0:T(8,128)S(1)} %collective-permute-done.1.refs_2_, ...), custom_call_target="tpu_custom_call" | custom-call | flops 1000000000 | bytes 3407872 | tf_op jit(solution)/shard_map/ports/pallas_call | solution.py:452
  142.3 0.2 collective-permute-done.10.refs_2_
  142.6 1.3 collective-permute-done.11.refs_3_
  143.8 0.7 join.1
  (36 shorter events, 0.1 us)
Async XLA Ops:
  0.6 0.7 copy-start.10
  0.6 0.7 copy-start.11
  0.7 0.7 copy-start.7
  0.7 0.7 copy-start.8
  0.7 0.7 copy-start.9
  1.4 0.9 copy-start
  2.3 0.9 copy-start.2
  3.3 0.9 copy-start.4
  6.1 26.4 %copy-start.6 = (f32[48,8,128]{2,1,0:T(8,128)S(1)}, f32[48,8,128]{2,1,0:T(8,128)}, u32[]{:S(2)}) copy-start(f32[48,8,128]{2,1,0:T(8,128)} %param.16) | copy-start | bytes 589828
  34.1 11.2 %copy-start.1 = (f32[64,8,128]{2,1,0:T(8,128)S(1)}, f32[64,8,128]{2,1,0:T(8,128)}, u32[]{:S(2)}) copy-start(f32[64,8,128]{2,1,0:T(8,128)} %param.15) | copy-start | bytes 786436
  34.1 11.2 %copy-start.3 = (f32[8,64,64]{2,1,0:T(8,128)S(1)}, f32[8,64,64]{2,1,0:T(8,128)}, u32[]{:S(2)}) copy-start(f32[8,64,64]{2,1,0:T(8,128)} %inverse_ref.3) | copy-start | bytes 393220
  34.1 11.2 %copy-start.5 = (f32[8,96,64]{1,2,0:T(8,128)S(1)}, f32[8,96,64]{1,2,0:T(8,128)}, u32[]{:S(2)}) copy-start(f32[8,96,64]{1,2,0:T(8,128)} %param.18) | copy-start | bytes 589828
  34.1 24.9 %all-to-all-start.1 = ((f32[64,1,2304]{2,1,0:T(1,128)}), f32[64,1,2304]{2,1,0:T(1,128)S(1)}, u32[]{:S(2)}, u32[]{:S(2)}) async-start(f32[64,1,2304]{2,1,0:T(1,128)} %bitcast.11), calls=%async_computation.1 | async-start | bytes 1179648 | tf_op jit(solution)/shard_map/all_to_all | solution.py:467
  40.5 8.3 %collective-permute-start.2 = (f32[384,128]{1,0:T(8,128)S(1)}, f32[384,128]{1,0:T(8,128)S(1)}, u32[]{:S(2)}, u32[]{:S(2)}) collective-permute-start(f32[384,128]{1,0:T(8,128)S(1)} %get-tuple-element.58.field_ref.refs_0_), channel_id=1, source_target_pairs={{0,1},{1,2},{2,3},{3,0},{4,5},{5,6},{6,7},{7,4},{8,9},{9,10},{10,1... | collective-permute-start | bytes 589832 | tf_op jit(solution)/shard_map/ppermute | solution.py:528
  41.7 11.2 %collective-permute-start.1 = (f32[384,128]{1,0:T(8,128)S(1)}, f32[384,128]{1,0:T(8,128)S(1)}, u32[]{:S(2)}, u32[]{:S(2)}) collective-permute-start(f32[384,128]{1,0:T(8,128)S(1)} %get-tuple-element.58.field_ref.refs_0_), channel_id=1, source_target_pairs={{0,2},{1,3},{2,0},{3,1},{4,6},{5,7},{6,4},{7,5},{8,10},{9,11},{10,... | collective-permute-start | bytes 589832 | tf_op jit(solution)/shard_map/ppermute | solution.py:528
  44.2 8.8 %collective-permute-start = (f32[384,128]{1,0:T(8,128)S(1)}, f32[384,128]{1,0:T(8,128)S(1)}, u32[]{:S(2)}, u32[]{:S(2)}) collective-permute-start(f32[384,128]{1,0:T(8,128)S(1)} %get-tuple-element.58.field_ref.refs_0_), channel_id=1, source_target_pairs={{0,3},{1,0},{2,1},{3,2},{4,7},{5,4},{6,5},{7,6},{8,11},{9,8},{10,9... | collective-permute-start | bytes 589832 | tf_op jit(solution)/shard_map/ppermute | solution.py:528
  45.4 1.0 copy-start.12
  48.7 21.4 %copy-start.17 = (bf16[512,96]{1,0:T(8,128)(2,1)}, bf16[512,96]{1,0:T(8,128)(2,1)S(1)}, u32[]{:S(2)}) copy-start(bf16[512,96]{1,0:T(8,128)(2,1)S(1)} %get-tuple-element.63.low_ref) | copy-start | bytes 294916
  63.6 29.1 %all-to-all-start.2 = ((f32[64,1,2304]{2,1,0:T(1,128)}), f32[64,1,2304]{2,1,0:T(1,128)S(1)}, u32[]{:S(2)}, u32[]{:S(2)}) async-start(f32[64,1,2304]{2,1,0:T(1,128)} %bitcast.13), calls=%async_computation.2 | async-start | bytes 1179648 | tf_op jit(solution)/shard_map/all_to_all | solution.py:467
  71.1 8.4 %collective-permute-start.3 = (f32[512,128]{1,0:T(8,128)S(1)}, f32[512,128]{1,0:T(8,128)S(1)}, u32[]{:S(2)}, u32[]{:S(2)}) collective-permute-start(f32[512,128]{1,0:T(8,128)S(1)} %get-tuple-element.64), channel_id=1, source_target_pairs={{0,3},{1,0},{2,1},{3,2},{4,7},{5,4},{6,5},{7,6},{8,11},{9,8},{10,9... | collective-permute-start | bytes 786440 | tf_op jit(solution)/shard_map/ppermute | solution.py:528
  73.7 8.5 %collective-permute-start.4 = (f32[512,128]{1,0:T(8,128)S(1)}, f32[512,128]{1,0:T(8,128)S(1)}, u32[]{:S(2)}, u32[]{:S(2)}) collective-permute-start(f32[512,128]{1,0:T(8,128)S(1)} %get-tuple-element.65), channel_id=1, source_target_pairs={{0,2},{1,3},{2,0},{3,1},{4,6},{5,7},{6,4},{7,5},{8,10},{9,11},{10,... | collective-permute-start | bytes 786440 | tf_op jit(solution)/shard_map/ppermute | solution.py:528
  74.2 14.8 %collective-permute-start.5 = (f32[512,128]{1,0:T(8,128)S(1)}, f32[512,128]{1,0:T(8,128)S(1)}, u32[]{:S(2)}, u32[]{:S(2)}) collective-permute-start(f32[512,128]{1,0:T(8,128)S(1)} %get-tuple-element.66), channel_id=1, source_target_pairs={{0,1},{1,2},{2,3},{3,0},{4,5},{5,6},{6,7},{7,4},{8,9},{9,10},{10,1... | collective-permute-start | bytes 786440 | tf_op jit(solution)/shard_map/ppermute | solution.py:528
  98.2 0.7 copy-start.13
  98.9 10.2 %copy-start.15 = (f32[384,128]{1,0:T(8,128)}, f32[384,128]{1,0:T(8,128)S(1)}, u32[]{:S(2)}) copy-start(f32[384,128]{1,0:T(8,128)S(1)} %get-tuple-element.72.field_ref.refs_8_) | copy-start | bytes 589828
  98.9 7.3 %copy-start.18 = (bf16[512,96]{1,0:T(8,128)(2,1)S(1)}, bf16[512,96]{1,0:T(8,128)(2,1)}, u32[]{:S(2)}) copy-start(bf16[512,96]{1,0:T(8,128)(2,1)} %copy-done.17) | copy-start | bytes 294916
  98.9 16.5 %all-to-all-start.3 = ((f32[32,8,128]{2,1,0:T(8,128)}), f32[32,8,128]{2,1,0:T(8,128)S(1)}, u32[]{:S(2)}, u32[]{:S(2)}) async-start(f32[32,8,128]{2,1,0:T(8,128)} %get-tuple-element.70), calls=%async_computation.3 | async-start | bytes 262144 | tf_op jit(solution)/shard_map/all_to_all | solution.py:557
  106.3 1.0 copy-start.14
  109.2 13.4 %collective-permute-start.6 = (f32[512,128]{1,0:T(8,128)}, f32[512,128]{1,0:T(8,128)S(1)}, u32[]{:S(2)}, u32[]{:S(2)}) collective-permute-start(f32[512,128]{1,0:T(8,128)} %get-tuple-element.73), channel_id=1, source_target_pairs={{0,3},{1,0},{2,1},{3,2},{4,7},{5,4},{6,5},{7,6},{8,11},{9,8},{10,9... | collective-permute-start | bytes 786440 | tf_op jit(solution)/shard_map/ppermute | solution.py:528
  111.7 11.0 %collective-permute-start.7 = (f32[512,128]{1,0:T(8,128)}, f32[512,128]{1,0:T(8,128)S(1)}, u32[]{:S(2)}, u32[]{:S(2)}) collective-permute-start(f32[512,128]{1,0:T(8,128)} %get-tuple-element.74), channel_id=1, source_target_pairs={{0,2},{1,3},{2,0},{3,1},{4,6},{5,7},{6,4},{7,5},{8,10},{9,11},{10,... | collective-permute-start | bytes 786440 | tf_op jit(solution)/shard_map/ppermute | solution.py:528
  112.2 15.2 %collective-permute-start.8 = (f32[512,128]{1,0:T(8,128)}, f32[512,128]{1,0:T(8,128)S(1)}, u32[]{:S(2)}, u32[]{:S(2)}) collective-permute-start(f32[512,128]{1,0:T(8,128)} %get-tuple-element.75), channel_id=1, source_target_pairs={{0,1},{1,2},{2,3},{3,0},{4,5},{5,6},{6,7},{7,4},{8,9},{9,10},{10,1... | collective-permute-start | bytes 786440 | tf_op jit(solution)/shard_map/ppermute | solution.py:528
  116.1 11.8 %all-to-all-start.4 = ((f32[8,32,128]{2,1,0:T(8,128)}), f32[8,32,128]{2,1,0:T(8,128)S(1)}, u32[]{:S(2)}, u32[]{:S(2)}) async-start(f32[8,32,128]{2,1,0:T(8,128)} %sum.1), calls=%async_computation.4 | async-start | bytes 262144 | tf_op jit(solution)/shard_map/all_to_all | solution.py:563
  136.7 2.5 %copy-start.16 = (f32[384,128]{1,0:T(8,128)S(1)}, f32[384,128]{1,0:T(8,128)}, u32[]{:S(2)}) copy-start(f32[384,128]{1,0:T(8,128)} %copy-done.15) | copy-start | bytes 589828
  137.1 5.3 %collective-permute-start.9 = (f32[128,128]{1,0:T(8,128)S(1)}, f32[128,128]{1,0:T(8,128)S(1)}, u32[]{:S(2)}, u32[]{:S(2)}) collective-permute-start(f32[128,128]{1,0:T(8,128)S(1)} %get-tuple-element.88), channel_id=1, source_target_pairs={{0,3},{1,0},{2,1},{3,2},{4,7},{5,4},{6,5},{7,6},{8,11},{9,8},{10,9... | collective-permute-start | bytes 196616 | tf_op jit(solution)/shard_map/ppermute | solution.py:528
  137.9 4.6 %collective-permute-start.10 = (f32[128,128]{1,0:T(8,128)S(1)}, f32[128,128]{1,0:T(8,128)S(1)}, u32[]{:S(2)}, u32[]{:S(2)}) collective-permute-start(f32[128,128]{1,0:T(8,128)S(1)} %get-tuple-element.89), channel_id=1, source_target_pairs={{0,2},{1,3},{2,0},{3,1},{4,6},{5,7},{6,4},{7,5},{8,10},{9,11},{10,... | collective-permute-start | bytes 196616 | tf_op jit(solution)/shard_map/ppermute | solution.py:528
  139.2 4.7 %collective-permute-start.11 = (f32[128,128]{1,0:T(8,128)S(1)}, f32[128,128]{1,0:T(8,128)S(1)}, u32[]{:S(2)}, u32[]{:S(2)}) collective-permute-start(f32[128,128]{1,0:T(8,128)S(1)} %get-tuple-element.90), channel_id=1, source_target_pairs={{0,1},{1,2},{2,3},{3,0},{4,5},{5,6},{6,7},{7,4},{8,9},{9,10},{10,1... | collective-permute-start | bytes 196616 | tf_op jit(solution)/shard_map/ppermute | solution.py:528

commit v3 on v2

--- a/solution.py
+++ b/solution.py
@@ -33,21 +33,24 @@
     return high, (x - high.astype(F32)).astype(BF16)
 
 
-def split3(x):
-    high = x.astype(BF16)
-    rest = x - high.astype(F32)
-    middle = rest.astype(BF16)
-    return high, middle, (rest - middle.astype(F32)).astype(BF16)
+def pick_right(x, onehot, dims):
+    (left,), (right,) = dims[0]
+    return dot(jnp.concatenate(split2(x), axis=left), jnp.concatenate([onehot, onehot], axis=right), dims)
 
 
 def pick_left(onehot, x, dims):
-    a, b, c = split3(x)
-    return dot(onehot, a, dims) + dot(onehot, b, dims) + dot(onehot, c, dims)
-
-
-def pick_right(x, onehot, dims):
-    a, b, c = split3(x)
-    return dot(a, onehot, dims) + dot(b, onehot, dims) + dot(c, onehot, dims)
+    (left,), (right,) = dims[0]
+    return dot(jnp.concatenate([onehot, onehot], axis=left), jnp.concatenate(split2(x), axis=right), dims)
+
+
+def stacked_table(table):
+    high, low = split2(table)
+    return jnp.concatenate([high, high, low], axis=1)
+
+
+def stacked_values(x):
+    high, low = split2(x)
+    return jnp.concatenate([high, low, high], axis=0)
 
 
 def iota(shape, dim):
@@ -124,30 +127,36 @@
     return chosen
 
 
-def table_product(high, low, x):
-    a, b = split2(x)
-    return dot(high, a) + (dot(high, b) + dot(low, a))
-
-
 def condense_kernel(
-    parts, kind_ref, stiff_ref, near_ref, owner_ref, far_ref, load_ref, inverse_ref, coupling_ref,
-    pay_ref, near_sum_ref, meta_ref, near_part, far_part,
+    parts, kind_hbm, stiff_hbm, near_hbm, owner_hbm, far_hbm, load_hbm, inverse_hbm, coupling_hbm,
+    pay_ref, near_sum_ref, meta_ref,
+    kind_ref, stiff_ref, near_ref, owner_ref, far_ref, load_ref, inverse_ref, coupling_ref, near_part, far_part, sems,
 ):
+    copies = [
+        pltpu.make_async_copy(source, target, sems.at[i])
+        for i, (source, target) in enumerate((
+            (inverse_hbm, inverse_ref), (coupling_hbm, coupling_ref), (load_hbm, load_ref), (kind_hbm, kind_ref),
+            (stiff_hbm, stiff_ref), (near_hbm, near_ref), (owner_hbm, owner_ref), (far_hbm, far_ref),
+        ))
+    ]
+    for copy in copies:
+        copy.start()
+    for copy in copies:
+        copy.wait()
     modes = load_ref.shape[0] // CASES
     dofs = near_sum_ref.shape[0] // CASES
-    table = jnp.concatenate(
-        [jnp.transpose(dot_high(inverse_ref[t], coupling_ref[t], TN)) for t in range(KINDS)], axis=0
+    left = stacked_table(
+        jnp.concatenate(
+            [jnp.transpose(dot_high(inverse_ref[t], coupling_ref[t], TN)) for t in range(KINDS)], axis=0
+        )
     )
-    high, low = split2(table)
-    left = jnp.concatenate([high, high, low], axis=1)
     kind = kind_ref[...]
     kind2 = jnp.concatenate([kind, kind], axis=1)
     for k in range(0, CASES, 2):
         loads = jnp.concatenate(
             [load_ref[pl.ds(k + i, modes, stride=CASES), :] for i in range(2)], axis=1
         )
-        a, b = split2(loads)
-        condensed = -by_kind(dot(left, jnp.concatenate([a, b, a], axis=0)), kind2, 2 * dofs)
+        condensed = -by_kind(dot(left, stacked_values(loads)), kind2, 2 * dofs)
         for i in range(2):
             lanes = slice(i * LANES, (i + 1) * LANES)
             near_part[pl.ds(k + i, dofs, stride=CASES), :] = condensed[:dofs, lanes]
@@ -174,7 +183,7 @@
 
 def tables_kernel(
     kind_ref, stiff_ref, load_ref, inverse_ref, coupling_ref, block_ref,
-    near_high, near_low, far_high, far_low, turned_high, turned_low, base_ref,
+    near_near, near_far, far_near, far_far, turned_near, turned_far, base_ref,
 ):
     dofs = block_ref.shape[1] // 2
     modes = inverse_ref.shape[1]
@@ -182,16 +191,27 @@
     for t in range(KINDS):
         turned = dot_high(inverse_ref[t], coupling_ref[t], TN)
         schur = block_ref[t] - dot_high(turned, coupling_ref[t], TN)
-        near_high[t * dofs : (t + 1) * dofs, :], near_low[t * dofs : (t + 1) * dofs, :] = split2(schur[:dofs])
-        far_high[t * dofs : (t + 1) * dofs, :], far_low[t * dofs : (t + 1) * dofs, :] = split2(schur[dofs:])
-        turned_high[t * modes : (t + 1) * modes, :], turned_low[t * modes : (t + 1) * modes, :] = split2(turned)
+        at = slice(t * dofs, (t + 1) * dofs)
+        near_near[at, :] = stacked_table(schur[:dofs, :dofs])
+        near_far[at, :] = stacked_table(schur[:dofs, dofs:])
+        far_near[at, :] = stacked_table(schur[dofs:, :dofs])
+        far_far[at, :] = stacked_table(schur[dofs:, dofs:])
+        at = slice(t * modes, (t + 1) * modes)
+        turned_near[at, :] = stacked_table(turned[:, :dofs])
+        turned_far[at, :] = stacked_table(turned[:, dofs:])
         inverses.append(inverse_ref[t])
-    high, low = split2(jnp.concatenate(inverses, axis=0))
+    left = stacked_table(jnp.concatenate(inverses, axis=0))
     kind = kind_ref[...]
     stiff = stiff_ref[...]
-    for k in range(CASES):
-        loads = load_ref[pl.ds(k, modes, stride=CASES), :]
-        base_ref[pl.ds(k, modes, stride=CASES), :] = by_kind(table_product(high, low, loads), kind, modes) / stiff
+    kind2 = jnp.concatenate([kind, kind], axis=1)
+    stiff2 = jnp.concatenate([stiff, stiff], axis=1)
+    for k in range(0, CASES, 2):
+        loads = jnp.concatenate(
+            [load_ref[pl.ds(k + i, modes, stride=CASES), :] for i in range(2)], axis=1
+        )
+        result = by_kind(dot(left, stacked_values(loads)), kind2, modes) / stiff2
+        for i in range(2):
+            base_ref[pl.ds(k + i, modes, stride=CASES), :] = result[:, i * LANES : (i + 1) * LANES]
 
 
 def send_ports(field, asked, own, pay_ref):
@@ -208,89 +228,148 @@
     send_ports(field, asked_hot, port_onehot(meta_ref[...]), pay_ref)
 
 
-def apply_kernel(
-    parts, groups, last, arrived_ref, meta_ref, asked_ref, kind_ref, stiff_ref, near_ref, owner_ref,
-    near_high, near_low, far_high, far_low, field_ref, *rest,
+def component_products(table_ref, part_ref, kind_ref, stiff_ref, out_ref):
+    dofs = part_ref.shape[0] // CASES
+    kind, stiff = kind_ref[...], stiff_ref[...]
+    kind2 = jnp.concatenate([kind, kind], axis=1)
+    stiff2 = jnp.concatenate([stiff, stiff], axis=1)
+    for k in range(0, CASES, 2):
+        values = jnp.concatenate(
+            [part_ref[pl.ds(k + i, dofs, stride=CASES), :] for i in range(2)], axis=1
+        )
+        result = by_kind(dot(table_ref[...], stacked_values(values)), kind2, dofs) * stiff2
+        for i in range(2):
+            out_ref[pl.ds(k + i, dofs, stride=CASES), :] = result[:, i * LANES : (i + 1) * LANES]
+
+
+def slot_products(table_ref, slot_ref, asked, out_ref):
+    tiles = slot_ref.shape[0]
+    dofs = slot_ref.shape[1] // CASES
+    spare = tiles * LANES - SLOTS * asked.shape[0]
+    kind = pad_lanes(stacked_rows(asked, SLOTS), spare).astype(jnp.int32)
+    stiff = pad_lanes(stacked_rows(asked, 2 * SLOTS), spare)
+    for k in range(CASES):
+        values = jnp.concatenate(
+            [slot_ref[g, pl.ds(k, dofs, stride=CASES), :] for g in range(tiles)], axis=1
+        )
+        result = by_kind(dot(table_ref[...], stacked_values(values)), kind, dofs) * stiff
+        for g in range(tiles):
+            out_ref[g, pl.ds(k, dofs, stride=CASES), :] = result[:, g * LANES : (g + 1) * LANES]
+
+
+def wide_onehot(asked_hot, tiles):
+    spare = tiles * LANES - asked_hot.shape[0]
+    if not spare:
+        return asked_hot
+    return jnp.concatenate([asked_hot, jnp.zeros((spare, LANES), BF16)], axis=0)
+
+
+def slots_to_ports(part_ref, asked_hot):
+    tiles = part_ref.shape[0]
+    hot = wide_onehot(asked_hot, tiles)
+    total = pick_right(part_ref[0], hot[:LANES], NN)
+    for g in range(1, tiles):
+        total = total + pick_right(part_ref[g], hot[g * LANES : (g + 1) * LANES], NN)
+    return total
+
+
+def inner_kernel(
+    field_ref, asked_ref, kind_ref, stiff_ref, near_ref, near_near, far_far,
+    inner_ref, near_values, near_part, slot_ref, slot_part,
+):
+    field, asked = field_ref[...], asked_ref[...]
+    near_hot, asked_hot = near_onehot(near_ref[...]), port_onehot(asked)
+    tiles = slot_ref.shape[0]
+    near_values[...] = pick_right(field, near_hot, NT)
+    values = pick_right(field, wide_onehot(asked_hot, tiles), NT)
+    for g in range(tiles):
+        slot_ref[g] = values[:, g * LANES : (g + 1) * LANES]
+    component_products(near_near, near_values, kind_ref, stiff_ref, near_part)
+    slot_products(far_far, slot_ref, asked, slot_part)
+    inner_ref[...] = pick_right(near_part[...], near_hot, NN) + slots_to_ports(slot_part, asked_hot)
+
+
+def near_cross(parts, arrived_ref, pitch, kind_ref, stiff_ref, near_ref, owner_ref, near_far, far_values, near_part):
+    slots = onehot(jnp.concatenate(owner_slots(owner_ref[...], parts), axis=0))
+    far_values[...] = pick_right(get(arrived_ref, 0, pitch, 3), slots, TN)
+    component_products(near_far, far_values, kind_ref, stiff_ref, near_part)
+    return pick_right(near_part[...], near_onehot(near_ref[...]), NN)
+
+
+def far_cross(arrived_ref, first, pitch, asked, asked_hot, far_near, slot_ref, slot_part):
+    tiles = slot_ref.shape[0]
+    values = jnp.transpose(get(arrived_ref, first, pitch, 3))
+    values = pad_lanes(values, tiles * LANES - values.shape[1])
+    for g in range(tiles):
+        slot_ref[g] = values[:, g * LANES : (g + 1) * LANES]
+    slot_products(far_near, slot_ref, asked, slot_part)
+    return slots_to_ports(slot_part, asked_hot)
+
+
+def image_kernel(
+    parts, groups, last, arrived_ref, inner_ref, asked_ref, kind_ref, stiff_ref, near_ref, owner_ref,
+    near_far, far_near, *rest,
 ):
     if last:
-        others, rest = rest[: groups - 1], rest[groups - 1 :]
-        gram_ref, case_ref, image_ref, spread_ref, copies_ref, slot_ref, near_part, far_part = rest
+        case_ref, gram_ref, rest = rest[0], rest[1], rest[2:]
+        images, (image_ref, far_values, copies_ref, near_part, slot_ref, slot_part) = rest[:groups], rest[groups:]
     else:
-        image_ref, spread_ref, pay_ref, slot_ref, near_part, far_part = rest
-    rows = field_ref.shape[0]
-    dofs = rows // CASES
-    field = field_ref[...]
+        meta_ref, image_ref, far_values, pay_ref, near_part, slot_ref, slot_part = rest
     asked = asked_ref[...]
     asked_hot = port_onehot(asked)
-    near_hot = near_onehot(near_ref[...])
     slots = onehot(jnp.concatenate(owner_slots(owner_ref[...], parts), axis=0))
-    spread_ref[:rows, :] = pick_right(field, near_hot, NT)
-    spread_ref[rows:, :] = pick_right(get(arrived_ref, 0, 18, 3), slots, TN)
+    far_values[...] = pick_right(get(arrived_ref, 0, 18, 3), slots, TN)
+    component_products(near_far, far_values, kind_ref, stiff_ref, near_part)
     tiles = slot_ref.shape[0]
-    spare = tiles * LANES - SLOTS * parts
-    wide_hot = asked_hot
-    if spare:
-        wide_hot = jnp.concatenate([asked_hot, jnp.zeros((spare, LANES), BF16)], axis=0)
-    from_near = pad_lanes(jnp.transpose(get(arrived_ref, 9, 18, 3)), spare)
-    from_far = pick_right(field, wide_hot, NT)
+    values = jnp.transpose(get(arrived_ref, 9, 18, 3))
+    values = pad_lanes(values, tiles * LANES - values.shape[1])
     for g in range(tiles):
-        lanes = slice(g * LANES, (g + 1) * LANES)
-        slot_ref[g, :rows, :] = from_near[:, lanes]
-        slot_ref[g, rows:, :] = from_far[:, lanes]
-    kind = kind_ref[...]
-    stiff = stiff_ref[...]
-    kind2 = jnp.concatenate([kind, kind], axis=1)
-    stiff2 = jnp.concatenate([stiff, stiff], axis=1)
-    asked_kind = pad_lanes(stacked_rows(asked, SLOTS), spare).astype(jnp.int32)
-    asked_stiff = pad_lanes(stacked_rows(asked, 2 * SLOTS), spare)
-    for k in range(0, CASES, 2):
-        values = jnp.concatenate(
-            [spread_ref[pl.ds(k + i, 2 * dofs, stride=CASES), :] for i in range(2)], axis=1
-        )
-        result = by_kind(table_product(near_high[...], near_low[...], values), kind2, dofs) * stiff2
-        for i in range(2):
-            near_part[pl.ds(k + i, dofs, stride=CASES), :] = result[:, i * LANES : (i + 1) * LANES]
-    for k in range(CASES):
-        values = jnp.concatenate(
-            [slot_ref[g, pl.ds(k, 2 * dofs, stride=CASES), :] for g in range(tiles)], axis=1
-        )
-        result = by_kind(table_product(far_high[...], far_low[...], values), asked_kind, dofs) * asked_stiff
-        for g in range(tiles):
-            far_part[g, pl.ds(k, dofs, stride=CASES), :] = result[:, g * LANES : (g + 1) * LANES]
-    image = pick_right(near_part[...], near_hot, NN)
-    for g in range(tiles):
-        image = image + pick_right(far_part[g], wide_hot[g * LANES : (g + 1) * LANES], NN)
+        slot_ref[g] = values[:, g * LANES : (g + 1) * LANES]
+    slot_products(far_near, slot_ref, asked, slot_part)
+    image = inner_ref[...] + pick_right(near_part[...], near_onehot(near_ref[...]), NN)
+    image = image + slots_to_ports(slot_part, asked_hot)
     image_ref[...] = image
     if last:
-        gram = add_products(
-            LANES, [field_ref, *others], [image_ref], [3 * groups * CASES], case_ref[0], gram_ref[...]
-        )
+        gram = add_products(LANES, images, [image_ref], [3 * groups * CASES], case_ref[0], gram_ref[...])
         for p in range(copies_ref.shape[0]):
             copies_ref[p] = gram
     else:
         send_ports(image, asked_hot, port_onehot(meta_ref[...]), pay_ref)
 
 
-def turned_kernel(groups, case_ref, spread_ref, field_ref, kind_ref, high_ref, low_ref, *rest):
-    own_ref, messages, out_ref = rest[0], rest[1:groups], rest[groups]
-    dofs2 = spread_ref.shape[0] // CASES
-    rows = field_ref.shape[0]
+def turned_rows(near_values, far_values, kind_ref, turned_near, turned_far, out_ref):
+    dofs = near_values.shape[0] // CASES
     modes = out_ref.shape[0] // CASES
-    part = out_ref.shape[0] // groups
     kind = kind_ref[...]
     kind2 = jnp.concatenate([kind, kind], axis=1)
     for k in range(0, CASES, 2):
-        values = jnp.concatenate(
-            [spread_ref[pl.ds(k + i, dofs2, stride=CASES), :] for i in range(2)], axis=1
-        )
-        result = by_kind(table_product(high_ref[...], low_ref[...], values), kind2, modes)
+        sums = 0.0
+        for table, part in ((turned_near, near_values), (turned_far, far_values)):
+            values = jnp.concatenate(
+                [part[pl.ds(k + i, dofs, stride=CASES), :] for i in range(2)], axis=1
+            )
+            sums = sums + dot(table[...], stacked_values(values))
+        result = by_kind(sums, kind2, modes)
         for i in range(2):
             out_ref[pl.ds(k + i, modes, stride=CASES), :] = result[:, i * LANES : (i + 1) * LANES]
-    own_ref[...] = out_ref[pl.ds(pl.multiple_of(case_ref[0] * part, part), part), :]
-    for h in range(1, groups):
-        at = lax.rem(case_ref[0] + h, groups)
-        messages[h - 1][:rows, :] = field_ref[...]
-        messages[h - 1][rows:, :] = out_ref[pl.ds(pl.multiple_of(at * part, part), part), :]
+
+
+def quarter(ref, case_ref, h, groups):
+    part = ref.shape[0] // groups
+    return ref[pl.ds(pl.multiple_of(lax.rem(case_ref[0] + h, groups) * part, part), part), :]
+
+
+def turned_kernel(groups, first, case_ref, near_values, far_values, kind_ref, turned_near, turned_far, *rest):
+    if not first:
+        field_ref, rest = rest[0], rest[1:]
+    outs, out_ref = rest[:groups], rest[groups]
+    turned_rows(near_values, far_values, kind_ref, turned_near, turned_far, out_ref)
+    for h in range(groups):
+        at = 0
+        if h and not first:
+            at = field_ref.shape[0]
+            outs[h][:at, :] = field_ref[...]
+        outs[h][at:, :] = quarter(out_ref, case_ref, h, groups)
 
 
 def add_products(lanes, lefts, rights, first, case, out):
@@ -335,19 +414,37 @@
             out_ref[p, q * CASES : (q + 1) * CASES, :] = total
 
 
+def inverse2(p, q, r, s):
+    scale = 1.0 / (p * s - q * r)
+    return s * scale, -q * scale, -r * scale, p * scale
+
+
 def spd_solve(matrix, target):
     n = matrix.shape[0]
     a = jnp.concatenate([matrix, target], axis=1)
     row_of = iota(a.shape, 0)
-    for k in range(0, n, 2):
-        r0, r1 = a[k : k + 1, :], a[k + 1 : k + 2, :]
-        c0, c1 = a[:, k : k + 1], a[:, k + 1 : k + 2]
-        p00, p01, p10, p11 = c0[k : k + 1], c1[k : k + 1], c0[k + 1 : k + 2], c1[k + 1 : k + 2]
-        scale = 1.0 / (p00 * p11 - p01 * p10)
-        u0 = (r0 * p11 - r1 * p01) * scale
-        u1 = (r1 * p00 - r0 * p10) * scale
-        a = a - (c0 * u0 + c1 * u1)
-        a = jnp.where(row_of == k, u0, jnp.where(row_of == k + 1, u1, a))
+    for k in range(0, n, 4):
+        c = [jnp.broadcast_to(a[:, k + i : k + i + 1], a.shape) for i in range(4)]
+        r = [a[k + i : k + i + 1] for i in range(4)]
+        p = [[c[j][k + i : k + i + 1] for j in range(4)] for i in range(4)]
+        a00, a01, a10, a11 = inverse2(p[0][0], p[0][1], p[1][0], p[1][1])
+        e00, e01 = p[2][0] * a00 + p[2][1] * a10, p[2][0] * a01 + p[2][1] * a11
+        e10, e11 = p[3][0] * a00 + p[3][1] * a10, p[3][0] * a01 + p[3][1] * a11
+        i00, i01, i10, i11 = inverse2(
+            p[2][2] - (e00 * p[0][2] + e01 * p[1][2]),
+            p[2][3] - (e00 * p[0][3] + e01 * p[1][3]),
+            p[3][2] - (e10 * p[0][2] + e11 * p[1][2]),
+            p[3][3] - (e10 * p[0][3] + e11 * p[1][3]),
+        )
+        t2 = r[2] - (e00 * r[0] + e01 * r[1])
+        t3 = r[3] - (e10 * r[0] + e11 * r[1])
+        u2, u3 = i00 * t2 + i01 * t3, i10 * t2 + i11 * t3
+        w0 = r[0] - (p[0][2] * u2 + p[0][3] * u3)
+        w1 = r[1] - (p[1][2] * u2 + p[1][3] * u3)
+        u = [a00 * w0 + a01 * w1, a10 * w0 + a11 * w1, u2, u3]
+        a = a - ((c[0] * u[0] + c[1] * u[1]) + (c[2] * u[2] + c[3] * u[3]))
+        for i in range(4):
+            a = jnp.where(row_of == k + i, u[i], a)
     return a[:, n:]
 
 
@@ -385,20 +482,15 @@
     n = groups * CASES
     part = turned0[0].shape[0]
     coef = jnp.concatenate([coef_ref[:, :n], coef_ref[:, LANES : LANES + n]], axis=1)
-    high, low = split2(coef)
-    left = jnp.concatenate([high, high, low], axis=1)
+    left = stacked_table(coef)
     for m in range(0, part // CASES, 2):
         values = []
         for i in range(2):
             at = (m + i) * CASES
-            pieces = [
-                ref[at + (0 if h == 0 else rows) : at + (0 if h == 0 else rows) + CASES, :]
-                for refs_ in (turned0, turned1)
-                for h, ref in enumerate(refs_)
-            ]
+            pieces = [ref[at : at + CASES, :] for ref in turned0]
+            pieces += [ref[at + shift : at + shift + CASES, :] for ref, shift in zip(turned1, [0] + [rows] * (groups - 1))]
             values.append(jnp.concatenate(pieces, axis=0))
-        a, b = split2(jnp.concatenate(values, axis=1))
-        result = dot(left, jnp.concatenate([a, b, a], axis=0))
+        result = dot(left, stacked_values(jnp.concatenate(values, axis=1)))
         for i in range(2):
             for h in range(groups):
                 outs[h][(m + i) * CASES : (m + i + 1) * CASES, :] = result[
@@ -442,20 +534,23 @@
         out_ref[at, :] = bubble_ref[at, :] - parts[h][...]
 
 
-def call(kernel, outs, scratch=(), name=None, flops=0, smem=(), limit=12):
+def call(kernel, outs, scratch=(), name=None, flops=0, smem=(), hbm=False):
     outs = [jax.ShapeDtypeStruct(shape, dtype) for shape, dtype in outs]
     vmem = pl.BlockSpec(memory_space=pltpu.VMEM)
 
     def run(*args):
-        specs = [pl.BlockSpec(memory_space=pltpu.SMEM) if i in smem else vmem for i in range(len(args))]
+        usual = pl.BlockSpec(memory_space=pltpu.HBM) if hbm else vmem
+        specs = [pl.BlockSpec(memory_space=pltpu.SMEM) if i in smem else usual for i in range(len(args))]
         moved = sum(a.size * a.dtype.itemsize for a in args) + sum(o.size * o.dtype.itemsize for o in outs)
+        fetched = [pltpu.VMEM(a.shape, a.dtype) for a in args] if hbm else []
+        sems = [pltpu.SemaphoreType.DMA((len(args),))] if hbm else []
         return pl.pallas_call(
             kernel,
             out_shape=outs,
             in_specs=specs,
             out_specs=[vmem] * len(outs),
-            scratch_shapes=[pltpu.VMEM(shape, F32) for shape in scratch],
-            compiler_params=pltpu.CompilerParams(vmem_limit_bytes=limit << 20),
+            scratch_shapes=fetched + [pltpu.VMEM(shape, F32) for shape in scratch] + sems,
+            compiler_params=pltpu.CompilerParams(vmem_limit_bytes=12 << 20),
             cost_estimate=pl.CostEstimate(flops=flops, bytes_accessed=moved, transcendentals=0),
             name=name,
         )(*args)
@@ -492,14 +587,14 @@
         [((parts * 10, LANES), F32), field_of, meta_of],
         [(rows, comps)] * 2,
         "condense",
+        hbm=True,
     )(kind, stiff, near, owner, far, loads, bubble_inverse, coupling)
-    tables = call(
+    near_near, near_far, far_near, far_far, turned_near, turned_far, bubble_base = call(
         tables_kernel,
-        [((KINDS * dofs, 2 * dofs), BF16)] * 4 + [((KINDS * modes, 2 * dofs), BF16)] * 2 + [((bubbles, comps), F32)],
+        [((KINDS * dofs, 3 * dofs), BF16)] * 4 + [((KINDS * modes, 3 * dofs), BF16)] * 2 + [((bubbles, comps), F32)],
         name="tables",
         flops=10**9,
     )(kind, stiff, loads, bubble_inverse, coupling, port_block)
-    schur, turned_tables, bubble_base = tables[:4], tables[4:6], tables[6]
     base, pay, asked = call(
         functools.partial(rhs_kernel, parts),
         [field_of, ((parts * 18, LANES), F32), meta_of],
@@ -507,21 +602,10 @@
     )(exchange(pay, parts), near_sum, port_load.reshape(rows, ports), meta)
 
     case = lax.axis_index("case").reshape(1)
-    spread_of = ((2 * rows, comps), F32)
-    scratch = [(slot_tiles, 2 * rows, LANES), (rows, comps), (slot_tiles, rows, LANES)]
-
     part = bubbles // groups
-
-    def turned(spread, field):
-        own, *messages = call(
-            functools.partial(turned_kernel, groups),
-            [((part, comps), F32)] + [((rows + part, comps), F32)] * (groups - 1),
-            [(bubbles, comps)],
-            name="turned",
-            flops=10**9,
-            smem=(0,),
-        )(case, spread, field, kind, *turned_tables)
-        return own, messages
+    part_of = ((part, comps), F32)
+    slot_scratch = [(slot_tiles, rows, LANES)] * 2
+    where = (kind, stiff, near, owner)
 
     def to_cases(messages):
         backward = [
@@ -530,38 +614,59 @@
         ]
         return backward[::-1]
 
+    def inner(field):
+        return call(inner_kernel, [field_of] * 2, [(rows, comps)] + slot_scratch, "inner", flops=10**9)(
+            field, asked, kind, stiff, near, near_near, far_far
+        )
+
     arrived = exchange(pay, parts)
-    base_all = [base, *to_cases([base] * (groups - 1))]
+    base_all = to_cases([base] * (groups - 1))
+    base_inner, base_near = inner(base)
     arrived, *base_all = lax.optimization_barrier((arrived, *base_all))
-    shared = (meta, asked, kind, stiff, near, owner, *schur)
-    image, spread, pay = call(
-        functools.partial(apply_kernel, parts, groups, False),
-        [field_of, spread_of, ((parts * 18, LANES), F32)],
-        scratch,
-        "apply",
-    )(arrived, *shared, base_all[0])
+    image, base_far, pay = call(
+        functools.partial(image_kernel, parts, groups, False),
+        [field_of] * 2 + [((parts * 18, LANES), F32)],
+        [(rows, comps)] + slot_scratch,
+        "image",
+    )(arrived, base_inner, asked, *where, near_far, far_near, meta)
     arrived = exchange(pay, parts)
-    turned0, messages = turned(spread, image)
-    both0 = to_cases(messages)
+    image_all = to_cases([image] * (groups - 1))
+    image_inner, image_near = inner(image)
+    turned0, *messages = call(
+        functools.partial(turned_kernel, groups, True),
+        [part_of] * groups,
+        [(bubbles, comps)],
+        name="turned",
+        flops=10**9,
+        smem=(0,),
+    )(case, base_near, base_far, kind, turned_near, turned_far)
+    turned0_all = to_cases(messages)
     (gram,) = call(functools.partial(gram_kernel, groups), [((cases, LANES), F32)], name="gram", smem=(0,))(
-        case, *base_all, image, *both0
+        case, base, *base_all, image, *image_all
     )
+    arrived, *turned0_all = lax.optimization_barrier((arrived, *turned0_all))
     minor = lax.axis_size("py")
-    second, spread, copies = call(
-        functools.partial(apply_kernel, parts, groups, True),
-        [field_of, spread_of, ((groups * minor, cases, LANES), F32)],
-        scratch,
-        "apply_last",
-        smem=(12 + groups,),
-    )(arrived, *shared, image, *both0, gram, case)
+    second, image_far, copies = call(
+        functools.partial(image_kernel, parts, groups, True),
+        [field_of] * 2 + [((groups * minor, cases, LANES), F32)],
+        [(rows, comps)] + slot_scratch,
+        "second",
+        smem=(9,),
+    )(arrived, image_inner, asked, *where, near_far, far_near, case, gram, image, *image_all)
     copies = lax.all_to_all(copies, ("case", "py"), split_axis=0, concat_axis=0)
-    turned1, messages = turned(spread, second)
+    turned1, *messages = call(
+        functools.partial(turned_kernel, groups, False),
+        [part_of] + [((rows + part, comps), F32)] * (groups - 1),
+        [(bubbles, comps)],
+        "turned_second",
+        flops=10**9,
+        smem=(0,),
+    )(case, image_near, image_far, kind, turned_near, turned_far, second)
     both1 = to_cases(messages)
     (copies,) = call(sum_kernel, [((parts // minor, groups * cases, LANES), F32)], name="sum")(
         copies.reshape(groups, minor, cases, LANES)
     )
     copies = lax.all_to_all(copies, "px", split_axis=0, concat_axis=0)
-    copies, *both1 = lax.optimization_barrier((copies, *both1))
     coef, coef_rows = call(
         functools.partial(solve_kernel, groups),
         [((2 * groups * cases, cases, LANES), F32), ((groups * cases, 2 * LANES), F32)],
@@ -570,12 +675,12 @@
         smem=(0,),
     )(case, copies)
     own, *messages = call(
-        functools.partial(bubble_kernel, groups, rows), [((part, comps), F32)] * groups, name="bubble"
-    )(coef_rows, turned0, *both0, turned1, *both1)
+        functools.partial(bubble_kernel, groups, rows), [part_of] * groups, name="bubble"
+    )(coef_rows, turned0, *turned0_all, turned1, *both1)
     back = to_cases(messages)
     x, residual = call(
         functools.partial(ports_kernel, groups), [field_of, field_of], name="ports", flops=10**9
-    )(coef, *base_all, image, *both0, second, *both1)
+    )(coef, base, *base_all, image, *image_all, second, *both1)
     (bubble,) = call(functools.partial(join_kernel, groups), [((bubbles, comps), F32)], name="join", smem=(0,))(
         case, bubble_base, own, *back
     )

time: 145 us -> 134 us (0.924)
  waiting for transfers between devices: 34 us -> 16.1 us
  blocking collectives: 26.4 us -> 39.2 us
  Pallas kernels: 36.2 us -> 29.6 us
  starting transfers between devices: 40.9 us -> 38 us
  local copies, waits for them, and re-layouts: 6.28 us -> 8.98 us
    ppermute x12 -> x15, waiting for transfers between devices: 24.7 us -> 6.6 us  [to_cases(): lax.ppermute(message, 'case', [(k, (k + h) % groups) for k in range(group...]
    all_to_all x0 -> x1, blocking collectives: none -> 12.9 us  [local(): copies = lax.all_to_all(copies, 'px', split_axis=0, concat_axis=0)]
    pallas_call x13 -> x15, Pallas kernels: 36.2 us -> 29.6 us  [run(): pl.pallas_call(kernel, out_shape=outs, in_specs=specs, out_specs=[vmem] *...]
    all_to_all x1 -> x0, starting transfers between devices: 6.5 us -> none  [local(): copies = lax.all_to_all(copies, 'px', split_axis=0, concat_axis=0)]
    ppermute x12 -> x15, starting transfers between devices: 14.3 us -> 17.8 us  [to_cases(): lax.ppermute(message, 'case', [(k, (k + h) % groups) for k in range(group...]
    unnamed x38 -> x54, local copies, waits for them, and re-layouts: 6.28 us -> 8.98 us
    all_to_all x2, waiting for transfers between devices: 6.06 us -> 8.38 us  [exchange(): lax.all_to_all(rows.reshape(parts, 1, -1), PLANE, split_axis=0, concat_ax...]
    all_to_all x1, waiting for transfers between devices: 2.67 us -> 1.08 us  [local(): copies = lax.all_to_all(copies, ('case', 'py'), split_axis=0, concat_axis=0)]
  transfers between devices with their start and end apart: 16 -> 18, of which waited for: 10 -> 7; matrix products, arithmetic and copies ran while one was open for 0% -> 0% of each run, Pallas kernels for 9% -> 14%
where the time goes in v3:
time: 134 us; the launch traced here: 133 us
  blocking collectives  39.2 us (29%)
  starting transfers between devices  38 us (28%)
  Pallas kernels  29.6 us (22%)
  waiting for transfers between devices  16.1 us (12%)
  local copies, waits for them, and re-layouts  8.98 us (7%)
    pallas_call x15, Pallas kernels, run(): pl.pallas_call(kernel, out_shape=outs, in_specs=specs, out_specs=[vmem] *...  29.6 us
    all_to_all x1, blocking collectives, exchange(): lax.all_to_all(rows.reshape(parts, 1, -1), PLANE, split_axis=0, concat_ax...  26.4 us
    ppermute x15, starting transfers between devices, to_cases(): lax.ppermute(message, 'case', [(k, (k + h) % groups) for k in range(group...  17.8 us
    all_to_all x1, blocking collectives, local(): copies = lax.all_to_all(copies, 'px', split_axis=0, concat_axis=0)  12.9 us
    all_to_all x2, starting transfers between devices, exchange(): lax.all_to_all(rows.reshape(parts, 1, -1), PLANE, split_axis=0, concat_ax...  12.8 us
    unnamed x54, local copies, waits for them, and re-layouts  8.98 us
    all_to_all x2, waiting for transfers between devices, exchange(): lax.all_to_all(rows.reshape(parts, 1, -1), PLANE, split_axis=0, concat_ax...  8.38 us
    all_to_all x1, starting transfers between devices, local(): copies = lax.all_to_all(copies, ('case', 'py'), split_axis=0, concat_axis=0)  7.35 us
  transfers between devices with their start and end apart: 18, of which 7 were waited for; matrix products, arithmetic and copies ran while one was open for 0% of the time, Pallas kernels for 14%

profile of v3, /device:TPU:1, one launch (start us, length us, event | category | flops | bytes accessed | tf_op | source)
XLA Modules:
  0.0 132.8 jit_solution(956307597880456251)
XLA Ops:
  0.7 0.6 copy-done.10
  1.4 0.9 copy-done
  2.3 0.9 copy-done.2
  3.3 0.9 copy-done.4
  4.2 1.8 %condense.1 = (f32[640,128]{1,0:T(8,128)S(1)}, f32[384,128]{1,0:T(8,128)S(1)}, f32[64,128]{1,0:T(8,128)S(1)}) custom-call(s32[1,128]{1,0:T(1,128)S(1)} %bitcast.43, f32[1,128]{1,0:T(1,128)S(1)} %bitcast.29, s32[1,128]{1,0:T(1,128)S(1)} %bitcast.35, s32[1,128]{1,0:T(1,128)S(1)} %bitcast.40, s32[1,128]{1,0:T(1,128)S(1)} %bitcast.51, f32[512,128]{1,0:T(8,128)S(1)} %bitcast.24, ...), custom_call_target="tpu_custom_call" | custom-call | bytes 1149440 | tf_op jit(solution)/shard_map/condense/pallas_call | solution.py:547
  6.0 26.4 %all_to_all.25 = f32[64,1,1280]{2,1,0:T(1,128)S(1)} all-to-all(f32[64,1,1280]{2,1,0:T(1,128)S(1)} %bitcast.23), channel_id=1, replica_groups=mesh['px'=8,'py'=8,'case'=4] {'px','py'}, dimensions={0} | all-to-all | bytes 655360 | tf_op jit(solution)/shard_map/all_to_all | solution.py:562
  32.4 1.4 %rhs.1 = (f32[384,128]{1,0:T(8,128)S(1)}, f32[1152,128]{1,0:T(8,128)}, f32[64,128]{1,0:T(8,128)S(1)}) custom-call(f32[640,128]{1,0:T(8,128)S(1)} %bitcast.21, f32[384,128]{1,0:T(8,128)S(1)} %get-tuple-element.51.near_sum_ref, f32[384,128]{1,0:T(8,128)S(1)} %bitcast.28, f32[64,128]{1,0:T(8,128)S(1)} %get-tuple-element.52.meta_ref.rest_0_), custom_call_target="tpu_custom_call" | custom-call | bytes 1572864 | tf_op jit(solution)/shard_map/rhs/pallas_call | solution.py:547
  33.8 6.3 %all-to-all-start.1 = ((f32[64,1,2304]{2,1,0:T(1,128)}), f32[64,1,2304]{2,1,0:T(1,128)S(1)}, u32[]{:S(2)}, u32[]{:S(2)}) async-start(f32[64,1,2304]{2,1,0:T(1,128)} %bitcast.11), calls=%async_computation.1 | async-start | bytes 1179648 | tf_op jit(solution)/shard_map/all_to_all | solution.py:562
  40.2 1.3 collective-permute-start.2
  41.5 2.4 %collective-permute-start.1 = (f32[384,128]{1,0:T(8,128)S(1)}, f32[384,128]{1,0:T(8,128)S(1)}, u32[]{:S(2)}, u32[]{:S(2)}) collective-permute-start(f32[384,128]{1,0:T(8,128)S(1)} %get-tuple-element.54.field_ref.refs_0_), channel_id=1, source_target_pairs={{0,2},{1,3},{2,0},{3,1},{4,6},{5,7},{6,4},{7,5},{8,10},{9,11},{10,... | collective-permute-start | bytes 589832 | tf_op jit(solution)/shard_map/ppermute | solution.py:612
  43.9 1.2 collective-permute-start
  45.1 1.8 %tables.1 = (bf16[384,144]{1,0:T(8,128)(2,1)S(1)}, bf16[384,144]{1,0:T(8,128)(2,1)S(1)}, bf16[384,144]{1,0:T(8,128)(2,1)S(1)}, bf16[384,144]{1,0:T(8,128)(2,1)S(...) custom-call(s32[1,128]{1,0:T(1,128)S(1)} %bitcast.44, ...), custom_call_target="tpu_custom_call" | custom-call | flops 1000000000 | bytes 1885184 | tf_op jit(solution)/shard_map/tables/pallas_call | solution.py:547
  47.0 1.7 %inner.2 = (f32[384,128]{1,0:T(8,128)S(1)}, f32[384,128]{1,0:T(8,128)S(1)}) custom-call(f32[384,128]{1,0:T(8,128)S(1)} %get-tuple-element.54.field_ref.refs_0_, f32[64,128]{1,0:T(8,128)S(1)} %get-tuple-element.56.asked_ref, s32[1,128]{1,0:T(1,128)S(1)} %bitcast.45, f32[1,128]{1,0:T(1,128)S(1)} %bitcast.31, s32[1,128]{1,0:T(1,128)S(1)} %bitcast.36, ...), custom_call_target="tpu_custom_call" | custom-call | flops 1000000000 | bytes 845312 | tf_op jit(solution)/shard_map/inner/pallas_call | solution.py:547
  48.7 4.0 %collective-permute-done.1.refs_2_ = f32[384,128]{1,0:T(8,128)S(1)} collective-permute-done((f32[384,128]{1,0:T(8,128)S(1)}, f32[384,128]{1,0:T(8,128)S(1)}, u32[]{:S(2)}, u32[]{:S(2)}) %collective-permute-start.1) | collective-permute-done | bytes 196640 | tf_op jit(solution)/shard_map/ppermute | solution.py:612
  52.7 6.0 %all-to-all-done.1 = f32[64,1,2304]{2,1,0:T(1,128)S(1)} async-done(((f32[64,1,2304]{2,1,0:T(1,128)}), f32[64,1,2304]{2,1,0:T(1,128)S(1)}, u32[]{:S(2)}, u32[]{:S(2)}) %all-to-all-start.1) | async-done | bytes 589856 | tf_op jit(solution)/shard_map/all_to_all | solution.py:562
  58.7 2.7 %image.1 = (f32[384,128]{1,0:T(8,128)S(1)}, f32[384,128]{1,0:T(8,128)S(1)}, f32[1152,128]{1,0:T(8,128)}) custom-call(f32[1152,128]{1,0:T(8,128)S(1)} %bitcast.19, f32[384,128]{1,0:T(8,128)S(1)} %get-tuple-element.59.inner_ref, f32[64,128]{1,0:T(8,128)S(1)} %get-tuple-element.56.asked_ref, s32[1,128]{1,0:T(1,128)S(1)} %bitcast.46, f32[1,128]{1,0:T(1,128)S(1)} %bitcast.32, ...), custom_call_target="tpu_custom_call" | custom-call | bytes 2058240 | tf_op jit(solution)/shard_map/image/pallas_call | solution.py:547
  61.4 6.5 %all-to-all-start.2 = ((f32[64,1,2304]{2,1,0:T(1,128)}), f32[64,1,2304]{2,1,0:T(1,128)S(1)}, u32[]{:S(2)}, u32[]{:S(2)}) async-start(f32[64,1,2304]{2,1,0:T(1,128)} %bitcast.13), calls=%async_computation.2 | async-start | bytes 1179648 | tf_op jit(solution)/shard_map/all_to_all | solution.py:562
  68.0 1.3 collective-permute-start.8
  69.3 2.5 %collective-permute-start.7 = (f32[384,128]{1,0:T(8,128)S(1)}, f32[384,128]{1,0:T(8,128)S(1)}, u32[]{:S(2)}, u32[]{:S(2)}) collective-permute-start(f32[384,128]{1,0:T(8,128)S(1)} %get-tuple-element.71.field_ref.refs_4_.rest_2_), channel_id=1, source_target_pairs={{0,2},{1,3},{2,0},{3,1},{4,6},{5,7},{6,4},{7,5},{8,10},{9,11},{10,... | collective-permute-start | bytes 589832 | tf_op jit(solution)/shard_map/ppermute | solution.py:612
  71.7 1.2 collective-permute-start.6
  72.9 0.9 copy-done.16
  73.8 0.9 copy-done.19
  74.8 0.7 turned.1
  75.6 2.1 %collective-permute-start.4 = (f32[128,128]{1,0:T(8,128)S(1)}, f32[128,128]{1,0:T(8,128)S(1)}, u32[]{:S(2)}, u32[]{:S(2)}) collective-permute-start(f32[128,128]{1,0:T(8,128)S(1)} %get-tuple-element.68), channel_id=1, source_target_pairs={{0,2},{1,3},{2,0},{3,1},{4,6},{5,7},{6,4},{7,5},{8,10},{9,11},{10,... | collective-permute-start | bytes 196616 | tf_op jit(solution)/shard_map/ppermute | solution.py:612
  77.7 1.7 %inner.3 = (f32[384,128]{1,0:T(8,128)S(1)}, f32[384,128]{1,0:T(8,128)S(1)}) custom-call(f32[384,128]{1,0:T(8,128)S(1)} %get-tuple-element.71.field_ref.refs_4_.rest_2_, f32[64,128]{1,0:T(8,128)S(1)} %get-tuple-element.56.asked_ref, s32[1,128]{1,0:T(1,128)S(1)} %bitcast.48, f32[1,128]{1,0:T(1,128)S(1)} %bitcast.33, s32[1,128]{1,0:T(1,128)S(1)} %bitcast.38, ...), custom_call_target="tpu_custom_call" | custom-call | flops 1000000000 | bytes 845312 | tf_op jit(solution)/shard_map/inner/pallas_call | solution.py:547
  79.4 1.1 collective-permute-done.7.refs_6_.rest_4_
  80.5 3.7 %gram.1.rest_1_ = f32[8,128]{1,0:T(8,128)S(1)} custom-call(s32[1]{0:T(128)} %bitcast.case_ref.rest_0_, f32[384,128]{1,0:T(8,128)S(1)} %get-tuple-element.54.field_ref.refs_0_, f32[384,128]{1,0:T(8,128)S(1)} %collective-permute-done.refs_1_, f32[384,128]{1,0:T(8,128)S(1)} %collective-permute-done.1.refs_2_, f32[384,128]{1,0:T(8,128)S(1)} %collective-permute-done.2.refs_3_, ...), custom_call_target="tpu_custom_call" | custom-call | bytes 1576964 | tf_op jit(solution)/shard_map/gram/pallas_call | solution.py:547
  84.2 2.3 %all-to-all-done.2 = f32[64,1,2304]{2,1,0:T(1,128)S(1)} async-done(((f32[64,1,2304]{2,1,0:T(1,128)}), f32[64,1,2304]{2,1,0:T(1,128)S(1)}, u32[]{:S(2)}, u32[]{:S(2)}) %all-to-all-start.2) | async-done | bytes 589856 | tf_op jit(solution)/shard_map/all_to_all | solution.py:562
  86.5 3.9 %second.1 = (f32[384,128]{1,0:T(8,128)S(1)}, f32[384,128]{1,0:T(8,128)S(1)}, f32[32,8,128]{2,1,0:T(8,128)}) custom-call(f32[1152,128]{1,0:T(8,128)S(1)} %bitcast.20, f32[384,128]{1,0:T(8,128)S(1)} %get-tuple-element.72.inner_ref, f32[64,128]{1,0:T(8,128)S(1)} %get-tuple-element.56.asked_ref, s32[1,128]{1,0:T(1,128)S(1)} %bitcast.49, f32[1,128]{1,0:T(1,128)S(1)} %bitcast.34, ...), custom_call_target="tpu_custom_call" | custom-call | bytes 2357252 | tf_op jit(solution)/shard_map/second/pallas_call | solution.py:547
  90.4 0.7 copy-done.13
  91.1 7.4 %all-to-all-start.3 = ((f32[32,8,128]{2,1,0:T(8,128)}), f32[32,8,128]{2,1,0:T(8,128)S(1)}, u32[]{:S(2)}, u32[]{:S(2)}) async-start(f32[32,8,128]{2,1,0:T(8,128)} %get-tuple-element.76), calls=%async_computation.3 | async-start | bytes 262144 | tf_op jit(solution)/shard_map/all_to_all | solution.py:656
  98.5 0.9 copy-done.17
  99.4 0.9 copy-done.20
  100.4 0.9 copy-done.26
  101.3 1.6 %turned_second.1 = (f32[128,128]{1,0:T(8,128)S(1)}, f32[512,128]{1,0:T(8,128)}, f32[512,128]{1,0:T(8,128)}, f32[512,128]{1,0:T(8,128)}) custom-call(s32[1]{0:T(128)} %bitcast.case_ref.rest_0_, f32[384,128]{1,0:T(8,128)S(1)} %copy-done.26, f32[384,128]{1,0:T(8,128)S(1)} %copy-done.14, s32[1,128]{1,0:T(1,128)S(1)} %bitcast.50, ...), custom_call_target="tpu_custom_call" | custom-call | flops 1000000000 | bytes 1737220 | tf_op jit(solution)/shard_map/turned_second/pallas_call | solution.py:547
  102.9 2.5 %collective-permute-start.9 = (f32[512,128]{1,0:T(8,128)}, f32[512,128]{1,0:T(8,128)S(1)}, u32[]{:S(2)}, u32[]{:S(2)}) collective-permute-start(f32[512,128]{1,0:T(8,128)} %get-tuple-element.81), channel_id=1, source_target_pairs={{0,3},{1,0},{2,1},{3,2},{4,7},{5,4},{6,5},{7,6},{8,11},{9,8},{10,9... | collective-permute-start | bytes 786440 | tf_op jit(solution)/shard_map/ppermute | solution.py:612
  105.4 0.5 collective-permute-start.10
  105.9 0.6 collective-permute-start.11
  106.5 1.1 all-to-all-done.3
  107.6 12.9 %all_to_all.26.gram_ref = f32[8,32,128]{2,1,0:T(8,128)S(1)} all-to-all(f32[8,32,128]{2,1,0:T(8,128)S(1)} %sum.1), channel_id=1, replica_groups=mesh['px'=8,'py'=8,'case'=4] {'px'}, dimensions={0} | all-to-all | bytes 262144 | tf_op jit(solution)/shard_map/all_to_all | solution.py:669
  120.5 4.3 %solve.1 = (f32[64,8,128]{2,1,0:T(8,128)S(1)}, f32[32,256]{1,0:T(8,128)S(1)}) custom-call(s32[1]{0:T(128)} %bitcast.case_ref.rest_0_, f32[8,32,128]{2,1,0:T(8,128)S(1)} %all_to_all.26.gram_ref), custom_call_target="tpu_custom_call" | custom-call | bytes 425988 | tf_op jit(solution)/shard_map/solve/pallas_call | solution.py:547
  124.8 0.4 bubble.1
  125.2 1.0 collective-permute-start.12
  126.2 1.2 collective-permute-start.13
  127.4 3.2 %ports.1 = (f32[384,128]{1,0:T(8,128)}, f32[384,128]{1,0:T(8,128)}) custom-call(f32[64,8,128]{2,1,0:T(8,128)S(1)} %get-tuple-element.77.coef, f32[384,128]{1,0:T(8,128)S(1)} %get-tuple-element.54.field_ref.refs_0_, f32[384,128]{1,0:T(8,128)S(1)} %collective-permute-done.refs_1_, f32[384,128]{1,0:T(8,128)S(1)} %collective-permute-done.1.refs_2_, ...), custom_call_target="tpu_custom_call" | custom-call | flops 1000000000 | bytes 3211264 | tf_op jit(solution)/shard_map/ports/pallas_call | solution.py:547
  130.6 0.2 collective-permute-done.13.refs_2_
  130.8 1.3 collective-permute-done.14.refs_3_
  132.1 0.7 join.1
  (59 shorter events, 0.3 us)
Async XLA Ops:
  0.6 0.7 copy-start.10
  0.6 0.7 copy-start.11
  0.7 0.7 copy-start.7
  0.7 0.7 copy-start.8
  0.7 0.7 copy-start.9
  1.4 0.9 copy-start
  2.3 0.9 copy-start.2
  3.3 0.9 copy-start.4
  6.0 26.4 %copy-start.6 = (f32[48,8,128]{2,1,0:T(8,128)S(1)}, f32[48,8,128]{2,1,0:T(8,128)}, u32[]{:S(2)}) copy-start(f32[48,8,128]{2,1,0:T(8,128)} %param.16) | copy-start | bytes 589828
  33.8 11.3 %copy-start.1 = (f32[64,8,128]{2,1,0:T(8,128)S(1)}, f32[64,8,128]{2,1,0:T(8,128)}, u32[]{:S(2)}) copy-start(f32[64,8,128]{2,1,0:T(8,128)} %param.15) | copy-start | bytes 786436
  33.8 11.3 %copy-start.3 = (f32[8,64,64]{2,1,0:T(8,128)S(1)}, f32[8,64,64]{2,1,0:T(8,128)}, u32[]{:S(2)}) copy-start(f32[8,64,64]{2,1,0:T(8,128)} %inverse_ref.1) | copy-start | bytes 393220
  33.8 11.3 %copy-start.5 = (f32[8,96,64]{1,2,0:T(8,128)S(1)}, f32[8,96,64]{1,2,0:T(8,128)}, u32[]{:S(2)}) copy-start(f32[8,96,64]{1,2,0:T(8,128)} %param.18) | copy-start | bytes 589828
  33.8 11.3 %copy-start.12 = (f32[8,96,96]{2,1,0:T(8,128)S(1)}, f32[8,96,96]{2,1,0:T(8,128)}, u32[]{:S(2)}) copy-start(f32[8,96,96]{2,1,0:T(8,128)} %block_ref.1) | copy-start | bytes 884740
  33.8 24.9 %all-to-all-start.1 = ((f32[64,1,2304]{2,1,0:T(1,128)}), f32[64,1,2304]{2,1,0:T(1,128)S(1)}, u32[]{:S(2)}, u32[]{:S(2)}) async-start(f32[64,1,2304]{2,1,0:T(1,128)} %bitcast.11), calls=%async_computation.1 | async-start | bytes 1179648 | tf_op jit(solution)/shard_map/all_to_all | solution.py:562
  40.2 8.5 %collective-permute-start.2 = (f32[384,128]{1,0:T(8,128)S(1)}, f32[384,128]{1,0:T(8,128)S(1)}, u32[]{:S(2)}, u32[]{:S(2)}) collective-permute-start(f32[384,128]{1,0:T(8,128)S(1)} %get-tuple-element.54.field_ref.refs_0_), channel_id=1, source_target_pairs={{0,1},{1,2},{2,3},{3,0},{4,5},{5,6},{6,7},{7,4},{8,9},{9,10},{10,1... | collective-permute-start | bytes 589832 | tf_op jit(solution)/shard_map/ppermute | solution.py:612
  41.5 11.2 %collective-permute-start.1 = (f32[384,128]{1,0:T(8,128)S(1)}, f32[384,128]{1,0:T(8,128)S(1)}, u32[]{:S(2)}, u32[]{:S(2)}) collective-permute-start(f32[384,128]{1,0:T(8,128)S(1)} %get-tuple-element.54.field_ref.refs_0_), channel_id=1, source_target_pairs={{0,2},{1,3},{2,0},{3,1},{4,6},{5,7},{6,4},{7,5},{8,10},{9,11},{10,... | collective-permute-start | bytes 589832 | tf_op jit(solution)/shard_map/ppermute | solution.py:612
  43.9 8.8 %collective-permute-start = (f32[384,128]{1,0:T(8,128)S(1)}, f32[384,128]{1,0:T(8,128)S(1)}, u32[]{:S(2)}, u32[]{:S(2)}) collective-permute-start(f32[384,128]{1,0:T(8,128)S(1)} %get-tuple-element.54.field_ref.refs_0_), channel_id=1, source_target_pairs={{0,3},{1,0},{2,1},{3,2},{4,7},{5,4},{6,5},{7,6},{8,11},{9,8},{10,9... | collective-permute-start | bytes 589832 | tf_op jit(solution)/shard_map/ppermute | solution.py:612
  46.9 1.7 %copy-start.15 = (bf16[512,144]{1,0:T(8,128)(2,1)}, bf16[512,144]{1,0:T(8,128)(2,1)S(1)}, u32[]{:S(2)}) copy-start(bf16[512,144]{1,0:T(8,128)(2,1)S(1)} %get-tuple-element.65.turned_near) | copy-start | bytes 442372
  46.9 1.7 %copy-start.18 = (bf16[512,144]{1,0:T(8,128)(2,1)}, bf16[512,144]{1,0:T(8,128)(2,1)S(1)}, u32[]{:S(2)}) copy-start(bf16[512,144]{1,0:T(8,128)(2,1)S(1)} %get-tuple-element.66.turned_far) | copy-start | bytes 442372
  46.9 1.7 %copy-start.21 = (bf16[384,144]{1,0:T(8,128)(2,1)}, bf16[384,144]{1,0:T(8,128)(2,1)S(1)}, u32[]{:S(2)}) copy-start(bf16[384,144]{1,0:T(8,128)(2,1)S(1)} %get-tuple-element.57.near_near) | copy-start | bytes 331780
  47.0 1.7 %copy-start.23 = (bf16[384,144]{1,0:T(8,128)(2,1)}, bf16[384,144]{1,0:T(8,128)(2,1)S(1)}, u32[]{:S(2)}) copy-start(bf16[384,144]{1,0:T(8,128)(2,1)S(1)} %get-tuple-element.58.far_far) | copy-start | bytes 331780
  61.4 25.1 %all-to-all-start.2 = ((f32[64,1,2304]{2,1,0:T(1,128)}), f32[64,1,2304]{2,1,0:T(1,128)S(1)}, u32[]{:S(2)}, u32[]{:S(2)}) async-start(f32[64,1,2304]{2,1,0:T(1,128)} %bitcast.13), calls=%async_computation.2 | async-start | bytes 1179648 | tf_op jit(solution)/shard_map/all_to_all | solution.py:562
  68.0 9.7 %collective-permute-start.8 = (f32[384,128]{1,0:T(8,128)S(1)}, f32[384,128]{1,0:T(8,128)S(1)}, u32[]{:S(2)}, u32[]{:S(2)}) collective-permute-start(f32[384,128]{1,0:T(8,128)S(1)} %get-tuple-element.71.field_ref.refs_4_.rest_2_), channel_id=1, source_target_pairs={{0,1},{1,2},{2,3},{3,0},{4,5},{5,6},{6,7},{7,4},{8,9},{9,10},{10,1... | collective-permute-start | bytes 589832 | tf_op jit(solution)/shard_map/ppermute | solution.py:612
  69.3 11.2 %collective-permute-start.7 = (f32[384,128]{1,0:T(8,128)S(1)}, f32[384,128]{1,0:T(8,128)S(1)}, u32[]{:S(2)}, u32[]{:S(2)}) collective-permute-start(f32[384,128]{1,0:T(8,128)S(1)} %get-tuple-element.71.field_ref.refs_4_.rest_2_), channel_id=1, source_target_pairs={{0,2},{1,3},{2,0},{3,1},{4,6},{5,7},{6,4},{7,5},{8,10},{9,11},{10,... | collective-permute-start | bytes 589832 | tf_op jit(solution)/shard_map/ppermute | solution.py:612
  71.7 8.8 %collective-permute-start.6 = (f32[384,128]{1,0:T(8,128)S(1)}, f32[384,128]{1,0:T(8,128)S(1)}, u32[]{:S(2)}, u32[]{:S(2)}) collective-permute-start(f32[384,128]{1,0:T(8,128)S(1)} %get-tuple-element.71.field_ref.refs_4_.rest_2_), channel_id=1, source_target_pairs={{0,3},{1,0},{2,1},{3,2},{4,7},{5,4},{6,5},{7,6},{8,11},{9,8},{10,9... | collective-permute-start | bytes 589832 | tf_op jit(solution)/shard_map/ppermute | solution.py:612
  72.9 0.9 copy-start.16
  73.8 0.9 copy-start.19
  74.8 2.9 %copy-start.22 = (bf16[384,144]{1,0:T(8,128)(2,1)S(1)}, bf16[384,144]{1,0:T(8,128)(2,1)}, u32[]{:S(2)}) copy-start(bf16[384,144]{1,0:T(8,128)(2,1)} %copy-done.21) | copy-start | bytes 331780
  74.8 2.9 %copy-start.24 = (bf16[384,144]{1,0:T(8,128)(2,1)S(1)}, bf16[384,144]{1,0:T(8,128)(2,1)}, u32[]{:S(2)}) copy-start(bf16[384,144]{1,0:T(8,128)(2,1)} %copy-done.23) | copy-start | bytes 331780
  75.5 8.7 %collective-permute-start.3 = (f32[128,128]{1,0:T(8,128)S(1)}, f32[128,128]{1,0:T(8,128)S(1)}, u32[]{:S(2)}, u32[]{:S(2)}) collective-permute-start(f32[128,128]{1,0:T(8,128)S(1)} %get-tuple-element.67), channel_id=1, source_target_pairs={{0,3},{1,0},{2,1},{3,2},{4,7},{5,4},{6,5},{7,6},{8,11},{9,8},{10,9... | collective-permute-start | bytes 196616 | tf_op jit(solution)/shard_map/ppermute | solution.py:612
  75.6 8.6 %collective-permute-start.4 = (f32[128,128]{1,0:T(8,128)S(1)}, f32[128,128]{1,0:T(8,128)S(1)}, u32[]{:S(2)}, u32[]{:S(2)}) collective-permute-start(f32[128,128]{1,0:T(8,128)S(1)} %get-tuple-element.68), channel_id=1, source_target_pairs={{0,2},{1,3},{2,0},{3,1},{4,6},{5,7},{6,4},{7,5},{8,10},{9,11},{10,... | collective-permute-start | bytes 196616 | tf_op jit(solution)/shard_map/ppermute | solution.py:612
  77.7 6.5 %collective-permute-start.5 = (f32[128,128]{1,0:T(8,128)S(1)}, f32[128,128]{1,0:T(8,128)S(1)}, u32[]{:S(2)}, u32[]{:S(2)}) collective-permute-start(f32[128,128]{1,0:T(8,128)S(1)} %get-tuple-element.69), channel_id=1, source_target_pairs={{0,1},{1,2},{2,3},{3,0},{4,5},{5,6},{6,7},{7,4},{8,9},{9,10},{10,1... | collective-permute-start | bytes 196616 | tf_op jit(solution)/shard_map/ppermute | solution.py:612
  79.4 4.8 %copy-start.25 = (f32[384,128]{1,0:T(8,128)}, f32[384,128]{1,0:T(8,128)S(1)}, u32[]{:S(2)}) copy-start(f32[384,128]{1,0:T(8,128)S(1)} %get-tuple-element.79.near_values) | copy-start | bytes 589828
  90.4 0.7 copy-start.13
  91.1 7.4 %copy-start.14 = (f32[384,128]{1,0:T(8,128)S(1)}, f32[384,128]{1,0:T(8,128)}, u32[]{:S(2)}) copy-start(f32[384,128]{1,0:T(8,128)} %copy-done.13) | copy-start | bytes 589828
  91.1 16.5 %all-to-all-start.3 = ((f32[32,8,128]{2,1,0:T(8,128)}), f32[32,8,128]{2,1,0:T(8,128)S(1)}, u32[]{:S(2)}, u32[]{:S(2)}) async-start(f32[32,8,128]{2,1,0:T(8,128)} %get-tuple-element.76), calls=%async_computation.3 | async-start | bytes 262144 | tf_op jit(solution)/shard_map/all_to_all | solution.py:656
  98.5 1.0 copy-start.17
  99.4 0.9 copy-start.20
  100.4 0.9 copy-start.26
  102.9 21.9 %collective-permute-start.9 = (f32[512,128]{1,0:T(8,128)}, f32[512,128]{1,0:T(8,128)S(1)}, u32[]{:S(2)}, u32[]{:S(2)}) collective-permute-start(f32[512,128]{1,0:T(8,128)} %get-tuple-element.81), channel_id=1, source_target_pairs={{0,3},{1,0},{2,1},{3,2},{4,7},{5,4},{6,5},{7,6},{8,11},{9,8},{10,9... | collective-permute-start | bytes 786440 | tf_op jit(solution)/shard_map/ppermute | solution.py:612
  105.4 19.4 %collective-permute-start.10 = (f32[512,128]{1,0:T(8,128)}, f32[512,128]{1,0:T(8,128)S(1)}, u32[]{:S(2)}, u32[]{:S(2)}) collective-permute-start(f32[512,128]{1,0:T(8,128)} %get-tuple-element.82), channel_id=1, source_target_pairs={{0,2},{1,3},{2,0},{3,1},{4,6},{5,7},{6,4},{7,5},{8,10},{9,11},{10,... | collective-permute-start | bytes 786440 | tf_op jit(solution)/shard_map/ppermute | solution.py:612
  105.9 18.9 %collective-permute-start.11 = (f32[512,128]{1,0:T(8,128)}, f32[512,128]{1,0:T(8,128)S(1)}, u32[]{:S(2)}, u32[]{:S(2)}) collective-permute-start(f32[512,128]{1,0:T(8,128)} %get-tuple-element.83), channel_id=1, source_target_pairs={{0,1},{1,2},{2,3},{3,0},{4,5},{5,6},{6,7},{7,4},{8,9},{9,10},{10,1... | collective-permute-start | bytes 786440 | tf_op jit(solution)/shard_map/ppermute | solution.py:612
  125.2 5.4 %collective-permute-start.12 = (f32[128,128]{1,0:T(8,128)S(1)}, f32[128,128]{1,0:T(8,128)S(1)}, u32[]{:S(2)}, u32[]{:S(2)}) collective-permute-start(f32[128,128]{1,0:T(8,128)S(1)} %get-tuple-element.94), channel_id=1, source_target_pairs={{0,3},{1,0},{2,1},{3,2},{4,7},{5,4},{6,5},{7,6},{8,11},{9,8},{10,9... | collective-permute-start | bytes 196616 | tf_op jit(solution)/shard_map/ppermute | solution.py:612
  126.2 4.6 %collective-permute-start.13 = (f32[128,128]{1,0:T(8,128)S(1)}, f32[128,128]{1,0:T(8,128)S(1)}, u32[]{:S(2)}, u32[]{:S(2)}) collective-permute-start(f32[128,128]{1,0:T(8,128)S(1)} %get-tuple-element.95), channel_id=1, source_target_pairs={{0,2},{1,3},{2,0},{3,1},{4,6},{5,7},{6,4},{7,5},{8,10},{9,11},{10,... | collective-permute-start | bytes 196616 | tf_op jit(solution)/shard_map/ppermute | solution.py:612
  127.4 4.6 %collective-permute-start.14 = (f32[128,128]{1,0:T(8,128)S(1)}, f32[128,128]{1,0:T(8,128)S(1)}, u32[]{:S(2)}, u32[]{:S(2)}) collective-permute-start(f32[128,128]{1,0:T(8,128)S(1)} %get-tuple-element.96), channel_id=1, source_target_pairs={{0,1},{1,2},{2,3},{3,0},{4,5},{5,6},{6,7},{7,4},{8,9},{9,10},{10,1... | collective-permute-start | bytes 196616 | tf_op jit(solution)/shard_map/ppermute | solution.py:612

commit v4 on v3

--- a/solution.py
+++ b/solution.py
@@ -9,6 +9,7 @@
 
 HIGH = lax.Precision.HIGHEST
 PLANE = ("px", "py")
+EVERY = ("px", "py", "case")
 F32 = jnp.float32
 BF16 = jnp.bfloat16
 KINDS = 8
@@ -311,8 +312,9 @@
     near_far, far_near, *rest,
 ):
     if last:
-        case_ref, gram_ref, rest = rest[0], rest[1], rest[2:]
-        images, (image_ref, far_values, copies_ref, near_part, slot_ref, slot_part) = rest[:groups], rest[groups:]
+        case_ref, gram_ref, near_values, turned_near, turned_far = rest[:5]
+        images, rest = rest[5 : 5 + groups], rest[5 + groups :]
+        image_ref, copies_ref, turned_ref, near_part, slot_ref, slot_part, far_values = rest
     else:
         meta_ref, image_ref, far_values, pay_ref, near_part, slot_ref, slot_part = rest
     asked = asked_ref[...]
@@ -333,6 +335,7 @@
         gram = add_products(LANES, images, [image_ref], [3 * groups * CASES], case_ref[0], gram_ref[...])
         for p in range(copies_ref.shape[0]):
             copies_ref[p] = gram
+        turned_rows(near_values, far_values, kind_ref, turned_near, turned_far, turned_ref)
     else:
         send_ports(image, asked_hot, port_onehot(meta_ref[...]), pay_ref)
 
@@ -359,17 +362,19 @@
     return ref[pl.ds(pl.multiple_of(lax.rem(case_ref[0] + h, groups) * part, part), part), :]
 
 
-def turned_kernel(groups, first, case_ref, near_values, far_values, kind_ref, turned_near, turned_far, *rest):
-    if not first:
-        field_ref, rest = rest[0], rest[1:]
+def turned_kernel(groups, case_ref, near_values, far_values, kind_ref, turned_near, turned_far, *rest):
     outs, out_ref = rest[:groups], rest[groups]
     turned_rows(near_values, far_values, kind_ref, turned_near, turned_far, out_ref)
     for h in range(groups):
-        at = 0
-        if h and not first:
-            at = field_ref.shape[0]
-            outs[h][:at, :] = field_ref[...]
-        outs[h][at:, :] = quarter(out_ref, case_ref, h, groups)
+        outs[h][...] = quarter(out_ref, case_ref, h, groups)
+
+
+def messages_kernel(groups, case_ref, field_ref, turned_ref, own_ref, *messages):
+    rows = field_ref.shape[0]
+    own_ref[...] = quarter(turned_ref, case_ref, 0, groups)
+    for h in range(1, groups):
+        messages[h - 1][:rows, :] = field_ref[...]
+        messages[h - 1][rows:, :] = quarter(turned_ref, case_ref, h, groups)
 
 
 def add_products(lanes, lefts, rights, first, case, out):
@@ -406,12 +411,11 @@
 
 
 def sum_kernel(in_ref, out_ref):
-    for q in range(in_ref.shape[0]):
-        total = in_ref[q, 0]
-        for p in range(1, in_ref.shape[1]):
-            total = total + in_ref[q, p]
-        for p in range(out_ref.shape[0]):
-            out_ref[p, q * CASES : (q + 1) * CASES, :] = total
+    total = in_ref[0]
+    for p in range(1, in_ref.shape[0]):
+        total = total + in_ref[p]
+    for p in range(out_ref.shape[0]):
+        out_ref[p] = total
 
 
 def inverse2(p, q, r, s):
@@ -454,9 +458,13 @@
 
 def solve_kernel(groups, case_ref, gram_ref, coef, coef_rows, turned_coef):
     n = groups * CASES
-    total = gram_ref[0]
-    for p in range(1, gram_ref.shape[0]):
-        total = total + gram_ref[p]
+    each = gram_ref.shape[0] // groups
+    rows = []
+    for q in range(groups):
+        rows.append(gram_ref[q * each])
+        for p in range(1, each):
+            rows[q] = rows[q] + gram_ref[q * each + p]
+    total = jnp.concatenate(rows, axis=0)
     g00, g01, g11, g12 = [symmetric(total[:, g * n : (g + 1) * n]) for g in range(4)]
     steps = spd_solve(g01, jnp.concatenate([g00, g11], axis=1))
     step0, step1 = steps[:, :n], steps[:, n:]
@@ -550,12 +558,31 @@
             in_specs=specs,
             out_specs=[vmem] * len(outs),
             scratch_shapes=fetched + [pltpu.VMEM(shape, F32) for shape in scratch] + sems,
-            compiler_params=pltpu.CompilerParams(vmem_limit_bytes=12 << 20),
+            compiler_params=pltpu.CompilerParams(vmem_limit_bytes=(60 if hbm else 12) << 20),
             cost_estimate=pl.CostEstimate(flops=flops, bytes_accessed=moved, transcendentals=0),
             name=name,
         )(*args)
 
     return run
+
+
+def reduction_groups():
+    majors, minors, cases = [lax.axis_size(axis) for axis in EVERY]
+
+    def at(half, odd, minor, case):
+        return ((half * 2 + odd) * minors + minor) * cases + case
+
+    within = [
+        [at(half, odd, minor, case) for odd in range(2) for minor in range(minors)]
+        for half in range(majors // 2)
+        for case in range(cases)
+    ]
+    across = [
+        [at(half, odd, minor, case) for case in range(cases) for half in range(majors // 2)]
+        for odd in range(2)
+        for minor in range(minors)
+    ]
+    return within, across
 
 
 def exchange(rows, parts):
@@ -633,7 +660,7 @@
     image_all = to_cases([image] * (groups - 1))
     image_inner, image_near = inner(image)
     turned0, *messages = call(
-        functools.partial(turned_kernel, groups, True),
+        functools.partial(turned_kernel, groups),
         [part_of] * groups,
         [(bubbles, comps)],
         name="turned",
@@ -645,28 +672,28 @@
         case, base, *base_all, image, *image_all
     )
     arrived, *turned0_all = lax.optimization_barrier((arrived, *turned0_all))
-    minor = lax.axis_size("py")
-    second, image_far, copies = call(
+    within, across = reduction_groups()
+    second, copies, turned1 = call(
         functools.partial(image_kernel, parts, groups, True),
-        [field_of] * 2 + [((groups * minor, cases, LANES), F32)],
-        [(rows, comps)] + slot_scratch,
+        [field_of, ((len(within[0]), cases, LANES), F32), ((bubbles, comps), F32)],
+        [(rows, comps)] + slot_scratch + [(rows, comps)],
         "second",
         smem=(9,),
-    )(arrived, image_inner, asked, *where, near_far, far_near, case, gram, image, *image_all)
-    copies = lax.all_to_all(copies, ("case", "py"), split_axis=0, concat_axis=0)
+    )(
+        arrived, image_inner, asked, *where, near_far, far_near, case, gram, image_near, turned_near, turned_far,
+        image, *image_all,
+    )
+    copies = lax.all_to_all(copies, EVERY, split_axis=0, concat_axis=0, axis_index_groups=within)
     turned1, *messages = call(
-        functools.partial(turned_kernel, groups, False),
+        functools.partial(messages_kernel, groups),
         [part_of] + [((rows + part, comps), F32)] * (groups - 1),
-        [(bubbles, comps)],
-        "turned_second",
+        name="messages",
         flops=10**9,
         smem=(0,),
-    )(case, image_near, image_far, kind, turned_near, turned_far, second)
+    )(case, second, turned1)
     both1 = to_cases(messages)
-    (copies,) = call(sum_kernel, [((parts // minor, groups * cases, LANES), F32)], name="sum")(
-        copies.reshape(groups, minor, cases, LANES)
-    )
-    copies = lax.all_to_all(copies, "px", split_axis=0, concat_axis=0)
+    (copies,) = call(sum_kernel, [((len(across[0]), cases, LANES), F32)], name="sum")(copies)
+    copies = lax.all_to_all(copies, EVERY, split_axis=0, concat_axis=0, axis_index_groups=across)
     coef, coef_rows = call(
         functools.partial(solve_kernel, groups),
         [((2 * groups * cases, cases, LANES), F32), ((groups * cases, 2 * LANES), F32)],

time: 134 us -> 137 us (1.022)
  blocking collectives: 39.2 us -> 55.1 us
  starting transfers between devices: 38 us -> 30.6 us
  waiting for transfers between devices: 16.1 us -> 10.9 us
    all_to_all x1 -> x2, blocking collectives: 12.9 us -> 28.5 us  [local(): lax.all_to_all(copies, EVERY, split_axis=0, concat_axis=0, axis_index_gro...]
    all_to_all x1 -> x0, starting transfers between devices: 7.35 us -> none  [local(): copies = lax.all_to_all(copies, ('case', 'py'), split_axis=0, concat_axis=0)]
    all_to_all x2, waiting for transfers between devices: 8.38 us -> 5.84 us  [exchange(): lax.all_to_all(rows.reshape(parts, 1, -1), PLANE, split_axis=0, concat_ax...]
    ppermute x15, waiting for transfers between devices: 6.6 us -> 5.11 us  [to_cases(): lax.ppermute(message, 'case', [(k, (k + h) % groups) for k in range(group...]
    unnamed x54 -> x64, local copies, waits for them, and re-layouts: 8.98 us -> 8.01 us
  transfers between devices with their start and end apart: 18 -> 17, of which waited for: 7 -> 6; matrix products, arithmetic and copies ran while one was open for 0% -> 0% of each run, Pallas kernels for 14% -> 12%
where the time goes in v4:
time: 137 us; the launch traced here: 135 us
  blocking collectives  55.1 us (40%)
  starting transfers between devices  30.6 us (22%)
  Pallas kernels  29.5 us (22%)
  waiting for transfers between devices  10.9 us (8%)
  local copies, waits for them, and re-layouts  8.01 us (6%)
    pallas_call x15, Pallas kernels, run(): pl.pallas_call(kernel, out_shape=outs, in_specs=specs, out_specs=[vmem] *...  29.5 us
    all_to_all x2, blocking collectives, local(): lax.all_to_all(copies, EVERY, split_axis=0, concat_axis=0, axis_index_gro...  28.5 us
    all_to_all x1, blocking collectives, exchange(): lax.all_to_all(rows.reshape(parts, 1, -1), PLANE, split_axis=0, concat_ax...  26.6 us
    ppermute x15, starting transfers between devices, to_cases(): lax.ppermute(message, 'case', [(k, (k + h) % groups) for k in range(group...  17.7 us
    all_to_all x2, starting transfers between devices, exchange(): lax.all_to_all(rows.reshape(parts, 1, -1), PLANE, split_axis=0, concat_ax...  12.8 us
    unnamed x64, local copies, waits for them, and re-layouts  8.01 us
    all_to_all x2, waiting for transfers between devices, exchange(): lax.all_to_all(rows.reshape(parts, 1, -1), PLANE, split_axis=0, concat_ax...  5.84 us
    ppermute x15, waiting for transfers between devices, to_cases(): lax.ppermute(message, 'case', [(k, (k + h) % groups) for k in range(group...  5.11 us
  transfers between devices with their start and end apart: 17, of which 6 were waited for; matrix products, arithmetic and copies ran while one was open for 0% of the time, Pallas kernels for 12%

profile of v4, /device:TPU:1, one launch (start us, length us, event | category | flops | bytes accessed | tf_op | source)
XLA Modules:
  0.0 135.2 jit_solution(18079744092778485623)
XLA Ops:
  0.6 3.6 %condense.1 = (f32[640,128]{1,0:T(8,128)}, f32[384,128]{1,0:T(8,128)}, f32[64,128]{1,0:T(8,128)}) custom-call(s32[1,128]{1,0:T(1,128)} %bitcast.26, f32[1,128]{1,0:T(1,128)} %bitcast.33, s32[1,128]{1,0:T(1,128)} %bitcast.39, s32[1,128]{1,0:T(1,128)} %bitcast.44, s32[1,128]{1,0:T(1,128)} %bitcast.49, f32[512,128]{1,0:T(8,128)} %bitcast.21, ...), custom_call_target="tpu_custom_call" | custom-call | bytes 1149440 | tf_op jit(solution)/shard_map/condense/pallas_call | solution.py:555
  4.3 26.6 %all_to_all.25 = f32[64,1,1280]{2,1,0:T(1,128)S(1)} all-to-all(f32[64,1,1280]{2,1,0:T(1,128)} %bitcast.47), channel_id=1, replica_groups=mesh['px'=8,'py'=8,'case'=4] {'px','py'}, dimensions={0} | all-to-all | bytes 655360 | tf_op jit(solution)/shard_map/all_to_all | solution.py:589
  30.9 1.4 %rhs.1 = (f32[384,128]{1,0:T(8,128)S(1)}, f32[1152,128]{1,0:T(8,128)}, f32[64,128]{1,0:T(8,128)S(1)}) custom-call(f32[640,128]{1,0:T(8,128)S(1)} %bitcast.20, f32[384,128]{1,0:T(8,128)S(1)} %copy-done.4, f32[384,128]{1,0:T(8,128)S(1)} %bitcast.25, f32[64,128]{1,0:T(8,128)S(1)} %copy-done.11), custom_call_target="tpu_custom_call" | custom-call | bytes 1572864 | tf_op jit(solution)/shard_map/rhs/pallas_call | solution.py:555
  32.3 6.3 %all-to-all-start.1 = ((f32[64,1,2304]{2,1,0:T(1,128)}), f32[64,1,2304]{2,1,0:T(1,128)S(1)}, u32[]{:S(2)}, u32[]{:S(2)}) async-start(f32[64,1,2304]{2,1,0:T(1,128)} %bitcast.11), calls=%async_computation.1 | async-start | bytes 1179648 | tf_op jit(solution)/shard_map/all_to_all | solution.py:589
  38.6 1.3 collective-permute-start.2
  39.9 2.4 %collective-permute-start.1 = (f32[384,128]{1,0:T(8,128)S(1)}, f32[384,128]{1,0:T(8,128)S(1)}, u32[]{:S(2)}, u32[]{:S(2)}) collective-permute-start(f32[384,128]{1,0:T(8,128)S(1)} %get-tuple-element.54.field_ref.refs_0_), channel_id=1, source_target_pairs={{0,2},{1,3},{2,0},{3,1},{4,6},{5,7},{6,4},{7,5},{8,10},{9,11},{10,... | collective-permute-start | bytes 589832 | tf_op jit(solution)/shard_map/ppermute | solution.py:639
  42.4 1.2 collective-permute-start
  43.6 1.0 copy-done.25
  44.6 1.8 %tables.1 = (bf16[384,144]{1,0:T(8,128)(2,1)S(1)}, bf16[384,144]{1,0:T(8,128)(2,1)S(1)}, bf16[384,144]{1,0:T(8,128)(2,1)S(1)}, bf16[384,144]{1,0:T(8,128)(2,1)S(...) custom-call(s32[1,128]{1,0:T(1,128)S(1)} %bitcast.27, ...), custom_call_target="tpu_custom_call" | custom-call | flops 1000000000 | bytes 1885184 | tf_op jit(solution)/shard_map/tables/pallas_call | solution.py:555
  46.4 0.7 copy-done.22
  47.1 1.6 %inner.2 = (f32[384,128]{1,0:T(8,128)S(1)}, f32[384,128]{1,0:T(8,128)S(1)}) custom-call(f32[384,128]{1,0:T(8,128)S(1)} %get-tuple-element.54.field_ref.refs_0_, f32[64,128]{1,0:T(8,128)S(1)} %get-tuple-element.56.asked_ref, s32[1,128]{1,0:T(1,128)S(1)} %bitcast.28, f32[1,128]{1,0:T(1,128)S(1)} %bitcast.35, s32[1,128]{1,0:T(1,128)S(1)} %bitcast.40, ...), custom_call_target="tpu_custom_call" | custom-call | flops 1000000000 | bytes 845312 | tf_op jit(solution)/shard_map/inner/pallas_call | solution.py:555
  48.8 0.7 copy-done.30
  49.5 1.7 %collective-permute-done.1.refs_2_ = f32[384,128]{1,0:T(8,128)S(1)} collective-permute-done((f32[384,128]{1,0:T(8,128)S(1)}, f32[384,128]{1,0:T(8,128)S(1)}, u32[]{:S(2)}, u32[]{:S(2)}) %collective-permute-start.1) | collective-permute-done | bytes 196640 | tf_op jit(solution)/shard_map/ppermute | solution.py:639
  51.1 0.7 copy-done.5
  51.8 5.4 %all-to-all-done.1 = f32[64,1,2304]{2,1,0:T(1,128)S(1)} async-done(((f32[64,1,2304]{2,1,0:T(1,128)}), f32[64,1,2304]{2,1,0:T(1,128)S(1)}, u32[]{:S(2)}, u32[]{:S(2)}) %all-to-all-start.1) | async-done | bytes 589856 | tf_op jit(solution)/shard_map/all_to_all | solution.py:589
  57.2 0.7 copy-done.23
  57.8 2.7 %image.1 = (f32[384,128]{1,0:T(8,128)S(1)}, f32[384,128]{1,0:T(8,128)S(1)}, f32[1152,128]{1,0:T(8,128)}) custom-call(f32[1152,128]{1,0:T(8,128)S(1)} %bitcast.19, f32[384,128]{1,0:T(8,128)S(1)} %get-tuple-element.59.inner_ref, f32[64,128]{1,0:T(8,128)S(1)} %get-tuple-element.56.asked_ref, s32[1,128]{1,0:T(1,128)S(1)} %bitcast.29, f32[1,128]{1,0:T(1,128)S(1)} %bitcast.36, ...), custom_call_target="tpu_custom_call" | custom-call | bytes 2058240 | tf_op jit(solution)/shard_map/image/pallas_call | solution.py:555
  60.5 6.5 %all-to-all-start.2 = ((f32[64,1,2304]{2,1,0:T(1,128)}), f32[64,1,2304]{2,1,0:T(1,128)S(1)}, u32[]{:S(2)}, u32[]{:S(2)}) async-start(f32[64,1,2304]{2,1,0:T(1,128)} %bitcast.13), calls=%async_computation.2 | async-start | bytes 1179648 | tf_op jit(solution)/shard_map/all_to_all | solution.py:589
  67.0 1.3 collective-permute-start.8
  68.3 2.4 %collective-permute-start.7 = (f32[384,128]{1,0:T(8,128)S(1)}, f32[384,128]{1,0:T(8,128)S(1)}, u32[]{:S(2)}, u32[]{:S(2)}) collective-permute-start(f32[384,128]{1,0:T(8,128)S(1)} %get-tuple-element.71.field_ref.refs_4_.rest_5_), channel_id=1, source_target_pairs={{0,2},{1,3},{2,0},{3,1},{4,6},{5,7},{6,4},{7,5},{8,10},{9,11},{10,... | collective-permute-start | bytes 589832 | tf_op jit(solution)/shard_map/ppermute | solution.py:639
  70.8 1.2 collective-permute-start.6
  71.9 0.9 copy-done.31
  72.9 0.7 turned.1
  73.6 0.1 collective-permute-start.3
  73.7 2.1 %collective-permute-start.4 = (f32[128,128]{1,0:T(8,128)S(1)}, f32[128,128]{1,0:T(8,128)S(1)}, u32[]{:S(2)}, u32[]{:S(2)}) collective-permute-start(f32[128,128]{1,0:T(8,128)S(1)} %get-tuple-element.68), channel_id=1, source_target_pairs={{0,2},{1,3},{2,0},{3,1},{4,6},{5,7},{6,4},{7,5},{8,10},{9,11},{10,... | collective-permute-start | bytes 196616 | tf_op jit(solution)/shard_map/ppermute | solution.py:639
  75.8 1.7 %inner.3 = (f32[384,128]{1,0:T(8,128)S(1)}, f32[384,128]{1,0:T(8,128)S(1)}) custom-call(f32[384,128]{1,0:T(8,128)S(1)} %get-tuple-element.71.field_ref.refs_4_.rest_5_, f32[64,128]{1,0:T(8,128)S(1)} %copy-done.9, s32[1,128]{1,0:T(1,128)S(1)} %bitcast.31, f32[1,128]{1,0:T(1,128)S(1)} %bitcast.37, s32[1,128]{1,0:T(1,128)S(1)} %bitcast.42, ...), custom_call_target="tpu_custom_call" | custom-call | flops 1000000000 | bytes 845312 | tf_op jit(solution)/shard_map/inner/pallas_call | solution.py:555
  77.5 2.0 %collective-permute-done.7.refs_6_.rest_7_ = f32[384,128]{1,0:T(8,128)S(1)} collective-permute-done((f32[384,128]{1,0:T(8,128)S(1)}, f32[384,128]{1,0:T(8,128)S(1)}, u32[]{:S(2)}, u32[]{:S(2)}) %collective-permute-start.7) | collective-permute-done | bytes 196640 | tf_op jit(solution)/shard_map/ppermute | solution.py:639
  79.5 3.7 %gram.1.rest_1_ = f32[8,128]{1,0:T(8,128)S(1)} custom-call(s32[1]{0:T(128)} %bitcast.case_ref.rest_0_, f32[384,128]{1,0:T(8,128)S(1)} %get-tuple-element.54.field_ref.refs_0_, f32[384,128]{1,0:T(8,128)S(1)} %copy-done.6, f32[384,128]{1,0:T(8,128)S(1)} %collective-permute-done.1.refs_2_, f32[384,128]{1,0:T(8,128)S(1)} %collective-permute-done.2.refs_3_, ...), custom_call_target="tpu_custom_call" | custom-call | bytes 1576964 | tf_op jit(solution)/shard_map/gram/pallas_call | solution.py:555
  83.2 0.6 copy-done.14
  83.9 0.6 copy-done.16
  84.5 0.6 copy-done.18
  85.1 0.5 all-to-all-done.2
  85.6 0.7 copy-done.24
  86.3 0.8 copy-done.10
  87.0 3.9 %second.1 = (f32[384,128]{1,0:T(8,128)S(1)}, f32[16,8,128]{2,1,0:T(8,128)S(1)}, f32[512,128]{1,0:T(8,128)S(1)}) custom-call(f32[1152,128]{1,0:T(8,128)S(1)} %bitcast.18, f32[384,128]{1,0:T(8,128)S(1)} %get-tuple-element.72.inner_ref, f32[64,128]{1,0:T(8,128)S(1)} %copy-done.10, s32[1,128]{1,0:T(1,128)S(1)} %bitcast.32, f32[1,128]{1,0:T(1,128)S(1)} %bitcast.38, ...), custom_call_target="tpu_custom_call" | custom-call | bytes 2848772 | tf_op jit(solution)/shard_map/second/pallas_call | solution.py:555
  91.0 2.5 %collective-permute-start.9 = (f32[512,128]{1,0:T(8,128)S(1)}, f32[512,128]{1,0:T(8,128)S(1)}, u32[]{:S(2)}, u32[]{:S(2)}) collective-permute-start(f32[512,128]{1,0:T(8,128)S(1)} %get-tuple-element.81), channel_id=1, source_target_pairs={{0,3},{1,0},{2,1},{3,2},{4,7},{5,4},{6,5},{7,6},{8,11},{9,8},{10,9... | collective-permute-start | bytes 786440 | tf_op jit(solution)/shard_map/ppermute | solution.py:639
  93.5 0.5 collective-permute-start.10
  94.0 0.6 collective-permute-start.11
  94.7 16.2 %all_to_all.26.in_ref = f32[16,8,128]{2,1,0:T(8,128)S(1)} all-to-all(f32[16,8,128]{2,1,0:T(8,128)S(1)} %get-tuple-element.77), channel_id=1, replica_groups={{0,4,8,12,16,20,24,28,32,36,40,44,48,52,56,60},{1,5,9,13,17,21,25,29,33..., dimensions={0} | all-to-all | bytes 131072 | tf_op jit(solution)/shard_map/all_to_all | solution.py:686
  110.9 12.4 %all_to_all.27.gram_ref = f32[16,8,128]{2,1,0:T(8,128)S(1)} all-to-all(f32[16,8,128]{2,1,0:T(8,128)S(1)} %sum.1), channel_id=1, replica_groups={{0,64,128,192,1,65,129,193,2,66,130,194,3,67,131,195},{4,68,132,196,5,6..., dimensions={0} | all-to-all | bytes 131072 | tf_op jit(solution)/shard_map/all_to_all | solution.py:696
  123.2 4.3 %solve.1 = (f32[64,8,128]{2,1,0:T(8,128)S(1)}, f32[32,256]{1,0:T(8,128)S(1)}) custom-call(s32[1]{0:T(128)} %bitcast.case_ref.rest_0_, f32[16,8,128]{2,1,0:T(8,128)S(1)} %all_to_all.27.gram_ref), custom_call_target="tpu_custom_call" | custom-call | bytes 360452 | tf_op jit(solution)/shard_map/solve/pallas_call | solution.py:555
  127.7 0.4 bubble.1
  128.0 0.9 collective-permute-start.12
  128.9 1.2 collective-permute-start.13
  130.1 2.9 %ports.1 = (f32[384,128]{1,0:T(8,128)}, f32[384,128]{1,0:T(8,128)}) custom-call(f32[64,8,128]{2,1,0:T(8,128)S(1)} %get-tuple-element.78.coef, f32[384,128]{1,0:T(8,128)S(1)} %get-tuple-element.54.field_ref.refs_0_, f32[384,128]{1,0:T(8,128)S(1)} %copy-done.7, f32[384,128]{1,0:T(8,128)S(1)} %collective-permute-done.1.refs_2_, ...), custom_call_target="tpu_custom_call" | custom-call | flops 1000000000 | bytes 3211264 | tf_op jit(solution)/shard_map/ports/pallas_call | solution.py:555
  133.1 0.5 collective-permute-done.13.refs_2_
  133.6 0.9 collective-permute-done.14.refs_3_
  134.5 0.7 join.1
  (68 shorter events, 0.2 us)
Async XLA Ops:
  4.3 26.6 %copy-start.3 = (f32[48,8,128]{2,1,0:T(8,128)S(1)}, f32[48,8,128]{2,1,0:T(8,128)}, u32[]{:S(2)}) copy-start(f32[48,8,128]{2,1,0:T(8,128)} %param.16) | copy-start | bytes 589828
  4.3 26.6 %copy-start.4 = (f32[384,128]{1,0:T(8,128)S(1)}, f32[384,128]{1,0:T(8,128)}, u32[]{:S(2)}) copy-start(f32[384,128]{1,0:T(8,128)} %get-tuple-element.51.near_sum_ref) | copy-start | bytes 589828
  4.3 26.6 %copy-start.11 = (f32[64,128]{1,0:T(8,128)S(1)}, f32[64,128]{1,0:T(8,128)}, u32[]{:S(2)}) copy-start(f32[64,128]{1,0:T(8,128)} %get-tuple-element.52.meta_ref.rest_0_) | copy-start | bytes 98308
  32.3 24.9 %copy-start.8 = (f32[64,128]{1,0:T(8,128)}, f32[64,128]{1,0:T(8,128)S(1)}, u32[]{:S(2)}) copy-start(f32[64,128]{1,0:T(8,128)S(1)} %get-tuple-element.56.asked_ref) | copy-start | bytes 98308
  32.3 11.3 %copy-start = (f32[64,8,128]{2,1,0:T(8,128)S(1)}, f32[64,8,128]{2,1,0:T(8,128)}, u32[]{:S(2)}) copy-start(f32[64,8,128]{2,1,0:T(8,128)} %param.15) | copy-start | bytes 786436
  32.3 11.3 %copy-start.1 = (f32[8,64,64]{2,1,0:T(8,128)S(1)}, f32[8,64,64]{2,1,0:T(8,128)}, u32[]{:S(2)}) copy-start(f32[8,64,64]{2,1,0:T(8,128)} %inverse_ref.1) | copy-start | bytes 393220
  32.3 11.3 %copy-start.2 = (f32[8,96,64]{1,2,0:T(8,128)S(1)}, f32[8,96,64]{1,2,0:T(8,128)}, u32[]{:S(2)}) copy-start(f32[8,96,64]{1,2,0:T(8,128)} %param.18) | copy-start | bytes 589828
  32.3 24.9 %all-to-all-start.1 = ((f32[64,1,2304]{2,1,0:T(1,128)}), f32[64,1,2304]{2,1,0:T(1,128)S(1)}, u32[]{:S(2)}, u32[]{:S(2)}) async-start(f32[64,1,2304]{2,1,0:T(1,128)} %bitcast.11), calls=%async_computation.1 | async-start | bytes 1179648 | tf_op jit(solution)/shard_map/all_to_all | solution.py:589
  38.6 4.9 %copy-start.20 = (s32[128]{0:T(128)S(1)}, s32[128]{0:T(128)}, u32[]{:S(2)}) copy-start(s32[128]{0:T(128)} %param.10) | copy-start | bytes 1540
  38.6 4.9 %copy-start.21 = (f32[128]{0:T(128)S(1)}, f32[128]{0:T(128)}, u32[]{:S(2)}) copy-start(f32[128]{0:T(128)} %param.11) | copy-start | bytes 1540
  38.6 10.8 %collective-permute-start.2 = (f32[384,128]{1,0:T(8,128)S(1)}, f32[384,128]{1,0:T(8,128)S(1)}, u32[]{:S(2)}, u32[]{:S(2)}) collective-permute-start(f32[384,128]{1,0:T(8,128)S(1)} %get-tuple-element.54.field_ref.refs_0_), channel_id=1, source_target_pairs={{0,1},{1,2},{2,3},{3,0},{4,5},{5,6},{6,7},{7,4},{8,9},{9,10},{10,1... | collective-permute-start | bytes 589832 | tf_op jit(solution)/shard_map/ppermute | solution.py:639
  39.9 11.2 %collective-permute-start.1 = (f32[384,128]{1,0:T(8,128)S(1)}, f32[384,128]{1,0:T(8,128)S(1)}, u32[]{:S(2)}, u32[]{:S(2)}) collective-permute-start(f32[384,128]{1,0:T(8,128)S(1)} %get-tuple-element.54.field_ref.refs_0_), channel_id=1, source_target_pairs={{0,2},{1,3},{2,0},{3,1},{4,6},{5,7},{6,4},{7,5},{8,10},{9,11},{10,... | collective-permute-start | bytes 589832 | tf_op jit(solution)/shard_map/ppermute | solution.py:639
  42.4 8.8 %collective-permute-start = (f32[384,128]{1,0:T(8,128)S(1)}, f32[384,128]{1,0:T(8,128)S(1)}, u32[]{:S(2)}, u32[]{:S(2)}) collective-permute-start(f32[384,128]{1,0:T(8,128)S(1)} %get-tuple-element.54.field_ref.refs_0_), channel_id=1, source_target_pairs={{0,3},{1,0},{2,1},{3,2},{4,7},{5,4},{6,5},{7,6},{8,11},{9,8},{10,9... | collective-permute-start | bytes 589832 | tf_op jit(solution)/shard_map/ppermute | solution.py:639
  43.6 1.0 copy-start.25
  46.4 2.4 %copy-start.26 = (bf16[384,144]{1,0:T(8,128)(2,1)}, bf16[384,144]{1,0:T(8,128)(2,1)S(1)}, u32[]{:S(2)}) copy-start(bf16[384,144]{1,0:T(8,128)(2,1)S(1)} %get-tuple-element.57.near_near) | copy-start | bytes 331780
  46.4 2.4 %copy-start.28 = (bf16[384,144]{1,0:T(8,128)(2,1)}, bf16[384,144]{1,0:T(8,128)(2,1)S(1)}, u32[]{:S(2)}) copy-start(bf16[384,144]{1,0:T(8,128)(2,1)S(1)} %get-tuple-element.58.far_far) | copy-start | bytes 331780
  46.4 0.7 copy-start.22
  48.8 0.7 copy-start.30
  51.1 0.7 copy-start.5
  57.2 0.7 copy-start.23
  60.5 25.1 %all-to-all-start.2 = ((f32[64,1,2304]{2,1,0:T(1,128)}), f32[64,1,2304]{2,1,0:T(1,128)S(1)}, u32[]{:S(2)}, u32[]{:S(2)}) async-start(f32[64,1,2304]{2,1,0:T(1,128)} %bitcast.13), calls=%async_computation.2 | async-start | bytes 1179648 | tf_op jit(solution)/shard_map/all_to_all | solution.py:589
  67.0 8.7 %collective-permute-start.8 = (f32[384,128]{1,0:T(8,128)S(1)}, f32[384,128]{1,0:T(8,128)S(1)}, u32[]{:S(2)}, u32[]{:S(2)}) collective-permute-start(f32[384,128]{1,0:T(8,128)S(1)} %get-tuple-element.71.field_ref.refs_4_.rest_5_), channel_id=1, source_target_pairs={{0,1},{1,2},{2,3},{3,0},{4,5},{5,6},{6,7},{7,4},{8,9},{9,10},{10,1... | collective-permute-start | bytes 589832 | tf_op jit(solution)/shard_map/ppermute | solution.py:639
  68.3 11.2 %collective-permute-start.7 = (f32[384,128]{1,0:T(8,128)S(1)}, f32[384,128]{1,0:T(8,128)S(1)}, u32[]{:S(2)}, u32[]{:S(2)}) collective-permute-start(f32[384,128]{1,0:T(8,128)S(1)} %get-tuple-element.71.field_ref.refs_4_.rest_5_), channel_id=1, source_target_pairs={{0,2},{1,3},{2,0},{3,1},{4,6},{5,7},{6,4},{7,5},{8,10},{9,11},{10,... | collective-permute-start | bytes 589832 | tf_op jit(solution)/shard_map/ppermute | solution.py:639
  70.8 8.8 %collective-permute-start.6 = (f32[384,128]{1,0:T(8,128)S(1)}, f32[384,128]{1,0:T(8,128)S(1)}, u32[]{:S(2)}, u32[]{:S(2)}) collective-permute-start(f32[384,128]{1,0:T(8,128)S(1)} %get-tuple-element.71.field_ref.refs_4_.rest_5_), channel_id=1, source_target_pairs={{0,3},{1,0},{2,1},{3,2},{4,7},{5,4},{6,5},{7,6},{8,11},{9,8},{10,9... | collective-permute-start | bytes 589832 | tf_op jit(solution)/shard_map/ppermute | solution.py:639
  71.9 0.9 copy-start.31
  72.9 2.9 %copy-start.9 = (f32[64,128]{1,0:T(8,128)S(1)}, f32[64,128]{1,0:T(8,128)}, u32[]{:S(2)}) copy-start(f32[64,128]{1,0:T(8,128)} %copy-done.8) | copy-start | bytes 98308
  72.9 2.9 %copy-start.27 = (bf16[384,144]{1,0:T(8,128)(2,1)S(1)}, bf16[384,144]{1,0:T(8,128)(2,1)}, u32[]{:S(2)}) copy-start(bf16[384,144]{1,0:T(8,128)(2,1)} %copy-done.26) | copy-start | bytes 331780
  72.9 2.9 %copy-start.29 = (bf16[384,144]{1,0:T(8,128)(2,1)S(1)}, bf16[384,144]{1,0:T(8,128)(2,1)}, u32[]{:S(2)}) copy-start(bf16[384,144]{1,0:T(8,128)(2,1)} %copy-done.28) | copy-start | bytes 331780
  73.6 3.9 %copy-start.12 = (f32[128,128]{1,0:T(8,128)}, f32[128,128]{1,0:T(8,128)S(1)}, u32[]{:S(2)}) copy-start(f32[128,128]{1,0:T(8,128)S(1)} %get-tuple-element.88.refs_0_) | copy-start | bytes 196612
  73.6 9.6 %collective-permute-start.3 = (f32[128,128]{1,0:T(8,128)S(1)}, f32[128,128]{1,0:T(8,128)S(1)}, u32[]{:S(2)}, u32[]{:S(2)}) collective-permute-start(f32[128,128]{1,0:T(8,128)S(1)} %get-tuple-element.67), channel_id=1, source_target_pairs={{0,3},{1,0},{2,1},{3,2},{4,7},{5,4},{6,5},{7,6},{8,11},{9,8},{10,9... | collective-permute-start | bytes 196616 | tf_op jit(solution)/shard_map/ppermute | solution.py:639
  73.7 10.2 %collective-permute-start.4 = (f32[128,128]{1,0:T(8,128)S(1)}, f32[128,128]{1,0:T(8,128)S(1)}, u32[]{:S(2)}, u32[]{:S(2)}) collective-permute-start(f32[128,128]{1,0:T(8,128)S(1)} %get-tuple-element.68), channel_id=1, source_target_pairs={{0,2},{1,3},{2,0},{3,1},{4,6},{5,7},{6,4},{7,5},{8,10},{9,11},{10,... | collective-permute-start | bytes 196616 | tf_op jit(solution)/shard_map/ppermute | solution.py:639
  75.8 3.8 %copy-start.6 = (f32[384,128]{1,0:T(8,128)S(1)}, f32[384,128]{1,0:T(8,128)}, u32[]{:S(2)}) copy-start(f32[384,128]{1,0:T(8,128)} %copy-done.5) | copy-start | bytes 589828
  75.8 8.7 %collective-permute-start.5 = (f32[128,128]{1,0:T(8,128)S(1)}, f32[128,128]{1,0:T(8,128)S(1)}, u32[]{:S(2)}, u32[]{:S(2)}) collective-permute-start(f32[128,128]{1,0:T(8,128)S(1)} %get-tuple-element.69), channel_id=1, source_target_pairs={{0,1},{1,2},{2,3},{3,0},{4,5},{5,6},{6,7},{7,4},{8,9},{9,10},{10,1... | collective-permute-start | bytes 196616 | tf_op jit(solution)/shard_map/ppermute | solution.py:639
  83.2 0.6 copy-start.14
  83.9 0.6 copy-start.16
  85.6 0.7 copy-start.24
  86.3 0.8 copy-start.10
  91.0 36.6 %collective-permute-start.9 = (f32[512,128]{1,0:T(8,128)S(1)}, f32[512,128]{1,0:T(8,128)S(1)}, u32[]{:S(2)}, u32[]{:S(2)}) collective-permute-start(f32[512,128]{1,0:T(8,128)S(1)} %get-tuple-element.81), channel_id=1, source_target_pairs={{0,3},{1,0},{2,1},{3,2},{4,7},{5,4},{6,5},{7,6},{8,11},{9,8},{10,9... | collective-permute-start | bytes 786440 | tf_op jit(solution)/shard_map/ppermute | solution.py:639
  93.5 34.1 %collective-permute-start.10 = (f32[512,128]{1,0:T(8,128)S(1)}, f32[512,128]{1,0:T(8,128)S(1)}, u32[]{:S(2)}, u32[]{:S(2)}) collective-permute-start(f32[512,128]{1,0:T(8,128)S(1)} %get-tuple-element.82), channel_id=1, source_target_pairs={{0,2},{1,3},{2,0},{3,1},{4,6},{5,7},{6,4},{7,5},{8,10},{9,11},{10,... | collective-permute-start | bytes 786440 | tf_op jit(solution)/shard_map/ppermute | solution.py:639
  94.0 33.6 %collective-permute-start.11 = (f32[512,128]{1,0:T(8,128)S(1)}, f32[512,128]{1,0:T(8,128)S(1)}, u32[]{:S(2)}, u32[]{:S(2)}) collective-permute-start(f32[512,128]{1,0:T(8,128)S(1)} %get-tuple-element.83), channel_id=1, source_target_pairs={{0,1},{1,2},{2,3},{3,0},{4,5},{5,6},{6,7},{7,4},{8,9},{9,10},{10,1... | collective-permute-start | bytes 786440 | tf_op jit(solution)/shard_map/ppermute | solution.py:639
  110.8 16.8 %copy-start.19 = (f32[128,128]{1,0:T(8,128)S(1)}, f32[128,128]{1,0:T(8,128)}, u32[]{:S(2)}) copy-start(f32[128,128]{1,0:T(8,128)} %copy-done.18) | copy-start | bytes 196612
  110.9 16.8 %copy-start.15 = (f32[128,128]{1,0:T(8,128)S(1)}, f32[128,128]{1,0:T(8,128)}, u32[]{:S(2)}) copy-start(f32[128,128]{1,0:T(8,128)} %copy-done.14) | copy-start | bytes 196612
  110.9 16.8 %copy-start.17 = (f32[128,128]{1,0:T(8,128)S(1)}, f32[128,128]{1,0:T(8,128)}, u32[]{:S(2)}) copy-start(f32[128,128]{1,0:T(8,128)} %copy-done.16) | copy-start | bytes 196612
  123.2 4.4 %copy-start.13 = (f32[128,128]{1,0:T(8,128)S(1)}, f32[128,128]{1,0:T(8,128)}, u32[]{:S(2)}) copy-start(f32[128,128]{1,0:T(8,128)} %copy-done.12) | copy-start | bytes 196612
  127.7 2.5 %copy-start.7 = (f32[384,128]{1,0:T(8,128)S(1)}, f32[384,128]{1,0:T(8,128)}, u32[]{:S(2)}) copy-start(f32[384,128]{1,0:T(8,128)} %copy-done.5) | copy-start | bytes 589828
  128.0 5.0 %collective-permute-start.12 = (f32[128,128]{1,0:T(8,128)S(1)}, f32[128,128]{1,0:T(8,128)S(1)}, u32[]{:S(2)}, u32[]{:S(2)}) collective-permute-start(f32[128,128]{1,0:T(8,128)S(1)} %get-tuple-element.94), channel_id=1, source_target_pairs={{0,3},{1,0},{2,1},{3,2},{4,7},{5,4},{6,5},{7,6},{8,11},{9,8},{10,9... | collective-permute-start | bytes 196616 | tf_op jit(solution)/shard_map/ppermute | solution.py:639
  128.9 4.6 %collective-permute-start.13 = (f32[128,128]{1,0:T(8,128)S(1)}, f32[128,128]{1,0:T(8,128)S(1)}, u32[]{:S(2)}, u32[]{:S(2)}) collective-permute-start(f32[128,128]{1,0:T(8,128)S(1)} %get-tuple-element.95), channel_id=1, source_target_pairs={{0,2},{1,3},{2,0},{3,1},{4,6},{5,7},{6,4},{7,5},{8,10},{9,11},{10,... | collective-permute-start | bytes 196616 | tf_op jit(solution)/shard_map/ppermute | solution.py:639
  130.1 4.3 %collective-permute-start.14 = (f32[128,128]{1,0:T(8,128)S(1)}, f32[128,128]{1,0:T(8,128)S(1)}, u32[]{:S(2)}, u32[]{:S(2)}) collective-permute-start(f32[128,128]{1,0:T(8,128)S(1)} %get-tuple-element.96), channel_id=1, source_target_pairs={{0,1},{1,2},{2,3},{3,0},{4,5},{5,6},{6,7},{7,4},{8,9},{9,10},{10,1... | collective-permute-start | bytes 196616 | tf_op jit(solution)/shard_map/ppermute | solution.py:639
  (1 other events, 0.6 us)

commit v5 on v3

--- a/solution.py
+++ b/solution.py
@@ -307,14 +307,17 @@
 
 
 def image_kernel(
-    parts, groups, last, arrived_ref, inner_ref, asked_ref, kind_ref, stiff_ref, near_ref, owner_ref,
+    parts, groups, last, arrived_ref, inner_hbm, asked_ref, kind_ref, stiff_ref, near_ref, owner_ref,
     near_far, far_near, *rest,
 ):
     if last:
-        case_ref, gram_ref, rest = rest[0], rest[1], rest[2:]
-        images, (image_ref, far_values, copies_ref, near_part, slot_ref, slot_part) = rest[:groups], rest[groups:]
+        case_ref, gram_ref, near_values, turned_near, turned_far = rest[:5]
+        images, rest = rest[5 : 5 + groups], rest[5 + groups :]
+        image_ref, copies_ref, turned_ref, near_part, slot_ref, slot_part, far_values, inner_ref, sem = rest
     else:
-        meta_ref, image_ref, far_values, pay_ref, near_part, slot_ref, slot_part = rest
+        meta_ref, image_ref, far_values, pay_ref, near_part, slot_ref, slot_part, inner_ref, sem = rest
+    fetch = pltpu.make_async_copy(inner_hbm, inner_ref, sem)
+    fetch.start()
     asked = asked_ref[...]
     asked_hot = port_onehot(asked)
     slots = onehot(jnp.concatenate(owner_slots(owner_ref[...], parts), axis=0))
@@ -326,6 +329,7 @@
     for g in range(tiles):
         slot_ref[g] = values[:, g * LANES : (g + 1) * LANES]
     slot_products(far_near, slot_ref, asked, slot_part)
+    fetch.wait()
     image = inner_ref[...] + pick_right(near_part[...], near_onehot(near_ref[...]), NN)
     image = image + slots_to_ports(slot_part, asked_hot)
     image_ref[...] = image
@@ -333,6 +337,7 @@
         gram = add_products(LANES, images, [image_ref], [3 * groups * CASES], case_ref[0], gram_ref[...])
         for p in range(copies_ref.shape[0]):
             copies_ref[p] = gram
+        turned_rows(near_values, far_values, kind_ref, turned_near, turned_far, turned_ref)
     else:
         send_ports(image, asked_hot, port_onehot(meta_ref[...]), pay_ref)
 
@@ -354,22 +359,23 @@
             out_ref[pl.ds(k + i, modes, stride=CASES), :] = result[:, i * LANES : (i + 1) * LANES]
 
 
-def quarter(ref, case_ref, h, groups):
-    part = ref.shape[0] // groups
-    return ref[pl.ds(pl.multiple_of(lax.rem(case_ref[0] + h, groups) * part, part), part), :]
-
-
-def turned_kernel(groups, first, case_ref, near_values, far_values, kind_ref, turned_near, turned_far, *rest):
-    if not first:
-        field_ref, rest = rest[0], rest[1:]
-    outs, out_ref = rest[:groups], rest[groups]
-    turned_rows(near_values, far_values, kind_ref, turned_near, turned_far, out_ref)
+def messages_kernel(groups, case_ref, field_ref, turned_ref, own_ref, *rest):
+    messages, sems = rest[: groups - 1], rest[groups - 1]
+    rows = field_ref.shape[0]
+    part = own_ref.shape[0]
+    copies = []
     for h in range(groups):
-        at = 0
-        if h and not first:
-            at = field_ref.shape[0]
-            outs[h][:at, :] = field_ref[...]
-        outs[h][at:, :] = quarter(out_ref, case_ref, h, groups)
+        at = pl.multiple_of(lax.rem(case_ref[0] + h, groups) * part, part)
+        target = messages[h - 1].at[pl.ds(rows, part), :] if h else own_ref
+        copies.append(pltpu.make_async_copy(turned_ref.at[pl.ds(at, part), :], target, sems.at[h]))
+        if h:
+            copies.append(
+                pltpu.make_async_copy(field_ref, messages[h - 1].at[pl.ds(0, rows), :], sems.at[groups + h])
+            )
+    for copy in copies:
+        copy.start()
+    for copy in copies:
+        copy.wait()
 
 
 def add_products(lanes, lefts, rights, first, case, out):
@@ -487,8 +493,11 @@
         values = []
         for i in range(2):
             at = (m + i) * CASES
-            pieces = [ref[at : at + CASES, :] for ref in turned0]
-            pieces += [ref[at + shift : at + shift + CASES, :] for ref, shift in zip(turned1, [0] + [rows] * (groups - 1))]
+            pieces = [
+                ref[at + shift : at + shift + CASES, :]
+                for turned in (turned0, turned1)
+                for ref, shift in zip(turned, [0] + [rows] * (groups - 1))
+            ]
             values.append(jnp.concatenate(pieces, axis=0))
         result = dot(left, stacked_values(jnp.concatenate(values, axis=1)))
         for i in range(2):
@@ -534,23 +543,27 @@
         out_ref[at, :] = bubble_ref[at, :] - parts[h][...]
 
 
-def call(kernel, outs, scratch=(), name=None, flops=0, smem=(), hbm=False):
-    outs = [jax.ShapeDtypeStruct(shape, dtype) for shape, dtype in outs]
+def call(kernel, outs, scratch=(), name=None, flops=0, smem=(), hbm=(), sems=0, limit=12):
+    results = [(pltpu.HBM if far else jax.ShapeDtypeStruct)(shape, dtype) for shape, dtype, far in outs]
     vmem = pl.BlockSpec(memory_space=pltpu.VMEM)
+    far_spec = pl.BlockSpec(memory_space=pltpu.HBM)
+    copies_only = name == "messages"
 
     def run(*args):
-        usual = pl.BlockSpec(memory_space=pltpu.HBM) if hbm else vmem
-        specs = [pl.BlockSpec(memory_space=pltpu.SMEM) if i in smem else usual for i in range(len(args))]
-        moved = sum(a.size * a.dtype.itemsize for a in args) + sum(o.size * o.dtype.itemsize for o in outs)
-        fetched = [pltpu.VMEM(a.shape, a.dtype) for a in args] if hbm else []
-        sems = [pltpu.SemaphoreType.DMA((len(args),))] if hbm else []
+        specs = [
+            pl.BlockSpec(memory_space=pltpu.SMEM) if i in smem else far_spec if i in hbm else vmem
+            for i in range(len(args))
+        ]
+        moved = sum(a.size * a.dtype.itemsize for a in args)
+        args = [pltpu.with_memory_space_constraint(a, pltpu.HBM) if i in hbm else a for i, a in enumerate(args)]
         return pl.pallas_call(
             kernel,
-            out_shape=outs,
+            out_shape=results,
             in_specs=specs,
-            out_specs=[vmem] * len(outs),
-            scratch_shapes=fetched + [pltpu.VMEM(shape, F32) for shape in scratch] + sems,
-            compiler_params=pltpu.CompilerParams(vmem_limit_bytes=12 << 20),
+            out_specs=[far_spec if copies_only else vmem] * len(outs),
+            scratch_shapes=[pltpu.VMEM(*shape) if isinstance(shape[0], tuple) else pltpu.VMEM(shape, F32) for shape in scratch]
+            + ([pltpu.SemaphoreType.DMA((sems,) if sems > 1 else ())] if sems else []),
+            compiler_params=pltpu.CompilerParams(vmem_limit_bytes=limit << 20),
             cost_estimate=pl.CostEstimate(flops=flops, bytes_accessed=moved, transcendentals=0),
             name=name,
         )(*args)
@@ -580,30 +593,33 @@
     owner = far_owner.reshape(1, comps)
     far = far_port.reshape(1, comps)
     loads = bubble_load.reshape(bubbles, comps)
-    field_of = ((rows, ports), F32)
-    meta_of = ((parts, LANES), F32)
+    field_of = ((rows, ports), F32, True)
+    meta_of = ((parts, LANES), F32, False)
+    bubble_of = ((bubbles, comps), F32, True)
+    given = (kind, stiff, near, owner, far, loads, bubble_inverse, coupling)
     pay, near_sum, meta = call(
         functools.partial(condense_kernel, parts),
-        [((parts * 10, LANES), F32), field_of, meta_of],
-        [(rows, comps)] * 2,
+        [((parts * 10, LANES), F32, False), field_of, meta_of],
+        [(a.shape, a.dtype) for a in given] + [(rows, comps)] * 2,
         "condense",
-        hbm=True,
-    )(kind, stiff, near, owner, far, loads, bubble_inverse, coupling)
+        hbm=range(len(given)),
+        sems=len(given),
+    )(*given)
     near_near, near_far, far_near, far_far, turned_near, turned_far, bubble_base = call(
         tables_kernel,
-        [((KINDS * dofs, 3 * dofs), BF16)] * 4 + [((KINDS * modes, 3 * dofs), BF16)] * 2 + [((bubbles, comps), F32)],
+        [((KINDS * dofs, 3 * dofs), BF16, False)] * 4 + [((KINDS * modes, 3 * dofs), BF16, True)] * 2 + [bubble_of],
         name="tables",
         flops=10**9,
     )(kind, stiff, loads, bubble_inverse, coupling, port_block)
     base, pay, asked = call(
         functools.partial(rhs_kernel, parts),
-        [field_of, ((parts * 18, LANES), F32), meta_of],
+        [field_of, ((parts * 18, LANES), F32, False), meta_of],
         name="rhs",
     )(exchange(pay, parts), near_sum, port_load.reshape(rows, ports), meta)
 
     case = lax.axis_index("case").reshape(1)
     part = bubbles // groups
-    part_of = ((part, comps), F32)
+    part_of = ((part, comps), F32, True)
     slot_scratch = [(slot_tiles, rows, LANES)] * 2
     where = (kind, stiff, near, owner)
 
@@ -625,63 +641,67 @@
     arrived, *base_all = lax.optimization_barrier((arrived, *base_all))
     image, base_far, pay = call(
         functools.partial(image_kernel, parts, groups, False),
-        [field_of] * 2 + [((parts * 18, LANES), F32)],
-        [(rows, comps)] + slot_scratch,
+        [field_of] * 2 + [((parts * 18, LANES), F32, False)],
+        [(rows, comps)] + slot_scratch + [(rows, ports)],
         "image",
+        hbm=(1,),
+        sems=1,
     )(arrived, base_inner, asked, *where, near_far, far_near, meta)
     arrived = exchange(pay, parts)
-    image_all = to_cases([image] * (groups - 1))
+    def messages(field, turned):
+        own, *others = call(
+            functools.partial(messages_kernel, groups),
+            [part_of] + [((rows + part, comps), F32, True)] * (groups - 1),
+            name="messages",
+            flops=10**9,
+            smem=(0,),
+            hbm=(1, 2),
+            sems=2 * groups,
+        )(case, field, turned)
+        return own, to_cases(others)
+
+    (turned0,) = call(turned_rows, [bubble_of], name="turned", flops=10**9)(
+        base_near, base_far, kind, turned_near, turned_far
+    )
+    turned0, both0 = messages(image, turned0)
     image_inner, image_near = inner(image)
-    turned0, *messages = call(
-        functools.partial(turned_kernel, groups, True),
-        [part_of] * groups,
-        [(bubbles, comps)],
-        name="turned",
-        flops=10**9,
-        smem=(0,),
-    )(case, base_near, base_far, kind, turned_near, turned_far)
-    turned0_all = to_cases(messages)
-    (gram,) = call(functools.partial(gram_kernel, groups), [((cases, LANES), F32)], name="gram", smem=(0,))(
-        case, base, *base_all, image, *image_all
-    )
-    arrived, *turned0_all = lax.optimization_barrier((arrived, *turned0_all))
+    (gram,) = call(functools.partial(gram_kernel, groups), [((cases, LANES), F32, False)], name="gram", smem=(0,))(
+        case, base, *base_all, image, *both0
+    )
     minor = lax.axis_size("py")
-    second, image_far, copies = call(
+    second, copies, turned1 = call(
         functools.partial(image_kernel, parts, groups, True),
-        [field_of] * 2 + [((groups * minor, cases, LANES), F32)],
-        [(rows, comps)] + slot_scratch,
+        [field_of, ((groups * minor, cases, LANES), F32, True), bubble_of],
+        [(rows, comps)] + slot_scratch + [(rows, comps), (rows, ports)],
         "second",
         smem=(9,),
-    )(arrived, image_inner, asked, *where, near_far, far_near, case, gram, image, *image_all)
+        hbm=(1,),
+        sems=1,
+    )(
+        arrived, image_inner, asked, *where, near_far, far_near, case, gram, image_near, turned_near, turned_far,
+        image, *both0,
+    )
     copies = lax.all_to_all(copies, ("case", "py"), split_axis=0, concat_axis=0)
-    turned1, *messages = call(
-        functools.partial(turned_kernel, groups, False),
-        [part_of] + [((rows + part, comps), F32)] * (groups - 1),
-        [(bubbles, comps)],
-        "turned_second",
-        flops=10**9,
-        smem=(0,),
-    )(case, image_near, image_far, kind, turned_near, turned_far, second)
-    both1 = to_cases(messages)
-    (copies,) = call(sum_kernel, [((parts // minor, groups * cases, LANES), F32)], name="sum")(
+    turned1, both1 = messages(second, turned1)
+    (copies,) = call(sum_kernel, [((parts // minor, groups * cases, LANES), F32, False)], name="sum")(
         copies.reshape(groups, minor, cases, LANES)
     )
     copies = lax.all_to_all(copies, "px", split_axis=0, concat_axis=0)
     coef, coef_rows = call(
         functools.partial(solve_kernel, groups),
-        [((2 * groups * cases, cases, LANES), F32), ((groups * cases, 2 * LANES), F32)],
+        [((2 * groups * cases, cases, LANES), F32, False), ((groups * cases, 2 * LANES), F32, False)],
         [(2, groups * cases, LANES)],
         "solve",
         smem=(0,),
     )(case, copies)
     own, *messages = call(
         functools.partial(bubble_kernel, groups, rows), [part_of] * groups, name="bubble"
-    )(coef_rows, turned0, *turned0_all, turned1, *both1)
+    )(coef_rows, turned0, *both0, turned1, *both1)
     back = to_cases(messages)
     x, residual = call(
         functools.partial(ports_kernel, groups), [field_of, field_of], name="ports", flops=10**9
-    )(coef, base, *base_all, image, *image_all, second, *both1)
-    (bubble,) = call(functools.partial(join_kernel, groups), [((bubbles, comps), F32)], name="join", smem=(0,))(
+    )(coef, base, *base_all, image, *both0, second, *both1)
+    (bubble,) = call(functools.partial(join_kernel, groups), [bubble_of], name="join", smem=(0,))(
         case, bubble_base, own, *back
     )
     return (

time: 134 us -> 189 us (1.41)
  Pallas kernels: 29.6 us -> 90 us
  local copies, waits for them, and re-layouts: 8.98 us -> 1.42 us
  waiting for transfers between devices: 16.1 us -> 21.7 us
  starting transfers between devices: 38 us -> 36 us
    pallas_call x15 -> x16, Pallas kernels: 29.6 us -> 90 us  [run(): pl.pallas_call(kernel, out_shape=results, in_specs=specs, out_specs=[far_...]
    ppermute x15 -> x12, waiting for transfers between devices: 6.6 us -> 15.7 us  [to_cases(): lax.ppermute(message, 'case', [(k, (k + h) % groups) for k in range(group...]
    unnamed x54 -> x52, local copies, waits for them, and re-layouts: 8.98 us -> 1.42 us
    all_to_all x2, waiting for transfers between devices: 8.38 us -> 6.03 us  [exchange(): lax.all_to_all(rows.reshape(parts, 1, -1), PLANE, split_axis=0, concat_ax...]
    ppermute x15 -> x12, starting transfers between devices: 17.8 us -> 15.8 us  [to_cases(): lax.ppermute(message, 'case', [(k, (k + h) % groups) for k in range(group...]
  transfers between devices with their start and end apart: 18 -> 15, of which waited for: 7 -> 7; matrix products, arithmetic and copies ran while one was open for 0% -> 0% of each run, Pallas kernels for 14% -> 39%
where the time goes in v5:
time: 189 us; the launch traced here: 188 us
  Pallas kernels  90 us (48%)
  blocking collectives  37.7 us (20%)
  starting transfers between devices  36 us (19%)
  waiting for transfers between devices  21.7 us (11%)
    pallas_call x16, Pallas kernels, run(): pl.pallas_call(kernel, out_shape=results, in_specs=specs, out_specs=[far_...  90 us
    all_to_all x1, blocking collectives, exchange(): lax.all_to_all(rows.reshape(parts, 1, -1), PLANE, split_axis=0, concat_ax...  26.4 us
    ppermute x12, starting transfers between devices, to_cases(): lax.ppermute(message, 'case', [(k, (k + h) % groups) for k in range(group...  15.8 us
    ppermute x12, waiting for transfers between devices, to_cases(): lax.ppermute(message, 'case', [(k, (k + h) % groups) for k in range(group...  15.7 us
    all_to_all x2, starting transfers between devices, exchange(): lax.all_to_all(rows.reshape(parts, 1, -1), PLANE, split_axis=0, concat_ax...  13 us
    all_to_all x1, blocking collectives, local(): copies = lax.all_to_all(copies, 'px', split_axis=0, concat_axis=0)  11.3 us
    all_to_all x1, starting transfers between devices, local(): copies = lax.all_to_all(copies, ('case', 'py'), split_axis=0, concat_axis=0)  7.22 us
    all_to_all x2, waiting for transfers between devices, exchange(): lax.all_to_all(rows.reshape(parts, 1, -1), PLANE, split_axis=0, concat_ax...  6.03 us
  transfers between devices with their start and end apart: 15, of which 7 were waited for; matrix products, arithmetic and copies ran while one was open for 0% of the time, Pallas kernels for 39%

profile of v5, /device:TPU:1, one launch (start us, length us, event | category | flops | bytes accessed | tf_op | source)
XLA Modules:
  0.0 187.8 jit_solution(14030859390802461493)
XLA Ops:
  0.6 3.5 %condense.1 = (f32[640,128]{1,0:T(8,128)S(1)}, f32[384,128]{1,0:T(8,128)}, f32[64,128]{1,0:T(8,128)S(1)}) custom-call(s32[1,128]{1,0:T(1,128)} %bitcast.29, f32[1,128]{1,0:T(1,128)} %bitcast.36, s32[1,128]{1,0:T(1,128)} %bitcast.42, s32[1,128]{1,0:T(1,128)} %bitcast.47, s32[1,128]{1,0:T(1,128)} %bitcast.51, f32[512,128]{1,0:T(8,128)} %bitcast.24, ...), custom_call_target="tpu_custom_call" | custom-call | bytes 592384 | tf_op jit(solution)/shard_map/condense/pallas_call | solution.py:559
  4.1 0.0 copy-start.7
  4.1 0.0 copy-start.8
  4.1 26.4 %all_to_all.25 = f32[64,1,1280]{2,1,0:T(1,128)S(1)} all-to-all(f32[64,1,1280]{2,1,0:T(1,128)S(1)} %bitcast.23), channel_id=1, replica_groups=mesh['px'=8,'py'=8,'case'=4] {'px','py'}, dimensions={0} | all-to-all | bytes 655360 | tf_op jit(solution)/shard_map/all_to_all | solution.py:575
  30.5 1.4 rhs.1
  31.9 6.3 %all-to-all-start.1 = ((f32[64,1,2304]{2,1,0:T(1,128)}), f32[64,1,2304]{2,1,0:T(1,128)S(1)}, u32[]{:S(2)}, u32[]{:S(2)}) async-start(f32[64,1,2304]{2,1,0:T(1,128)} %bitcast.11), calls=%async_computation.1 | async-start | bytes 1179648 | tf_op jit(solution)/shard_map/all_to_all | solution.py:575
  38.2 0.0 copy-start.14
  38.3 0.0 copy-start.15
  38.3 1.3 collective-permute-start.2
  39.6 2.4 %collective-permute-start.1 = (f32[384,128]{1,0:T(8,128)S(1)}, f32[384,128]{1,0:T(8,128)S(1)}, u32[]{:S(2)}, u32[]{:S(2)}) collective-permute-start(f32[384,128]{1,0:T(8,128)S(1)} %copy-done.9), channel_id=1, source_target_pairs={{0,2},{1,3},{2,0},{3,1},{4,6},{5,7},{6,4},{7,5},{8,10},{9,11},{10,... | collective-permute-start | bytes 589832 | tf_op jit(solution)/shard_map/ppermute | solution.py:628
  42.0 1.2 collective-permute-start
  43.2 2.6 %tables.1 = (bf16[384,144]{1,0:T(8,128)(2,1)S(1)}, bf16[384,144]{1,0:T(8,128)(2,1)S(1)}, bf16[384,144]{1,0:T(8,128)(2,1)S(1)}, bf16[384,144]{1,0:T(8,128)(2,1)S(...) custom-call(s32[1,128]{1,0:T(1,128)S(1)} %bitcast.30, f32[1,128]{1,0:T(1,128)S(1)} %bitcast.37, ...), custom_call_target="tpu_custom_call" | custom-call | flops 1000000000 | bytes 885760 | tf_op jit(solution)/shard_map/tables/pallas_call | solution.py:559
  45.8 0.7 copy-done.16
  46.5 2.3 %inner.2 = (f32[384,128]{1,0:T(8,128)}, f32[384,128]{1,0:T(8,128)}) custom-call(f32[384,128]{1,0:T(8,128)S(1)} %copy-done.9, f32[64,128]{1,0:T(8,128)S(1)} %get-tuple-element.52.asked_ref, s32[1,128]{1,0:T(1,128)S(1)} %bitcast.31, f32[1,128]{1,0:T(1,128)S(1)} %bitcast.38, s32[1,128]{1,0:T(1,128)S(1)} %bitcast.43, ...), custom_call_target="tpu_custom_call" | custom-call | flops 1000000000 | bytes 452096 | tf_op jit(solution)/shard_map/inner/pallas_call | solution.py:559
  48.8 0.0 collective-permute-done.2.refs_3_
  48.8 2.0 %collective-permute-done.1.refs_2_ = f32[384,128]{1,0:T(8,128)S(1)} collective-permute-done((f32[384,128]{1,0:T(8,128)S(1)}, f32[384,128]{1,0:T(8,128)S(1)}, u32[]{:S(2)}, u32[]{:S(2)}) %collective-permute-start.1) | collective-permute-done | bytes 196640 | tf_op jit(solution)/shard_map/ppermute | solution.py:628
  50.8 6.0 %all-to-all-done.1 = f32[64,1,2304]{2,1,0:T(1,128)S(1)} async-done(((f32[64,1,2304]{2,1,0:T(1,128)}), f32[64,1,2304]{2,1,0:T(1,128)S(1)}, u32[]{:S(2)}, u32[]{:S(2)}) %all-to-all-start.1) | async-done | bytes 589856 | tf_op jit(solution)/shard_map/all_to_all | solution.py:575
  56.8 0.7 copy-done.17
  57.5 3.8 %image.1 = (f32[384,128]{1,0:T(8,128)}, f32[384,128]{1,0:T(8,128)}, f32[1152,128]{1,0:T(8,128)}) custom-call(f32[1152,128]{1,0:T(8,128)S(1)} %bitcast.19, f32[384,128]{1,0:T(8,128)} %get-tuple-element.55.inner_hbm, f32[64,128]{1,0:T(8,128)S(1)} %get-tuple-element.52.asked_ref, s32[1,128]{1,0:T(1,128)S(1)} %bitcast.32, f32[1,128]{1,0:T(1,128)S(1)} %bitcast.39, ...), custom_call_target="tpu_custom_call" | custom-call | bytes 1075200 | tf_op jit(solution)/shard_map/image/pallas_call | solution.py:559
  61.3 0.0 copy-start.5
  61.3 0.0 copy-start.25
  61.3 6.7 %all-to-all-start.2 = ((f32[64,1,2304]{2,1,0:T(1,128)}), f32[64,1,2304]{2,1,0:T(1,128)S(1)}, u32[]{:S(2)}, u32[]{:S(2)}) async-start(f32[64,1,2304]{2,1,0:T(1,128)} %bitcast.13), calls=%async_computation.2 | async-start | bytes 1179648 | tf_op jit(solution)/shard_map/all_to_all | solution.py:575
  68.0 1.4 turned.1.turned_ref
  69.5 27.0 %messages.2 = (f32[128,128]{1,0:T(8,128)}, f32[512,128]{1,0:T(8,128)}, f32[512,128]{1,0:T(8,128)}, f32[512,128]{1,0:T(8,128)}) custom-call(s32[1]{0:T(128)} %bitcast.case_ref.rest_0_, f32[384,128]{1,0:T(8,128)} %get-tuple-element.59.field_ref.refs_4_.rest_5_, f32[512,128]{1,0:T(8,128)} %turned.1.turned_ref), custom_call_target="tpu_custom_call" | custom-call | flops 1000000000 | bytes 458756 | tf_op jit(solution)/shard_map/messages/pallas_call | solution.py:559
  96.4 2.7 %collective-permute-start.3 = (f32[512,128]{1,0:T(8,128)}, f32[512,128]{1,0:T(8,128)S(1)}, u32[]{:S(2)}, u32[]{:S(2)}) collective-permute-start(f32[512,128]{1,0:T(8,128)} %get-tuple-element.68), channel_id=1, source_target_pairs={{0,3},{1,0},{2,1},{3,2},{4,7},{5,4},{6,5},{7,6},{8,11},{9,8},{10,9... | collective-permute-start | bytes 786440 | tf_op jit(solution)/shard_map/ppermute | solution.py:628
  99.2 0.5 collective-permute-start.4
  99.7 0.6 collective-permute-start.5
  100.3 2.3 %inner.3 = (f32[384,128]{1,0:T(8,128)}, f32[384,128]{1,0:T(8,128)}) custom-call(f32[384,128]{1,0:T(8,128)S(1)} %copy-done, f32[64,128]{1,0:T(8,128)S(1)} %get-tuple-element.52.asked_ref, s32[1,128]{1,0:T(1,128)S(1)} %bitcast.34, f32[1,128]{1,0:T(1,128)S(1)} %bitcast.40, s32[1,128]{1,0:T(1,128)S(1)} %bitcast.45, bf16[384,144]{1,0:T(8,128)(2,1)S(1)} %copy-done.22, ...), custom_call_target="tpu_custom_call" | custom-call | flops 1000000000 | bytes 452096 | tf_op jit(solution)/shard_map/inner/pallas_call | solution.py:559
  102.7 2.8 %collective-permute-done.3.refs_5_.rest_6_.refs_1_ = f32[512,128]{1,0:T(8,128)S(1)} collective-permute-done((f32[512,128]{1,0:T(8,128)}, f32[512,128]{1,0:T(8,128)S(1)}, u32[]{:S(2)}, u32[]{:S(2)}) %collective-permute-start.3) | collective-permute-done | bytes 262176 | tf_op jit(solution)/shard_map/ppermute | solution.py:628
  105.5 2.6 %collective-permute-done.4.refs_6_.rest_7_.refs_2_ = f32[512,128]{1,0:T(8,128)S(1)} collective-permute-done((f32[512,128]{1,0:T(8,128)}, f32[512,128]{1,0:T(8,128)S(1)}, u32[]{:S(2)}, u32[]{:S(2)}) %collective-permute-start.4) | collective-permute-done | bytes 262176 | tf_op jit(solution)/shard_map/ppermute | solution.py:628
  108.0 6.7 %collective-permute-done.5.refs_7_.rest_8_.refs_3_ = f32[512,128]{1,0:T(8,128)S(1)} collective-permute-done((f32[512,128]{1,0:T(8,128)}, f32[512,128]{1,0:T(8,128)S(1)}, u32[]{:S(2)}, u32[]{:S(2)}) %collective-permute-start.5) | collective-permute-done | bytes 262176 | tf_op jit(solution)/shard_map/ppermute | solution.py:628
  114.7 3.7 %gram.1.rest_1_ = f32[8,128]{1,0:T(8,128)S(1)} custom-call(s32[1]{0:T(128)} %bitcast.case_ref.rest_0_, f32[384,128]{1,0:T(8,128)S(1)} %copy-done.9, f32[384,128]{1,0:T(8,128)S(1)} %collective-permute-done.refs_1_, f32[384,128]{1,0:T(8,128)S(1)} %collective-permute-done.1.refs_2_, f32[384,128]{1,0:T(8,128)S(1)} %collective-permute-done.2.refs_3_, ...), custom_call_target="tpu_custom_call" | custom-call | bytes 1769476 | tf_op jit(solution)/shard_map/gram/pallas_call | solution.py:559
  118.4 5.7 %second.1 = (f32[384,128]{1,0:T(8,128)}, f32[32,8,128]{2,1,0:T(8,128)}, f32[512,128]{1,0:T(8,128)}) custom-call(f32[1152,128]{1,0:T(8,128)S(1)} %bitcast.20, f32[384,128]{1,0:T(8,128)} %get-tuple-element.60.inner_hbm, f32[64,128]{1,0:T(8,128)S(1)} %get-tuple-element.52.asked_ref, s32[1,128]{1,0:T(1,128)S(1)} %bitcast.35, f32[1,128]{1,0:T(1,128)S(1)} %bitcast.41, ...), custom_call_target="tpu_custom_call" | custom-call | bytes 2521092 | tf_op jit(solution)/shard_map/second/pallas_call | solution.py:559
  124.1 7.2 %all-to-all-start.3 = ((f32[32,8,128]{2,1,0:T(8,128)}), f32[32,8,128]{2,1,0:T(8,128)S(1)}, u32[]{:S(2)}, u32[]{:S(2)}) async-start(f32[32,8,128]{2,1,0:T(8,128)} %get-tuple-element.72), calls=%async_computation.3 | async-start | bytes 262144 | tf_op jit(solution)/shard_map/all_to_all | solution.py:684
  131.4 27.0 %messages.3 = (f32[128,128]{1,0:T(8,128)}, f32[512,128]{1,0:T(8,128)}, f32[512,128]{1,0:T(8,128)}, f32[512,128]{1,0:T(8,128)}) custom-call(s32[1]{0:T(128)} %bitcast.case_ref.rest_0_, f32[384,128]{1,0:T(8,128)} %get-tuple-element.74.field_ref.refs_8_, f32[512,128]{1,0:T(8,128)} %get-tuple-element.75.turned_ref), custom_call_target="tpu_custom_call" | custom-call | flops 1000000000 | bytes 458756 | tf_op jit(solution)/shard_map/messages/pallas_call | solution.py:559
  158.4 2.6 %collective-permute-start.6 = (f32[512,128]{1,0:T(8,128)}, f32[512,128]{1,0:T(8,128)S(1)}, u32[]{:S(2)}, u32[]{:S(2)}) collective-permute-start(f32[512,128]{1,0:T(8,128)} %get-tuple-element.76), channel_id=1, source_target_pairs={{0,3},{1,0},{2,1},{3,2},{4,7},{5,4},{6,5},{7,6},{8,11},{9,8},{10,9... | collective-permute-start | bytes 786440 | tf_op jit(solution)/shard_map/ppermute | solution.py:628
  160.9 0.5 collective-permute-start.7
  161.5 0.6 collective-permute-start.8
  162.1 11.3 %all_to_all.26.gram_ref = f32[8,32,128]{2,1,0:T(8,128)S(1)} all-to-all(f32[8,32,128]{2,1,0:T(8,128)S(1)} %sum.1), channel_id=1, replica_groups=mesh['px'=8,'py'=8,'case'=4] {'px'}, dimensions={0} | all-to-all | bytes 262144 | tf_op jit(solution)/shard_map/all_to_all | solution.py:689
  173.4 4.3 %solve.1 = (f32[64,8,128]{2,1,0:T(8,128)S(1)}, f32[32,256]{1,0:T(8,128)S(1)}) custom-call(s32[1]{0:T(128)} %bitcast.case_ref.rest_0_, f32[8,32,128]{2,1,0:T(8,128)S(1)} %all_to_all.26.gram_ref), custom_call_target="tpu_custom_call" | custom-call | bytes 131076 | tf_op jit(solution)/shard_map/solve/pallas_call | solution.py:559
  177.8 0.0 copy-start.19
  177.8 1.0 bubble.1
  178.9 2.1 %collective-permute-start.9 = (f32[128,128]{1,0:T(8,128)}, f32[128,128]{1,0:T(8,128)S(1)}, u32[]{:S(2)}, u32[]{:S(2)}) collective-permute-start(f32[128,128]{1,0:T(8,128)} %get-tuple-element.86), channel_id=1, source_target_pairs={{0,3},{1,0},{2,1},{3,2},{4,7},{5,4},{6,5},{7,6},{8,11},{9,8},{10,9... | collective-permute-start | bytes 196616 | tf_op jit(solution)/shard_map/ppermute | solution.py:628
  181.0 1.2 collective-permute-start.10
  182.2 3.2 %ports.1 = (f32[384,128]{1,0:T(8,128)}, f32[384,128]{1,0:T(8,128)}) custom-call(f32[64,8,128]{2,1,0:T(8,128)S(1)} %get-tuple-element.73.coef, f32[384,128]{1,0:T(8,128)S(1)} %copy-done.9, f32[384,128]{1,0:T(8,128)S(1)} %collective-permute-done.refs_1_, f32[384,128]{1,0:T(8,128)S(1)} %collective-permute-done.1.refs_2_, ...), custom_call_target="tpu_custom_call" | custom-call | flops 1000000000 | bytes 3014656 | tf_op jit(solution)/shard_map/ports/pallas_call | solution.py:559
  185.4 0.4 collective-permute-done.10.refs_2_
  185.8 1.2 collective-permute-done.11.refs_3_
  187.0 0.7 join.1
  (52 shorter events, 0.1 us)
Async XLA Ops:
  4.1 26.4 %copy-start.7 = (f32[48,8,128]{2,1,0:T(8,128)S(1)}, f32[48,8,128]{2,1,0:T(8,128)}, u32[]{:S(2)}) copy-start(f32[48,8,128]{2,1,0:T(8,128)} %param.16) | copy-start | bytes 589828
  4.1 26.4 %copy-start.8 = (f32[384,128]{1,0:T(8,128)S(1)}, f32[384,128]{1,0:T(8,128)}, u32[]{:S(2)}) copy-start(f32[384,128]{1,0:T(8,128)} %get-tuple-element.47.near_sum_ref) | copy-start | bytes 589828
  30.5 12.7 %copy-start.18 = (f32[8,96,96]{2,1,0:T(8,128)S(1)}, f32[8,96,96]{2,1,0:T(8,128)}, u32[]{:S(2)}) copy-start(f32[8,96,96]{2,1,0:T(8,128)} %block_ref.1) | copy-start | bytes 884740
  31.9 6.4 %copy-start.9 = (f32[384,128]{1,0:T(8,128)S(1)}, f32[384,128]{1,0:T(8,128)}, u32[]{:S(2)}) copy-start(f32[384,128]{1,0:T(8,128)} %get-tuple-element.50.field_ref.refs_0_) | copy-start | bytes 589828
  31.9 11.3 %copy-start.1 = (f32[64,8,128]{2,1,0:T(8,128)S(1)}, f32[64,8,128]{2,1,0:T(8,128)}, u32[]{:S(2)}) copy-start(f32[64,8,128]{2,1,0:T(8,128)} %param.15) | copy-start | bytes 786436
  31.9 11.3 %copy-start.2 = (f32[8,64,64]{2,1,0:T(8,128)S(1)}, f32[8,64,64]{2,1,0:T(8,128)}, u32[]{:S(2)}) copy-start(f32[8,64,64]{2,1,0:T(8,128)} %inverse_ref.1) | copy-start | bytes 393220
  31.9 11.3 %copy-start.3 = (f32[8,96,64]{1,2,0:T(8,128)S(1)}, f32[8,96,64]{1,2,0:T(8,128)}, u32[]{:S(2)}) copy-start(f32[8,96,64]{1,2,0:T(8,128)} %param.18) | copy-start | bytes 589828
  31.9 24.9 %all-to-all-start.1 = ((f32[64,1,2304]{2,1,0:T(1,128)}), f32[64,1,2304]{2,1,0:T(1,128)S(1)}, u32[]{:S(2)}, u32[]{:S(2)}) async-start(f32[64,1,2304]{2,1,0:T(1,128)} %bitcast.11), calls=%async_computation.1 | async-start | bytes 1179648 | tf_op jit(solution)/shard_map/all_to_all | solution.py:575
  38.2 4.9 %copy-start.14 = (s32[128]{0:T(128)S(1)}, s32[128]{0:T(128)}, u32[]{:S(2)}) copy-start(s32[128]{0:T(128)} %param.10) | copy-start | bytes 1540
  38.3 4.9 %copy-start.15 = (f32[128]{0:T(128)S(1)}, f32[128]{0:T(128)}, u32[]{:S(2)}) copy-start(f32[128]{0:T(128)} %param.11) | copy-start | bytes 1540
  38.3 10.5 %collective-permute-start.2 = (f32[384,128]{1,0:T(8,128)S(1)}, f32[384,128]{1,0:T(8,128)S(1)}, u32[]{:S(2)}, u32[]{:S(2)}) collective-permute-start(f32[384,128]{1,0:T(8,128)S(1)} %copy-done.9), channel_id=1, source_target_pairs={{0,1},{1,2},{2,3},{3,0},{4,5},{5,6},{6,7},{7,4},{8,9},{9,10},{10,1... | collective-permute-start | bytes 589832 | tf_op jit(solution)/shard_map/ppermute | solution.py:628
  39.6 11.2 %collective-permute-start.1 = (f32[384,128]{1,0:T(8,128)S(1)}, f32[384,128]{1,0:T(8,128)S(1)}, u32[]{:S(2)}, u32[]{:S(2)}) collective-permute-start(f32[384,128]{1,0:T(8,128)S(1)} %copy-done.9), channel_id=1, source_target_pairs={{0,2},{1,3},{2,0},{3,1},{4,6},{5,7},{6,4},{7,5},{8,10},{9,11},{10,... | collective-permute-start | bytes 589832 | tf_op jit(solution)/shard_map/ppermute | solution.py:628
  42.0 8.8 %collective-permute-start = (f32[384,128]{1,0:T(8,128)S(1)}, f32[384,128]{1,0:T(8,128)S(1)}, u32[]{:S(2)}, u32[]{:S(2)}) collective-permute-start(f32[384,128]{1,0:T(8,128)S(1)} %copy-done.9), channel_id=1, source_target_pairs={{0,3},{1,0},{2,1},{3,2},{4,7},{5,4},{6,5},{7,6},{8,11},{9,8},{10,9... | collective-permute-start | bytes 589832 | tf_op jit(solution)/shard_map/ppermute | solution.py:628
  45.8 3.0 %copy-start.21 = (bf16[384,144]{1,0:T(8,128)(2,1)}, bf16[384,144]{1,0:T(8,128)(2,1)S(1)}, u32[]{:S(2)}) copy-start(bf16[384,144]{1,0:T(8,128)(2,1)S(1)} %get-tuple-element.53.near_near) | copy-start | bytes 331780
  45.8 3.0 %copy-start.23 = (bf16[384,144]{1,0:T(8,128)(2,1)}, bf16[384,144]{1,0:T(8,128)(2,1)S(1)}, u32[]{:S(2)}) copy-start(bf16[384,144]{1,0:T(8,128)(2,1)S(1)} %get-tuple-element.54.far_far) | copy-start | bytes 331780
  45.8 0.7 copy-start.16
  56.8 0.7 copy-start.17
  61.3 6.7 %copy-start.5 = (bf16[512,144]{1,0:T(8,128)(2,1)S(1)}, bf16[512,144]{1,0:T(8,128)(2,1)}, u32[]{:S(2)}) copy-start(bf16[512,144]{1,0:T(8,128)(2,1)} %get-tuple-element.66.turned_near.rest_3_) | copy-start | bytes 442372
  61.3 6.7 %copy-start.6 = (bf16[512,144]{1,0:T(8,128)(2,1)S(1)}, bf16[512,144]{1,0:T(8,128)(2,1)}, u32[]{:S(2)}) copy-start(bf16[512,144]{1,0:T(8,128)(2,1)} %get-tuple-element.67.turned_far.rest_4_) | copy-start | bytes 442372
  61.3 6.7 %copy-start.20 = (f32[384,128]{1,0:T(8,128)S(1)}, f32[384,128]{1,0:T(8,128)}, u32[]{:S(2)}) copy-start(f32[384,128]{1,0:T(8,128)} %get-tuple-element.65.far_values) | copy-start | bytes 589828
  61.3 6.7 %copy-start.25 = (f32[384,128]{1,0:T(8,128)S(1)}, f32[384,128]{1,0:T(8,128)}, u32[]{:S(2)}) copy-start(f32[384,128]{1,0:T(8,128)} %get-tuple-element.64.near_values) | copy-start | bytes 589828
  61.3 57.1 %all-to-all-start.2 = ((f32[64,1,2304]{2,1,0:T(1,128)}), f32[64,1,2304]{2,1,0:T(1,128)S(1)}, u32[]{:S(2)}, u32[]{:S(2)}) async-start(f32[64,1,2304]{2,1,0:T(1,128)} %bitcast.13), calls=%async_computation.2 | async-start | bytes 1179648 | tf_op jit(solution)/shard_map/all_to_all | solution.py:575
  69.5 30.9 %copy-start = (f32[384,128]{1,0:T(8,128)S(1)}, f32[384,128]{1,0:T(8,128)}, u32[]{:S(2)}) copy-start(f32[384,128]{1,0:T(8,128)} %get-tuple-element.59.field_ref.refs_4_.rest_5_) | copy-start | bytes 589828
  69.5 30.9 %copy-start.22 = (bf16[384,144]{1,0:T(8,128)(2,1)S(1)}, bf16[384,144]{1,0:T(8,128)(2,1)}, u32[]{:S(2)}) copy-start(bf16[384,144]{1,0:T(8,128)(2,1)} %copy-done.21) | copy-start | bytes 331780
  69.5 30.9 %copy-start.24 = (bf16[384,144]{1,0:T(8,128)(2,1)S(1)}, bf16[384,144]{1,0:T(8,128)(2,1)}, u32[]{:S(2)}) copy-start(bf16[384,144]{1,0:T(8,128)(2,1)} %copy-done.23) | copy-start | bytes 331780
  96.4 9.0 %collective-permute-start.3 = (f32[512,128]{1,0:T(8,128)}, f32[512,128]{1,0:T(8,128)S(1)}, u32[]{:S(2)}, u32[]{:S(2)}) collective-permute-start(f32[512,128]{1,0:T(8,128)} %get-tuple-element.68), channel_id=1, source_target_pairs={{0,3},{1,0},{2,1},{3,2},{4,7},{5,4},{6,5},{7,6},{8,11},{9,8},{10,9... | collective-permute-start | bytes 786440 | tf_op jit(solution)/shard_map/ppermute | solution.py:628
  99.2 8.9 %collective-permute-start.4 = (f32[512,128]{1,0:T(8,128)}, f32[512,128]{1,0:T(8,128)S(1)}, u32[]{:S(2)}, u32[]{:S(2)}) collective-permute-start(f32[512,128]{1,0:T(8,128)} %get-tuple-element.69), channel_id=1, source_target_pairs={{0,2},{1,3},{2,0},{3,1},{4,6},{5,7},{6,4},{7,5},{8,10},{9,11},{10,... | collective-permute-start | bytes 786440 | tf_op jit(solution)/shard_map/ppermute | solution.py:628
  99.7 15.0 %collective-permute-start.5 = (f32[512,128]{1,0:T(8,128)}, f32[512,128]{1,0:T(8,128)S(1)}, u32[]{:S(2)}, u32[]{:S(2)}) collective-permute-start(f32[512,128]{1,0:T(8,128)} %get-tuple-element.70), channel_id=1, source_target_pairs={{0,1},{1,2},{2,3},{3,0},{4,5},{5,6},{6,7},{7,4},{8,9},{9,10},{10,1... | collective-permute-start | bytes 786440 | tf_op jit(solution)/shard_map/ppermute | solution.py:628
  102.7 15.8 %copy-start.10 = (f32[384,128]{1,0:T(8,128)S(1)}, f32[384,128]{1,0:T(8,128)}, u32[]{:S(2)}) copy-start(f32[384,128]{1,0:T(8,128)} %get-tuple-element.71.rest_2_) | copy-start | bytes 589828
  124.1 37.9 %all-to-all-start.3 = ((f32[32,8,128]{2,1,0:T(8,128)}), f32[32,8,128]{2,1,0:T(8,128)S(1)}, u32[]{:S(2)}, u32[]{:S(2)}) async-start(f32[32,8,128]{2,1,0:T(8,128)} %get-tuple-element.72), calls=%async_computation.3 | async-start | bytes 262144 | tf_op jit(solution)/shard_map/all_to_all | solution.py:684
  158.4 19.4 %collective-permute-start.6 = (f32[512,128]{1,0:T(8,128)}, f32[512,128]{1,0:T(8,128)S(1)}, u32[]{:S(2)}, u32[]{:S(2)}) collective-permute-start(f32[512,128]{1,0:T(8,128)} %get-tuple-element.76), channel_id=1, source_target_pairs={{0,3},{1,0},{2,1},{3,2},{4,7},{5,4},{6,5},{7,6},{8,11},{9,8},{10,9... | collective-permute-start | bytes 786440 | tf_op jit(solution)/shard_map/ppermute | solution.py:628
  160.9 16.8 %collective-permute-start.7 = (f32[512,128]{1,0:T(8,128)}, f32[512,128]{1,0:T(8,128)S(1)}, u32[]{:S(2)}, u32[]{:S(2)}) collective-permute-start(f32[512,128]{1,0:T(8,128)} %get-tuple-element.77), channel_id=1, source_target_pairs={{0,2},{1,3},{2,0},{3,1},{4,6},{5,7},{6,4},{7,5},{8,10},{9,11},{10,... | collective-permute-start | bytes 786440 | tf_op jit(solution)/shard_map/ppermute | solution.py:628
  161.5 16.3 %collective-permute-start.8 = (f32[512,128]{1,0:T(8,128)}, f32[512,128]{1,0:T(8,128)S(1)}, u32[]{:S(2)}, u32[]{:S(2)}) collective-permute-start(f32[512,128]{1,0:T(8,128)} %get-tuple-element.78), channel_id=1, source_target_pairs={{0,1},{1,2},{2,3},{3,0},{4,5},{5,6},{6,7},{7,4},{8,9},{9,10},{10,1... | collective-permute-start | bytes 786440 | tf_op jit(solution)/shard_map/ppermute | solution.py:628
  173.4 4.4 %copy-start.12 = (f32[128,128]{1,0:T(8,128)S(1)}, f32[128,128]{1,0:T(8,128)}, u32[]{:S(2)}) copy-start(f32[128,128]{1,0:T(8,128)} %get-tuple-element.83.refs_0_) | copy-start | bytes 196612
  173.4 4.4 %copy-start.13 = (f32[128,128]{1,0:T(8,128)S(1)}, f32[128,128]{1,0:T(8,128)}, u32[]{:S(2)}) copy-start(f32[128,128]{1,0:T(8,128)} %get-tuple-element.84.refs_4_) | copy-start | bytes 196612
  177.8 4.4 %copy-start.19 = (f32[384,128]{1,0:T(8,128)S(1)}, f32[384,128]{1,0:T(8,128)}, u32[]{:S(2)}) copy-start(f32[384,128]{1,0:T(8,128)} %get-tuple-element.74.field_ref.refs_8_) | copy-start | bytes 589828
  178.9 6.5 %collective-permute-start.9 = (f32[128,128]{1,0:T(8,128)}, f32[128,128]{1,0:T(8,128)S(1)}, u32[]{:S(2)}, u32[]{:S(2)}) collective-permute-start(f32[128,128]{1,0:T(8,128)} %get-tuple-element.86), channel_id=1, source_target_pairs={{0,3},{1,0},{2,1},{3,2},{4,7},{5,4},{6,5},{7,6},{8,11},{9,8},{10,9... | collective-permute-start | bytes 196616 | tf_op jit(solution)/shard_map/ppermute | solution.py:628
  181.0 4.8 %collective-permute-start.10 = (f32[128,128]{1,0:T(8,128)}, f32[128,128]{1,0:T(8,128)S(1)}, u32[]{:S(2)}, u32[]{:S(2)}) collective-permute-start(f32[128,128]{1,0:T(8,128)} %get-tuple-element.87), channel_id=1, source_target_pairs={{0,2},{1,3},{2,0},{3,1},{4,6},{5,7},{6,4},{7,5},{8,10},{9,11},{10,... | collective-permute-start | bytes 196616 | tf_op jit(solution)/shard_map/ppermute | solution.py:628
  182.2 4.8 %collective-permute-start.11 = (f32[128,128]{1,0:T(8,128)}, f32[128,128]{1,0:T(8,128)S(1)}, u32[]{:S(2)}, u32[]{:S(2)}) collective-permute-start(f32[128,128]{1,0:T(8,128)} %get-tuple-element.88), channel_id=1, source_target_pairs={{0,1},{1,2},{2,3},{3,0},{4,5},{5,6},{6,7},{7,4},{8,9},{9,10},{10,1... | collective-permute-start | bytes 196616 | tf_op jit(solution)/shard_map/ppermute | solution.py:628
  182.2 4.8 %copy-start.4 = (f32[512,128]{1,0:T(8,128)S(1)}, f32[512,128]{1,0:T(8,128)}, u32[]{:S(2)}) copy-start(f32[512,128]{1,0:T(8,128)} %get-tuple-element.81.bubble_ref) | copy-start | bytes 786436
  182.2 4.8 %copy-start.11 = (f32[128,128]{1,0:T(8,128)S(1)}, f32[128,128]{1,0:T(8,128)}, u32[]{:S(2)}) copy-start(f32[128,128]{1,0:T(8,128)} %get-tuple-element.85.refs_0_) | copy-start | bytes 196612

commit v6 on v5

--- a/solution.py
+++ b/solution.py
@@ -65,12 +65,15 @@
     return mask.astype(F32).astype(BF16)
 
 
+KIND, STIFF, NEAR, OWNER = [slice(i, i + 1) for i in range(4)]
+
+
 def owner_slots(owner, parts):
     count = owner.shape[1]
     owner_f = owner.astype(F32)
     same = (column(owner_f) == owner_f) & (iota((count, count), 0) < iota((count, count), 1))
     rank = jnp.sum(same.astype(F32), axis=0, keepdims=True).astype(jnp.int32)
-    to = iota((parts, count), 0) == owner
+    to = iota((parts, count), 0).astype(F32) == owner_f
     return [to & (rank == s) for s in range(SLOTS)]
 
 
@@ -129,7 +132,7 @@
 
 def condense_kernel(
     parts, kind_hbm, stiff_hbm, near_hbm, owner_hbm, far_hbm, load_hbm, inverse_hbm, coupling_hbm,
-    pay_ref, near_sum_ref, meta_ref,
+    pay_ref, near_sum_ref, meta_ref, where_ref,
     kind_ref, stiff_ref, near_ref, owner_ref, far_ref, load_ref, inverse_ref, coupling_ref, near_part, far_part, sems,
 ):
     copies = [
@@ -178,11 +181,13 @@
         value = jnp.sum(jnp.where(slots[s], near_row, 0.0), axis=1, keepdims=True)
         own = jnp.where(lane == s, value, own)
     pay_ref[pl.ds(9, parts, stride=10), :] = message
+    packed = [kind.astype(F32), stiff_ref[...], near.astype(F32), owner_ref[...].astype(F32)]
+    where_ref[...] = jnp.concatenate(packed + packed, axis=0)
     meta_ref[...] = own
 
 
 def tables_kernel(
-    kind_ref, stiff_ref, load_ref, inverse_ref, coupling_ref, block_ref,
+    where_ref, load_ref, inverse_ref, coupling_ref, block_ref,
     near_near, near_far, far_near, far_far, turned_near, turned_far, base_ref,
 ):
     dofs = block_ref.shape[1] // 2
@@ -201,8 +206,8 @@
         turned_far[at, :] = stacked_table(turned[:, dofs:])
         inverses.append(inverse_ref[t])
     left = stacked_table(jnp.concatenate(inverses, axis=0))
-    kind = kind_ref[...]
-    stiff = stiff_ref[...]
+    kind = where_ref[KIND]
+    stiff = where_ref[STIFF]
     kind2 = jnp.concatenate([kind, kind], axis=1)
     stiff2 = jnp.concatenate([stiff, stiff], axis=1)
     for k in range(0, CASES, 2):
@@ -228,9 +233,9 @@
     send_ports(field, asked_hot, port_onehot(meta_ref[...]), pay_ref)
 
 
-def component_products(table_ref, part_ref, kind_ref, stiff_ref, out_ref):
+def component_products(table_ref, part_ref, where_ref, out_ref):
     dofs = part_ref.shape[0] // CASES
-    kind, stiff = kind_ref[...], stiff_ref[...]
+    kind, stiff = where_ref[KIND], where_ref[STIFF]
     kind2 = jnp.concatenate([kind, kind], axis=1)
     stiff2 = jnp.concatenate([stiff, stiff], axis=1)
     for k in range(0, CASES, 2):
@@ -246,7 +251,7 @@
     tiles = slot_ref.shape[0]
     dofs = slot_ref.shape[1] // CASES
     spare = tiles * LANES - SLOTS * asked.shape[0]
-    kind = pad_lanes(stacked_rows(asked, SLOTS), spare).astype(jnp.int32)
+    kind = pad_lanes(stacked_rows(asked, SLOTS), spare)
     stiff = pad_lanes(stacked_rows(asked, 2 * SLOTS), spare)
     for k in range(CASES):
         values = jnp.concatenate(
@@ -274,25 +279,25 @@
 
 
 def inner_kernel(
-    field_ref, asked_ref, kind_ref, stiff_ref, near_ref, near_near, far_far,
+    field_ref, asked_ref, where_ref, near_near, far_far,
     inner_ref, near_values, near_part, slot_ref, slot_part,
 ):
     field, asked = field_ref[...], asked_ref[...]
-    near_hot, asked_hot = near_onehot(near_ref[...]), port_onehot(asked)
+    near_hot, asked_hot = near_onehot(where_ref[NEAR]), port_onehot(asked)
     tiles = slot_ref.shape[0]
     near_values[...] = pick_right(field, near_hot, NT)
     values = pick_right(field, wide_onehot(asked_hot, tiles), NT)
     for g in range(tiles):
         slot_ref[g] = values[:, g * LANES : (g + 1) * LANES]
-    component_products(near_near, near_values, kind_ref, stiff_ref, near_part)
+    component_products(near_near, near_values, where_ref, near_part)
     slot_products(far_far, slot_ref, asked, slot_part)
     inner_ref[...] = pick_right(near_part[...], near_hot, NN) + slots_to_ports(slot_part, asked_hot)
 
 
 def near_cross(parts, arrived_ref, pitch, kind_ref, stiff_ref, near_ref, owner_ref, near_far, far_values, near_part):
-    slots = onehot(jnp.concatenate(owner_slots(owner_ref[...], parts), axis=0))
+    slots = onehot(jnp.concatenate(owner_slots(where_ref[OWNER], parts), axis=0))
     far_values[...] = pick_right(get(arrived_ref, 0, pitch, 3), slots, TN)
-    component_products(near_far, far_values, kind_ref, stiff_ref, near_part)
+    component_products(near_far, far_values, where_ref, near_part)
     return pick_right(near_part[...], near_onehot(near_ref[...]), NN)
 
 
@@ -307,7 +312,7 @@
 
 
 def image_kernel(
-    parts, groups, last, arrived_ref, inner_hbm, asked_ref, kind_ref, stiff_ref, near_ref, owner_ref,
+    parts, groups, last, arrived_ref, inner_hbm, asked_ref, where_ref,
     near_far, far_near, *rest,
 ):
     if last:
@@ -320,9 +325,9 @@
     fetch.start()
     asked = asked_ref[...]
     asked_hot = port_onehot(asked)
-    slots = onehot(jnp.concatenate(owner_slots(owner_ref[...], parts), axis=0))
+    slots = onehot(jnp.concatenate(owner_slots(where_ref[OWNER], parts), axis=0))
     far_values[...] = pick_right(get(arrived_ref, 0, 18, 3), slots, TN)
-    component_products(near_far, far_values, kind_ref, stiff_ref, near_part)
+    component_products(near_far, far_values, where_ref, near_part)
     tiles = slot_ref.shape[0]
     values = jnp.transpose(get(arrived_ref, 9, 18, 3))
     values = pad_lanes(values, tiles * LANES - values.shape[1])
@@ -330,22 +335,22 @@
         slot_ref[g] = values[:, g * LANES : (g + 1) * LANES]
     slot_products(far_near, slot_ref, asked, slot_part)
     fetch.wait()
-    image = inner_ref[...] + pick_right(near_part[...], near_onehot(near_ref[...]), NN)
+    image = inner_ref[...] + pick_right(near_part[...], near_onehot(where_ref[NEAR]), NN)
     image = image + slots_to_ports(slot_part, asked_hot)
     image_ref[...] = image
     if last:
         gram = add_products(LANES, images, [image_ref], [3 * groups * CASES], case_ref[0], gram_ref[...])
         for p in range(copies_ref.shape[0]):
             copies_ref[p] = gram
-        turned_rows(near_values, far_values, kind_ref, turned_near, turned_far, turned_ref)
+        turned_rows(near_values, far_values, where_ref, turned_near, turned_far, turned_ref)
     else:
         send_ports(image, asked_hot, port_onehot(meta_ref[...]), pay_ref)
 
 
-def turned_rows(near_values, far_values, kind_ref, turned_near, turned_far, out_ref):
+def turned_rows(near_values, far_values, where_ref, turned_near, turned_far, out_ref):
     dofs = near_values.shape[0] // CASES
     modes = out_ref.shape[0] // CASES
-    kind = kind_ref[...]
+    kind = where_ref[KIND]
     kind2 = jnp.concatenate([kind, kind], axis=1)
     for k in range(0, CASES, 2):
         sums = 0.0
@@ -359,19 +364,34 @@
             out_ref[pl.ds(k + i, modes, stride=CASES), :] = result[:, i * LANES : (i + 1) * LANES]
 
 
+def turned_kernel(groups, case_ref, near_values, far_values, where_ref, turned_near, turned_far, *rest):
+    outs, out_ref = rest[:groups], rest[groups]
+    turned_rows(near_values, far_values, where_ref, turned_near, turned_far, out_ref)
+    part = outs[0].shape[0]
+    for h in range(groups):
+        at = pl.multiple_of(lax.rem(case_ref[0] + h, groups) * part, part)
+        outs[h][...] = out_ref[pl.ds(at, part), :]
+
+
 def messages_kernel(groups, case_ref, field_ref, turned_ref, own_ref, *rest):
-    messages, sems = rest[: groups - 1], rest[groups - 1]
+    messages, (field, turned, sems) = rest[: groups - 1], rest[groups - 1 :]
     rows = field_ref.shape[0]
     part = own_ref.shape[0]
+    fetches = [
+        pltpu.make_async_copy(turned_ref, turned, sems.at[0]),
+        pltpu.make_async_copy(field_ref, field, sems.at[groups]),
+    ]
+    for fetch in fetches:
+        fetch.start()
+    for fetch in fetches:
+        fetch.wait()
     copies = []
     for h in range(groups):
         at = pl.multiple_of(lax.rem(case_ref[0] + h, groups) * part, part)
         target = messages[h - 1].at[pl.ds(rows, part), :] if h else own_ref
-        copies.append(pltpu.make_async_copy(turned_ref.at[pl.ds(at, part), :], target, sems.at[h]))
+        copies.append(pltpu.make_async_copy(turned.at[pl.ds(at, part), :], target, sems.at[h]))
         if h:
-            copies.append(
-                pltpu.make_async_copy(field_ref, messages[h - 1].at[pl.ds(0, rows), :], sems.at[groups + h])
-            )
+            copies.append(pltpu.make_async_copy(field, messages[h - 1].at[pl.ds(0, rows), :], sems.at[groups + h]))
     for copy in copies:
         copy.start()
     for copy in copies:
@@ -458,7 +478,17 @@
     return 0.5 * (m + jnp.transpose(m))
 
 
-def solve_kernel(groups, case_ref, gram_ref, coef, coef_rows, turned_coef):
+def solve_kernel(groups, case_ref, gram_ref, *rest):
+    pieces, (coef, *outs), (held, coef_rows, turned_coef, sems) = (
+        rest[: 2 * groups], rest[2 * groups : 3 * groups + 1], rest[3 * groups + 1 :]
+    )
+    part = held.shape[1]
+    fetches = [
+        pltpu.make_async_copy(piece.at[pl.ds(piece.shape[0] - part, part), :], held.at[i], sems.at[i])
+        for i, piece in enumerate(pieces)
+    ]
+    for fetch in fetches:
+        fetch.start()
     n = groups * CASES
     total = gram_ref[0]
     for p in range(1, gram_ref.shape[0]):
@@ -481,24 +511,14 @@
             if q == 0:
                 for j in range(n):
                     coef[h * n + j] = jnp.broadcast_to(mine[:, j : j + 1], (CASES, LANES))
-
-
-def bubble_kernel(groups, rows, coef_ref, *refs):
-    turned0, turned1, outs = refs[:groups], refs[groups : 2 * groups], refs[2 * groups :]
-    n = groups * CASES
-    part = turned0[0].shape[0]
-    coef = jnp.concatenate([coef_ref[:, :n], coef_ref[:, LANES : LANES + n]], axis=1)
-    left = stacked_table(coef)
+    for fetch in fetches:
+        fetch.wait()
+    left = stacked_table(jnp.concatenate([coef_rows[:, :n], coef_rows[:, LANES : LANES + n]], axis=1))
     for m in range(0, part // CASES, 2):
-        values = []
-        for i in range(2):
-            at = (m + i) * CASES
-            pieces = [
-                ref[at + shift : at + shift + CASES, :]
-                for turned in (turned0, turned1)
-                for ref, shift in zip(turned, [0] + [rows] * (groups - 1))
-            ]
-            values.append(jnp.concatenate(pieces, axis=0))
+        values = [
+            jnp.concatenate([held[i, at : at + CASES, :] for i in range(2 * groups)], axis=0)
+            for at in (m * CASES, (m + 1) * CASES)
+        ]
         result = dot(left, stacked_values(jnp.concatenate(values, axis=1)))
         for i in range(2):
             for h in range(groups):
@@ -543,7 +563,7 @@
         out_ref[at, :] = bubble_ref[at, :] - parts[h][...]
 
 
-def call(kernel, outs, scratch=(), name=None, flops=0, smem=(), hbm=(), sems=0, limit=12):
+def call(kernel, outs, scratch=(), name=None, flops=0, smem=(), hbm=(), anywhere=(), sems=0, limit=12):
     results = [(pltpu.HBM if far else jax.ShapeDtypeStruct)(shape, dtype) for shape, dtype, far in outs]
     vmem = pl.BlockSpec(memory_space=pltpu.VMEM)
     far_spec = pl.BlockSpec(memory_space=pltpu.HBM)
@@ -551,7 +571,7 @@
 
     def run(*args):
         specs = [
-            pl.BlockSpec(memory_space=pltpu.SMEM) if i in smem else far_spec if i in hbm else vmem
+            pl.BlockSpec(memory_space=pltpu.SMEM) if i in smem else far_spec if i in hbm else pl.BlockSpec(memory_space=pl.ANY) if i in anywhere else vmem
             for i in range(len(args))
         ]
         moved = sum(a.size * a.dtype.itemsize for a in args)
@@ -597,9 +617,9 @@
     meta_of = ((parts, LANES), F32, False)
     bubble_of = ((bubbles, comps), F32, True)
     given = (kind, stiff, near, owner, far, loads, bubble_inverse, coupling)
-    pay, near_sum, meta = call(
+    pay, near_sum, meta, where = call(
         functools.partial(condense_kernel, parts),
-        [((parts * 10, LANES), F32, False), field_of, meta_of],
+        [((parts * 10, LANES), F32, False), field_of, meta_of, ((8, LANES), F32, False)],
         [(a.shape, a.dtype) for a in given] + [(rows, comps)] * 2,
         "condense",
         hbm=range(len(given)),
@@ -610,7 +630,7 @@
         [((KINDS * dofs, 3 * dofs), BF16, False)] * 4 + [((KINDS * modes, 3 * dofs), BF16, True)] * 2 + [bubble_of],
         name="tables",
         flops=10**9,
-    )(kind, stiff, loads, bubble_inverse, coupling, port_block)
+    )(where, loads, bubble_inverse, coupling, port_block)
     base, pay, asked = call(
         functools.partial(rhs_kernel, parts),
         [field_of, ((parts * 18, LANES), F32, False), meta_of],
@@ -621,7 +641,6 @@
     part = bubbles // groups
     part_of = ((part, comps), F32, True)
     slot_scratch = [(slot_tiles, rows, LANES)] * 2
-    where = (kind, stiff, near, owner)
 
     def to_cases(messages):
         backward = [
@@ -632,7 +651,7 @@
 
     def inner(field):
         return call(inner_kernel, [field_of] * 2, [(rows, comps)] + slot_scratch, "inner", flops=10**9)(
-            field, asked, kind, stiff, near, near_near, far_far
+            field, asked, where, near_near, far_far
         )
 
     arrived = exchange(pay, parts)
@@ -641,66 +660,71 @@
     arrived, *base_all = lax.optimization_barrier((arrived, *base_all))
     image, base_far, pay = call(
         functools.partial(image_kernel, parts, groups, False),
-        [field_of] * 2 + [((parts * 18, LANES), F32, False)],
+        [((rows, ports), F32, False)] * 2 + [((parts * 18, LANES), F32, False)],
         [(rows, comps)] + slot_scratch + [(rows, ports)],
         "image",
         hbm=(1,),
         sems=1,
-    )(arrived, base_inner, asked, *where, near_far, far_near, meta)
+    )(arrived, base_inner, asked, where, near_far, far_near, meta)
     arrived = exchange(pay, parts)
-    def messages(field, turned):
-        own, *others = call(
-            functools.partial(messages_kernel, groups),
-            [part_of] + [((rows + part, comps), F32, True)] * (groups - 1),
-            name="messages",
-            flops=10**9,
-            smem=(0,),
-            hbm=(1, 2),
-            sems=2 * groups,
-        )(case, field, turned)
-        return own, to_cases(others)
-
-    (turned0,) = call(turned_rows, [bubble_of], name="turned", flops=10**9)(
-        base_near, base_far, kind, turned_near, turned_far
-    )
-    turned0, both0 = messages(image, turned0)
+    image_all = to_cases([image] * (groups - 1))
+    turned0, *messages = call(
+        functools.partial(turned_kernel, groups),
+        [part_of] * groups,
+        [(bubbles, comps)],
+        "turned",
+        flops=10**9,
+        smem=(0,),
+    )(case, base_near, base_far, where, turned_near, turned_far)
+    turned0_all = to_cases(messages)
     image_inner, image_near = inner(image)
     (gram,) = call(functools.partial(gram_kernel, groups), [((cases, LANES), F32, False)], name="gram", smem=(0,))(
-        case, base, *base_all, image, *both0
-    )
+        case, base, *base_all, image, *image_all
+    )
+    arrived, *turned0_all = lax.optimization_barrier((arrived, *turned0_all))
     minor = lax.axis_size("py")
     second, copies, turned1 = call(
         functools.partial(image_kernel, parts, groups, True),
         [field_of, ((groups * minor, cases, LANES), F32, True), bubble_of],
         [(rows, comps)] + slot_scratch + [(rows, comps), (rows, ports)],
         "second",
-        smem=(9,),
+        smem=(6,),
         hbm=(1,),
         sems=1,
     )(
-        arrived, image_inner, asked, *where, near_far, far_near, case, gram, image_near, turned_near, turned_far,
-        image, *both0,
+        arrived, image_inner, asked, where, near_far, far_near, case, gram, image_near, turned_near, turned_far,
+        image, *image_all,
     )
     copies = lax.all_to_all(copies, ("case", "py"), split_axis=0, concat_axis=0)
-    turned1, both1 = messages(second, turned1)
+    turned1, *messages = call(
+        functools.partial(messages_kernel, groups),
+        [part_of] + [((rows + part, comps), F32, True)] * (groups - 1),
+        [(rows, ports), (bubbles, comps)],
+        "messages",
+        flops=10**9,
+        smem=(0,),
+        hbm=(1, 2),
+        sems=2 * groups,
+    )(case, second, turned1)
+    both1 = to_cases(messages)
     (copies,) = call(sum_kernel, [((parts // minor, groups * cases, LANES), F32, False)], name="sum")(
         copies.reshape(groups, minor, cases, LANES)
     )
     copies = lax.all_to_all(copies, "px", split_axis=0, concat_axis=0)
-    coef, coef_rows = call(
+    pieces = [turned0, *turned0_all, turned1, *both1]
+    coef, own, *messages = call(
         functools.partial(solve_kernel, groups),
-        [((2 * groups * cases, cases, LANES), F32, False), ((groups * cases, 2 * LANES), F32, False)],
-        [(2, groups * cases, LANES)],
+        [((2 * groups * cases, cases, LANES), F32, False)] + [((part, comps), F32, False)] * groups,
+        [(2 * groups, part, comps), (groups * cases, 2 * LANES), (2, groups * cases, LANES)],
         "solve",
         smem=(0,),
-    )(case, copies)
-    own, *messages = call(
-        functools.partial(bubble_kernel, groups, rows), [part_of] * groups, name="bubble"
-    )(coef_rows, turned0, *both0, turned1, *both1)
+        anywhere=range(2, 2 + len(pieces)),
+        sems=len(pieces),
+    )(case, copies, *pieces)
     back = to_cases(messages)
     x, residual = call(
         functools.partial(ports_kernel, groups), [field_of, field_of], name="ports", flops=10**9
-    )(coef, base, *base_all, image, *both0, second, *both1)
+    )(coef, base, *base_all, image, *image_all, second, *both1)
     (bubble,) = call(functools.partial(join_kernel, groups), [bubble_of], name="join", smem=(0,))(
         case, bubble_base, own, *back
     )

time: 189 us -> 136 us (0.72)
  Pallas kernels: 90 us -> 38.8 us
  blocking collectives: 37.7 us -> 26.4 us
  starting transfers between devices: 36 us -> 45.9 us
    pallas_call x16 -> x14, Pallas kernels: 90 us -> 38.8 us  [run(): pl.pallas_call(kernel, out_shape=results, in_specs=specs, out_specs=[far_...]
    all_to_all x1 -> x0, blocking collectives: 11.3 us -> none  [local(): copies = lax.all_to_all(copies, 'px', split_axis=0, concat_axis=0)]
    all_to_all x0 -> x1, starting transfers between devices: none -> 7.9 us  [local(): copies = lax.all_to_all(copies, 'px', split_axis=0, concat_axis=0)]
    ppermute x12 -> x15, waiting for transfers between devices: 15.7 us -> 8.49 us  [to_cases(): lax.ppermute(message, 'case', [(k, (k + h) % groups) for k in range(group...]
    all_to_all x1, waiting for transfers between devices: 0.01 us -> 3.52 us  [local(): copies = lax.all_to_all(copies, ('case', 'py'), split_axis=0, concat_axis=0)]
    all_to_all x0 -> x1, waiting for transfers between devices: none -> 2.53 us  [local(): copies = lax.all_to_all(copies, 'px', split_axis=0, concat_axis=0)]
    all_to_all x2, waiting for transfers between devices: 6.03 us -> 8.4 us  [exchange(): lax.all_to_all(rows.reshape(parts, 1, -1), PLANE, split_axis=0, concat_ax...]
    ppermute x12 -> x15, starting transfers between devices: 15.8 us -> 17.8 us  [to_cases(): lax.ppermute(message, 'case', [(k, (k + h) % groups) for k in range(group...]
  transfers between devices with their start and end apart: 15 -> 19, of which waited for: 7 -> 9; matrix products, arithmetic and copies ran while one was open for 0% -> 0% of each run, Pallas kernels for 39% -> 14%
where the time goes in v6:
time: 136 us; the launch traced here: 135 us
  starting transfers between devices  45.9 us (34%)
  Pallas kernels  38.8 us (29%)
  blocking collectives  26.4 us (19%)
  waiting for transfers between devices  22.9 us (17%)
    pallas_call x14, Pallas kernels, run(): pl.pallas_call(kernel, out_shape=results, in_specs=specs, out_specs=[far_...  38.8 us
    all_to_all x1, blocking collectives, exchange(): lax.all_to_all(rows.reshape(parts, 1, -1), PLANE, split_axis=0, concat_ax...  26.4 us
    ppermute x15, starting transfers between devices, to_cases(): lax.ppermute(message, 'case', [(k, (k + h) % groups) for k in range(group...  17.8 us
    all_to_all x2, starting transfers between devices, exchange(): lax.all_to_all(rows.reshape(parts, 1, -1), PLANE, split_axis=0, concat_ax...  13 us
    ppermute x15, waiting for transfers between devices, to_cases(): lax.ppermute(message, 'case', [(k, (k + h) % groups) for k in range(group...  8.49 us
    all_to_all x2, waiting for transfers between devices, exchange(): lax.all_to_all(rows.reshape(parts, 1, -1), PLANE, split_axis=0, concat_ax...  8.4 us
    all_to_all x1, starting transfers between devices, local(): copies = lax.all_to_all(copies, 'px', split_axis=0, concat_axis=0)  7.9 us
    all_to_all x1, starting transfers between devices, local(): copies = lax.all_to_all(copies, ('case', 'py'), split_axis=0, concat_axis=0)  7.22 us
  transfers between devices with their start and end apart: 19, of which 9 were waited for; matrix products, arithmetic and copies ran while one was open for 0% of the time, Pallas kernels for 14%

profile of v6, /device:TPU:1, one launch (start us, length us, event | category | flops | bytes accessed | tf_op | source)
XLA Modules:
  0.0 135.0 jit_solution(14887288765605640958)
XLA Ops:
  0.6 3.5 %condense.1 = (f32[640,128]{1,0:T(8,128)S(1)}, f32[384,128]{1,0:T(8,128)}, f32[64,128]{1,0:T(8,128)S(1)}, f32[8,128]{1,0:T(8,128)S(1)}) custom-call(s32[1,128]{1,0:T(1,128)} %bitcast.30, f32[1,128]{1,0:T(1,128)} %bitcast.31, s32[1,128]{1,0:T(1,128)} %bitcast.32, s32[1,128]{1,0:T(1,128)} %bitcast.33, s32[1,128]{1,0:T(1,128)} %bitcast.34, ...), custom_call_target="tpu_custom_call" | custom-call | bytes 592384 | tf_op jit(solution)/shard_map/condense/pallas_call | solution.py:579
  4.1 0.0 copy-start.7
  4.1 0.0 copy-start.8
  4.1 26.4 %all_to_all.25 = f32[64,1,1280]{2,1,0:T(1,128)S(1)} all-to-all(f32[64,1,1280]{2,1,0:T(1,128)S(1)} %bitcast.23), channel_id=1, replica_groups=mesh['px'=8,'py'=8,'case'=4] {'px','py'}, dimensions={0} | all-to-all | bytes 655360 | tf_op jit(solution)/shard_map/all_to_all | solution.py:595
  30.5 1.4 %rhs.1 = (f32[384,128]{1,0:T(8,128)}, f32[1152,128]{1,0:T(8,128)}, f32[64,128]{1,0:T(8,128)S(1)}) custom-call(f32[640,128]{1,0:T(8,128)S(1)} %bitcast.21, f32[384,128]{1,0:T(8,128)S(1)} %copy-done.8, f32[384,128]{1,0:T(8,128)S(1)} %bitcast.28, f32[64,128]{1,0:T(8,128)S(1)} %get-tuple-element.52.meta_ref.rest_0_), custom_call_target="tpu_custom_call" | custom-call | bytes 753664 | tf_op jit(solution)/shard_map/rhs/pallas_call | solution.py:579
  31.9 6.3 %all-to-all-start.1 = ((f32[64,1,2304]{2,1,0:T(1,128)}), f32[64,1,2304]{2,1,0:T(1,128)S(1)}, u32[]{:S(2)}, u32[]{:S(2)}) async-start(f32[64,1,2304]{2,1,0:T(1,128)} %bitcast.11), calls=%async_computation.1 | async-start | bytes 1179648 | tf_op jit(solution)/shard_map/all_to_all | solution.py:595
  38.3 1.3 collective-permute-start.2
  39.5 2.4 %collective-permute-start.1 = (f32[384,128]{1,0:T(8,128)S(1)}, f32[384,128]{1,0:T(8,128)S(1)}, u32[]{:S(2)}, u32[]{:S(2)}) collective-permute-start(f32[384,128]{1,0:T(8,128)S(1)} %copy-done.9), channel_id=1, source_target_pairs={{0,2},{1,3},{2,0},{3,1},{4,6},{5,7},{6,4},{7,5},{8,10},{9,11},{10,... | collective-permute-start | bytes 589832 | tf_op jit(solution)/shard_map/ppermute | solution.py:647
  42.0 1.2 collective-permute-start
  43.2 2.6 %tables.1 = (bf16[384,144]{1,0:T(8,128)(2,1)S(1)}, bf16[384,144]{1,0:T(8,128)(2,1)S(1)}, bf16[384,144]{1,0:T(8,128)(2,1)S(1)}, bf16[384,144]{1,0:T(8,128)(2,1)S(...) custom-call(f32[8,128]{1,0:T(8,128)S(1)} %get-tuple-element.57.where_ref, ...), custom_call_target="tpu_custom_call" | custom-call | flops 1000000000 | bytes 888832 | tf_op jit(solution)/shard_map/tables/pallas_call | solution.py:579
  45.8 2.3 %inner.2 = (f32[384,128]{1,0:T(8,128)}, f32[384,128]{1,0:T(8,128)}) custom-call(f32[384,128]{1,0:T(8,128)S(1)} %copy-done.9, f32[64,128]{1,0:T(8,128)S(1)} %get-tuple-element.56.asked_ref, f32[8,128]{1,0:T(8,128)S(1)} %get-tuple-element.57.where_ref, bf16[384,144]{1,0:T(8,128)(2,1)S(1)} %get-tuple-element.58.near_near, ...), custom_call_target="tpu_custom_call" | custom-call | flops 1000000000 | bytes 454656 | tf_op jit(solution)/shard_map/inner/pallas_call | solution.py:579
  48.1 0.0 collective-permute-done.2.refs_3_
  48.1 2.6 %collective-permute-done.1.refs_2_ = f32[384,128]{1,0:T(8,128)S(1)} collective-permute-done((f32[384,128]{1,0:T(8,128)S(1)}, f32[384,128]{1,0:T(8,128)S(1)}, u32[]{:S(2)}, u32[]{:S(2)}) %collective-permute-start.1) | collective-permute-done | bytes 196640 | tf_op jit(solution)/shard_map/ppermute | solution.py:647
  50.8 6.0 %all-to-all-done.1 = f32[64,1,2304]{2,1,0:T(1,128)S(1)} async-done(((f32[64,1,2304]{2,1,0:T(1,128)}), f32[64,1,2304]{2,1,0:T(1,128)S(1)}, u32[]{:S(2)}, u32[]{:S(2)}) %all-to-all-start.1) | async-done | bytes 589856 | tf_op jit(solution)/shard_map/all_to_all | solution.py:595
  56.8 3.8 %image.1 = (f32[384,128]{1,0:T(8,128)S(1)}, f32[384,128]{1,0:T(8,128)S(1)}, f32[1152,128]{1,0:T(8,128)}) custom-call(f32[1152,128]{1,0:T(8,128)S(1)} %bitcast.19, f32[384,128]{1,0:T(8,128)} %get-tuple-element.60.inner_hbm, f32[64,128]{1,0:T(8,128)S(1)} %get-tuple-element.56.asked_ref, f32[8,128]{1,0:T(8,128)S(1)} %get-tuple-element.57.where_ref, ...), custom_call_target="tpu_custom_call" | custom-call | bytes 1077248 | tf_op jit(solution)/shard_map/image/pallas_call | solution.py:579
  60.6 0.0 copy-start
  60.6 0.0 copy-start.18
  60.6 6.7 %all-to-all-start.2 = ((f32[64,1,2304]{2,1,0:T(1,128)}), f32[64,1,2304]{2,1,0:T(1,128)S(1)}, u32[]{:S(2)}, u32[]{:S(2)}) async-start(f32[64,1,2304]{2,1,0:T(1,128)} %bitcast.13), calls=%async_computation.2 | async-start | bytes 1179648 | tf_op jit(solution)/shard_map/all_to_all | solution.py:595
  67.3 1.3 collective-permute-start.8
  68.6 2.4 %collective-permute-start.7 = (f32[384,128]{1,0:T(8,128)S(1)}, f32[384,128]{1,0:T(8,128)S(1)}, u32[]{:S(2)}, u32[]{:S(2)}) collective-permute-start(f32[384,128]{1,0:T(8,128)S(1)} %get-tuple-element.72.field_ref.refs_4_.rest_5_), channel_id=1, source_target_pairs={{0,2},{1,3},{2,0},{3,1},{4,6},{5,7},{6,4},{7,5},{8,10},{9,11},{10,... | collective-permute-start | bytes 589832 | tf_op jit(solution)/shard_map/ppermute | solution.py:647
  71.0 1.2 collective-permute-start.6
  72.2 1.4 %turned.1 = (f32[128,128]{1,0:T(8,128)}, f32[128,128]{1,0:T(8,128)}, f32[128,128]{1,0:T(8,128)}, f32[128,128]{1,0:T(8,128)}) custom-call(s32[1]{0:T(128)} %bitcast.case_ref.rest_0_, f32[384,128]{1,0:T(8,128)S(1)} %copy-done.18, f32[384,128]{1,0:T(8,128)S(1)} %get-tuple-element.65.far_values, f32[8,128]{1,0:T(8,128)S(1)} %get-tuple-element.57.where_ref, ...), custom_call_target="tpu_custom_call" | custom-call | flops 1000000000 | bytes 692228 | tf_op jit(solution)/shard_map/turned/pallas_call | solution.py:579
  73.6 0.0 collective-permute-start.3
  73.7 2.1 %collective-permute-start.4 = (f32[128,128]{1,0:T(8,128)}, f32[128,128]{1,0:T(8,128)S(1)}, u32[]{:S(2)}, u32[]{:S(2)}) collective-permute-start(f32[128,128]{1,0:T(8,128)} %get-tuple-element.69), channel_id=1, source_target_pairs={{0,2},{1,3},{2,0},{3,1},{4,6},{5,7},{6,4},{7,5},{8,10},{9,11},{10,... | collective-permute-start | bytes 196616 | tf_op jit(solution)/shard_map/ppermute | solution.py:647
  75.7 0.0 collective-permute-done.8.refs_7_.rest_8_
  75.7 0.0 collective-permute-start.5
  75.8 2.3 %inner.3 = (f32[384,128]{1,0:T(8,128)}, f32[384,128]{1,0:T(8,128)}) custom-call(f32[384,128]{1,0:T(8,128)S(1)} %get-tuple-element.72.field_ref.refs_4_.rest_5_, f32[64,128]{1,0:T(8,128)S(1)} %get-tuple-element.56.asked_ref, f32[8,128]{1,0:T(8,128)S(1)} %get-tuple-element.57.where_ref, bf16[384,144]{1,0:T(8,128)(2,1)S(1)} %copy-done.15, ...), custom_call_target="tpu_custom_call" | custom-call | flops 1000000000 | bytes 454656 | tf_op jit(solution)/shard_map/inner/pallas_call | solution.py:579
  78.1 1.7 %collective-permute-done.7.refs_6_.rest_7_ = f32[384,128]{1,0:T(8,128)S(1)} collective-permute-done((f32[384,128]{1,0:T(8,128)S(1)}, f32[384,128]{1,0:T(8,128)S(1)}, u32[]{:S(2)}, u32[]{:S(2)}) %collective-permute-start.7) | collective-permute-done | bytes 196640 | tf_op jit(solution)/shard_map/ppermute | solution.py:647
  79.8 3.7 %gram.1.rest_1_ = f32[8,128]{1,0:T(8,128)S(1)} custom-call(s32[1]{0:T(128)} %bitcast.case_ref.rest_0_, f32[384,128]{1,0:T(8,128)S(1)} %copy-done.9, f32[384,128]{1,0:T(8,128)S(1)} %collective-permute-done.refs_1_, f32[384,128]{1,0:T(8,128)S(1)} %collective-permute-done.1.refs_2_, f32[384,128]{1,0:T(8,128)S(1)} %collective-permute-done.2.refs_3_, ...), custom_call_target="tpu_custom_call" | custom-call | bytes 1572868 | tf_op jit(solution)/shard_map/gram/pallas_call | solution.py:579
  83.5 2.4 %all-to-all-done.2 = f32[64,1,2304]{2,1,0:T(1,128)S(1)} async-done(((f32[64,1,2304]{2,1,0:T(1,128)}), f32[64,1,2304]{2,1,0:T(1,128)S(1)}, u32[]{:S(2)}, u32[]{:S(2)}) %all-to-all-start.2) | async-done | bytes 589856 | tf_op jit(solution)/shard_map/all_to_all | solution.py:595
  85.9 5.7 %second.1 = (f32[384,128]{1,0:T(8,128)}, f32[32,8,128]{2,1,0:T(8,128)}, f32[512,128]{1,0:T(8,128)}) custom-call(f32[1152,128]{1,0:T(8,128)S(1)} %bitcast.20, f32[384,128]{1,0:T(8,128)} %get-tuple-element.73.inner_hbm, f32[64,128]{1,0:T(8,128)S(1)} %get-tuple-element.56.asked_ref, f32[8,128]{1,0:T(8,128)S(1)} %get-tuple-element.57.where_ref, ...), custom_call_target="tpu_custom_call" | custom-call | bytes 2326532 | tf_op jit(solution)/shard_map/second/pallas_call | solution.py:579
  91.6 7.2 %all-to-all-start.3 = ((f32[32,8,128]{2,1,0:T(8,128)}), f32[32,8,128]{2,1,0:T(8,128)S(1)}, u32[]{:S(2)}, u32[]{:S(2)}) async-start(f32[32,8,128]{2,1,0:T(8,128)} %get-tuple-element.78), calls=%async_computation.3 | async-start | bytes 262144 | tf_op jit(solution)/shard_map/all_to_all | solution.py:698
  98.8 2.0 %messages.1 = (f32[128,128]{1,0:T(8,128)}, f32[512,128]{1,0:T(8,128)}, f32[512,128]{1,0:T(8,128)}, f32[512,128]{1,0:T(8,128)}) custom-call(s32[1]{0:T(128)} %bitcast.case_ref.rest_0_, f32[384,128]{1,0:T(8,128)} %get-tuple-element.83.field_ref.refs_8_, f32[512,128]{1,0:T(8,128)} %get-tuple-element.84.turned_ref), custom_call_target="tpu_custom_call" | custom-call | flops 1000000000 | bytes 458756 | tf_op jit(solution)/shard_map/messages/pallas_call | solution.py:579
  100.8 2.6 %collective-permute-start.9 = (f32[512,128]{1,0:T(8,128)}, f32[512,128]{1,0:T(8,128)S(1)}, u32[]{:S(2)}, u32[]{:S(2)}) collective-permute-start(f32[512,128]{1,0:T(8,128)} %get-tuple-element.86), channel_id=1, source_target_pairs={{0,3},{1,0},{2,1},{3,2},{4,7},{5,4},{6,5},{7,6},{8,11},{9,8},{10,9... | collective-permute-start | bytes 786440 | tf_op jit(solution)/shard_map/ppermute | solution.py:647
  103.4 0.5 collective-permute-start.10
  103.9 0.6 collective-permute-start.11
  104.5 3.5 %all-to-all-done.3 = f32[32,8,128]{2,1,0:T(8,128)S(1)} async-done(((f32[32,8,128]{2,1,0:T(8,128)}), f32[32,8,128]{2,1,0:T(8,128)S(1)}, u32[]{:S(2)}, u32[]{:S(2)}) %all-to-all-start.3) | async-done | bytes 131104 | tf_op jit(solution)/shard_map/all_to_all | solution.py:698
  108.0 0.7 sum.1
  108.7 7.9 %all-to-all-start.4 = ((f32[8,32,128]{2,1,0:T(8,128)}), f32[8,32,128]{2,1,0:T(8,128)S(1)}, u32[]{:S(2)}, u32[]{:S(2)}) async-start(f32[8,32,128]{2,1,0:T(8,128)} %sum.1), calls=%async_computation.4 | async-start | bytes 262144 | tf_op jit(solution)/shard_map/all_to_all | solution.py:713
  116.6 2.7 %collective-permute-done.11.rest_7_.refs_11_ = f32[512,128]{1,0:T(8,128)S(1)} collective-permute-done((f32[512,128]{1,0:T(8,128)}, f32[512,128]{1,0:T(8,128)S(1)}, u32[]{:S(2)}, u32[]{:S(2)}) %collective-permute-start.11) | collective-permute-done | bytes 262176 | tf_op jit(solution)/shard_map/ppermute | solution.py:647
  119.3 2.5 %all-to-all-done.4.gram_ref = f32[8,32,128]{2,1,0:T(8,128)S(1)} async-done(((f32[8,32,128]{2,1,0:T(8,128)}), f32[8,32,128]{2,1,0:T(8,128)S(1)}, u32[]{:S(2)}, u32[]{:S(2)}) %all-to-all-start.4) | async-done | bytes 131104 | tf_op jit(solution)/shard_map/all_to_all | solution.py:713
  121.9 5.5 %solve.1 = (f32[64,8,128]{2,1,0:T(8,128)S(1)}, f32[128,128]{1,0:T(8,128)S(1)}, f32[128,128]{1,0:T(8,128)S(1)}, f32[128,128]{1,0:T(8,128)S(1)}, f32[128,128]{1,0:T(8,128)S(1)}) custom-call(s32[1]{0:T(128)} %bitcast.case_ref.rest_0_, f32[8,32,128]{2,1,0:T(8,128)S(1)} %all-to-all-done.4.gram_ref, f32[128,128]{1,0:T(8,128)S(1)} %copy-done.10, ...), custom_call_target="tpu_custom_call" | custom-call | bytes 1245188 | tf_op jit(solution)/shard_map/solve/pallas_call | solution.py:579
  127.3 1.0 collective-permute-start.12
  128.3 1.2 collective-permute-start.13
  129.6 3.2 %ports.1 = (f32[384,128]{1,0:T(8,128)}, f32[384,128]{1,0:T(8,128)}) custom-call(f32[64,8,128]{2,1,0:T(8,128)S(1)} %get-tuple-element.89.coef, f32[384,128]{1,0:T(8,128)S(1)} %copy-done.9, f32[384,128]{1,0:T(8,128)S(1)} %collective-permute-done.refs_1_, f32[384,128]{1,0:T(8,128)S(1)} %collective-permute-done.1.refs_2_, ...), custom_call_target="tpu_custom_call" | custom-call | flops 1000000000 | bytes 2818048 | tf_op jit(solution)/shard_map/ports/pallas_call | solution.py:579
  132.8 0.1 collective-permute-done.13.refs_2_
  133.0 1.3 collective-permute-done.14.refs_3_
  134.2 0.7 join.1
  (43 shorter events, 0.1 us)
Async XLA Ops:
  4.1 26.4 %copy-start.7 = (f32[48,8,128]{2,1,0:T(8,128)S(1)}, f32[48,8,128]{2,1,0:T(8,128)}, u32[]{:S(2)}) copy-start(f32[48,8,128]{2,1,0:T(8,128)} %param.16) | copy-start | bytes 589828
  4.1 26.4 %copy-start.8 = (f32[384,128]{1,0:T(8,128)S(1)}, f32[384,128]{1,0:T(8,128)}, u32[]{:S(2)}) copy-start(f32[384,128]{1,0:T(8,128)} %get-tuple-element.51.near_sum_ref) | copy-start | bytes 589828
  30.5 12.6 %copy-start.12 = (f32[8,96,96]{2,1,0:T(8,128)S(1)}, f32[8,96,96]{2,1,0:T(8,128)}, u32[]{:S(2)}) copy-start(f32[8,96,96]{2,1,0:T(8,128)} %block_ref.1) | copy-start | bytes 884740
  31.9 6.3 %copy-start.9 = (f32[384,128]{1,0:T(8,128)S(1)}, f32[384,128]{1,0:T(8,128)}, u32[]{:S(2)}) copy-start(f32[384,128]{1,0:T(8,128)} %get-tuple-element.54.field_ref.refs_0_) | copy-start | bytes 589828
  31.9 11.3 %copy-start.2 = (f32[64,8,128]{2,1,0:T(8,128)S(1)}, f32[64,8,128]{2,1,0:T(8,128)}, u32[]{:S(2)}) copy-start(f32[64,8,128]{2,1,0:T(8,128)} %param.15) | copy-start | bytes 786436
  31.9 11.3 %copy-start.3 = (f32[8,64,64]{2,1,0:T(8,128)S(1)}, f32[8,64,64]{2,1,0:T(8,128)}, u32[]{:S(2)}) copy-start(f32[8,64,64]{2,1,0:T(8,128)} %inverse_ref.1) | copy-start | bytes 393220
  31.9 11.3 %copy-start.4 = (f32[8,96,64]{1,2,0:T(8,128)S(1)}, f32[8,96,64]{1,2,0:T(8,128)}, u32[]{:S(2)}) copy-start(f32[8,96,64]{1,2,0:T(8,128)} %param.18) | copy-start | bytes 589828
  31.9 24.9 %all-to-all-start.1 = ((f32[64,1,2304]{2,1,0:T(1,128)}), f32[64,1,2304]{2,1,0:T(1,128)S(1)}, u32[]{:S(2)}, u32[]{:S(2)}) async-start(f32[64,1,2304]{2,1,0:T(1,128)} %bitcast.11), calls=%async_computation.1 | async-start | bytes 1179648 | tf_op jit(solution)/shard_map/all_to_all | solution.py:595
  38.3 9.9 %collective-permute-start.2 = (f32[384,128]{1,0:T(8,128)S(1)}, f32[384,128]{1,0:T(8,128)S(1)}, u32[]{:S(2)}, u32[]{:S(2)}) collective-permute-start(f32[384,128]{1,0:T(8,128)S(1)} %copy-done.9), channel_id=1, source_target_pairs={{0,1},{1,2},{2,3},{3,0},{4,5},{5,6},{6,7},{7,4},{8,9},{9,10},{10,1... | collective-permute-start | bytes 589832 | tf_op jit(solution)/shard_map/ppermute | solution.py:647
  39.5 11.2 %collective-permute-start.1 = (f32[384,128]{1,0:T(8,128)S(1)}, f32[384,128]{1,0:T(8,128)S(1)}, u32[]{:S(2)}, u32[]{:S(2)}) collective-permute-start(f32[384,128]{1,0:T(8,128)S(1)} %copy-done.9), channel_id=1, source_target_pairs={{0,2},{1,3},{2,0},{3,1},{4,6},{5,7},{6,4},{7,5},{8,10},{9,11},{10,... | collective-permute-start | bytes 589832 | tf_op jit(solution)/shard_map/ppermute | solution.py:647
  42.0 8.8 %collective-permute-start = (f32[384,128]{1,0:T(8,128)S(1)}, f32[384,128]{1,0:T(8,128)S(1)}, u32[]{:S(2)}, u32[]{:S(2)}) collective-permute-start(f32[384,128]{1,0:T(8,128)S(1)} %copy-done.9), channel_id=1, source_target_pairs={{0,3},{1,0},{2,1},{3,2},{4,7},{5,4},{6,5},{7,6},{8,11},{9,8},{10,9... | collective-permute-start | bytes 589832 | tf_op jit(solution)/shard_map/ppermute | solution.py:647
  45.8 2.3 %copy-start.14 = (bf16[384,144]{1,0:T(8,128)(2,1)}, bf16[384,144]{1,0:T(8,128)(2,1)S(1)}, u32[]{:S(2)}) copy-start(bf16[384,144]{1,0:T(8,128)(2,1)S(1)} %get-tuple-element.58.near_near) | copy-start | bytes 331780
  45.8 2.3 %copy-start.16 = (bf16[384,144]{1,0:T(8,128)(2,1)}, bf16[384,144]{1,0:T(8,128)(2,1)S(1)}, u32[]{:S(2)}) copy-start(bf16[384,144]{1,0:T(8,128)(2,1)S(1)} %get-tuple-element.59.far_far) | copy-start | bytes 331780
  60.6 11.6 %copy-start = (bf16[512,144]{1,0:T(8,128)(2,1)S(1)}, bf16[512,144]{1,0:T(8,128)(2,1)}, u32[]{:S(2)}) copy-start(bf16[512,144]{1,0:T(8,128)(2,1)} %get-tuple-element.66.turned_near.rest_3_) | copy-start | bytes 442372
  60.6 11.6 %copy-start.1 = (bf16[512,144]{1,0:T(8,128)(2,1)S(1)}, bf16[512,144]{1,0:T(8,128)(2,1)}, u32[]{:S(2)}) copy-start(bf16[512,144]{1,0:T(8,128)(2,1)} %get-tuple-element.67.turned_far.rest_4_) | copy-start | bytes 442372
  60.6 11.6 %copy-start.18 = (f32[384,128]{1,0:T(8,128)S(1)}, f32[384,128]{1,0:T(8,128)}, u32[]{:S(2)}) copy-start(f32[384,128]{1,0:T(8,128)} %get-tuple-element.64.near_values) | copy-start | bytes 589828
  60.6 25.2 %all-to-all-start.2 = ((f32[64,1,2304]{2,1,0:T(1,128)}), f32[64,1,2304]{2,1,0:T(1,128)S(1)}, u32[]{:S(2)}, u32[]{:S(2)}) async-start(f32[64,1,2304]{2,1,0:T(1,128)} %bitcast.13), calls=%async_computation.2 | async-start | bytes 1179648 | tf_op jit(solution)/shard_map/all_to_all | solution.py:595
  67.3 8.4 %collective-permute-start.8 = (f32[384,128]{1,0:T(8,128)S(1)}, f32[384,128]{1,0:T(8,128)S(1)}, u32[]{:S(2)}, u32[]{:S(2)}) collective-permute-start(f32[384,128]{1,0:T(8,128)S(1)} %get-tuple-element.72.field_ref.refs_4_.rest_5_), channel_id=1, source_target_pairs={{0,1},{1,2},{2,3},{3,0},{4,5},{5,6},{6,7},{7,4},{8,9},{9,10},{10,1... | collective-permute-start | bytes 589832 | tf_op jit(solution)/shard_map/ppermute | solution.py:647
  68.6 11.2 %collective-permute-start.7 = (f32[384,128]{1,0:T(8,128)S(1)}, f32[384,128]{1,0:T(8,128)S(1)}, u32[]{:S(2)}, u32[]{:S(2)}) collective-permute-start(f32[384,128]{1,0:T(8,128)S(1)} %get-tuple-element.72.field_ref.refs_4_.rest_5_), channel_id=1, source_target_pairs={{0,2},{1,3},{2,0},{3,1},{4,6},{5,7},{6,4},{7,5},{8,10},{9,11},{10,... | collective-permute-start | bytes 589832 | tf_op jit(solution)/shard_map/ppermute | solution.py:647
  71.0 8.8 %collective-permute-start.6 = (f32[384,128]{1,0:T(8,128)S(1)}, f32[384,128]{1,0:T(8,128)S(1)}, u32[]{:S(2)}, u32[]{:S(2)}) collective-permute-start(f32[384,128]{1,0:T(8,128)S(1)} %get-tuple-element.72.field_ref.refs_4_.rest_5_), channel_id=1, source_target_pairs={{0,3},{1,0},{2,1},{3,2},{4,7},{5,4},{6,5},{7,6},{8,11},{9,8},{10,9... | collective-permute-start | bytes 589832 | tf_op jit(solution)/shard_map/ppermute | solution.py:647
  72.2 3.5 %copy-start.15 = (bf16[384,144]{1,0:T(8,128)(2,1)S(1)}, bf16[384,144]{1,0:T(8,128)(2,1)}, u32[]{:S(2)}) copy-start(bf16[384,144]{1,0:T(8,128)(2,1)} %copy-done.14) | copy-start | bytes 331780
  72.2 3.5 %copy-start.17 = (bf16[384,144]{1,0:T(8,128)(2,1)S(1)}, bf16[384,144]{1,0:T(8,128)(2,1)}, u32[]{:S(2)}) copy-start(bf16[384,144]{1,0:T(8,128)(2,1)} %copy-done.16) | copy-start | bytes 331780
  73.6 9.8 %collective-permute-start.3 = (f32[128,128]{1,0:T(8,128)}, f32[128,128]{1,0:T(8,128)S(1)}, u32[]{:S(2)}, u32[]{:S(2)}) collective-permute-start(f32[128,128]{1,0:T(8,128)} %get-tuple-element.68), channel_id=1, source_target_pairs={{0,3},{1,0},{2,1},{3,2},{4,7},{5,4},{6,5},{7,6},{8,11},{9,8},{10,9... | collective-permute-start | bytes 196616 | tf_op jit(solution)/shard_map/ppermute | solution.py:647
  73.7 9.8 %collective-permute-start.4 = (f32[128,128]{1,0:T(8,128)}, f32[128,128]{1,0:T(8,128)S(1)}, u32[]{:S(2)}, u32[]{:S(2)}) collective-permute-start(f32[128,128]{1,0:T(8,128)} %get-tuple-element.69), channel_id=1, source_target_pairs={{0,2},{1,3},{2,0},{3,1},{4,6},{5,7},{6,4},{7,5},{8,10},{9,11},{10,... | collective-permute-start | bytes 196616 | tf_op jit(solution)/shard_map/ppermute | solution.py:647
  75.7 7.8 %collective-permute-start.5 = (f32[128,128]{1,0:T(8,128)}, f32[128,128]{1,0:T(8,128)S(1)}, u32[]{:S(2)}, u32[]{:S(2)}) collective-permute-start(f32[128,128]{1,0:T(8,128)} %get-tuple-element.70), channel_id=1, source_target_pairs={{0,1},{1,2},{2,3},{3,0},{4,5},{5,6},{6,7},{7,4},{8,9},{9,10},{10,1... | collective-permute-start | bytes 196616 | tf_op jit(solution)/shard_map/ppermute | solution.py:647
  78.1 7.8 %copy-start.6 = (f32[384,128]{1,0:T(8,128)S(1)}, f32[384,128]{1,0:T(8,128)}, u32[]{:S(2)}) copy-start(f32[384,128]{1,0:T(8,128)} %get-tuple-element.77.rest_2_) | copy-start | bytes 589828
  91.6 16.4 %all-to-all-start.3 = ((f32[32,8,128]{2,1,0:T(8,128)}), f32[32,8,128]{2,1,0:T(8,128)S(1)}, u32[]{:S(2)}, u32[]{:S(2)}) async-start(f32[32,8,128]{2,1,0:T(8,128)} %get-tuple-element.78), calls=%async_computation.3 | async-start | bytes 262144 | tf_op jit(solution)/shard_map/all_to_all | solution.py:698
  100.8 15.8 %collective-permute-start.9 = (f32[512,128]{1,0:T(8,128)}, f32[512,128]{1,0:T(8,128)S(1)}, u32[]{:S(2)}, u32[]{:S(2)}) collective-permute-start(f32[512,128]{1,0:T(8,128)} %get-tuple-element.86), channel_id=1, source_target_pairs={{0,3},{1,0},{2,1},{3,2},{4,7},{5,4},{6,5},{7,6},{8,11},{9,8},{10,9... | collective-permute-start | bytes 786440 | tf_op jit(solution)/shard_map/ppermute | solution.py:647
  103.4 13.2 %collective-permute-start.10 = (f32[512,128]{1,0:T(8,128)}, f32[512,128]{1,0:T(8,128)S(1)}, u32[]{:S(2)}, u32[]{:S(2)}) collective-permute-start(f32[512,128]{1,0:T(8,128)} %get-tuple-element.87), channel_id=1, source_target_pairs={{0,2},{1,3},{2,0},{3,1},{4,6},{5,7},{6,4},{7,5},{8,10},{9,11},{10,... | collective-permute-start | bytes 786440 | tf_op jit(solution)/shard_map/ppermute | solution.py:647
  103.9 15.4 %collective-permute-start.11 = (f32[512,128]{1,0:T(8,128)}, f32[512,128]{1,0:T(8,128)S(1)}, u32[]{:S(2)}, u32[]{:S(2)}) collective-permute-start(f32[512,128]{1,0:T(8,128)} %get-tuple-element.88), channel_id=1, source_target_pairs={{0,1},{1,2},{2,3},{3,0},{4,5},{5,6},{6,7},{7,4},{8,9},{9,10},{10,1... | collective-permute-start | bytes 786440 | tf_op jit(solution)/shard_map/ppermute | solution.py:647
  108.7 13.2 %copy-start.10 = (f32[128,128]{1,0:T(8,128)S(1)}, f32[128,128]{1,0:T(8,128)}, u32[]{:S(2)}) copy-start(f32[128,128]{1,0:T(8,128)} %get-tuple-element.79.rest_0_) | copy-start | bytes 196612
  108.7 13.2 %copy-start.11 = (f32[128,128]{1,0:T(8,128)S(1)}, f32[128,128]{1,0:T(8,128)}, u32[]{:S(2)}) copy-start(f32[128,128]{1,0:T(8,128)} %get-tuple-element.85.rest_4_) | copy-start | bytes 196612
  108.7 13.2 %all-to-all-start.4 = ((f32[8,32,128]{2,1,0:T(8,128)}), f32[8,32,128]{2,1,0:T(8,128)S(1)}, u32[]{:S(2)}, u32[]{:S(2)}) async-start(f32[8,32,128]{2,1,0:T(8,128)} %sum.1), calls=%async_computation.4 | async-start | bytes 262144 | tf_op jit(solution)/shard_map/all_to_all | solution.py:713
  121.9 7.7 %copy-start.13 = (f32[384,128]{1,0:T(8,128)S(1)}, f32[384,128]{1,0:T(8,128)}, u32[]{:S(2)}) copy-start(f32[384,128]{1,0:T(8,128)} %get-tuple-element.83.field_ref.refs_8_) | copy-start | bytes 589828
  127.3 5.5 %collective-permute-start.12 = (f32[128,128]{1,0:T(8,128)S(1)}, f32[128,128]{1,0:T(8,128)S(1)}, u32[]{:S(2)}, u32[]{:S(2)}) collective-permute-start(f32[128,128]{1,0:T(8,128)S(1)} %get-tuple-element.94), channel_id=1, source_target_pairs={{0,3},{1,0},{2,1},{3,2},{4,7},{5,4},{6,5},{7,6},{8,11},{9,8},{10,9... | collective-permute-start | bytes 196616 | tf_op jit(solution)/shard_map/ppermute | solution.py:647
  128.3 4.6 %collective-permute-start.13 = (f32[128,128]{1,0:T(8,128)S(1)}, f32[128,128]{1,0:T(8,128)S(1)}, u32[]{:S(2)}, u32[]{:S(2)}) collective-permute-start(f32[128,128]{1,0:T(8,128)S(1)} %get-tuple-element.95), channel_id=1, source_target_pairs={{0,2},{1,3},{2,0},{3,1},{4,6},{5,7},{6,4},{7,5},{8,10},{9,11},{10,... | collective-permute-start | bytes 196616 | tf_op jit(solution)/shard_map/ppermute | solution.py:647
  129.6 4.6 %collective-permute-start.14 = (f32[128,128]{1,0:T(8,128)S(1)}, f32[128,128]{1,0:T(8,128)S(1)}, u32[]{:S(2)}, u32[]{:S(2)}) collective-permute-start(f32[128,128]{1,0:T(8,128)S(1)} %get-tuple-element.96), channel_id=1, source_target_pairs={{0,1},{1,2},{2,3},{3,0},{4,5},{5,6},{6,7},{7,4},{8,9},{9,10},{10,1... | collective-permute-start | bytes 196616 | tf_op jit(solution)/shard_map/ppermute | solution.py:647
  129.6 4.6 %copy-start.5 = (f32[512,128]{1,0:T(8,128)S(1)}, f32[512,128]{1,0:T(8,128)}, u32[]{:S(2)}) copy-start(f32[512,128]{1,0:T(8,128)} %get-tuple-element.92.bubble_ref) | copy-start | bytes 786436

commit v7 on v6

--- a/solution.py
+++ b/solution.py
@@ -312,17 +312,15 @@
 
 
 def image_kernel(
-    parts, groups, last, arrived_ref, inner_hbm, asked_ref, where_ref,
+    parts, groups, last, arrived_ref, inner_ref, asked_ref, where_ref,
     near_far, far_near, *rest,
 ):
     if last:
         case_ref, gram_ref, near_values, turned_near, turned_far = rest[:5]
         images, rest = rest[5 : 5 + groups], rest[5 + groups :]
-        image_ref, copies_ref, turned_ref, near_part, slot_ref, slot_part, far_values, inner_ref, sem = rest
+        image_ref, copies_ref, turned_ref, near_part, slot_ref, slot_part, far_values = rest
     else:
-        meta_ref, image_ref, far_values, pay_ref, near_part, slot_ref, slot_part, inner_ref, sem = rest
-    fetch = pltpu.make_async_copy(inner_hbm, inner_ref, sem)
-    fetch.start()
+        meta_ref, image_ref, far_values, pay_ref, near_part, slot_ref, slot_part = rest
     asked = asked_ref[...]
     asked_hot = port_onehot(asked)
     slots = onehot(jnp.concatenate(owner_slots(where_ref[OWNER], parts), axis=0))
@@ -334,7 +332,6 @@
     for g in range(tiles):
         slot_ref[g] = values[:, g * LANES : (g + 1) * LANES]
     slot_products(far_near, slot_ref, asked, slot_part)
-    fetch.wait()
     image = inner_ref[...] + pick_right(near_part[...], near_onehot(where_ref[NEAR]), NN)
     image = image + slots_to_ports(slot_part, asked_hot)
     image_ref[...] = image
@@ -423,11 +420,15 @@
     return out
 
 
-def gram_kernel(groups, case_ref, *refs):
+def base_gram_kernel(groups, case_ref, *refs):
+    base, out_ref = refs[:groups], refs[groups]
+    out_ref[...] = add_products(LANES, base, [base[0]], [0], case_ref[0], jnp.zeros((CASES, LANES), F32))
+
+
+def gram_kernel(groups, case_ref, gram_ref, *refs):
     base, image, out_ref = refs[:groups], refs[groups : 2 * groups], refs[2 * groups]
     total = groups * CASES
-    out = jnp.zeros((CASES, LANES), F32)
-    out = add_products(LANES, base, [base[0], image[0]], [0, total], case_ref[0], out)
+    out = add_products(LANES, base, [image[0]], [total], case_ref[0], gram_ref[...])
     out_ref[...] = add_products(LANES, image, [image[0]], [2 * total], case_ref[0], out)
 
 
@@ -650,21 +651,23 @@
         return backward[::-1]
 
     def inner(field):
-        return call(inner_kernel, [field_of] * 2, [(rows, comps)] + slot_scratch, "inner", flops=10**9)(
+        return call(inner_kernel, [((rows, ports), F32, False)] * 2, [(rows, comps)] + slot_scratch, "inner", flops=10**9)(
             field, asked, where, near_near, far_far
         )
 
     arrived = exchange(pay, parts)
     base_all = to_cases([base] * (groups - 1))
     base_inner, base_near = inner(base)
-    arrived, *base_all = lax.optimization_barrier((arrived, *base_all))
+    gram_of = [((cases, LANES), F32, False)]
+    (gram,) = call(functools.partial(base_gram_kernel, groups), gram_of, name="base_gram", smem=(0,))(
+        case, base, *base_all
+    )
+    arrived, gram = lax.optimization_barrier((arrived, gram))
     image, base_far, pay = call(
         functools.partial(image_kernel, parts, groups, False),
         [((rows, ports), F32, False)] * 2 + [((parts * 18, LANES), F32, False)],
-        [(rows, comps)] + slot_scratch + [(rows, ports)],
+        [(rows, comps)] + slot_scratch,
         "image",
-        hbm=(1,),
-        sems=1,
     )(arrived, base_inner, asked, where, near_far, far_near, meta)
     arrived = exchange(pay, parts)
     image_all = to_cases([image] * (groups - 1))
@@ -678,19 +681,17 @@
     )(case, base_near, base_far, where, turned_near, turned_far)
     turned0_all = to_cases(messages)
     image_inner, image_near = inner(image)
-    (gram,) = call(functools.partial(gram_kernel, groups), [((cases, LANES), F32, False)], name="gram", smem=(0,))(
-        case, base, *base_all, image, *image_all
+    (gram,) = call(functools.partial(gram_kernel, groups), gram_of, name="gram", smem=(0,))(
+        case, gram, base, *base_all, image, *image_all
     )
     arrived, *turned0_all = lax.optimization_barrier((arrived, *turned0_all))
     minor = lax.axis_size("py")
     second, copies, turned1 = call(
         functools.partial(image_kernel, parts, groups, True),
         [field_of, ((groups * minor, cases, LANES), F32, True), bubble_of],
-        [(rows, comps)] + slot_scratch + [(rows, comps), (rows, ports)],
+        [(rows, comps)] + slot_scratch + [(rows, comps)],
         "second",
         smem=(6,),
-        hbm=(1,),
-        sems=1,
     )(
         arrived, image_inner, asked, where, near_far, far_near, case, gram, image_near, turned_near, turned_far,
         image, *image_all,

time: 136 us -> 135 us (level)
  Pallas kernels: 38.8 us -> 36.2 us
  local copies, waits for them, and re-layouts: 0.08 us -> 1.96 us
    pallas_call x14 -> x15, Pallas kernels: 38.8 us -> 36.2 us  [run(): pl.pallas_call(kernel, out_shape=results, in_specs=specs, out_specs=[far_...]
    all_to_all x2, waiting for transfers between devices: 8.4 us -> 5.85 us  [exchange(): lax.all_to_all(rows.reshape(parts, 1, -1), PLANE, split_axis=0, concat_ax...]
    unnamed x38 -> x46, local copies, waits for them, and re-layouts: 0.08 us -> 1.96 us
    ppermute x15, waiting for transfers between devices: 8.49 us -> 10 us  [to_cases(): lax.ppermute(message, 'case', [(k, (k + h) % groups) for k in range(group...]
  transfers between devices with their start and end apart: 19 -> 19, of which waited for: 9 -> 9; matrix products, arithmetic and copies ran while one was open for 0% -> 0% of each run, Pallas kernels for 14% -> 13%
where the time goes in v7:
time: 135 us; the launch traced here: 134 us
  starting transfers between devices  46.9 us (35%)
  Pallas kernels  36.2 us (27%)
  blocking collectives  26.4 us (20%)
  waiting for transfers between devices  21.7 us (16%)
  local copies, waits for them, and re-layouts  1.96 us (1%)
    pallas_call x15, Pallas kernels, run(): pl.pallas_call(kernel, out_shape=results, in_specs=specs, out_specs=[far_...  36.2 us
    all_to_all x1, blocking collectives, exchange(): lax.all_to_all(rows.reshape(parts, 1, -1), PLANE, split_axis=0, concat_ax...  26.4 us
    ppermute x15, starting transfers between devices, to_cases(): lax.ppermute(message, 'case', [(k, (k + h) % groups) for k in range(group...  17.5 us
    all_to_all x2, starting transfers between devices, exchange(): lax.all_to_all(rows.reshape(parts, 1, -1), PLANE, split_axis=0, concat_ax...  13.2 us
    ppermute x15, waiting for transfers between devices, to_cases(): lax.ppermute(message, 'case', [(k, (k + h) % groups) for k in range(group...  10 us
    all_to_all x1, starting transfers between devices, local(): copies = lax.all_to_all(copies, ('case', 'py'), split_axis=0, concat_axis=0)  8.35 us
    all_to_all x1, starting transfers between devices, local(): copies = lax.all_to_all(copies, 'px', split_axis=0, concat_axis=0)  7.82 us
    all_to_all x2, waiting for transfers between devices, exchange(): lax.all_to_all(rows.reshape(parts, 1, -1), PLANE, split_axis=0, concat_ax...  5.85 us
  transfers between devices with their start and end apart: 19, of which 9 were waited for; matrix products, arithmetic and copies ran while one was open for 0% of the time, Pallas kernels for 13%

profile of v7, /device:TPU:1, one launch (start us, length us, event | category | flops | bytes accessed | tf_op | source)
XLA Modules:
  0.0 134.0 jit_solution(1878567446124053265)
XLA Ops:
  0.6 3.5 %condense.1 = (f32[640,128]{1,0:T(8,128)S(1)}, f32[384,128]{1,0:T(8,128)}, f32[64,128]{1,0:T(8,128)S(1)}, f32[8,128]{1,0:T(8,128)S(1)}) custom-call(s32[1,128]{1,0:T(1,128)} %bitcast.30, f32[1,128]{1,0:T(1,128)} %bitcast.31, s32[1,128]{1,0:T(1,128)} %bitcast.32, s32[1,128]{1,0:T(1,128)} %bitcast.33, s32[1,128]{1,0:T(1,128)} %bitcast.34, ...), custom_call_target="tpu_custom_call" | custom-call | bytes 592384 | tf_op jit(solution)/shard_map/condense/pallas_call | solution.py:580
  4.1 0.0 copy-start.7
  4.1 0.0 copy-start.8
  4.1 26.4 %all_to_all.25 = f32[64,1,1280]{2,1,0:T(1,128)S(1)} all-to-all(f32[64,1,1280]{2,1,0:T(1,128)S(1)} %bitcast.23), channel_id=1, replica_groups=mesh['px'=8,'py'=8,'case'=4] {'px','py'}, dimensions={0} | all-to-all | bytes 655360 | tf_op jit(solution)/shard_map/all_to_all | solution.py:596
  30.5 1.4 %rhs.1 = (f32[384,128]{1,0:T(8,128)}, f32[1152,128]{1,0:T(8,128)}, f32[64,128]{1,0:T(8,128)S(1)}) custom-call(f32[640,128]{1,0:T(8,128)S(1)} %bitcast.21, f32[384,128]{1,0:T(8,128)S(1)} %copy-done.8, f32[384,128]{1,0:T(8,128)S(1)} %bitcast.28, f32[64,128]{1,0:T(8,128)S(1)} %get-tuple-element.50.meta_ref.rest_0_), custom_call_target="tpu_custom_call" | custom-call | bytes 753664 | tf_op jit(solution)/shard_map/rhs/pallas_call | solution.py:580
  31.9 6.3 %all-to-all-start.1 = ((f32[64,1,2304]{2,1,0:T(1,128)}), f32[64,1,2304]{2,1,0:T(1,128)S(1)}, u32[]{:S(2)}, u32[]{:S(2)}) async-start(f32[64,1,2304]{2,1,0:T(1,128)} %bitcast.11), calls=%async_computation.1 | async-start | bytes 1179648 | tf_op jit(solution)/shard_map/all_to_all | solution.py:596
  38.3 1.3 collective-permute-start.2
  39.6 2.4 %collective-permute-start.1 = (f32[384,128]{1,0:T(8,128)S(1)}, f32[384,128]{1,0:T(8,128)S(1)}, u32[]{:S(2)}, u32[]{:S(2)}) collective-permute-start(f32[384,128]{1,0:T(8,128)S(1)} %copy-done), channel_id=1, source_target_pairs={{0,2},{1,3},{2,0},{3,1},{4,6},{5,7},{6,4},{7,5},{8,10},{9,11},{10,... | collective-permute-start | bytes 589832 | tf_op jit(solution)/shard_map/ppermute | solution.py:648
  42.0 1.2 collective-permute-start
  43.2 2.6 %tables.1 = (bf16[384,144]{1,0:T(8,128)(2,1)S(1)}, bf16[384,144]{1,0:T(8,128)(2,1)S(1)}, bf16[384,144]{1,0:T(8,128)(2,1)S(1)}, bf16[384,144]{1,0:T(8,128)(2,1)S(...) custom-call(f32[8,128]{1,0:T(8,128)S(1)} %get-tuple-element.55.where_ref, ...), custom_call_target="tpu_custom_call" | custom-call | flops 1000000000 | bytes 888832 | tf_op jit(solution)/shard_map/tables/pallas_call | solution.py:580
  45.8 1.6 %inner.2 = (f32[384,128]{1,0:T(8,128)S(1)}, f32[384,128]{1,0:T(8,128)S(1)}) custom-call(f32[384,128]{1,0:T(8,128)S(1)} %copy-done, f32[64,128]{1,0:T(8,128)S(1)} %get-tuple-element.54.asked_ref, f32[8,128]{1,0:T(8,128)S(1)} %get-tuple-element.55.where_ref, bf16[384,144]{1,0:T(8,128)(2,1)S(1)} %get-tuple-element.56.near_near, ...), custom_call_target="tpu_custom_call" | custom-call | flops 1000000000 | bytes 454656 | tf_op jit(solution)/shard_map/inner/pallas_call | solution.py:580
  47.5 3.3 %collective-permute-done.1.refs_2_ = f32[384,128]{1,0:T(8,128)S(1)} collective-permute-done((f32[384,128]{1,0:T(8,128)S(1)}, f32[384,128]{1,0:T(8,128)S(1)}, u32[]{:S(2)}, u32[]{:S(2)}) %collective-permute-start.1) | collective-permute-done | bytes 196640 | tf_op jit(solution)/shard_map/ppermute | solution.py:648
  50.8 1.5 %base_gram.1.gram_ref = f32[8,128]{1,0:T(8,128)S(1)} custom-call(s32[1]{0:T(128)} %bitcast.case_ref.rest_0_, f32[384,128]{1,0:T(8,128)S(1)} %copy-done, f32[384,128]{1,0:T(8,128)S(1)} %collective-permute-done.refs_1_, f32[384,128]{1,0:T(8,128)S(1)} %collective-permute-done.1.refs_2_, f32[384,128]{1,0:T(8,128)S(1)} %collective-permute-done.2.refs_3_), custom_call_target="tpu_custom_call" | custom-call | bytes 786436 | tf_op jit(solution)/shard_map/base_gram/pallas_call | solution.py:580
  52.3 4.5 %all-to-all-done.1 = f32[64,1,2304]{2,1,0:T(1,128)S(1)} async-done(((f32[64,1,2304]{2,1,0:T(1,128)}), f32[64,1,2304]{2,1,0:T(1,128)S(1)}, u32[]{:S(2)}, u32[]{:S(2)}) %all-to-all-start.1) | async-done | bytes 589856 | tf_op jit(solution)/shard_map/all_to_all | solution.py:596
  56.8 2.7 %image.1 = (f32[384,128]{1,0:T(8,128)S(1)}, f32[384,128]{1,0:T(8,128)S(1)}, f32[1152,128]{1,0:T(8,128)}) custom-call(f32[1152,128]{1,0:T(8,128)S(1)} %bitcast.19, f32[384,128]{1,0:T(8,128)S(1)} %get-tuple-element.58.inner_ref, f32[64,128]{1,0:T(8,128)S(1)} %get-tuple-element.54.asked_ref, f32[8,128]{1,0:T(8,128)S(1)} %get-tuple-element.55.where_ref, ...), custom_call_target="tpu_custom_call" | custom-call | bytes 1077248 | tf_op jit(solution)/shard_map/image/pallas_call | solution.py:580
  59.5 6.9 %all-to-all-start.2 = ((f32[64,1,2304]{2,1,0:T(1,128)}), f32[64,1,2304]{2,1,0:T(1,128)S(1)}, u32[]{:S(2)}, u32[]{:S(2)}) async-start(f32[64,1,2304]{2,1,0:T(1,128)} %bitcast.13), calls=%async_computation.2 | async-start | bytes 1179648 | tf_op jit(solution)/shard_map/all_to_all | solution.py:596
  66.4 1.1 collective-permute-start.8
  67.6 2.4 %collective-permute-start.7 = (f32[384,128]{1,0:T(8,128)S(1)}, f32[384,128]{1,0:T(8,128)S(1)}, u32[]{:S(2)}, u32[]{:S(2)}) collective-permute-start(f32[384,128]{1,0:T(8,128)S(1)} %get-tuple-element.70.field_ref.refs_4_.rest_5_), channel_id=1, source_target_pairs={{0,2},{1,3},{2,0},{3,1},{4,6},{5,7},{6,4},{7,5},{8,10},{9,11},{10,... | collective-permute-start | bytes 589832 | tf_op jit(solution)/shard_map/ppermute | solution.py:648
  69.9 1.2 collective-permute-start.6
  71.1 1.4 %turned.1 = (f32[128,128]{1,0:T(8,128)}, f32[128,128]{1,0:T(8,128)}, f32[128,128]{1,0:T(8,128)}, f32[128,128]{1,0:T(8,128)}) custom-call(s32[1]{0:T(128)} %bitcast.case_ref.rest_0_, f32[384,128]{1,0:T(8,128)S(1)} %get-tuple-element.62.near_values, f32[384,128]{1,0:T(8,128)S(1)} %get-tuple-element.63.far_values, f32[8,128]{1,0:T(8,128)S(1)} %get-tuple-element.55.where_ref, ...), custom_call_target="tpu_custom_call" | custom-call | flops 1000000000 | bytes 692228 | tf_op jit(solution)/shard_map/turned/pallas_call | solution.py:580
  72.5 0.0 collective-permute-start.3
  72.5 2.1 %collective-permute-start.4 = (f32[128,128]{1,0:T(8,128)}, f32[128,128]{1,0:T(8,128)S(1)}, u32[]{:S(2)}, u32[]{:S(2)}) collective-permute-start(f32[128,128]{1,0:T(8,128)} %get-tuple-element.67), channel_id=1, source_target_pairs={{0,2},{1,3},{2,0},{3,1},{4,6},{5,7},{6,4},{7,5},{8,10},{9,11},{10,... | collective-permute-start | bytes 196616 | tf_op jit(solution)/shard_map/ppermute | solution.py:648
  74.6 1.6 %inner.3 = (f32[384,128]{1,0:T(8,128)S(1)}, f32[384,128]{1,0:T(8,128)S(1)}) custom-call(f32[384,128]{1,0:T(8,128)S(1)} %get-tuple-element.70.field_ref.refs_4_.rest_5_, f32[64,128]{1,0:T(8,128)S(1)} %get-tuple-element.54.asked_ref, f32[8,128]{1,0:T(8,128)S(1)} %get-tuple-element.55.where_ref, bf16[384,144]{1,0:T(8,128)(2,1)S(1)} %copy-done.20, ...), custom_call_target="tpu_custom_call" | custom-call | flops 1000000000 | bytes 454656 | tf_op jit(solution)/shard_map/inner/pallas_call | solution.py:580
  76.3 2.4 %collective-permute-done.7.refs_6_.rest_7_ = f32[384,128]{1,0:T(8,128)S(1)} collective-permute-done((f32[384,128]{1,0:T(8,128)S(1)}, f32[384,128]{1,0:T(8,128)S(1)}, u32[]{:S(2)}, u32[]{:S(2)}) %collective-permute-start.7) | collective-permute-done | bytes 196640 | tf_op jit(solution)/shard_map/ppermute | solution.py:648
  78.7 3.0 %gram.1.rest_1_ = f32[8,128]{1,0:T(8,128)S(1)} custom-call(s32[1]{0:T(128)} %bitcast.case_ref.rest_0_, f32[8,128]{1,0:T(8,128)S(1)} %base_gram.1.gram_ref, f32[384,128]{1,0:T(8,128)S(1)} %copy-done, f32[384,128]{1,0:T(8,128)S(1)} %collective-permute-done.refs_1_, f32[384,128]{1,0:T(8,128)S(1)} %collective-permute-done.1.refs_2_, ...), custom_call_target="tpu_custom_call" | custom-call | bytes 1576964 | tf_op jit(solution)/shard_map/gram/pallas_call | solution.py:580
  81.8 0.6 copy-done.10
  82.4 0.6 copy-done.12
  83.0 0.6 copy-done.14
  83.6 1.3 all-to-all-done.2
  85.0 4.6 %second.1 = (f32[384,128]{1,0:T(8,128)}, f32[32,8,128]{2,1,0:T(8,128)}, f32[512,128]{1,0:T(8,128)}) custom-call(f32[1152,128]{1,0:T(8,128)S(1)} %bitcast.20, f32[384,128]{1,0:T(8,128)S(1)} %get-tuple-element.71.inner_ref, f32[64,128]{1,0:T(8,128)S(1)} %get-tuple-element.54.asked_ref, f32[8,128]{1,0:T(8,128)S(1)} %get-tuple-element.55.where_ref, ...), custom_call_target="tpu_custom_call" | custom-call | bytes 2326532 | tf_op jit(solution)/shard_map/second/pallas_call | solution.py:580
  89.6 8.4 %all-to-all-start.3 = ((f32[32,8,128]{2,1,0:T(8,128)}), f32[32,8,128]{2,1,0:T(8,128)S(1)}, u32[]{:S(2)}, u32[]{:S(2)}) async-start(f32[32,8,128]{2,1,0:T(8,128)} %get-tuple-element.74), calls=%async_computation.3 | async-start | bytes 262144 | tf_op jit(solution)/shard_map/all_to_all | solution.py:699
  97.9 2.0 %messages.1 = (f32[128,128]{1,0:T(8,128)}, f32[512,128]{1,0:T(8,128)}, f32[512,128]{1,0:T(8,128)}, f32[512,128]{1,0:T(8,128)}) custom-call(s32[1]{0:T(128)} %bitcast.case_ref.rest_0_, f32[384,128]{1,0:T(8,128)} %get-tuple-element.79.field_ref.refs_8_, f32[512,128]{1,0:T(8,128)} %get-tuple-element.80.turned_ref), custom_call_target="tpu_custom_call" | custom-call | flops 1000000000 | bytes 458756 | tf_op jit(solution)/shard_map/messages/pallas_call | solution.py:580
  100.0 2.6 %collective-permute-start.9 = (f32[512,128]{1,0:T(8,128)}, f32[512,128]{1,0:T(8,128)S(1)}, u32[]{:S(2)}, u32[]{:S(2)}) collective-permute-start(f32[512,128]{1,0:T(8,128)} %get-tuple-element.82), channel_id=1, source_target_pairs={{0,3},{1,0},{2,1},{3,2},{4,7},{5,4},{6,5},{7,6},{8,11},{9,8},{10,9... | collective-permute-start | bytes 786440 | tf_op jit(solution)/shard_map/ppermute | solution.py:648
  102.5 0.5 collective-permute-start.10
  103.1 0.6 collective-permute-start.11
  103.7 3.5 %all-to-all-done.3 = f32[32,8,128]{2,1,0:T(8,128)S(1)} async-done(((f32[32,8,128]{2,1,0:T(8,128)}), f32[32,8,128]{2,1,0:T(8,128)S(1)}, u32[]{:S(2)}, u32[]{:S(2)}) %all-to-all-start.3) | async-done | bytes 131104 | tf_op jit(solution)/shard_map/all_to_all | solution.py:699
  107.1 0.7 sum.1
  107.8 7.8 %all-to-all-start.4 = ((f32[8,32,128]{2,1,0:T(8,128)}), f32[8,32,128]{2,1,0:T(8,128)S(1)}, u32[]{:S(2)}, u32[]{:S(2)}) async-start(f32[8,32,128]{2,1,0:T(8,128)} %sum.1), calls=%async_computation.4 | async-start | bytes 262144 | tf_op jit(solution)/shard_map/all_to_all | solution.py:714
  115.6 2.9 %collective-permute-done.11.rest_7_.refs_11_ = f32[512,128]{1,0:T(8,128)S(1)} collective-permute-done((f32[512,128]{1,0:T(8,128)}, f32[512,128]{1,0:T(8,128)S(1)}, u32[]{:S(2)}, u32[]{:S(2)}) %collective-permute-start.11) | collective-permute-done | bytes 262176 | tf_op jit(solution)/shard_map/ppermute | solution.py:648
  118.5 2.4 %all-to-all-done.4.gram_ref = f32[8,32,128]{2,1,0:T(8,128)S(1)} async-done(((f32[8,32,128]{2,1,0:T(8,128)}), f32[8,32,128]{2,1,0:T(8,128)S(1)}, u32[]{:S(2)}, u32[]{:S(2)}) %all-to-all-start.4) | async-done | bytes 131104 | tf_op jit(solution)/shard_map/all_to_all | solution.py:714
  120.9 0.0 copy-start.18
  120.9 5.5 %solve.1 = (f32[64,8,128]{2,1,0:T(8,128)S(1)}, f32[128,128]{1,0:T(8,128)S(1)}, f32[128,128]{1,0:T(8,128)S(1)}, f32[128,128]{1,0:T(8,128)S(1)}, f32[128,128]{1,0:T(8,128)S(1)}) custom-call(s32[1]{0:T(128)} %bitcast.case_ref.rest_0_, f32[8,32,128]{2,1,0:T(8,128)S(1)} %all-to-all-done.4.gram_ref, f32[128,128]{1,0:T(8,128)S(1)} %copy-done.9, ...), custom_call_target="tpu_custom_call" | custom-call | bytes 1245188 | tf_op jit(solution)/shard_map/solve/pallas_call | solution.py:580
  126.4 0.9 collective-permute-start.12
  127.4 1.2 collective-permute-start.13
  128.6 3.2 %ports.1 = (f32[384,128]{1,0:T(8,128)}, f32[384,128]{1,0:T(8,128)}) custom-call(f32[64,8,128]{2,1,0:T(8,128)S(1)} %get-tuple-element.85.coef, f32[384,128]{1,0:T(8,128)S(1)} %copy-done, f32[384,128]{1,0:T(8,128)S(1)} %collective-permute-done.refs_1_, f32[384,128]{1,0:T(8,128)S(1)} %collective-permute-done.1.refs_2_, ...), custom_call_target="tpu_custom_call" | custom-call | flops 1000000000 | bytes 2818048 | tf_op jit(solution)/shard_map/ports/pallas_call | solution.py:580
  131.9 0.1 collective-permute-done.13.refs_2_
  132.0 1.2 collective-permute-done.14.refs_3_
  133.3 0.7 join.1
  (52 shorter events, 0.1 us)
Async XLA Ops:
  4.1 26.4 %copy-start.7 = (f32[48,8,128]{2,1,0:T(8,128)S(1)}, f32[48,8,128]{2,1,0:T(8,128)}, u32[]{:S(2)}) copy-start(f32[48,8,128]{2,1,0:T(8,128)} %param.16) | copy-start | bytes 589828
  4.1 26.4 %copy-start.8 = (f32[384,128]{1,0:T(8,128)S(1)}, f32[384,128]{1,0:T(8,128)}, u32[]{:S(2)}) copy-start(f32[384,128]{1,0:T(8,128)} %get-tuple-element.49.near_sum_ref) | copy-start | bytes 589828
  30.5 12.7 %copy-start.17 = (f32[8,96,96]{2,1,0:T(8,128)S(1)}, f32[8,96,96]{2,1,0:T(8,128)}, u32[]{:S(2)}) copy-start(f32[8,96,96]{2,1,0:T(8,128)} %block_ref.1) | copy-start | bytes 884740
  31.9 6.3 %copy-start = (f32[384,128]{1,0:T(8,128)S(1)}, f32[384,128]{1,0:T(8,128)}, u32[]{:S(2)}) copy-start(f32[384,128]{1,0:T(8,128)} %get-tuple-element.52.refs_0_.field_ref) | copy-start | bytes 589828
  31.9 11.3 %copy-start.3 = (f32[64,8,128]{2,1,0:T(8,128)S(1)}, f32[64,8,128]{2,1,0:T(8,128)}, u32[]{:S(2)}) copy-start(f32[64,8,128]{2,1,0:T(8,128)} %param.15) | copy-start | bytes 786436
  31.9 11.3 %copy-start.4 = (f32[8,64,64]{2,1,0:T(8,128)S(1)}, f32[8,64,64]{2,1,0:T(8,128)}, u32[]{:S(2)}) copy-start(f32[8,64,64]{2,1,0:T(8,128)} %inverse_ref.1) | copy-start | bytes 393220
  31.9 11.3 %copy-start.5 = (f32[8,96,64]{1,2,0:T(8,128)S(1)}, f32[8,96,64]{1,2,0:T(8,128)}, u32[]{:S(2)}) copy-start(f32[8,96,64]{1,2,0:T(8,128)} %param.18) | copy-start | bytes 589828
  31.9 24.9 %all-to-all-start.1 = ((f32[64,1,2304]{2,1,0:T(1,128)}), f32[64,1,2304]{2,1,0:T(1,128)S(1)}, u32[]{:S(2)}, u32[]{:S(2)}) async-start(f32[64,1,2304]{2,1,0:T(1,128)} %bitcast.11), calls=%async_computation.1 | async-start | bytes 1179648 | tf_op jit(solution)/shard_map/all_to_all | solution.py:596
  38.3 9.2 %collective-permute-start.2 = (f32[384,128]{1,0:T(8,128)S(1)}, f32[384,128]{1,0:T(8,128)S(1)}, u32[]{:S(2)}, u32[]{:S(2)}) collective-permute-start(f32[384,128]{1,0:T(8,128)S(1)} %copy-done), channel_id=1, source_target_pairs={{0,1},{1,2},{2,3},{3,0},{4,5},{5,6},{6,7},{7,4},{8,9},{9,10},{10,1... | collective-permute-start | bytes 589832 | tf_op jit(solution)/shard_map/ppermute | solution.py:648
  39.6 11.2 %collective-permute-start.1 = (f32[384,128]{1,0:T(8,128)S(1)}, f32[384,128]{1,0:T(8,128)S(1)}, u32[]{:S(2)}, u32[]{:S(2)}) collective-permute-start(f32[384,128]{1,0:T(8,128)S(1)} %copy-done), channel_id=1, source_target_pairs={{0,2},{1,3},{2,0},{3,1},{4,6},{5,7},{6,4},{7,5},{8,10},{9,11},{10,... | collective-permute-start | bytes 589832 | tf_op jit(solution)/shard_map/ppermute | solution.py:648
  42.0 8.8 %collective-permute-start = (f32[384,128]{1,0:T(8,128)S(1)}, f32[384,128]{1,0:T(8,128)S(1)}, u32[]{:S(2)}, u32[]{:S(2)}) collective-permute-start(f32[384,128]{1,0:T(8,128)S(1)} %copy-done), channel_id=1, source_target_pairs={{0,3},{1,0},{2,1},{3,2},{4,7},{5,4},{6,5},{7,6},{8,11},{9,8},{10,9... | collective-permute-start | bytes 589832 | tf_op jit(solution)/shard_map/ppermute | solution.py:648
  45.8 1.7 %copy-start.19 = (bf16[384,144]{1,0:T(8,128)(2,1)}, bf16[384,144]{1,0:T(8,128)(2,1)S(1)}, u32[]{:S(2)}) copy-start(bf16[384,144]{1,0:T(8,128)(2,1)S(1)} %get-tuple-element.56.near_near) | copy-start | bytes 331780
  45.8 1.7 %copy-start.21 = (bf16[384,144]{1,0:T(8,128)(2,1)}, bf16[384,144]{1,0:T(8,128)(2,1)S(1)}, u32[]{:S(2)}) copy-start(bf16[384,144]{1,0:T(8,128)(2,1)S(1)} %get-tuple-element.57.far_far) | copy-start | bytes 331780
  59.5 11.6 %copy-start.1 = (bf16[512,144]{1,0:T(8,128)(2,1)S(1)}, bf16[512,144]{1,0:T(8,128)(2,1)}, u32[]{:S(2)}) copy-start(bf16[512,144]{1,0:T(8,128)(2,1)} %get-tuple-element.64.turned_near.rest_3_) | copy-start | bytes 442372
  59.5 11.6 %copy-start.2 = (bf16[512,144]{1,0:T(8,128)(2,1)S(1)}, bf16[512,144]{1,0:T(8,128)(2,1)}, u32[]{:S(2)}) copy-start(bf16[512,144]{1,0:T(8,128)(2,1)} %get-tuple-element.65.turned_far.rest_4_) | copy-start | bytes 442372
  59.5 25.4 %all-to-all-start.2 = ((f32[64,1,2304]{2,1,0:T(1,128)}), f32[64,1,2304]{2,1,0:T(1,128)S(1)}, u32[]{:S(2)}, u32[]{:S(2)}) async-start(f32[64,1,2304]{2,1,0:T(1,128)} %bitcast.13), calls=%async_computation.2 | async-start | bytes 1179648 | tf_op jit(solution)/shard_map/all_to_all | solution.py:596
  66.4 8.2 %collective-permute-start.8 = (f32[384,128]{1,0:T(8,128)S(1)}, f32[384,128]{1,0:T(8,128)S(1)}, u32[]{:S(2)}, u32[]{:S(2)}) collective-permute-start(f32[384,128]{1,0:T(8,128)S(1)} %get-tuple-element.70.field_ref.refs_4_.rest_5_), channel_id=1, source_target_pairs={{0,1},{1,2},{2,3},{3,0},{4,5},{5,6},{6,7},{7,4},{8,9},{9,10},{10,1... | collective-permute-start | bytes 589832 | tf_op jit(solution)/shard_map/ppermute | solution.py:648
  67.6 11.1 %collective-permute-start.7 = (f32[384,128]{1,0:T(8,128)S(1)}, f32[384,128]{1,0:T(8,128)S(1)}, u32[]{:S(2)}, u32[]{:S(2)}) collective-permute-start(f32[384,128]{1,0:T(8,128)S(1)} %get-tuple-element.70.field_ref.refs_4_.rest_5_), channel_id=1, source_target_pairs={{0,2},{1,3},{2,0},{3,1},{4,6},{5,7},{6,4},{7,5},{8,10},{9,11},{10,... | collective-permute-start | bytes 589832 | tf_op jit(solution)/shard_map/ppermute | solution.py:648
  69.9 8.8 %collective-permute-start.6 = (f32[384,128]{1,0:T(8,128)S(1)}, f32[384,128]{1,0:T(8,128)S(1)}, u32[]{:S(2)}, u32[]{:S(2)}) collective-permute-start(f32[384,128]{1,0:T(8,128)S(1)} %get-tuple-element.70.field_ref.refs_4_.rest_5_), channel_id=1, source_target_pairs={{0,3},{1,0},{2,1},{3,2},{4,7},{5,4},{6,5},{7,6},{8,11},{9,8},{10,9... | collective-permute-start | bytes 589832 | tf_op jit(solution)/shard_map/ppermute | solution.py:648
  71.1 3.5 %copy-start.20 = (bf16[384,144]{1,0:T(8,128)(2,1)S(1)}, bf16[384,144]{1,0:T(8,128)(2,1)}, u32[]{:S(2)}) copy-start(bf16[384,144]{1,0:T(8,128)(2,1)} %copy-done.19) | copy-start | bytes 331780
  71.1 3.5 %copy-start.22 = (bf16[384,144]{1,0:T(8,128)(2,1)S(1)}, bf16[384,144]{1,0:T(8,128)(2,1)}, u32[]{:S(2)}) copy-start(bf16[384,144]{1,0:T(8,128)(2,1)} %copy-done.21) | copy-start | bytes 331780
  72.5 9.2 %collective-permute-start.3 = (f32[128,128]{1,0:T(8,128)}, f32[128,128]{1,0:T(8,128)S(1)}, u32[]{:S(2)}, u32[]{:S(2)}) collective-permute-start(f32[128,128]{1,0:T(8,128)} %get-tuple-element.66), channel_id=1, source_target_pairs={{0,3},{1,0},{2,1},{3,2},{4,7},{5,4},{6,5},{7,6},{8,11},{9,8},{10,9... | collective-permute-start | bytes 196616 | tf_op jit(solution)/shard_map/ppermute | solution.py:648
  72.5 9.8 %collective-permute-start.4 = (f32[128,128]{1,0:T(8,128)}, f32[128,128]{1,0:T(8,128)S(1)}, u32[]{:S(2)}, u32[]{:S(2)}) collective-permute-start(f32[128,128]{1,0:T(8,128)} %get-tuple-element.67), channel_id=1, source_target_pairs={{0,2},{1,3},{2,0},{3,1},{4,6},{5,7},{6,4},{7,5},{8,10},{9,11},{10,... | collective-permute-start | bytes 196616 | tf_op jit(solution)/shard_map/ppermute | solution.py:648
  74.6 8.4 %collective-permute-start.5 = (f32[128,128]{1,0:T(8,128)}, f32[128,128]{1,0:T(8,128)S(1)}, u32[]{:S(2)}, u32[]{:S(2)}) collective-permute-start(f32[128,128]{1,0:T(8,128)} %get-tuple-element.68), channel_id=1, source_target_pairs={{0,1},{1,2},{2,3},{3,0},{4,5},{5,6},{6,7},{7,4},{8,9},{9,10},{10,1... | collective-permute-start | bytes 196616 | tf_op jit(solution)/shard_map/ppermute | solution.py:648
  81.7 0.6 copy-start.10
  82.4 0.6 copy-start.12
  83.0 0.6 copy-start.14
  89.6 17.5 %all-to-all-start.3 = ((f32[32,8,128]{2,1,0:T(8,128)}), f32[32,8,128]{2,1,0:T(8,128)S(1)}, u32[]{:S(2)}, u32[]{:S(2)}) async-start(f32[32,8,128]{2,1,0:T(8,128)} %get-tuple-element.74), calls=%async_computation.3 | async-start | bytes 262144 | tf_op jit(solution)/shard_map/all_to_all | solution.py:699
  100.0 15.6 %collective-permute-start.9 = (f32[512,128]{1,0:T(8,128)}, f32[512,128]{1,0:T(8,128)S(1)}, u32[]{:S(2)}, u32[]{:S(2)}) collective-permute-start(f32[512,128]{1,0:T(8,128)} %get-tuple-element.82), channel_id=1, source_target_pairs={{0,3},{1,0},{2,1},{3,2},{4,7},{5,4},{6,5},{7,6},{8,11},{9,8},{10,9... | collective-permute-start | bytes 786440 | tf_op jit(solution)/shard_map/ppermute | solution.py:648
  102.5 13.1 %collective-permute-start.10 = (f32[512,128]{1,0:T(8,128)}, f32[512,128]{1,0:T(8,128)S(1)}, u32[]{:S(2)}, u32[]{:S(2)}) collective-permute-start(f32[512,128]{1,0:T(8,128)} %get-tuple-element.83), channel_id=1, source_target_pairs={{0,2},{1,3},{2,0},{3,1},{4,6},{5,7},{6,4},{7,5},{8,10},{9,11},{10,... | collective-permute-start | bytes 786440 | tf_op jit(solution)/shard_map/ppermute | solution.py:648
  103.1 15.5 %collective-permute-start.11 = (f32[512,128]{1,0:T(8,128)}, f32[512,128]{1,0:T(8,128)S(1)}, u32[]{:S(2)}, u32[]{:S(2)}) collective-permute-start(f32[512,128]{1,0:T(8,128)} %get-tuple-element.84), channel_id=1, source_target_pairs={{0,1},{1,2},{2,3},{3,0},{4,5},{5,6},{6,7},{7,4},{8,9},{9,10},{10,1... | collective-permute-start | bytes 786440 | tf_op jit(solution)/shard_map/ppermute | solution.py:648
  107.1 13.8 %copy-start.16 = (f32[128,128]{1,0:T(8,128)S(1)}, f32[128,128]{1,0:T(8,128)}, u32[]{:S(2)}) copy-start(f32[128,128]{1,0:T(8,128)} %get-tuple-element.81.rest_4_) | copy-start | bytes 196612
  107.8 13.1 %copy-start.9 = (f32[128,128]{1,0:T(8,128)S(1)}, f32[128,128]{1,0:T(8,128)}, u32[]{:S(2)}) copy-start(f32[128,128]{1,0:T(8,128)} %get-tuple-element.75.rest_0_) | copy-start | bytes 196612
  107.8 13.1 %copy-start.11 = (f32[128,128]{1,0:T(8,128)S(1)}, f32[128,128]{1,0:T(8,128)}, u32[]{:S(2)}) copy-start(f32[128,128]{1,0:T(8,128)} %copy-done.10) | copy-start | bytes 196612
  107.8 13.1 %copy-start.13 = (f32[128,128]{1,0:T(8,128)S(1)}, f32[128,128]{1,0:T(8,128)}, u32[]{:S(2)}) copy-start(f32[128,128]{1,0:T(8,128)} %copy-done.12) | copy-start | bytes 196612
  107.8 13.1 %copy-start.15 = (f32[128,128]{1,0:T(8,128)S(1)}, f32[128,128]{1,0:T(8,128)}, u32[]{:S(2)}) copy-start(f32[128,128]{1,0:T(8,128)} %copy-done.14) | copy-start | bytes 196612
  107.8 13.1 %all-to-all-start.4 = ((f32[8,32,128]{2,1,0:T(8,128)}), f32[8,32,128]{2,1,0:T(8,128)S(1)}, u32[]{:S(2)}, u32[]{:S(2)}) async-start(f32[8,32,128]{2,1,0:T(8,128)} %sum.1), calls=%async_computation.4 | async-start | bytes 262144 | tf_op jit(solution)/shard_map/all_to_all | solution.py:714
  120.9 7.7 %copy-start.18 = (f32[384,128]{1,0:T(8,128)S(1)}, f32[384,128]{1,0:T(8,128)}, u32[]{:S(2)}) copy-start(f32[384,128]{1,0:T(8,128)} %get-tuple-element.79.field_ref.refs_8_) | copy-start | bytes 589828
  126.4 5.4 %collective-permute-start.12 = (f32[128,128]{1,0:T(8,128)S(1)}, f32[128,128]{1,0:T(8,128)S(1)}, u32[]{:S(2)}, u32[]{:S(2)}) collective-permute-start(f32[128,128]{1,0:T(8,128)S(1)} %get-tuple-element.90), channel_id=1, source_target_pairs={{0,3},{1,0},{2,1},{3,2},{4,7},{5,4},{6,5},{7,6},{8,11},{9,8},{10,9... | collective-permute-start | bytes 196616 | tf_op jit(solution)/shard_map/ppermute | solution.py:648
  127.4 4.6 %collective-permute-start.13 = (f32[128,128]{1,0:T(8,128)S(1)}, f32[128,128]{1,0:T(8,128)S(1)}, u32[]{:S(2)}, u32[]{:S(2)}) collective-permute-start(f32[128,128]{1,0:T(8,128)S(1)} %get-tuple-element.91), channel_id=1, source_target_pairs={{0,2},{1,3},{2,0},{3,1},{4,6},{5,7},{6,4},{7,5},{8,10},{9,11},{10,... | collective-permute-start | bytes 196616 | tf_op jit(solution)/shard_map/ppermute | solution.py:648
  128.6 4.6 %collective-permute-start.14 = (f32[128,128]{1,0:T(8,128)S(1)}, f32[128,128]{1,0:T(8,128)S(1)}, u32[]{:S(2)}, u32[]{:S(2)}) collective-permute-start(f32[128,128]{1,0:T(8,128)S(1)} %get-tuple-element.92), channel_id=1, source_target_pairs={{0,1},{1,2},{2,3},{3,0},{4,5},{5,6},{6,7},{7,4},{8,9},{9,10},{10,1... | collective-permute-start | bytes 196616 | tf_op jit(solution)/shard_map/ppermute | solution.py:648
  128.6 4.6 %copy-start.6 = (f32[512,128]{1,0:T(8,128)S(1)}, f32[512,128]{1,0:T(8,128)}, u32[]{:S(2)}) copy-start(f32[512,128]{1,0:T(8,128)} %get-tuple-element.88.bubble_ref) | copy-start | bytes 786436

commit v8 on v7

--- a/solution.py
+++ b/solution.py
@@ -144,7 +144,7 @@
     ]
     for copy in copies:
         copy.start()
-    for copy in copies:
+    for copy in copies[:2]:
         copy.wait()
     modes = load_ref.shape[0] // CASES
     dofs = near_sum_ref.shape[0] // CASES
@@ -153,6 +153,8 @@
             [jnp.transpose(dot_high(inverse_ref[t], coupling_ref[t], TN)) for t in range(KINDS)], axis=0
         )
     )
+    for copy in copies[2:]:
+        copy.wait()
     kind = kind_ref[...]
     kind2 = jnp.concatenate([kind, kind], axis=1)
     for k in range(0, CASES, 2):
@@ -318,7 +320,8 @@
     if last:
         case_ref, gram_ref, near_values, turned_near, turned_far = rest[:5]
         images, rest = rest[5 : 5 + groups], rest[5 + groups :]
-        image_ref, copies_ref, turned_ref, near_part, slot_ref, slot_part, far_values = rest
+        image_ref, copies_ref, own_ref = rest[:3]
+        messages, (near_part, slot_ref, slot_part, far_values, turned_ref) = rest[3 : 2 + groups], rest[2 + groups :]
     else:
         meta_ref, image_ref, far_values, pay_ref, near_part, slot_ref, slot_part = rest
     asked = asked_ref[...]
@@ -336,10 +339,21 @@
     image = image + slots_to_ports(slot_part, asked_hot)
     image_ref[...] = image
     if last:
-        gram = add_products(LANES, images, [image_ref], [3 * groups * CASES], case_ref[0], gram_ref[...])
+        total = groups * CASES
+        gram = add_products(
+            LANES, images, [images[0], image_ref], [2 * total, 3 * total], case_ref[0], gram_ref[...]
+        )
         for p in range(copies_ref.shape[0]):
             copies_ref[p] = gram
         turned_rows(near_values, far_values, where_ref, turned_near, turned_far, turned_ref)
+        rows, part = image.shape[0], own_ref.shape[0]
+        for h in range(groups):
+            at = pl.multiple_of(lax.rem(case_ref[0] + h, groups) * part, part)
+            if h:
+                messages[h - 1][:rows, :] = image
+                messages[h - 1][rows:, :] = turned_ref[pl.ds(at, part), :]
+            else:
+                own_ref[...] = turned_ref[pl.ds(at, part), :]
     else:
         send_ports(image, asked_hot, port_onehot(meta_ref[...]), pay_ref)
 
@@ -370,29 +384,8 @@
         outs[h][...] = out_ref[pl.ds(at, part), :]
 
 
-def messages_kernel(groups, case_ref, field_ref, turned_ref, own_ref, *rest):
-    messages, (field, turned, sems) = rest[: groups - 1], rest[groups - 1 :]
-    rows = field_ref.shape[0]
-    part = own_ref.shape[0]
-    fetches = [
-        pltpu.make_async_copy(turned_ref, turned, sems.at[0]),
-        pltpu.make_async_copy(field_ref, field, sems.at[groups]),
-    ]
-    for fetch in fetches:
-        fetch.start()
-    for fetch in fetches:
-        fetch.wait()
-    copies = []
-    for h in range(groups):
-        at = pl.multiple_of(lax.rem(case_ref[0] + h, groups) * part, part)
-        target = messages[h - 1].at[pl.ds(rows, part), :] if h else own_ref
-        copies.append(pltpu.make_async_copy(turned.at[pl.ds(at, part), :], target, sems.at[h]))
-        if h:
-            copies.append(pltpu.make_async_copy(field, messages[h - 1].at[pl.ds(0, rows), :], sems.at[groups + h]))
-    for copy in copies:
-        copy.start()
-    for copy in copies:
-        copy.wait()
+def pass_kernel(*refs):
+    pass
 
 
 def add_products(lanes, lefts, rights, first, case, out):
@@ -426,10 +419,8 @@
 
 
 def gram_kernel(groups, case_ref, gram_ref, *refs):
-    base, image, out_ref = refs[:groups], refs[groups : 2 * groups], refs[2 * groups]
-    total = groups * CASES
-    out = add_products(LANES, base, [image[0]], [total], case_ref[0], gram_ref[...])
-    out_ref[...] = add_products(LANES, image, [image[0]], [2 * total], case_ref[0], out)
+    base, image_ref, out_ref = refs[:groups], refs[groups], refs[groups + 1]
+    out_ref[...] = add_products(LANES, base, [image_ref], [groups * CASES], case_ref[0], gram_ref[...])
 
 
 def sum_kernel(in_ref, out_ref):
@@ -568,7 +559,6 @@
     results = [(pltpu.HBM if far else jax.ShapeDtypeStruct)(shape, dtype) for shape, dtype, far in outs]
     vmem = pl.BlockSpec(memory_space=pltpu.VMEM)
     far_spec = pl.BlockSpec(memory_space=pltpu.HBM)
-    copies_only = name == "messages"
 
     def run(*args):
         specs = [
@@ -581,7 +571,7 @@
             kernel,
             out_shape=results,
             in_specs=specs,
-            out_specs=[far_spec if copies_only else vmem] * len(outs),
+            out_specs=[vmem] * len(outs),
             scratch_shapes=[pltpu.VMEM(*shape) if isinstance(shape[0], tuple) else pltpu.VMEM(shape, F32) for shape in scratch]
             + ([pltpu.SemaphoreType.DMA((sems,) if sems > 1 else ())] if sems else []),
             compiler_params=pltpu.CompilerParams(vmem_limit_bytes=limit << 20),
@@ -682,14 +672,15 @@
     turned0_all = to_cases(messages)
     image_inner, image_near = inner(image)
     (gram,) = call(functools.partial(gram_kernel, groups), gram_of, name="gram", smem=(0,))(
-        case, gram, base, *base_all, image, *image_all
+        case, gram, base, *base_all, image
     )
     arrived, *turned0_all = lax.optimization_barrier((arrived, *turned0_all))
     minor = lax.axis_size("py")
-    second, copies, turned1 = call(
+    second, copies, turned1, *messages = call(
         functools.partial(image_kernel, parts, groups, True),
-        [field_of, ((groups * minor, cases, LANES), F32, True), bubble_of],
-        [(rows, comps)] + slot_scratch + [(rows, comps)],
+        [field_of, ((groups * minor, cases, LANES), F32, True), part_of]
+        + [((rows + part, comps), F32, True)] * (groups - 1),
+        [(rows, comps)] + slot_scratch + [(rows, comps), (bubbles, comps)],
         "second",
         smem=(6,),
     )(
@@ -697,16 +688,15 @@
         image, *image_all,
     )
     copies = lax.all_to_all(copies, ("case", "py"), split_axis=0, concat_axis=0)
-    turned1, *messages = call(
-        functools.partial(messages_kernel, groups),
-        [part_of] + [((rows + part, comps), F32, True)] * (groups - 1),
-        [(rows, ports), (bubbles, comps)],
-        "messages",
-        flops=10**9,
-        smem=(0,),
-        hbm=(1, 2),
-        sems=2 * groups,
-    )(case, second, turned1)
+    messages = pl.pallas_call(
+        pass_kernel,
+        out_shape=[pltpu.HBM(m.shape, m.dtype) for m in messages],
+        in_specs=[pl.BlockSpec(memory_space=pltpu.HBM)] * len(messages),
+        out_specs=[pl.BlockSpec(memory_space=pltpu.HBM)] * len(messages),
+        input_output_aliases={i: i for i in range(len(messages))},
+        cost_estimate=pl.CostEstimate(flops=10**9, bytes_accessed=1 << 20, transcendentals=0),
+        name="pass_on",
+    )(*messages)
     both1 = to_cases(messages)
     (copies,) = call(sum_kernel, [((parts // minor, groups * cases, LANES), F32, False)], name="sum")(
         copies.reshape(groups, minor, cases, LANES)

time: 135 us -> 137 us (1.015)
  waiting for transfers between devices: 21.7 us -> 24.9 us
  Pallas kernels: 36.2 us -> 33.4 us
    pallas_call x15, Pallas kernels: 36.2 us -> 33.4 us  [the longest x14 33.4 us: run(): pl.pallas_call(kernel, out_shape=results, in_specs=specs, out_specs=[vmem...]
    all_to_all x1, waiting for transfers between devices: 3.46 us -> 5.61 us  [local(): copies = lax.all_to_all(copies, ('case', 'py'), split_axis=0, concat_axis=0)]
    ppermute x15, starting transfers between devices: 17.5 us -> 18.9 us  [to_cases(): lax.ppermute(message, 'case', [(k, (k + h) % groups) for k in range(group...]
    unnamed x46 -> x52, local copies, waits for them, and re-layouts: 1.96 us -> 2.87 us
  transfers between devices with their start and end apart: 19 -> 19, of which waited for: 9 -> 9; matrix products, arithmetic and copies ran while one was open for 0% -> 0% of each run, Pallas kernels for 13% -> 10%
where the time goes in v8:
time: 137 us; the launch traced here: 136 us
  starting transfers between devices  48.1 us (35%)
  Pallas kernels  33.4 us (24%)
  blocking collectives  26.4 us (19%)
  waiting for transfers between devices  24.9 us (18%)
  local copies, waits for them, and re-layouts  2.87 us (2%)
    pallas_call x14, Pallas kernels, run(): pl.pallas_call(kernel, out_shape=results, in_specs=specs, out_specs=[vmem...  33.4 us
    all_to_all x1, blocking collectives, exchange(): lax.all_to_all(rows.reshape(parts, 1, -1), PLANE, split_axis=0, concat_ax...  26.4 us
    ppermute x15, starting transfers between devices, to_cases(): lax.ppermute(message, 'case', [(k, (k + h) % groups) for k in range(group...  18.9 us
    all_to_all x2, starting transfers between devices, exchange(): lax.all_to_all(rows.reshape(parts, 1, -1), PLANE, split_axis=0, concat_ax...  13.2 us
    ppermute x15, waiting for transfers between devices, to_cases(): lax.ppermute(message, 'case', [(k, (k + h) % groups) for k in range(group...  11.2 us
    all_to_all x1, starting transfers between devices, local(): copies = lax.all_to_all(copies, ('case', 'py'), split_axis=0, concat_axis=0)  8.5 us
    all_to_all x1, starting transfers between devices, local(): copies = lax.all_to_all(copies, 'px', split_axis=0, concat_axis=0)  7.41 us
    all_to_all x1, waiting for transfers between devices, local(): copies = lax.all_to_all(copies, ('case', 'py'), split_axis=0, concat_axis=0)  5.61 us
  transfers between devices with their start and end apart: 19, of which 9 were waited for; matrix products, arithmetic and copies ran while one was open for 0% of the time, Pallas kernels for 10%

profile of v8, /device:TPU:1, one launch (start us, length us, event | category | flops | bytes accessed | tf_op | source)
XLA Modules:
  0.0 136.4 jit_solution(16143882496776860963)
XLA Ops:
  0.6 3.4 %condense.1 = (f32[640,128]{1,0:T(8,128)S(1)}, f32[384,128]{1,0:T(8,128)}, f32[64,128]{1,0:T(8,128)S(1)}, f32[8,128]{1,0:T(8,128)S(1)}) custom-call(s32[1,128]{1,0:T(1,128)} %bitcast.30, f32[1,128]{1,0:T(1,128)} %bitcast.31, s32[1,128]{1,0:T(1,128)} %bitcast.32, s32[1,128]{1,0:T(1,128)} %bitcast.33, s32[1,128]{1,0:T(1,128)} %bitcast.34, ...), custom_call_target="tpu_custom_call" | custom-call | bytes 592384 | tf_op jit(solution)/shard_map/condense/pallas_call | solution.py:570
  4.0 0.0 copy-start.7
  4.0 0.0 copy-start.8
  4.0 26.4 %all_to_all.25 = f32[64,1,1280]{2,1,0:T(1,128)S(1)} all-to-all(f32[64,1,1280]{2,1,0:T(1,128)S(1)} %bitcast.23), channel_id=1, replica_groups=mesh['px'=8,'py'=8,'case'=4] {'px','py'}, dimensions={0} | all-to-all | bytes 655360 | tf_op jit(solution)/shard_map/all_to_all | solution.py:586
  30.4 1.4 %rhs.1 = (f32[384,128]{1,0:T(8,128)}, f32[1152,128]{1,0:T(8,128)}, f32[64,128]{1,0:T(8,128)S(1)}) custom-call(f32[640,128]{1,0:T(8,128)S(1)} %bitcast.21, f32[384,128]{1,0:T(8,128)S(1)} %copy-done.8, f32[384,128]{1,0:T(8,128)S(1)} %bitcast.28, f32[64,128]{1,0:T(8,128)S(1)} %get-tuple-element.52.meta_ref.rest_0_), custom_call_target="tpu_custom_call" | custom-call | bytes 753664 | tf_op jit(solution)/shard_map/rhs/pallas_call | solution.py:570
  31.8 6.3 %all-to-all-start.1 = ((f32[64,1,2304]{2,1,0:T(1,128)}), f32[64,1,2304]{2,1,0:T(1,128)S(1)}, u32[]{:S(2)}, u32[]{:S(2)}) async-start(f32[64,1,2304]{2,1,0:T(1,128)} %bitcast.11), calls=%async_computation.1 | async-start | bytes 1179648 | tf_op jit(solution)/shard_map/all_to_all | solution.py:586
  38.2 1.3 collective-permute-start.2
  39.5 2.4 %collective-permute-start.1 = (f32[384,128]{1,0:T(8,128)S(1)}, f32[384,128]{1,0:T(8,128)S(1)}, u32[]{:S(2)}, u32[]{:S(2)}) collective-permute-start(f32[384,128]{1,0:T(8,128)S(1)} %copy-done), channel_id=1, source_target_pairs={{0,2},{1,3},{2,0},{3,1},{4,6},{5,7},{6,4},{7,5},{8,10},{9,11},{10,... | collective-permute-start | bytes 589832 | tf_op jit(solution)/shard_map/ppermute | solution.py:638
  41.9 1.2 collective-permute-start
  43.1 2.6 %tables.1 = (bf16[384,144]{1,0:T(8,128)(2,1)S(1)}, bf16[384,144]{1,0:T(8,128)(2,1)S(1)}, bf16[384,144]{1,0:T(8,128)(2,1)S(1)}, bf16[384,144]{1,0:T(8,128)(2,1)S(...) custom-call(f32[8,128]{1,0:T(8,128)S(1)} %get-tuple-element.57.where_ref, ...), custom_call_target="tpu_custom_call" | custom-call | flops 1000000000 | bytes 888832 | tf_op jit(solution)/shard_map/tables/pallas_call | solution.py:570
  45.7 1.6 %inner.2 = (f32[384,128]{1,0:T(8,128)S(1)}, f32[384,128]{1,0:T(8,128)S(1)}) custom-call(f32[384,128]{1,0:T(8,128)S(1)} %copy-done, f32[64,128]{1,0:T(8,128)S(1)} %get-tuple-element.56.asked_ref, f32[8,128]{1,0:T(8,128)S(1)} %get-tuple-element.57.where_ref, bf16[384,144]{1,0:T(8,128)(2,1)S(1)} %get-tuple-element.58.near_near, ...), custom_call_target="tpu_custom_call" | custom-call | flops 1000000000 | bytes 454656 | tf_op jit(solution)/shard_map/inner/pallas_call | solution.py:570
  47.4 3.3 %collective-permute-done.1.refs_2_ = f32[384,128]{1,0:T(8,128)S(1)} collective-permute-done((f32[384,128]{1,0:T(8,128)S(1)}, f32[384,128]{1,0:T(8,128)S(1)}, u32[]{:S(2)}, u32[]{:S(2)}) %collective-permute-start.1) | collective-permute-done | bytes 196640 | tf_op jit(solution)/shard_map/ppermute | solution.py:638
  50.7 1.5 %base_gram.1.gram_ref = f32[8,128]{1,0:T(8,128)S(1)} custom-call(s32[1]{0:T(128)} %bitcast.case_ref.rest_0_, f32[384,128]{1,0:T(8,128)S(1)} %copy-done, f32[384,128]{1,0:T(8,128)S(1)} %collective-permute-done.refs_1_, f32[384,128]{1,0:T(8,128)S(1)} %collective-permute-done.1.refs_2_, f32[384,128]{1,0:T(8,128)S(1)} %collective-permute-done.2.refs_3_), custom_call_target="tpu_custom_call" | custom-call | bytes 786436 | tf_op jit(solution)/shard_map/base_gram/pallas_call | solution.py:570
  52.2 4.5 %all-to-all-done.1 = f32[64,1,2304]{2,1,0:T(1,128)S(1)} async-done(((f32[64,1,2304]{2,1,0:T(1,128)}), f32[64,1,2304]{2,1,0:T(1,128)S(1)}, u32[]{:S(2)}, u32[]{:S(2)}) %all-to-all-start.1) | async-done | bytes 589856 | tf_op jit(solution)/shard_map/all_to_all | solution.py:586
  56.7 2.7 %image.1 = (f32[384,128]{1,0:T(8,128)S(1)}, f32[384,128]{1,0:T(8,128)S(1)}, f32[1152,128]{1,0:T(8,128)}) custom-call(f32[1152,128]{1,0:T(8,128)S(1)} %bitcast.19, f32[384,128]{1,0:T(8,128)S(1)} %get-tuple-element.60.inner_ref, f32[64,128]{1,0:T(8,128)S(1)} %get-tuple-element.56.asked_ref, f32[8,128]{1,0:T(8,128)S(1)} %get-tuple-element.57.where_ref, ...), custom_call_target="tpu_custom_call" | custom-call | bytes 1077248 | tf_op jit(solution)/shard_map/image/pallas_call | solution.py:570
  59.4 6.9 %all-to-all-start.2 = ((f32[64,1,2304]{2,1,0:T(1,128)}), f32[64,1,2304]{2,1,0:T(1,128)S(1)}, u32[]{:S(2)}, u32[]{:S(2)}) async-start(f32[64,1,2304]{2,1,0:T(1,128)} %bitcast.13), calls=%async_computation.2 | async-start | bytes 1179648 | tf_op jit(solution)/shard_map/all_to_all | solution.py:586
  66.3 1.1 collective-permute-start.8
  67.5 2.4 %collective-permute-start.7 = (f32[384,128]{1,0:T(8,128)S(1)}, f32[384,128]{1,0:T(8,128)S(1)}, u32[]{:S(2)}, u32[]{:S(2)}) collective-permute-start(f32[384,128]{1,0:T(8,128)S(1)} %get-tuple-element.72.field_ref.refs_4_.rest_5_), channel_id=1, source_target_pairs={{0,2},{1,3},{2,0},{3,1},{4,6},{5,7},{6,4},{7,5},{8,10},{9,11},{10,... | collective-permute-start | bytes 589832 | tf_op jit(solution)/shard_map/ppermute | solution.py:638
  69.8 1.2 collective-permute-start.6
  71.0 0.9 copy-done.24
  71.9 1.4 %turned.1 = (f32[128,128]{1,0:T(8,128)}, f32[128,128]{1,0:T(8,128)}, f32[128,128]{1,0:T(8,128)}, f32[128,128]{1,0:T(8,128)}) custom-call(s32[1]{0:T(128)} %bitcast.case_ref.rest_0_, f32[384,128]{1,0:T(8,128)S(1)} %copy-done.24, f32[384,128]{1,0:T(8,128)S(1)} %get-tuple-element.65.far_values, f32[8,128]{1,0:T(8,128)S(1)} %get-tuple-element.57.where_ref, ...), custom_call_target="tpu_custom_call" | custom-call | flops 1000000000 | bytes 692228 | tf_op jit(solution)/shard_map/turned/pallas_call | solution.py:570
  73.3 0.0 collective-permute-start.3
  73.4 2.1 %collective-permute-start.4 = (f32[128,128]{1,0:T(8,128)}, f32[128,128]{1,0:T(8,128)S(1)}, u32[]{:S(2)}, u32[]{:S(2)}) collective-permute-start(f32[128,128]{1,0:T(8,128)} %get-tuple-element.69), channel_id=1, source_target_pairs={{0,2},{1,3},{2,0},{3,1},{4,6},{5,7},{6,4},{7,5},{8,10},{9,11},{10,... | collective-permute-start | bytes 196616 | tf_op jit(solution)/shard_map/ppermute | solution.py:638
  75.4 1.5 %gram.1.rest_1_ = f32[8,128]{1,0:T(8,128)S(1)} custom-call(s32[1]{0:T(128)} %bitcast.case_ref.rest_0_, f32[8,128]{1,0:T(8,128)S(1)} %base_gram.1.gram_ref, f32[384,128]{1,0:T(8,128)S(1)} %copy-done, f32[384,128]{1,0:T(8,128)S(1)} %collective-permute-done.refs_1_, f32[384,128]{1,0:T(8,128)S(1)} %collective-permute-done.1.refs_2_, ...), custom_call_target="tpu_custom_call" | custom-call | bytes 987140 | tf_op jit(solution)/shard_map/gram/pallas_call | solution.py:570
  76.9 3.3 %collective-permute-done.3.rest_1_ = f32[128,128]{1,0:T(8,128)S(1)} collective-permute-done((f32[128,128]{1,0:T(8,128)}, f32[128,128]{1,0:T(8,128)S(1)}, u32[]{:S(2)}, u32[]{:S(2)}) %collective-permute-start.3) | collective-permute-done | bytes 65568 | tf_op jit(solution)/shard_map/ppermute | solution.py:638
  80.3 0.6 copy-done.10
  80.9 1.4 collective-permute-start.5
  82.3 1.6 %inner.3 = (f32[384,128]{1,0:T(8,128)S(1)}, f32[384,128]{1,0:T(8,128)S(1)}) custom-call(f32[384,128]{1,0:T(8,128)S(1)} %get-tuple-element.72.field_ref.refs_4_.rest_5_, f32[64,128]{1,0:T(8,128)S(1)} %get-tuple-element.56.asked_ref, f32[8,128]{1,0:T(8,128)S(1)} %get-tuple-element.57.where_ref, bf16[384,144]{1,0:T(8,128)(2,1)S(1)} %copy-done.20, ...), custom_call_target="tpu_custom_call" | custom-call | flops 1000000000 | bytes 454656 | tf_op jit(solution)/shard_map/inner/pallas_call | solution.py:570
  83.9 0.6 copy-done.12
  84.6 1.4 %collective-permute-done.5.rest_3_ = f32[128,128]{1,0:T(8,128)S(1)} collective-permute-done((f32[128,128]{1,0:T(8,128)S(1)}, f32[128,128]{1,0:T(8,128)S(1)}, u32[]{:S(2)}, u32[]{:S(2)}) %collective-permute-start.5) | collective-permute-done | bytes 65568 | tf_op jit(solution)/shard_map/ppermute | solution.py:638
  86.0 0.6 copy-done.14
  86.6 5.5 %second.1 = (f32[384,128]{1,0:T(8,128)}, f32[32,8,128]{2,1,0:T(8,128)}, f32[128,128]{1,0:T(8,128)}, f32[512,128]{1,0:T(8,128)}, f32[512,128]{1,0:T(8,128)}, /*index=5*/f32[512,128]{1,0:T(8,128)}) custom-call(f32[1152,128]{1,0:T(8,128)S(1)} %bitcast.20, f32[384,128]{1,0:T(8,128)S(1)} %get-tuple-element.73.inner_ref, ...), custom_call_target="tpu_custom_call" | custom-call | bytes 2326532 | tf_op jit(solution)/shard_map/second/pallas_call | solution.py:570
  92.1 8.5 %all-to-all-start.3 = ((f32[32,8,128]{2,1,0:T(8,128)}), f32[32,8,128]{2,1,0:T(8,128)S(1)}, u32[]{:S(2)}, u32[]{:S(2)}) async-start(f32[32,8,128]{2,1,0:T(8,128)} %get-tuple-element.76), calls=%async_computation.3 | async-start | bytes 262144 | tf_op jit(solution)/shard_map/all_to_all | solution.py:690
  100.6 2.6 %collective-permute-start.9 = (f32[512,128]{1,0:T(8,128)}, f32[512,128]{1,0:T(8,128)S(1)}, u32[]{:S(2)}, u32[]{:S(2)}) collective-permute-start(f32[512,128]{1,0:T(8,128)} %get-tuple-element.85), channel_id=1, source_target_pairs={{0,3},{1,0},{2,1},{3,2},{4,7},{5,4},{6,5},{7,6},{8,11},{9,8},{10,9... | collective-permute-start | bytes 786440 | tf_op jit(solution)/shard_map/ppermute | solution.py:638
  103.2 0.5 collective-permute-start.10
  103.7 0.6 collective-permute-start.11
  104.3 5.6 %all-to-all-done.3 = f32[32,8,128]{2,1,0:T(8,128)S(1)} async-done(((f32[32,8,128]{2,1,0:T(8,128)}), f32[32,8,128]{2,1,0:T(8,128)S(1)}, u32[]{:S(2)}, u32[]{:S(2)}) %all-to-all-start.3) | async-done | bytes 131104 | tf_op jit(solution)/shard_map/all_to_all | solution.py:690
  109.9 0.7 sum.1
  110.6 7.4 %all-to-all-start.4 = ((f32[8,32,128]{2,1,0:T(8,128)}), f32[8,32,128]{2,1,0:T(8,128)S(1)}, u32[]{:S(2)}, u32[]{:S(2)}) async-start(f32[8,32,128]{2,1,0:T(8,128)} %sum.1), calls=%async_computation.4 | async-start | bytes 262144 | tf_op jit(solution)/shard_map/all_to_all | solution.py:704
  118.0 1.7 %collective-permute-done.11.rest_7_.refs_11_ = f32[512,128]{1,0:T(8,128)S(1)} collective-permute-done((f32[512,128]{1,0:T(8,128)}, f32[512,128]{1,0:T(8,128)S(1)}, u32[]{:S(2)}, u32[]{:S(2)}) %collective-permute-start.11) | collective-permute-done | bytes 262176 | tf_op jit(solution)/shard_map/ppermute | solution.py:638
  119.8 3.5 %all-to-all-done.4.gram_ref = f32[8,32,128]{2,1,0:T(8,128)S(1)} async-done(((f32[8,32,128]{2,1,0:T(8,128)}), f32[8,32,128]{2,1,0:T(8,128)S(1)}, u32[]{:S(2)}, u32[]{:S(2)}) %all-to-all-start.4) | async-done | bytes 131104 | tf_op jit(solution)/shard_map/all_to_all | solution.py:704
  123.3 5.5 %solve.1 = (f32[64,8,128]{2,1,0:T(8,128)S(1)}, f32[128,128]{1,0:T(8,128)S(1)}, f32[128,128]{1,0:T(8,128)S(1)}, f32[128,128]{1,0:T(8,128)S(1)}, f32[128,128]{1,0:T(8,128)S(1)}) custom-call(s32[1]{0:T(128)} %bitcast.case_ref.rest_0_, f32[8,32,128]{2,1,0:T(8,128)S(1)} %all-to-all-done.4.gram_ref, f32[128,128]{1,0:T(8,128)S(1)} %copy-done.9, ...), custom_call_target="tpu_custom_call" | custom-call | bytes 1245188 | tf_op jit(solution)/shard_map/solve/pallas_call | solution.py:570
  128.8 1.0 collective-permute-start.12
  129.8 1.2 collective-permute-start.13
  131.1 3.2 %ports.1 = (f32[384,128]{1,0:T(8,128)}, f32[384,128]{1,0:T(8,128)}) custom-call(f32[64,8,128]{2,1,0:T(8,128)S(1)} %get-tuple-element.88.coef, f32[384,128]{1,0:T(8,128)S(1)} %copy-done, f32[384,128]{1,0:T(8,128)S(1)} %collective-permute-done.refs_1_, f32[384,128]{1,0:T(8,128)S(1)} %collective-permute-done.1.refs_2_, ...), custom_call_target="tpu_custom_call" | custom-call | flops 1000000000 | bytes 2818048 | tf_op jit(solution)/shard_map/ports/pallas_call | solution.py:570
  134.3 0.1 collective-permute-done.13.refs_2_
  134.5 1.2 collective-permute-done.14.refs_3_
  135.7 0.7 join.1
  (58 shorter events, 0.1 us)
Async XLA Ops:
  4.0 26.4 %copy-start.7 = (f32[48,8,128]{2,1,0:T(8,128)S(1)}, f32[48,8,128]{2,1,0:T(8,128)}, u32[]{:S(2)}) copy-start(f32[48,8,128]{2,1,0:T(8,128)} %param.16) | copy-start | bytes 589828
  4.0 26.4 %copy-start.8 = (f32[384,128]{1,0:T(8,128)S(1)}, f32[384,128]{1,0:T(8,128)}, u32[]{:S(2)}) copy-start(f32[384,128]{1,0:T(8,128)} %get-tuple-element.51.near_sum_ref) | copy-start | bytes 589828
  30.4 12.7 %copy-start.17 = (f32[8,96,96]{2,1,0:T(8,128)S(1)}, f32[8,96,96]{2,1,0:T(8,128)}, u32[]{:S(2)}) copy-start(f32[8,96,96]{2,1,0:T(8,128)} %block_ref.1) | copy-start | bytes 884740
  31.8 6.3 %copy-start = (f32[384,128]{1,0:T(8,128)S(1)}, f32[384,128]{1,0:T(8,128)}, u32[]{:S(2)}) copy-start(f32[384,128]{1,0:T(8,128)} %get-tuple-element.54.refs_0_.field_ref) | copy-start | bytes 589828
  31.8 11.3 %copy-start.3 = (f32[64,8,128]{2,1,0:T(8,128)S(1)}, f32[64,8,128]{2,1,0:T(8,128)}, u32[]{:S(2)}) copy-start(f32[64,8,128]{2,1,0:T(8,128)} %param.15) | copy-start | bytes 786436
  31.8 11.3 %copy-start.4 = (f32[8,64,64]{2,1,0:T(8,128)S(1)}, f32[8,64,64]{2,1,0:T(8,128)}, u32[]{:S(2)}) copy-start(f32[8,64,64]{2,1,0:T(8,128)} %inverse_ref.1) | copy-start | bytes 393220
  31.8 11.3 %copy-start.5 = (f32[8,96,64]{1,2,0:T(8,128)S(1)}, f32[8,96,64]{1,2,0:T(8,128)}, u32[]{:S(2)}) copy-start(f32[8,96,64]{1,2,0:T(8,128)} %param.18) | copy-start | bytes 589828
  31.8 24.9 %all-to-all-start.1 = ((f32[64,1,2304]{2,1,0:T(1,128)}), f32[64,1,2304]{2,1,0:T(1,128)S(1)}, u32[]{:S(2)}, u32[]{:S(2)}) async-start(f32[64,1,2304]{2,1,0:T(1,128)} %bitcast.11), calls=%async_computation.1 | async-start | bytes 1179648 | tf_op jit(solution)/shard_map/all_to_all | solution.py:586
  38.2 9.2 %collective-permute-start.2 = (f32[384,128]{1,0:T(8,128)S(1)}, f32[384,128]{1,0:T(8,128)S(1)}, u32[]{:S(2)}, u32[]{:S(2)}) collective-permute-start(f32[384,128]{1,0:T(8,128)S(1)} %copy-done), channel_id=1, source_target_pairs={{0,1},{1,2},{2,3},{3,0},{4,5},{5,6},{6,7},{7,4},{8,9},{9,10},{10,1... | collective-permute-start | bytes 589832 | tf_op jit(solution)/shard_map/ppermute | solution.py:638
  39.5 11.2 %collective-permute-start.1 = (f32[384,128]{1,0:T(8,128)S(1)}, f32[384,128]{1,0:T(8,128)S(1)}, u32[]{:S(2)}, u32[]{:S(2)}) collective-permute-start(f32[384,128]{1,0:T(8,128)S(1)} %copy-done), channel_id=1, source_target_pairs={{0,2},{1,3},{2,0},{3,1},{4,6},{5,7},{6,4},{7,5},{8,10},{9,11},{10,... | collective-permute-start | bytes 589832 | tf_op jit(solution)/shard_map/ppermute | solution.py:638
  41.9 8.8 %collective-permute-start = (f32[384,128]{1,0:T(8,128)S(1)}, f32[384,128]{1,0:T(8,128)S(1)}, u32[]{:S(2)}, u32[]{:S(2)}) collective-permute-start(f32[384,128]{1,0:T(8,128)S(1)} %copy-done), channel_id=1, source_target_pairs={{0,3},{1,0},{2,1},{3,2},{4,7},{5,4},{6,5},{7,6},{8,11},{9,8},{10,9... | collective-permute-start | bytes 589832 | tf_op jit(solution)/shard_map/ppermute | solution.py:638
  45.7 1.7 %copy-start.19 = (bf16[384,144]{1,0:T(8,128)(2,1)}, bf16[384,144]{1,0:T(8,128)(2,1)S(1)}, u32[]{:S(2)}) copy-start(bf16[384,144]{1,0:T(8,128)(2,1)S(1)} %get-tuple-element.58.near_near) | copy-start | bytes 331780
  45.7 1.7 %copy-start.21 = (bf16[384,144]{1,0:T(8,128)(2,1)}, bf16[384,144]{1,0:T(8,128)(2,1)S(1)}, u32[]{:S(2)}) copy-start(bf16[384,144]{1,0:T(8,128)(2,1)S(1)} %get-tuple-element.59.far_far) | copy-start | bytes 331780
  47.4 4.9 %copy-start.23 = (f32[384,128]{1,0:T(8,128)}, f32[384,128]{1,0:T(8,128)S(1)}, u32[]{:S(2)}) copy-start(f32[384,128]{1,0:T(8,128)S(1)} %get-tuple-element.64.near_values) | copy-start | bytes 589828
  59.4 11.6 %copy-start.1 = (bf16[512,144]{1,0:T(8,128)(2,1)S(1)}, bf16[512,144]{1,0:T(8,128)(2,1)}, u32[]{:S(2)}) copy-start(bf16[512,144]{1,0:T(8,128)(2,1)} %get-tuple-element.66.turned_near.rest_3_) | copy-start | bytes 442372
  59.4 11.6 %copy-start.2 = (bf16[512,144]{1,0:T(8,128)(2,1)S(1)}, bf16[512,144]{1,0:T(8,128)(2,1)}, u32[]{:S(2)}) copy-start(bf16[512,144]{1,0:T(8,128)(2,1)} %get-tuple-element.67.turned_far.rest_4_) | copy-start | bytes 442372
  59.4 27.2 %all-to-all-start.2 = ((f32[64,1,2304]{2,1,0:T(1,128)}), f32[64,1,2304]{2,1,0:T(1,128)S(1)}, u32[]{:S(2)}, u32[]{:S(2)}) async-start(f32[64,1,2304]{2,1,0:T(1,128)} %bitcast.13), calls=%async_computation.2 | async-start | bytes 1179648 | tf_op jit(solution)/shard_map/all_to_all | solution.py:586
  66.3 20.3 %collective-permute-start.8 = (f32[384,128]{1,0:T(8,128)S(1)}, f32[384,128]{1,0:T(8,128)S(1)}, u32[]{:S(2)}, u32[]{:S(2)}) collective-permute-start(f32[384,128]{1,0:T(8,128)S(1)} %get-tuple-element.72.field_ref.refs_4_.rest_5_), channel_id=1, source_target_pairs={{0,1},{1,2},{2,3},{3,0},{4,5},{5,6},{6,7},{7,4},{8,9},{9,10},{10,1... | collective-permute-start | bytes 589832 | tf_op jit(solution)/shard_map/ppermute | solution.py:638
  67.5 19.2 %collective-permute-start.7 = (f32[384,128]{1,0:T(8,128)S(1)}, f32[384,128]{1,0:T(8,128)S(1)}, u32[]{:S(2)}, u32[]{:S(2)}) collective-permute-start(f32[384,128]{1,0:T(8,128)S(1)} %get-tuple-element.72.field_ref.refs_4_.rest_5_), channel_id=1, source_target_pairs={{0,2},{1,3},{2,0},{3,1},{4,6},{5,7},{6,4},{7,5},{8,10},{9,11},{10,... | collective-permute-start | bytes 589832 | tf_op jit(solution)/shard_map/ppermute | solution.py:638
  69.8 16.8 %collective-permute-start.6 = (f32[384,128]{1,0:T(8,128)S(1)}, f32[384,128]{1,0:T(8,128)S(1)}, u32[]{:S(2)}, u32[]{:S(2)}) collective-permute-start(f32[384,128]{1,0:T(8,128)S(1)} %get-tuple-element.72.field_ref.refs_4_.rest_5_), channel_id=1, source_target_pairs={{0,3},{1,0},{2,1},{3,2},{4,7},{5,4},{6,5},{7,6},{8,11},{9,8},{10,9... | collective-permute-start | bytes 589832 | tf_op jit(solution)/shard_map/ppermute | solution.py:638
  71.0 0.9 copy-start.24
  73.3 6.9 %collective-permute-start.3 = (f32[128,128]{1,0:T(8,128)}, f32[128,128]{1,0:T(8,128)S(1)}, u32[]{:S(2)}, u32[]{:S(2)}) collective-permute-start(f32[128,128]{1,0:T(8,128)} %get-tuple-element.68), channel_id=1, source_target_pairs={{0,3},{1,0},{2,1},{3,2},{4,7},{5,4},{6,5},{7,6},{8,11},{9,8},{10,9... | collective-permute-start | bytes 196616 | tf_op jit(solution)/shard_map/ppermute | solution.py:638
  73.3 7.6 %copy-start.25 = (f32[128,128]{1,0:T(8,128)S(1)}, f32[128,128]{1,0:T(8,128)}, u32[]{:S(2)}) copy-start(f32[128,128]{1,0:T(8,128)} %get-tuple-element.70) | copy-start | bytes 196612
  73.3 8.9 %copy-start.20 = (bf16[384,144]{1,0:T(8,128)(2,1)S(1)}, bf16[384,144]{1,0:T(8,128)(2,1)}, u32[]{:S(2)}) copy-start(bf16[384,144]{1,0:T(8,128)(2,1)} %copy-done.19) | copy-start | bytes 331780
  73.3 8.9 %copy-start.22 = (bf16[384,144]{1,0:T(8,128)(2,1)S(1)}, bf16[384,144]{1,0:T(8,128)(2,1)}, u32[]{:S(2)}) copy-start(bf16[384,144]{1,0:T(8,128)(2,1)} %copy-done.21) | copy-start | bytes 331780
  73.4 10.6 %collective-permute-start.4 = (f32[128,128]{1,0:T(8,128)}, f32[128,128]{1,0:T(8,128)S(1)}, u32[]{:S(2)}, u32[]{:S(2)}) collective-permute-start(f32[128,128]{1,0:T(8,128)} %get-tuple-element.69), channel_id=1, source_target_pairs={{0,2},{1,3},{2,0},{3,1},{4,6},{5,7},{6,4},{7,5},{8,10},{9,11},{10,... | collective-permute-start | bytes 196616 | tf_op jit(solution)/shard_map/ppermute | solution.py:638
  80.3 0.6 copy-start.10
  80.9 5.1 %collective-permute-start.5 = (f32[128,128]{1,0:T(8,128)S(1)}, f32[128,128]{1,0:T(8,128)S(1)}, u32[]{:S(2)}, u32[]{:S(2)}) collective-permute-start(f32[128,128]{1,0:T(8,128)S(1)} %copy-done.25), channel_id=1, source_target_pairs={{0,1},{1,2},{2,3},{3,0},{4,5},{5,6},{6,7},{7,4},{8,9},{9,10},{10,1... | collective-permute-start | bytes 196616 | tf_op jit(solution)/shard_map/ppermute | solution.py:638
  83.9 0.6 copy-start.12
  86.0 0.6 copy-start.14
  92.1 17.8 %all-to-all-start.3 = ((f32[32,8,128]{2,1,0:T(8,128)}), f32[32,8,128]{2,1,0:T(8,128)S(1)}, u32[]{:S(2)}, u32[]{:S(2)}) async-start(f32[32,8,128]{2,1,0:T(8,128)} %get-tuple-element.76), calls=%async_computation.3 | async-start | bytes 262144 | tf_op jit(solution)/shard_map/all_to_all | solution.py:690
  100.6 17.4 %collective-permute-start.9 = (f32[512,128]{1,0:T(8,128)}, f32[512,128]{1,0:T(8,128)S(1)}, u32[]{:S(2)}, u32[]{:S(2)}) collective-permute-start(f32[512,128]{1,0:T(8,128)} %get-tuple-element.85), channel_id=1, source_target_pairs={{0,3},{1,0},{2,1},{3,2},{4,7},{5,4},{6,5},{7,6},{8,11},{9,8},{10,9... | collective-permute-start | bytes 786440 | tf_op jit(solution)/shard_map/ppermute | solution.py:638
  103.2 14.8 %collective-permute-start.10 = (f32[512,128]{1,0:T(8,128)}, f32[512,128]{1,0:T(8,128)S(1)}, u32[]{:S(2)}, u32[]{:S(2)}) collective-permute-start(f32[512,128]{1,0:T(8,128)} %get-tuple-element.86), channel_id=1, source_target_pairs={{0,2},{1,3},{2,0},{3,1},{4,6},{5,7},{6,4},{7,5},{8,10},{9,11},{10,... | collective-permute-start | bytes 786440 | tf_op jit(solution)/shard_map/ppermute | solution.py:638
  103.7 16.0 %collective-permute-start.11 = (f32[512,128]{1,0:T(8,128)}, f32[512,128]{1,0:T(8,128)S(1)}, u32[]{:S(2)}, u32[]{:S(2)}) collective-permute-start(f32[512,128]{1,0:T(8,128)} %get-tuple-element.87), channel_id=1, source_target_pairs={{0,1},{1,2},{2,3},{3,0},{4,5},{5,6},{6,7},{7,4},{8,9},{9,10},{10,1... | collective-permute-start | bytes 786440 | tf_op jit(solution)/shard_map/ppermute | solution.py:638
  109.9 13.4 %copy-start.16 = (f32[128,128]{1,0:T(8,128)S(1)}, f32[128,128]{1,0:T(8,128)}, u32[]{:S(2)}) copy-start(f32[128,128]{1,0:T(8,128)} %get-tuple-element.81.rest_4_) | copy-start | bytes 196612
  110.6 12.7 %copy-start.9 = (f32[128,128]{1,0:T(8,128)S(1)}, f32[128,128]{1,0:T(8,128)}, u32[]{:S(2)}) copy-start(f32[128,128]{1,0:T(8,128)} %get-tuple-element.77.rest_0_) | copy-start | bytes 196612
  110.6 12.7 %copy-start.11 = (f32[128,128]{1,0:T(8,128)S(1)}, f32[128,128]{1,0:T(8,128)}, u32[]{:S(2)}) copy-start(f32[128,128]{1,0:T(8,128)} %copy-done.10) | copy-start | bytes 196612
  110.6 12.7 %copy-start.13 = (f32[128,128]{1,0:T(8,128)S(1)}, f32[128,128]{1,0:T(8,128)}, u32[]{:S(2)}) copy-start(f32[128,128]{1,0:T(8,128)} %copy-done.12) | copy-start | bytes 196612
  110.6 12.7 %copy-start.15 = (f32[128,128]{1,0:T(8,128)S(1)}, f32[128,128]{1,0:T(8,128)}, u32[]{:S(2)}) copy-start(f32[128,128]{1,0:T(8,128)} %copy-done.14) | copy-start | bytes 196612
  110.6 12.7 %all-to-all-start.4 = ((f32[8,32,128]{2,1,0:T(8,128)}), f32[8,32,128]{2,1,0:T(8,128)S(1)}, u32[]{:S(2)}, u32[]{:S(2)}) async-start(f32[8,32,128]{2,1,0:T(8,128)} %sum.1), calls=%async_computation.4 | async-start | bytes 262144 | tf_op jit(solution)/shard_map/all_to_all | solution.py:704
  123.3 7.8 %copy-start.18 = (f32[384,128]{1,0:T(8,128)S(1)}, f32[384,128]{1,0:T(8,128)}, u32[]{:S(2)}) copy-start(f32[384,128]{1,0:T(8,128)} %get-tuple-element.89.refs_8_) | copy-start | bytes 589828
  128.8 5.5 %collective-permute-start.12 = (f32[128,128]{1,0:T(8,128)S(1)}, f32[128,128]{1,0:T(8,128)S(1)}, u32[]{:S(2)}, u32[]{:S(2)}) collective-permute-start(f32[128,128]{1,0:T(8,128)S(1)} %get-tuple-element.94), channel_id=1, source_target_pairs={{0,3},{1,0},{2,1},{3,2},{4,7},{5,4},{6,5},{7,6},{8,11},{9,8},{10,9... | collective-permute-start | bytes 196616 | tf_op jit(solution)/shard_map/ppermute | solution.py:638
  129.8 4.6 %collective-permute-start.13 = (f32[128,128]{1,0:T(8,128)S(1)}, f32[128,128]{1,0:T(8,128)S(1)}, u32[]{:S(2)}, u32[]{:S(2)}) collective-permute-start(f32[128,128]{1,0:T(8,128)S(1)} %get-tuple-element.95), channel_id=1, source_target_pairs={{0,2},{1,3},{2,0},{3,1},{4,6},{5,7},{6,4},{7,5},{8,10},{9,11},{10,... | collective-permute-start | bytes 196616 | tf_op jit(solution)/shard_map/ppermute | solution.py:638
  131.1 4.6 %collective-permute-start.14 = (f32[128,128]{1,0:T(8,128)S(1)}, f32[128,128]{1,0:T(8,128)S(1)}, u32[]{:S(2)}, u32[]{:S(2)}) collective-permute-start(f32[128,128]{1,0:T(8,128)S(1)} %get-tuple-element.96), channel_id=1, source_target_pairs={{0,1},{1,2},{2,3},{3,0},{4,5},{5,6},{6,7},{7,4},{8,9},{9,10},{10,1... | collective-permute-start | bytes 196616 | tf_op jit(solution)/shard_map/ppermute | solution.py:638
  131.1 4.6 %copy-start.6 = (f32[512,128]{1,0:T(8,128)S(1)}, f32[512,128]{1,0:T(8,128)}, u32[]{:S(2)}) copy-start(f32[512,128]{1,0:T(8,128)} %get-tuple-element.92.bubble_ref) | copy-start | bytes 786436

commit v9 on v8

--- a/solution.py
+++ b/solution.py
@@ -318,10 +318,13 @@
     near_far, far_near, *rest,
 ):
     if last:
-        case_ref, gram_ref, near_values, turned_near, turned_far = rest[:5]
+        case_ref, gram_ref, turned_near, turned_far, turned0_hbm = rest[:5]
         images, rest = rest[5 : 5 + groups], rest[5 + groups :]
         image_ref, copies_ref, own_ref = rest[:3]
-        messages, (near_part, slot_ref, slot_part, far_values, turned_ref) = rest[3 : 2 + groups], rest[2 + groups :]
+        messages = rest[3 : 2 + groups]
+        near_part, slot_ref, slot_part, far_values, near_values, turned_ref, turned0_ref, sem = rest[2 + groups :]
+        fetch = pltpu.make_async_copy(turned0_hbm, turned0_ref, sem)
+        fetch.start()
     else:
         meta_ref, image_ref, far_values, pay_ref, near_part, slot_ref, slot_part = rest
     asked = asked_ref[...]
@@ -345,15 +348,17 @@
         )
         for p in range(copies_ref.shape[0]):
             copies_ref[p] = gram
+        near_values[...] = pick_right(images[0][...], near_onehot(where_ref[NEAR]), NT)
         turned_rows(near_values, far_values, where_ref, turned_near, turned_far, turned_ref)
-        rows, part = image.shape[0], own_ref.shape[0]
+        fetch.wait()
+        rows, part = image.shape[0], own_ref.shape[0] // 2
         for h in range(groups):
-            at = pl.multiple_of(lax.rem(case_ref[0] + h, groups) * part, part)
+            at = pl.ds(pl.multiple_of(lax.rem(case_ref[0] + h, groups) * part, part), part)
+            target, first = (messages[h - 1], rows) if h else (own_ref, 0)
             if h:
-                messages[h - 1][:rows, :] = image
-                messages[h - 1][rows:, :] = turned_ref[pl.ds(at, part), :]
-            else:
-                own_ref[...] = turned_ref[pl.ds(at, part), :]
+                target[:rows, :] = image
+            target[first : first + part, :] = turned0_ref[at, :]
+            target[first + part :, :] = turned_ref[at, :]
     else:
         send_ports(image, asked_hot, port_onehot(meta_ref[...]), pay_ref)
 
@@ -375,15 +380,6 @@
             out_ref[pl.ds(k + i, modes, stride=CASES), :] = result[:, i * LANES : (i + 1) * LANES]
 
 
-def turned_kernel(groups, case_ref, near_values, far_values, where_ref, turned_near, turned_far, *rest):
-    outs, out_ref = rest[:groups], rest[groups]
-    turned_rows(near_values, far_values, where_ref, turned_near, turned_far, out_ref)
-    part = outs[0].shape[0]
-    for h in range(groups):
-        at = pl.multiple_of(lax.rem(case_ref[0] + h, groups) * part, part)
-        outs[h][...] = out_ref[pl.ds(at, part), :]
-
-
 def pass_kernel(*refs):
     pass
 
@@ -424,10 +420,10 @@
 
 
 def sum_kernel(in_ref, out_ref):
-    for q in range(in_ref.shape[0]):
-        total = in_ref[q, 0]
-        for p in range(1, in_ref.shape[1]):
-            total = total + in_ref[q, p]
+    for q in range(in_ref.shape[1]):
+        total = in_ref[0, q]
+        for p in range(1, in_ref.shape[0]):
+            total = total + in_ref[p, q]
         for p in range(out_ref.shape[0]):
             out_ref[p, q * CASES : (q + 1) * CASES, :] = total
 
@@ -470,17 +466,7 @@
     return 0.5 * (m + jnp.transpose(m))
 
 
-def solve_kernel(groups, case_ref, gram_ref, *rest):
-    pieces, (coef, *outs), (held, coef_rows, turned_coef, sems) = (
-        rest[: 2 * groups], rest[2 * groups : 3 * groups + 1], rest[3 * groups + 1 :]
-    )
-    part = held.shape[1]
-    fetches = [
-        pltpu.make_async_copy(piece.at[pl.ds(piece.shape[0] - part, part), :], held.at[i], sems.at[i])
-        for i, piece in enumerate(pieces)
-    ]
-    for fetch in fetches:
-        fetch.start()
+def solve_kernel(groups, case_ref, gram_ref, coef, coef_rows, turned_coef):
     n = groups * CASES
     total = gram_ref[0]
     for p in range(1, gram_ref.shape[0]):
@@ -503,12 +489,24 @@
             if q == 0:
                 for j in range(n):
                     coef[h * n + j] = jnp.broadcast_to(mine[:, j : j + 1], (CASES, LANES))
-    for fetch in fetches:
-        fetch.wait()
-    left = stacked_table(jnp.concatenate([coef_rows[:, :n], coef_rows[:, LANES : LANES + n]], axis=1))
+
+
+def bubble_kernel(groups, rows, coef_ref, *refs):
+    turned, outs = refs[:groups], refs[groups:]
+    n = groups * CASES
+    part = outs[0].shape[0]
+    firsts = [0] + [rows] * (groups - 1)
+    left = stacked_table(jnp.concatenate([coef_ref[:, :n], coef_ref[:, LANES : LANES + n]], axis=1))
     for m in range(0, part // CASES, 2):
         values = [
-            jnp.concatenate([held[i, at : at + CASES, :] for i in range(2 * groups)], axis=0)
+            jnp.concatenate(
+                [
+                    ref[first + half * part + at : first + half * part + at + CASES, :]
+                    for half in range(2)
+                    for ref, first in zip(turned, firsts)
+                ],
+                axis=0,
+            )
             for at in (m * CASES, (m + 1) * CASES)
         ]
         result = dot(left, stacked_values(jnp.concatenate(values, axis=1)))
@@ -655,39 +653,35 @@
     arrived, gram = lax.optimization_barrier((arrived, gram))
     image, base_far, pay = call(
         functools.partial(image_kernel, parts, groups, False),
-        [((rows, ports), F32, False)] * 2 + [((parts * 18, LANES), F32, False)],
+        [((rows, ports), F32, False), field_of, ((parts * 18, LANES), F32, False)],
         [(rows, comps)] + slot_scratch,
         "image",
     )(arrived, base_inner, asked, where, near_far, far_near, meta)
     arrived = exchange(pay, parts)
     image_all = to_cases([image] * (groups - 1))
-    turned0, *messages = call(
-        functools.partial(turned_kernel, groups),
-        [part_of] * groups,
-        [(bubbles, comps)],
-        "turned",
-        flops=10**9,
-        smem=(0,),
-    )(case, base_near, base_far, where, turned_near, turned_far)
-    turned0_all = to_cases(messages)
-    image_inner, image_near = inner(image)
+    (turned0,) = call(turned_rows, [bubble_of], name="turned", flops=10**9)(
+        base_near, base_far, where, turned_near, turned_far
+    )
+    image_inner, _ = inner(image)
     (gram,) = call(functools.partial(gram_kernel, groups), gram_of, name="gram", smem=(0,))(
         case, gram, base, *base_all, image
     )
-    arrived, *turned0_all = lax.optimization_barrier((arrived, *turned0_all))
+    arrived, turned0 = lax.optimization_barrier((arrived, turned0))
     minor = lax.axis_size("py")
-    second, copies, turned1, *messages = call(
+    second, copies, turned_own, *messages = call(
         functools.partial(image_kernel, parts, groups, True),
-        [field_of, ((groups * minor, cases, LANES), F32, True), part_of]
-        + [((rows + part, comps), F32, True)] * (groups - 1),
-        [(rows, comps)] + slot_scratch + [(rows, comps), (bubbles, comps)],
+        [field_of, ((groups * minor, cases, LANES), F32, True), ((2 * part, comps), F32, True)]
+        + [((rows + 2 * part, comps), F32, True)] * (groups - 1),
+        [(rows, comps)] + slot_scratch + [(rows, comps)] * 2 + [(bubbles, comps)] * 2,
         "second",
         smem=(6,),
+        hbm=(10,),
+        sems=1,
     )(
-        arrived, image_inner, asked, where, near_far, far_near, case, gram, image_near, turned_near, turned_far,
+        arrived, image_inner, asked, where, near_far, far_near, case, gram, turned_near, turned_far, turned0,
         image, *image_all,
     )
-    copies = lax.all_to_all(copies, ("case", "py"), split_axis=0, concat_axis=0)
+    copies = lax.all_to_all(copies, ("py", "case"), split_axis=0, concat_axis=0)
     messages = pl.pallas_call(
         pass_kernel,
         out_shape=[pltpu.HBM(m.shape, m.dtype) for m in messages],
@@ -699,19 +693,19 @@
     )(*messages)
     both1 = to_cases(messages)
     (copies,) = call(sum_kernel, [((parts // minor, groups * cases, LANES), F32, False)], name="sum")(
-        copies.reshape(groups, minor, cases, LANES)
+        copies.reshape(minor, groups, cases, LANES)
     )
     copies = lax.all_to_all(copies, "px", split_axis=0, concat_axis=0)
-    pieces = [turned0, *turned0_all, turned1, *both1]
-    coef, own, *messages = call(
+    coef, coef_rows = call(
         functools.partial(solve_kernel, groups),
-        [((2 * groups * cases, cases, LANES), F32, False)] + [((part, comps), F32, False)] * groups,
-        [(2 * groups, part, comps), (groups * cases, 2 * LANES), (2, groups * cases, LANES)],
+        [((2 * groups * cases, cases, LANES), F32, False), ((groups * cases, 2 * LANES), F32, False)],
+        [(2, groups * cases, LANES)],
         "solve",
         smem=(0,),
-        anywhere=range(2, 2 + len(pieces)),
-        sems=len(pieces),
-    )(case, copies, *pieces)
+    )(case, copies)
+    own, *messages = call(
+        functools.partial(bubble_kernel, groups, rows), [((part, comps), F32, False)] * groups, name="bubble"
+    )(coef_rows, turned_own, *both1)
     back = to_cases(messages)
     x, residual = call(
         functools.partial(ports_kernel, groups), [field_of, field_of], name="ports", flops=10**9

time: 137 us -> 129 us (0.942)
  starting transfers between devices: 48.1 us -> 35.4 us
  blocking collectives: 26.4 us -> 36.1 us
  local copies, waits for them, and re-layouts: 2.87 us -> 0.09 us
    all_to_all x0 -> x1, blocking collectives: none -> 9.74 us  [local(): copies = lax.all_to_all(copies, 'px', split_axis=0, concat_axis=0)]
    all_to_all x2, waiting for transfers between devices: 4.51 us -> 13.7 us  [exchange(): lax.all_to_all(rows.reshape(parts, 1, -1), PLANE, split_axis=0, concat_ax...]
    all_to_all x2 -> x1, starting transfers between devices: 15.9 us -> 6.88 us  [local(): copies = lax.all_to_all(copies, ('py', 'case'), split_axis=0, concat_axis=0)]
    ppermute x15 -> x12, waiting for transfers between devices: 11.2 us -> 4.59 us  [to_cases(): lax.ppermute(message, 'case', [(k, (k + h) % groups) for k in range(group...]
    ppermute x15 -> x12, starting transfers between devices: 18.9 us -> 15.5 us  [to_cases(): lax.ppermute(message, 'case', [(k, (k + h) % groups) for k in range(group...]
    all_to_all x2 -> x1, waiting for transfers between devices: 9.14 us -> 5.76 us  [local(): copies = lax.all_to_all(copies, ('py', 'case'), split_axis=0, concat_axis=0)]
    unnamed x52 -> x38, local copies, waits for them, and re-layouts: 2.87 us -> 0.09 us
    pallas_call x14 -> x15, Pallas kernels: 33.4 us -> 32.4 us  [run(): pl.pallas_call(kernel, out_shape=results, in_specs=specs, out_specs=[vmem...]
  transfers between devices with their start and end apart: 19 -> 15, of which waited for: 9 -> 6; matrix products, arithmetic and copies ran while one was open for 0% -> 0% of each run, Pallas kernels for 10% -> 14%
where the time goes in v9:
time: 129 us
  blocking collectives  36.1 us (28%)
  starting transfers between devices  35.4 us (27%)
  Pallas kernels  32.4 us (25%)
  waiting for transfers between devices  24 us (19%)
    pallas_call x15, Pallas kernels, run(): pl.pallas_call(kernel, out_shape=results, in_specs=specs, out_specs=[vmem...  32.4 us
    all_to_all x1, blocking collectives, exchange(): lax.all_to_all(rows.reshape(parts, 1, -1), PLANE, split_axis=0, concat_ax...  26.4 us
    ppermute x12, starting transfers between devices, to_cases(): lax.ppermute(message, 'case', [(k, (k + h) % groups) for k in range(group...  15.5 us
    all_to_all x2, waiting for transfers between devices, exchange(): lax.all_to_all(rows.reshape(parts, 1, -1), PLANE, split_axis=0, concat_ax...  13.7 us
    all_to_all x2, starting transfers between devices, exchange(): lax.all_to_all(rows.reshape(parts, 1, -1), PLANE, split_axis=0, concat_ax...  13.1 us
    all_to_all x1, blocking collectives, local(): copies = lax.all_to_all(copies, 'px', split_axis=0, concat_axis=0)  9.74 us
    all_to_all x1, starting transfers between devices, local(): copies = lax.all_to_all(copies, ('py', 'case'), split_axis=0, concat_axis=0)  6.88 us
    all_to_all x1, waiting for transfers between devices, local(): copies = lax.all_to_all(copies, ('py', 'case'), split_axis=0, concat_axis=0)  5.76 us
  transfers between devices with their start and end apart: 15, of which 6 were waited for; matrix products, arithmetic and copies ran while one was open for 0% of the time, Pallas kernels for 14%

profile of v9, /device:TPU:1, one launch (start us, length us, event | category | flops | bytes accessed | tf_op | source)
XLA Modules:
  0.0 129.0 jit_solution(12010035751616289019)
XLA Ops:
  0.6 3.4 %condense.1 = (f32[640,128]{1,0:T(8,128)S(1)}, f32[384,128]{1,0:T(8,128)}, f32[64,128]{1,0:T(8,128)S(1)}, f32[8,128]{1,0:T(8,128)S(1)}) custom-call(s32[1,128]{1,0:T(1,128)} %bitcast.30, f32[1,128]{1,0:T(1,128)} %bitcast.31, s32[1,128]{1,0:T(1,128)} %bitcast.32, s32[1,128]{1,0:T(1,128)} %bitcast.33, s32[1,128]{1,0:T(1,128)} %bitcast.34, ...), custom_call_target="tpu_custom_call" | custom-call | bytes 592384 | tf_op jit(solution)/shard_map/condense/pallas_call | solution.py:568
  4.0 0.0 copy-start.7
  4.0 0.0 copy-start.8
  4.0 26.4 %all_to_all.25 = f32[64,1,1280]{2,1,0:T(1,128)S(1)} all-to-all(f32[64,1,1280]{2,1,0:T(1,128)S(1)} %bitcast.23), channel_id=1, replica_groups=mesh['px'=8,'py'=8,'case'=4] {'px','py'}, dimensions={0} | all-to-all | bytes 655360 | tf_op jit(solution)/shard_map/all_to_all | solution.py:584
  30.4 1.4 %rhs.1 = (f32[384,128]{1,0:T(8,128)}, f32[1152,128]{1,0:T(8,128)}, f32[64,128]{1,0:T(8,128)S(1)}) custom-call(f32[640,128]{1,0:T(8,128)S(1)} %bitcast.21, f32[384,128]{1,0:T(8,128)S(1)} %copy-done.8, f32[384,128]{1,0:T(8,128)S(1)} %bitcast.28, f32[64,128]{1,0:T(8,128)S(1)} %get-tuple-element.46.meta_ref.rest_0_), custom_call_target="tpu_custom_call" | custom-call | bytes 753664 | tf_op jit(solution)/shard_map/rhs/pallas_call | solution.py:568
  31.8 6.3 %all-to-all-start.1 = ((f32[64,1,2304]{2,1,0:T(1,128)}), f32[64,1,2304]{2,1,0:T(1,128)S(1)}, u32[]{:S(2)}, u32[]{:S(2)}) async-start(f32[64,1,2304]{2,1,0:T(1,128)} %bitcast.11), calls=%async_computation.1 | async-start | bytes 1179648 | tf_op jit(solution)/shard_map/all_to_all | solution.py:584
  38.2 1.3 collective-permute-start.2
  39.5 2.4 %collective-permute-start.1 = (f32[384,128]{1,0:T(8,128)S(1)}, f32[384,128]{1,0:T(8,128)S(1)}, u32[]{:S(2)}, u32[]{:S(2)}) collective-permute-start(f32[384,128]{1,0:T(8,128)S(1)} %copy-done), channel_id=1, source_target_pairs={{0,2},{1,3},{2,0},{3,1},{4,6},{5,7},{6,4},{7,5},{8,10},{9,11},{10,... | collective-permute-start | bytes 589832 | tf_op jit(solution)/shard_map/ppermute | solution.py:636
  41.9 1.2 collective-permute-start
  43.1 2.6 %tables.1 = (bf16[384,144]{1,0:T(8,128)(2,1)S(1)}, bf16[384,144]{1,0:T(8,128)(2,1)S(1)}, bf16[384,144]{1,0:T(8,128)(2,1)S(1)}, bf16[384,144]{1,0:T(8,128)(2,1)S(...) custom-call(f32[8,128]{1,0:T(8,128)S(1)} %get-tuple-element.51.where_ref, ...), custom_call_target="tpu_custom_call" | custom-call | flops 1000000000 | bytes 888832 | tf_op jit(solution)/shard_map/tables/pallas_call | solution.py:568
  45.7 1.7 %inner.2 = (f32[384,128]{1,0:T(8,128)S(1)}, f32[384,128]{1,0:T(8,128)S(1)}) custom-call(f32[384,128]{1,0:T(8,128)S(1)} %copy-done, f32[64,128]{1,0:T(8,128)S(1)} %get-tuple-element.50.asked_ref, f32[8,128]{1,0:T(8,128)S(1)} %get-tuple-element.51.where_ref, bf16[384,144]{1,0:T(8,128)(2,1)S(1)} %get-tuple-element.52.near_near, ...), custom_call_target="tpu_custom_call" | custom-call | flops 1000000000 | bytes 454656 | tf_op jit(solution)/shard_map/inner/pallas_call | solution.py:568
  47.4 0.0 collective-permute-done.2.refs_3_
  47.4 3.3 %collective-permute-done.1.refs_2_ = f32[384,128]{1,0:T(8,128)S(1)} collective-permute-done((f32[384,128]{1,0:T(8,128)S(1)}, f32[384,128]{1,0:T(8,128)S(1)}, u32[]{:S(2)}, u32[]{:S(2)}) %collective-permute-start.1) | collective-permute-done | bytes 196640 | tf_op jit(solution)/shard_map/ppermute | solution.py:636
  50.7 1.5 %base_gram.1.gram_ref = f32[8,128]{1,0:T(8,128)S(1)} custom-call(s32[1]{0:T(128)} %bitcast.case_ref.rest_0_, f32[384,128]{1,0:T(8,128)S(1)} %copy-done, f32[384,128]{1,0:T(8,128)S(1)} %collective-permute-done.refs_1_, f32[384,128]{1,0:T(8,128)S(1)} %collective-permute-done.1.refs_2_, f32[384,128]{1,0:T(8,128)S(1)} %collective-permute-done.2.refs_3_), custom_call_target="tpu_custom_call" | custom-call | bytes 786436 | tf_op jit(solution)/shard_map/base_gram/pallas_call | solution.py:568
  52.2 4.5 %all-to-all-done.1 = f32[64,1,2304]{2,1,0:T(1,128)S(1)} async-done(((f32[64,1,2304]{2,1,0:T(1,128)}), f32[64,1,2304]{2,1,0:T(1,128)S(1)}, u32[]{:S(2)}, u32[]{:S(2)}) %all-to-all-start.1) | async-done | bytes 589856 | tf_op jit(solution)/shard_map/all_to_all | solution.py:584
  56.7 2.7 %image.1 = (f32[384,128]{1,0:T(8,128)S(1)}, f32[384,128]{1,0:T(8,128)}, f32[1152,128]{1,0:T(8,128)}) custom-call(f32[1152,128]{1,0:T(8,128)S(1)} %bitcast.19, f32[384,128]{1,0:T(8,128)S(1)} %get-tuple-element.54.inner_ref, f32[64,128]{1,0:T(8,128)S(1)} %get-tuple-element.50.asked_ref, f32[8,128]{1,0:T(8,128)S(1)} %get-tuple-element.51.where_ref, ...), custom_call_target="tpu_custom_call" | custom-call | bytes 1077248 | tf_op jit(solution)/shard_map/image/pallas_call | solution.py:568
  59.4 6.8 %all-to-all-start.2 = ((f32[64,1,2304]{2,1,0:T(1,128)}), f32[64,1,2304]{2,1,0:T(1,128)S(1)}, u32[]{:S(2)}, u32[]{:S(2)}) async-start(f32[64,1,2304]{2,1,0:T(1,128)} %bitcast.13), calls=%async_computation.2 | async-start | bytes 1179648 | tf_op jit(solution)/shard_map/all_to_all | solution.py:584
  66.2 0.0 copy-start.14
  66.2 1.1 collective-permute-start.5
  67.3 2.4 %collective-permute-start.4 = (f32[384,128]{1,0:T(8,128)S(1)}, f32[384,128]{1,0:T(8,128)S(1)}, u32[]{:S(2)}, u32[]{:S(2)}) collective-permute-start(f32[384,128]{1,0:T(8,128)S(1)} %get-tuple-element.63.field_ref.refs_4_.rest_5_), channel_id=1, source_target_pairs={{0,2},{1,3},{2,0},{3,1},{4,6},{5,7},{6,4},{7,5},{8,10},{9,11},{10,... | collective-permute-start | bytes 589832 | tf_op jit(solution)/shard_map/ppermute | solution.py:636
  69.7 1.2 collective-permute-start.3
  70.9 1.5 %gram.1.rest_1_ = f32[8,128]{1,0:T(8,128)S(1)} custom-call(s32[1]{0:T(128)} %bitcast.case_ref.rest_0_, f32[8,128]{1,0:T(8,128)S(1)} %base_gram.1.gram_ref, f32[384,128]{1,0:T(8,128)S(1)} %copy-done, f32[384,128]{1,0:T(8,128)S(1)} %collective-permute-done.refs_1_, f32[384,128]{1,0:T(8,128)S(1)} %collective-permute-done.1.refs_2_, ...), custom_call_target="tpu_custom_call" | custom-call | bytes 987140 | tf_op jit(solution)/shard_map/gram/pallas_call | solution.py:568
  72.4 0.0 copy-start.1
  72.4 0.0 copy-start.12
  72.4 1.7 %inner.3 = (f32[384,128]{1,0:T(8,128)S(1)}, f32[384,128]{1,0:T(8,128)}) custom-call(f32[384,128]{1,0:T(8,128)S(1)} %get-tuple-element.63.field_ref.refs_4_.rest_5_, f32[64,128]{1,0:T(8,128)S(1)} %get-tuple-element.50.asked_ref, f32[8,128]{1,0:T(8,128)S(1)} %get-tuple-element.51.where_ref, bf16[384,144]{1,0:T(8,128)(2,1)S(1)} %copy-done.14, ...), custom_call_target="tpu_custom_call" | custom-call | flops 1000000000 | bytes 454656 | tf_op jit(solution)/shard_map/inner/pallas_call | solution.py:568
  74.1 1.4 %turned.1.rest_4_ = f32[512,128]{1,0:T(8,128)} custom-call(f32[384,128]{1,0:T(8,128)S(1)} %copy-done.18, f32[384,128]{1,0:T(8,128)S(1)} %copy-done.12, f32[8,128]{1,0:T(8,128)S(1)} %get-tuple-element.51.where_ref, bf16[512,144]{1,0:T(8,128)(2,1)S(1)} %copy-done.1, bf16[512,144]{1,0:T(8,128)(2,1)S(1)} %copy-done.2), custom_call_target="tpu_custom_call" | custom-call | flops 1000000000 | bytes 692224 | tf_op jit(solution)/shard_map/turned/pallas_call | solution.py:568
  75.6 9.2 %all-to-all-done.2 = f32[64,1,2304]{2,1,0:T(1,128)S(1)} async-done(((f32[64,1,2304]{2,1,0:T(1,128)}), f32[64,1,2304]{2,1,0:T(1,128)S(1)}, u32[]{:S(2)}, u32[]{:S(2)}) %all-to-all-start.2) | async-done | bytes 589856 | tf_op jit(solution)/shard_map/all_to_all | solution.py:584
  84.8 0.0 collective-permute-done.5.rest_8_.refs_7_
  84.8 0.0 collective-permute-done.4.rest_7_.refs_6_
  84.8 0.0 collective-permute-done.3.rest_6_.refs_5_
  84.8 5.9 %second.1 = (f32[384,128]{1,0:T(8,128)}, f32[32,8,128]{2,1,0:T(8,128)}, f32[256,128]{1,0:T(8,128)}, f32[640,128]{1,0:T(8,128)}, f32[640,128]{1,0:T(8,128)}, /*index=5*/f32[640,128]{1,0:T(8,128)}) custom-call(f32[1152,128]{1,0:T(8,128)S(1)} %bitcast.20, f32[384,128]{1,0:T(8,128)S(1)} %get-tuple-element.64.inner_ref, ...), custom_call_target="tpu_custom_call" | custom-call | bytes 2392068 | tf_op jit(solution)/shard_map/second/pallas_call | solution.py:568
  90.6 6.9 %all-to-all-start.3 = ((f32[32,8,128]{2,1,0:T(8,128)}), f32[32,8,128]{2,1,0:T(8,128)S(1)}, u32[]{:S(2)}, u32[]{:S(2)}) async-start(f32[32,8,128]{2,1,0:T(8,128)} %get-tuple-element.67), calls=%async_computation.3 | async-start | bytes 262144 | tf_op jit(solution)/shard_map/all_to_all | solution.py:684
  97.5 2.5 %collective-permute-start.6 = (f32[640,128]{1,0:T(8,128)}, f32[640,128]{1,0:T(8,128)S(1)}, u32[]{:S(2)}, u32[]{:S(2)}) collective-permute-start(f32[640,128]{1,0:T(8,128)} %get-tuple-element.73), channel_id=1, source_target_pairs={{0,3},{1,0},{2,1},{3,2},{4,7},{5,4},{6,5},{7,6},{8,11},{9,8},{10,9... | collective-permute-start | bytes 983048 | tf_op jit(solution)/shard_map/ppermute | solution.py:636
  100.1 0.6 collective-permute-start.7
  100.6 0.6 collective-permute-start.8
  101.2 5.8 %all-to-all-done.3 = f32[32,8,128]{2,1,0:T(8,128)S(1)} async-done(((f32[32,8,128]{2,1,0:T(8,128)}), f32[32,8,128]{2,1,0:T(8,128)S(1)}, u32[]{:S(2)}, u32[]{:S(2)}) %all-to-all-start.3) | async-done | bytes 131104 | tf_op jit(solution)/shard_map/all_to_all | solution.py:684
  107.0 9.7 %all_to_all.26.gram_ref = f32[8,32,128]{2,1,0:T(8,128)S(1)} all-to-all(f32[8,32,128]{2,1,0:T(8,128)S(1)} %sum.1), channel_id=1, replica_groups=mesh['px'=8,'py'=8,'case'=4] {'px'}, dimensions={0} | all-to-all | bytes 262144 | tf_op jit(solution)/shard_map/all_to_all | solution.py:698
  116.7 4.3 %solve.1 = (f32[64,8,128]{2,1,0:T(8,128)S(1)}, f32[32,256]{1,0:T(8,128)S(1)}) custom-call(s32[1]{0:T(128)} %bitcast.case_ref.rest_0_, f32[8,32,128]{2,1,0:T(8,128)S(1)} %all_to_all.26.gram_ref), custom_call_target="tpu_custom_call" | custom-call | bytes 131076 | tf_op jit(solution)/shard_map/solve/pallas_call | solution.py:568
  121.1 0.0 collective-permute-done.6.refs_9_.refs_1_
  121.1 0.0 copy-start.11
  121.1 0.4 bubble.1
  121.5 1.5 %collective-permute-start.9 = (f32[128,128]{1,0:T(8,128)S(1)}, f32[128,128]{1,0:T(8,128)S(1)}, u32[]{:S(2)}, u32[]{:S(2)}) collective-permute-start(f32[128,128]{1,0:T(8,128)S(1)} %get-tuple-element.82), channel_id=1, source_target_pairs={{0,3},{1,0},{2,1},{3,2},{4,7},{5,4},{6,5},{7,6},{8,11},{9,8},{10,9... | collective-permute-start | bytes 196616 | tf_op jit(solution)/shard_map/ppermute | solution.py:636
  123.0 0.2 collective-permute-start.10
  123.2 0.5 collective-permute-start.11
  123.7 3.2 %ports.1 = (f32[384,128]{1,0:T(8,128)}, f32[384,128]{1,0:T(8,128)}) custom-call(f32[64,8,128]{2,1,0:T(8,128)S(1)} %get-tuple-element.68.coef, f32[384,128]{1,0:T(8,128)S(1)} %copy-done, f32[384,128]{1,0:T(8,128)S(1)} %collective-permute-done.refs_1_, f32[384,128]{1,0:T(8,128)S(1)} %collective-permute-done.1.refs_2_, ...), custom_call_target="tpu_custom_call" | custom-call | flops 1000000000 | bytes 3014656 | tf_op jit(solution)/shard_map/ports/pallas_call | solution.py:568
  126.9 0.8 collective-permute-done.10.refs_2_
  127.8 0.5 collective-permute-done.11.refs_3_
  128.2 0.7 join.1
  (38 shorter events, 0.1 us)
Async XLA Ops:
  4.0 26.4 %copy-start.7 = (f32[48,8,128]{2,1,0:T(8,128)S(1)}, f32[48,8,128]{2,1,0:T(8,128)}, u32[]{:S(2)}) copy-start(f32[48,8,128]{2,1,0:T(8,128)} %param.16) | copy-start | bytes 589828
  4.0 26.4 %copy-start.8 = (f32[384,128]{1,0:T(8,128)S(1)}, f32[384,128]{1,0:T(8,128)}, u32[]{:S(2)}) copy-start(f32[384,128]{1,0:T(8,128)} %get-tuple-element.45.near_sum_ref) | copy-start | bytes 589828
  30.4 12.7 %copy-start.10 = (f32[8,96,96]{2,1,0:T(8,128)S(1)}, f32[8,96,96]{2,1,0:T(8,128)}, u32[]{:S(2)}) copy-start(f32[8,96,96]{2,1,0:T(8,128)} %block_ref.1) | copy-start | bytes 884740
  31.8 6.3 %copy-start = (f32[384,128]{1,0:T(8,128)S(1)}, f32[384,128]{1,0:T(8,128)}, u32[]{:S(2)}) copy-start(f32[384,128]{1,0:T(8,128)} %get-tuple-element.48.refs_0_.field_ref) | copy-start | bytes 589828
  31.8 11.3 %copy-start.3 = (f32[64,8,128]{2,1,0:T(8,128)S(1)}, f32[64,8,128]{2,1,0:T(8,128)}, u32[]{:S(2)}) copy-start(f32[64,8,128]{2,1,0:T(8,128)} %param.15) | copy-start | bytes 786436
  31.8 11.3 %copy-start.4 = (f32[8,64,64]{2,1,0:T(8,128)S(1)}, f32[8,64,64]{2,1,0:T(8,128)}, u32[]{:S(2)}) copy-start(f32[8,64,64]{2,1,0:T(8,128)} %inverse_ref.1) | copy-start | bytes 393220
  31.8 11.3 %copy-start.5 = (f32[8,96,64]{1,2,0:T(8,128)S(1)}, f32[8,96,64]{1,2,0:T(8,128)}, u32[]{:S(2)}) copy-start(f32[8,96,64]{1,2,0:T(8,128)} %param.18) | copy-start | bytes 589828
  31.8 24.9 %all-to-all-start.1 = ((f32[64,1,2304]{2,1,0:T(1,128)}), f32[64,1,2304]{2,1,0:T(1,128)S(1)}, u32[]{:S(2)}, u32[]{:S(2)}) async-start(f32[64,1,2304]{2,1,0:T(1,128)} %bitcast.11), calls=%async_computation.1 | async-start | bytes 1179648 | tf_op jit(solution)/shard_map/all_to_all | solution.py:584
  38.2 9.2 %collective-permute-start.2 = (f32[384,128]{1,0:T(8,128)S(1)}, f32[384,128]{1,0:T(8,128)S(1)}, u32[]{:S(2)}, u32[]{:S(2)}) collective-permute-start(f32[384,128]{1,0:T(8,128)S(1)} %copy-done), channel_id=1, source_target_pairs={{0,1},{1,2},{2,3},{3,0},{4,5},{5,6},{6,7},{7,4},{8,9},{9,10},{10,1... | collective-permute-start | bytes 589832 | tf_op jit(solution)/shard_map/ppermute | solution.py:636
  39.5 11.2 %collective-permute-start.1 = (f32[384,128]{1,0:T(8,128)S(1)}, f32[384,128]{1,0:T(8,128)S(1)}, u32[]{:S(2)}, u32[]{:S(2)}) collective-permute-start(f32[384,128]{1,0:T(8,128)S(1)} %copy-done), channel_id=1, source_target_pairs={{0,2},{1,3},{2,0},{3,1},{4,6},{5,7},{6,4},{7,5},{8,10},{9,11},{10,... | collective-permute-start | bytes 589832 | tf_op jit(solution)/shard_map/ppermute | solution.py:636
  41.9 8.8 %collective-permute-start = (f32[384,128]{1,0:T(8,128)S(1)}, f32[384,128]{1,0:T(8,128)S(1)}, u32[]{:S(2)}, u32[]{:S(2)}) collective-permute-start(f32[384,128]{1,0:T(8,128)S(1)} %copy-done), channel_id=1, source_target_pairs={{0,3},{1,0},{2,1},{3,2},{4,7},{5,4},{6,5},{7,6},{8,11},{9,8},{10,9... | collective-permute-start | bytes 589832 | tf_op jit(solution)/shard_map/ppermute | solution.py:636
  45.7 1.7 %copy-start.13 = (bf16[384,144]{1,0:T(8,128)(2,1)}, bf16[384,144]{1,0:T(8,128)(2,1)S(1)}, u32[]{:S(2)}) copy-start(bf16[384,144]{1,0:T(8,128)(2,1)S(1)} %get-tuple-element.52.near_near) | copy-start | bytes 331780
  45.7 1.7 %copy-start.15 = (bf16[384,144]{1,0:T(8,128)(2,1)}, bf16[384,144]{1,0:T(8,128)(2,1)S(1)}, u32[]{:S(2)}) copy-start(bf16[384,144]{1,0:T(8,128)(2,1)S(1)} %get-tuple-element.53.far_far) | copy-start | bytes 331780
  47.4 4.8 %copy-start.17 = (f32[384,128]{1,0:T(8,128)}, f32[384,128]{1,0:T(8,128)S(1)}, u32[]{:S(2)}) copy-start(f32[384,128]{1,0:T(8,128)S(1)} %get-tuple-element.58.near_values) | copy-start | bytes 589828
  59.4 25.3 %all-to-all-start.2 = ((f32[64,1,2304]{2,1,0:T(1,128)}), f32[64,1,2304]{2,1,0:T(1,128)S(1)}, u32[]{:S(2)}, u32[]{:S(2)}) async-start(f32[64,1,2304]{2,1,0:T(1,128)} %bitcast.13), calls=%async_computation.2 | async-start | bytes 1179648 | tf_op jit(solution)/shard_map/all_to_all | solution.py:584
  66.2 6.2 %copy-start.14 = (bf16[384,144]{1,0:T(8,128)(2,1)S(1)}, bf16[384,144]{1,0:T(8,128)(2,1)}, u32[]{:S(2)}) copy-start(bf16[384,144]{1,0:T(8,128)(2,1)} %copy-done.13) | copy-start | bytes 331780
  66.2 6.2 %copy-start.16 = (bf16[384,144]{1,0:T(8,128)(2,1)S(1)}, bf16[384,144]{1,0:T(8,128)(2,1)}, u32[]{:S(2)}) copy-start(bf16[384,144]{1,0:T(8,128)(2,1)} %copy-done.15) | copy-start | bytes 331780
  66.2 18.5 %collective-permute-start.5 = (f32[384,128]{1,0:T(8,128)S(1)}, f32[384,128]{1,0:T(8,128)S(1)}, u32[]{:S(2)}, u32[]{:S(2)}) collective-permute-start(f32[384,128]{1,0:T(8,128)S(1)} %get-tuple-element.63.field_ref.refs_4_.rest_5_), channel_id=1, source_target_pairs={{0,1},{1,2},{2,3},{3,0},{4,5},{5,6},{6,7},{7,4},{8,9},{9,10},{10,1... | collective-permute-start | bytes 589832 | tf_op jit(solution)/shard_map/ppermute | solution.py:636
  67.3 17.4 %collective-permute-start.4 = (f32[384,128]{1,0:T(8,128)S(1)}, f32[384,128]{1,0:T(8,128)S(1)}, u32[]{:S(2)}, u32[]{:S(2)}) collective-permute-start(f32[384,128]{1,0:T(8,128)S(1)} %get-tuple-element.63.field_ref.refs_4_.rest_5_), channel_id=1, source_target_pairs={{0,2},{1,3},{2,0},{3,1},{4,6},{5,7},{6,4},{7,5},{8,10},{9,11},{10,... | collective-permute-start | bytes 589832 | tf_op jit(solution)/shard_map/ppermute | solution.py:636
  69.7 15.1 %collective-permute-start.3 = (f32[384,128]{1,0:T(8,128)S(1)}, f32[384,128]{1,0:T(8,128)S(1)}, u32[]{:S(2)}, u32[]{:S(2)}) collective-permute-start(f32[384,128]{1,0:T(8,128)S(1)} %get-tuple-element.63.field_ref.refs_4_.rest_5_), channel_id=1, source_target_pairs={{0,3},{1,0},{2,1},{3,2},{4,7},{5,4},{6,5},{7,6},{8,11},{9,8},{10,9... | collective-permute-start | bytes 589832 | tf_op jit(solution)/shard_map/ppermute | solution.py:636
  72.4 1.7 %copy-start.1 = (bf16[512,144]{1,0:T(8,128)(2,1)S(1)}, bf16[512,144]{1,0:T(8,128)(2,1)}, u32[]{:S(2)}) copy-start(bf16[512,144]{1,0:T(8,128)(2,1)} %get-tuple-element.60.turned_near.rest_2_) | copy-start | bytes 442372
  72.4 1.7 %copy-start.2 = (bf16[512,144]{1,0:T(8,128)(2,1)S(1)}, bf16[512,144]{1,0:T(8,128)(2,1)}, u32[]{:S(2)}) copy-start(bf16[512,144]{1,0:T(8,128)(2,1)} %get-tuple-element.61.turned_far.rest_3_) | copy-start | bytes 442372
  72.4 1.7 %copy-start.12 = (f32[384,128]{1,0:T(8,128)S(1)}, f32[384,128]{1,0:T(8,128)}, u32[]{:S(2)}) copy-start(f32[384,128]{1,0:T(8,128)} %get-tuple-element.59.far_values) | copy-start | bytes 589828
  72.4 1.7 %copy-start.18 = (f32[384,128]{1,0:T(8,128)S(1)}, f32[384,128]{1,0:T(8,128)}, u32[]{:S(2)}) copy-start(f32[384,128]{1,0:T(8,128)} %copy-done.17) | copy-start | bytes 589828
  90.6 16.3 %all-to-all-start.3 = ((f32[32,8,128]{2,1,0:T(8,128)}), f32[32,8,128]{2,1,0:T(8,128)S(1)}, u32[]{:S(2)}, u32[]{:S(2)}) async-start(f32[32,8,128]{2,1,0:T(8,128)} %get-tuple-element.67), calls=%async_computation.3 | async-start | bytes 262144 | tf_op jit(solution)/shard_map/all_to_all | solution.py:684
  97.5 23.5 %collective-permute-start.6 = (f32[640,128]{1,0:T(8,128)}, f32[640,128]{1,0:T(8,128)S(1)}, u32[]{:S(2)}, u32[]{:S(2)}) collective-permute-start(f32[640,128]{1,0:T(8,128)} %get-tuple-element.73), channel_id=1, source_target_pairs={{0,3},{1,0},{2,1},{3,2},{4,7},{5,4},{6,5},{7,6},{8,11},{9,8},{10,9... | collective-permute-start | bytes 983048 | tf_op jit(solution)/shard_map/ppermute | solution.py:636
  100.1 21.0 %collective-permute-start.7 = (f32[640,128]{1,0:T(8,128)}, f32[640,128]{1,0:T(8,128)S(1)}, u32[]{:S(2)}, u32[]{:S(2)}) collective-permute-start(f32[640,128]{1,0:T(8,128)} %get-tuple-element.74), channel_id=1, source_target_pairs={{0,2},{1,3},{2,0},{3,1},{4,6},{5,7},{6,4},{7,5},{8,10},{9,11},{10,... | collective-permute-start | bytes 983048 | tf_op jit(solution)/shard_map/ppermute | solution.py:636
  100.6 20.5 %collective-permute-start.8 = (f32[640,128]{1,0:T(8,128)}, f32[640,128]{1,0:T(8,128)S(1)}, u32[]{:S(2)}, u32[]{:S(2)}) collective-permute-start(f32[640,128]{1,0:T(8,128)} %get-tuple-element.75), channel_id=1, source_target_pairs={{0,1},{1,2},{2,3},{3,0},{4,5},{5,6},{6,7},{7,4},{8,9},{9,10},{10,1... | collective-permute-start | bytes 983048 | tf_op jit(solution)/shard_map/ppermute | solution.py:636
  116.7 4.4 %copy-start.9 = (f32[256,128]{1,0:T(8,128)S(1)}, f32[256,128]{1,0:T(8,128)}, u32[]{:S(2)}) copy-start(f32[256,128]{1,0:T(8,128)} %get-tuple-element.80.refs_0_) | copy-start | bytes 393220
  121.1 2.6 %copy-start.11 = (f32[384,128]{1,0:T(8,128)S(1)}, f32[384,128]{1,0:T(8,128)}, u32[]{:S(2)}) copy-start(f32[384,128]{1,0:T(8,128)} %get-tuple-element.69.refs_8_) | copy-start | bytes 589828
  121.5 5.5 %collective-permute-start.9 = (f32[128,128]{1,0:T(8,128)S(1)}, f32[128,128]{1,0:T(8,128)S(1)}, u32[]{:S(2)}, u32[]{:S(2)}) collective-permute-start(f32[128,128]{1,0:T(8,128)S(1)} %get-tuple-element.82), channel_id=1, source_target_pairs={{0,3},{1,0},{2,1},{3,2},{4,7},{5,4},{6,5},{7,6},{8,11},{9,8},{10,9... | collective-permute-start | bytes 196616 | tf_op jit(solution)/shard_map/ppermute | solution.py:636
  123.0 4.7 %collective-permute-start.10 = (f32[128,128]{1,0:T(8,128)S(1)}, f32[128,128]{1,0:T(8,128)S(1)}, u32[]{:S(2)}, u32[]{:S(2)}) collective-permute-start(f32[128,128]{1,0:T(8,128)S(1)} %get-tuple-element.83), channel_id=1, source_target_pairs={{0,2},{1,3},{2,0},{3,1},{4,6},{5,7},{6,4},{7,5},{8,10},{9,11},{10,... | collective-permute-start | bytes 196616 | tf_op jit(solution)/shard_map/ppermute | solution.py:636
  123.2 5.0 %collective-permute-start.11 = (f32[128,128]{1,0:T(8,128)S(1)}, f32[128,128]{1,0:T(8,128)S(1)}, u32[]{:S(2)}, u32[]{:S(2)}) collective-permute-start(f32[128,128]{1,0:T(8,128)S(1)} %get-tuple-element.84), channel_id=1, source_target_pairs={{0,1},{1,2},{2,3},{3,0},{4,5},{5,6},{6,7},{7,4},{8,9},{9,10},{10,1... | collective-permute-start | bytes 196616 | tf_op jit(solution)/shard_map/ppermute | solution.py:636
  123.7 4.5 %copy-start.6 = (f32[512,128]{1,0:T(8,128)S(1)}, f32[512,128]{1,0:T(8,128)}, u32[]{:S(2)}) copy-start(f32[512,128]{1,0:T(8,128)} %get-tuple-element.78.bubble_ref) | copy-start | bytes 786436

commit v10 on v9

--- a/solution.py
+++ b/solution.py
@@ -318,13 +318,17 @@
     near_far, far_near, *rest,
 ):
     if last:
-        case_ref, gram_ref, turned_near, turned_far, turned0_hbm = rest[:5]
+        case_ref, gram_ref, turned_far, turned0_hbm, turned1_hbm = rest[:5]
         images, rest = rest[5 : 5 + groups], rest[5 + groups :]
         image_ref, copies_ref, own_ref = rest[:3]
         messages = rest[3 : 2 + groups]
-        near_part, slot_ref, slot_part, far_values, near_values, turned_ref, turned0_ref, sem = rest[2 + groups :]
-        fetch = pltpu.make_async_copy(turned0_hbm, turned0_ref, sem)
-        fetch.start()
+        near_part, slot_ref, slot_part, far_values, turned_ref, turned0_ref, turned1_ref, sems = rest[2 + groups :]
+        fetches = [
+            pltpu.make_async_copy(turned1_hbm, turned1_ref, sems.at[0]),
+            pltpu.make_async_copy(turned0_hbm, turned0_ref, sems.at[1]),
+        ]
+        for fetch in fetches:
+            fetch.start()
     else:
         meta_ref, image_ref, far_values, pay_ref, near_part, slot_ref, slot_part = rest
     asked = asked_ref[...]
@@ -348,9 +352,9 @@
         )
         for p in range(copies_ref.shape[0]):
             copies_ref[p] = gram
-        near_values[...] = pick_right(images[0][...], near_onehot(where_ref[NEAR]), NT)
-        turned_rows(near_values, far_values, where_ref, turned_near, turned_far, turned_ref)
-        fetch.wait()
+        for fetch in fetches:
+            fetch.wait()
+        turned_sums([(turned_far, far_values)], where_ref, turned_ref, turned1_ref)
         rows, part = image.shape[0], own_ref.shape[0] // 2
         for h in range(groups):
             at = pl.ds(pl.multiple_of(lax.rem(case_ref[0] + h, groups) * part, part), part)
@@ -363,21 +367,31 @@
         send_ports(image, asked_hot, port_onehot(meta_ref[...]), pay_ref)
 
 
-def turned_rows(near_values, far_values, where_ref, turned_near, turned_far, out_ref):
-    dofs = near_values.shape[0] // CASES
+def turned_sums(pairs, where_ref, out_ref, first=None):
+    dofs = pairs[0][1].shape[0] // CASES
     modes = out_ref.shape[0] // CASES
     kind = where_ref[KIND]
     kind2 = jnp.concatenate([kind, kind], axis=1)
     for k in range(0, CASES, 2):
         sums = 0.0
-        for table, part in ((turned_near, near_values), (turned_far, far_values)):
+        for table, part in pairs:
             values = jnp.concatenate(
                 [part[pl.ds(k + i, dofs, stride=CASES), :] for i in range(2)], axis=1
             )
             sums = sums + dot(table[...], stacked_values(values))
         result = by_kind(sums, kind2, modes)
         for i in range(2):
-            out_ref[pl.ds(k + i, modes, stride=CASES), :] = result[:, i * LANES : (i + 1) * LANES]
+            rows = pl.ds(k + i, modes, stride=CASES)
+            mine = result[:, i * LANES : (i + 1) * LANES]
+            out_ref[rows, :] = mine if first is None else first[rows, :] + mine
+
+
+def turned_rows(near_values, far_values, where_ref, turned_near, turned_far, out_ref):
+    turned_sums([(turned_near, near_values), (turned_far, far_values)], where_ref, out_ref)
+
+
+def turned_near_rows(near_values, where_ref, turned_near, out_ref):
+    turned_sums([(turned_near, near_values)], where_ref, out_ref)
 
 
 def pass_kernel(*refs):
@@ -491,10 +505,10 @@
                     coef[h * n + j] = jnp.broadcast_to(mine[:, j : j + 1], (CASES, LANES))
 
 
-def bubble_kernel(groups, rows, coef_ref, *refs):
-    turned, outs = refs[:groups], refs[groups:]
+def bubble_kernel(groups, rows, case_ref, coef_ref, *refs):
+    turned, out_ref = refs[:groups], refs[groups]
     n = groups * CASES
-    part = outs[0].shape[0]
+    part = out_ref.shape[1]
     firsts = [0] + [rows] * (groups - 1)
     left = stacked_table(jnp.concatenate([coef_ref[:, :n], coef_ref[:, LANES : LANES + n]], axis=1))
     for m in range(0, part // CASES, 2):
@@ -512,7 +526,7 @@
         result = dot(left, stacked_values(jnp.concatenate(values, axis=1)))
         for i in range(2):
             for h in range(groups):
-                outs[h][(m + i) * CASES : (m + i + 1) * CASES, :] = result[
+                out_ref[lax.rem(case_ref[0] + h, groups), (m + i) * CASES : (m + i + 1) * CASES, :] = result[
                     h * CASES : (h + 1) * CASES, i * LANES : (i + 1) * LANES
                 ]
 
@@ -545,12 +559,8 @@
     lax.fori_loop(0, dofs // wide, ports, 0)
 
 
-def join_kernel(groups, case_ref, bubble_ref, *refs):
-    parts, out_ref = refs[:groups], refs[groups]
-    part = parts[0].shape[0]
-    for h in range(groups):
-        at = pl.ds(pl.multiple_of(lax.rem(case_ref[0] + h, groups) * part, part), part)
-        out_ref[at, :] = bubble_ref[at, :] - parts[h][...]
+def join_kernel(bubble_ref, sums_ref, out_ref):
+    out_ref[...] = bubble_ref[...] - sums_ref[...]
 
 
 def call(kernel, outs, scratch=(), name=None, flops=0, smem=(), hbm=(), anywhere=(), sems=0, limit=12):
@@ -662,23 +672,24 @@
     (turned0,) = call(turned_rows, [bubble_of], name="turned", flops=10**9)(
         base_near, base_far, where, turned_near, turned_far
     )
-    image_inner, _ = inner(image)
+    image_inner, image_near = inner(image)
+    (turned1,) = call(turned_near_rows, [bubble_of], name="turned_near", flops=10**9)(image_near, where, turned_near)
     (gram,) = call(functools.partial(gram_kernel, groups), gram_of, name="gram", smem=(0,))(
         case, gram, base, *base_all, image
     )
-    arrived, turned0 = lax.optimization_barrier((arrived, turned0))
+    arrived, turned0, turned1 = lax.optimization_barrier((arrived, turned0, turned1))
     minor = lax.axis_size("py")
     second, copies, turned_own, *messages = call(
         functools.partial(image_kernel, parts, groups, True),
         [field_of, ((groups * minor, cases, LANES), F32, True), ((2 * part, comps), F32, True)]
         + [((rows + 2 * part, comps), F32, True)] * (groups - 1),
-        [(rows, comps)] + slot_scratch + [(rows, comps)] * 2 + [(bubbles, comps)] * 2,
+        [(rows, comps)] + slot_scratch + [(rows, comps)] + [(bubbles, comps)] * 3,
         "second",
         smem=(6,),
-        hbm=(10,),
-        sems=1,
+        hbm=(9, 10),
+        sems=2,
     )(
-        arrived, image_inner, asked, where, near_far, far_near, case, gram, turned_near, turned_far, turned0,
+        arrived, image_inner, asked, where, near_far, far_near, case, gram, turned_far, turned0, turned1,
         image, *image_all,
     )
     copies = lax.all_to_all(copies, ("py", "case"), split_axis=0, concat_axis=0)
@@ -703,16 +714,14 @@
         "solve",
         smem=(0,),
     )(case, copies)
-    own, *messages = call(
-        functools.partial(bubble_kernel, groups, rows), [((part, comps), F32, False)] * groups, name="bubble"
-    )(coef_rows, turned_own, *both1)
-    back = to_cases(messages)
+    (sums,) = call(
+        functools.partial(bubble_kernel, groups, rows), [((groups, part, comps), F32, False)], name="bubble", smem=(0,)
+    )(case, coef_rows, turned_own, *both1)
+    sums = lax.all_to_all(sums, "case", split_axis=0, concat_axis=0)
     x, residual = call(
         functools.partial(ports_kernel, groups), [field_of, field_of], name="ports", flops=10**9
     )(coef, base, *base_all, image, *image_all, second, *both1)
-    (bubble,) = call(functools.partial(join_kernel, groups), [bubble_of], name="join", smem=(0,))(
-        case, bubble_base, own, *back
-    )
+    (bubble,) = call(join_kernel, [bubble_of], name="join")(bubble_base, sums.reshape(bubbles, comps))
     return (
         x.reshape(port_load.shape),
         residual.reshape(port_load.shape),

time: 129 us -> 132 us (1.023)
    all_to_all x0 -> x1, starting transfers between devices: none -> 3.41 us  [local(): sums = lax.all_to_all(sums, 'case', split_axis=0, concat_axis=0)]
    ppermute x12 -> x9, starting transfers between devices: 15.5 us -> 13.2 us  [to_cases(): lax.ppermute(message, 'case', [(k, (k + h) % groups) for k in range(group...]
    all_to_all x0 -> x1, waiting for transfers between devices: none -> 1.69 us  [local(): sums = lax.all_to_all(sums, 'case', split_axis=0, concat_axis=0)]
    ppermute x12 -> x9, waiting for transfers between devices: 4.59 us -> 3.34 us  [to_cases(): lax.ppermute(message, 'case', [(k, (k + h) % groups) for k in range(group...]
    pallas_call x15 -> x16, Pallas kernels: 32.4 us -> 33.4 us  [run(): pl.pallas_call(kernel, out_shape=results, in_specs=specs, out_specs=[vmem...]
  transfers between devices with their start and end apart: 15 -> 13, of which waited for: 6 -> 5; matrix products, arithmetic and copies ran while one was open for 0% -> 0% of each run, Pallas kernels for 14% -> 14%
where the time goes in v10:
time: 132 us; the launch traced here: 131 us
  starting transfers between devices  36.7 us (28%)
  blocking collectives  36.1 us (27%)
  Pallas kernels  33.4 us (25%)
  waiting for transfers between devices  23.4 us (18%)
    pallas_call x16, Pallas kernels, run(): pl.pallas_call(kernel, out_shape=results, in_specs=specs, out_specs=[vmem...  33.4 us
    all_to_all x1, blocking collectives, exchange(): lax.all_to_all(rows.reshape(parts, 1, -1), PLANE, split_axis=0, concat_ax...  26.4 us
    ppermute x9, starting transfers between devices, to_cases(): lax.ppermute(message, 'case', [(k, (k + h) % groups) for k in range(group...  13.2 us
    all_to_all x2, starting transfers between devices, exchange(): lax.all_to_all(rows.reshape(parts, 1, -1), PLANE, split_axis=0, concat_ax...  13.2 us
    all_to_all x2, waiting for transfers between devices, exchange(): lax.all_to_all(rows.reshape(parts, 1, -1), PLANE, split_axis=0, concat_ax...  12.6 us
    all_to_all x1, blocking collectives, local(): copies = lax.all_to_all(copies, 'px', split_axis=0, concat_axis=0)  9.74 us
    all_to_all x1, starting transfers between devices, local(): copies = lax.all_to_all(copies, ('py', 'case'), split_axis=0, concat_axis=0)  6.88 us
    all_to_all x1, waiting for transfers between devices, local(): copies = lax.all_to_all(copies, ('py', 'case'), split_axis=0, concat_axis=0)  5.76 us
  transfers between devices with their start and end apart: 13, of which 5 were waited for; matrix products, arithmetic and copies ran while one was open for 0% of the time, Pallas kernels for 14%

profile of v10, /device:TPU:1, one launch (start us, length us, event | category | flops | bytes accessed | tf_op | source)
XLA Modules:
  0.0 131.4 jit_solution(10960429644255551806)
XLA Ops:
  0.6 3.4 %condense.1 = (f32[640,128]{1,0:T(8,128)S(1)}, f32[384,128]{1,0:T(8,128)}, f32[64,128]{1,0:T(8,128)S(1)}, f32[8,128]{1,0:T(8,128)S(1)}) custom-call(s32[1,128]{1,0:T(1,128)} %bitcast.32, f32[1,128]{1,0:T(1,128)} %bitcast.33, s32[1,128]{1,0:T(1,128)} %bitcast.34, s32[1,128]{1,0:T(1,128)} %bitcast.35, s32[1,128]{1,0:T(1,128)} %bitcast.36, ...), custom_call_target="tpu_custom_call" | custom-call | bytes 592384 | tf_op jit(solution)/shard_map/condense/pallas_call | solution.py:578
  4.0 0.0 copy-start.6
  4.0 0.0 copy-start.7
  4.0 26.4 %all_to_all.30 = f32[64,1,1280]{2,1,0:T(1,128)S(1)} all-to-all(f32[64,1,1280]{2,1,0:T(1,128)S(1)} %bitcast.25), channel_id=1, replica_groups=mesh['px'=8,'py'=8,'case'=4] {'px','py'}, dimensions={0} | all-to-all | bytes 655360 | tf_op jit(solution)/shard_map/all_to_all | solution.py:594
  30.4 1.4 %rhs.1 = (f32[384,128]{1,0:T(8,128)}, f32[1152,128]{1,0:T(8,128)}, f32[64,128]{1,0:T(8,128)S(1)}) custom-call(f32[640,128]{1,0:T(8,128)S(1)} %bitcast.22, f32[384,128]{1,0:T(8,128)S(1)} %copy-done.7, f32[384,128]{1,0:T(8,128)S(1)} %bitcast.30, f32[64,128]{1,0:T(8,128)S(1)} %get-tuple-element.44.meta_ref.rest_0_), custom_call_target="tpu_custom_call" | custom-call | bytes 753664 | tf_op jit(solution)/shard_map/rhs/pallas_call | solution.py:578
  31.8 6.3 %all-to-all-start.1 = ((f32[64,1,2304]{2,1,0:T(1,128)}), f32[64,1,2304]{2,1,0:T(1,128)S(1)}, u32[]{:S(2)}, u32[]{:S(2)}) async-start(f32[64,1,2304]{2,1,0:T(1,128)} %bitcast.11), calls=%async_computation.1 | async-start | bytes 1179648 | tf_op jit(solution)/shard_map/all_to_all | solution.py:594
  38.2 1.3 collective-permute-start.2
  39.5 2.4 %collective-permute-start.1 = (f32[384,128]{1,0:T(8,128)S(1)}, f32[384,128]{1,0:T(8,128)S(1)}, u32[]{:S(2)}, u32[]{:S(2)}) collective-permute-start(f32[384,128]{1,0:T(8,128)S(1)} %copy-done), channel_id=1, source_target_pairs={{0,2},{1,3},{2,0},{3,1},{4,6},{5,7},{6,4},{7,5},{8,10},{9,11},{10,... | collective-permute-start | bytes 589832 | tf_op jit(solution)/shard_map/ppermute | solution.py:646
  41.9 1.2 collective-permute-start
  43.1 2.6 %tables.1 = (bf16[384,144]{1,0:T(8,128)(2,1)S(1)}, bf16[384,144]{1,0:T(8,128)(2,1)S(1)}, bf16[384,144]{1,0:T(8,128)(2,1)S(1)}, bf16[384,144]{1,0:T(8,128)(2,1)S(...) custom-call(f32[8,128]{1,0:T(8,128)S(1)} %get-tuple-element.49.where_ref, ...), custom_call_target="tpu_custom_call" | custom-call | flops 1000000000 | bytes 888832 | tf_op jit(solution)/shard_map/tables/pallas_call | solution.py:578
  45.7 1.6 %inner.2 = (f32[384,128]{1,0:T(8,128)S(1)}, f32[384,128]{1,0:T(8,128)S(1)}) custom-call(f32[384,128]{1,0:T(8,128)S(1)} %copy-done, f32[64,128]{1,0:T(8,128)S(1)} %get-tuple-element.48.asked_ref, f32[8,128]{1,0:T(8,128)S(1)} %get-tuple-element.49.where_ref, bf16[384,144]{1,0:T(8,128)(2,1)S(1)} %get-tuple-element.50.near_near, ...), custom_call_target="tpu_custom_call" | custom-call | flops 1000000000 | bytes 454656 | tf_op jit(solution)/shard_map/inner/pallas_call | solution.py:578
  47.4 0.0 collective-permute-done.2.refs_3_
  47.4 3.3 %collective-permute-done.1.refs_2_ = f32[384,128]{1,0:T(8,128)S(1)} collective-permute-done((f32[384,128]{1,0:T(8,128)S(1)}, f32[384,128]{1,0:T(8,128)S(1)}, u32[]{:S(2)}, u32[]{:S(2)}) %collective-permute-start.1) | collective-permute-done | bytes 196640 | tf_op jit(solution)/shard_map/ppermute | solution.py:646
  50.7 0.0 collective-permute-done.refs_1_
  50.7 1.5 %base_gram.1.gram_ref = f32[8,128]{1,0:T(8,128)S(1)} custom-call(s32[1]{0:T(128)} %bitcast.case_ref.rest_0_, f32[384,128]{1,0:T(8,128)S(1)} %copy-done, f32[384,128]{1,0:T(8,128)S(1)} %collective-permute-done.refs_1_, f32[384,128]{1,0:T(8,128)S(1)} %collective-permute-done.1.refs_2_, f32[384,128]{1,0:T(8,128)S(1)} %collective-permute-done.2.refs_3_), custom_call_target="tpu_custom_call" | custom-call | bytes 786436 | tf_op jit(solution)/shard_map/base_gram/pallas_call | solution.py:578
  52.2 4.5 %all-to-all-done.1 = f32[64,1,2304]{2,1,0:T(1,128)S(1)} async-done(((f32[64,1,2304]{2,1,0:T(1,128)}), f32[64,1,2304]{2,1,0:T(1,128)S(1)}, u32[]{:S(2)}, u32[]{:S(2)}) %all-to-all-start.1) | async-done | bytes 589856 | tf_op jit(solution)/shard_map/all_to_all | solution.py:594
  56.7 2.7 %image.1 = (f32[384,128]{1,0:T(8,128)S(1)}, f32[384,128]{1,0:T(8,128)}, f32[1152,128]{1,0:T(8,128)}) custom-call(f32[1152,128]{1,0:T(8,128)S(1)} %bitcast.20, f32[384,128]{1,0:T(8,128)S(1)} %get-tuple-element.52.inner_ref, f32[64,128]{1,0:T(8,128)S(1)} %get-tuple-element.48.asked_ref, f32[8,128]{1,0:T(8,128)S(1)} %get-tuple-element.49.where_ref, ...), custom_call_target="tpu_custom_call" | custom-call | bytes 1077248 | tf_op jit(solution)/shard_map/image/pallas_call | solution.py:578
  59.4 6.9 %all-to-all-start.2 = ((f32[64,1,2304]{2,1,0:T(1,128)}), f32[64,1,2304]{2,1,0:T(1,128)S(1)}, u32[]{:S(2)}, u32[]{:S(2)}) async-start(f32[64,1,2304]{2,1,0:T(1,128)} %bitcast.13), calls=%async_computation.2 | async-start | bytes 1179648 | tf_op jit(solution)/shard_map/all_to_all | solution.py:594
  66.3 1.1 collective-permute-start.5
  67.5 2.4 %collective-permute-start.4 = (f32[384,128]{1,0:T(8,128)S(1)}, f32[384,128]{1,0:T(8,128)S(1)}, u32[]{:S(2)}, u32[]{:S(2)}) collective-permute-start(f32[384,128]{1,0:T(8,128)S(1)} %get-tuple-element.60.field_ref.refs_4_.rest_5_), channel_id=1, source_target_pairs={{0,2},{1,3},{2,0},{3,1},{4,6},{5,7},{6,4},{7,5},{8,10},{9,11},{10,... | collective-permute-start | bytes 589832 | tf_op jit(solution)/shard_map/ppermute | solution.py:646
  69.8 1.2 collective-permute-start.3
  71.0 1.6 %inner.3 = (f32[384,128]{1,0:T(8,128)S(1)}, f32[384,128]{1,0:T(8,128)S(1)}) custom-call(f32[384,128]{1,0:T(8,128)S(1)} %get-tuple-element.60.field_ref.refs_4_.rest_5_, f32[64,128]{1,0:T(8,128)S(1)} %get-tuple-element.48.asked_ref, f32[8,128]{1,0:T(8,128)S(1)} %get-tuple-element.49.where_ref, bf16[384,144]{1,0:T(8,128)(2,1)S(1)} %get-tuple-element.50.near_near, ...), custom_call_target="tpu_custom_call" | custom-call | flops 1000000000 | bytes 454656 | tf_op jit(solution)/shard_map/inner/pallas_call | solution.py:578
  72.7 0.0 copy-start.12
  72.7 1.5 %gram.1.rest_1_ = f32[8,128]{1,0:T(8,128)S(1)} custom-call(s32[1]{0:T(128)} %bitcast.case_ref.rest_0_, f32[8,128]{1,0:T(8,128)S(1)} %base_gram.1.gram_ref, f32[384,128]{1,0:T(8,128)S(1)} %copy-done, f32[384,128]{1,0:T(8,128)S(1)} %collective-permute-done.refs_1_, f32[384,128]{1,0:T(8,128)S(1)} %collective-permute-done.1.refs_2_, ...), custom_call_target="tpu_custom_call" | custom-call | bytes 987140 | tf_op jit(solution)/shard_map/gram/pallas_call | solution.py:578
  74.2 0.0 copy-start.11
  74.2 1.2 turned_near.1.rest_4_
  75.4 1.4 %turned.1.rest_3_ = f32[512,128]{1,0:T(8,128)} custom-call(f32[384,128]{1,0:T(8,128)S(1)} %copy-done.16, f32[384,128]{1,0:T(8,128)S(1)} %copy-done.11, f32[8,128]{1,0:T(8,128)S(1)} %get-tuple-element.49.where_ref, bf16[512,144]{1,0:T(8,128)(2,1)S(1)} %copy-done.12, bf16[512,144]{1,0:T(8,128)(2,1)S(1)} %copy-done.2), custom_call_target="tpu_custom_call" | custom-call | flops 1000000000 | bytes 692224 | tf_op jit(solution)/shard_map/turned/pallas_call | solution.py:578
  76.8 8.1 %all-to-all-done.2 = f32[64,1,2304]{2,1,0:T(1,128)S(1)} async-done(((f32[64,1,2304]{2,1,0:T(1,128)}), f32[64,1,2304]{2,1,0:T(1,128)S(1)}, u32[]{:S(2)}, u32[]{:S(2)}) %all-to-all-start.2) | async-done | bytes 589856 | tf_op jit(solution)/shard_map/all_to_all | solution.py:594
  84.9 0.0 collective-permute-done.5.rest_8_.refs_7_
  84.9 0.0 collective-permute-done.4.rest_7_.refs_6_
  84.9 0.0 collective-permute-done.3.rest_6_.refs_5_
  84.9 5.3 %second.1 = (f32[384,128]{1,0:T(8,128)}, f32[32,8,128]{2,1,0:T(8,128)}, f32[256,128]{1,0:T(8,128)}, f32[640,128]{1,0:T(8,128)}, f32[640,128]{1,0:T(8,128)}, /*index=5*/f32[640,128]{1,0:T(8,128)}) custom-call(f32[1152,128]{1,0:T(8,128)S(1)} %bitcast.21, f32[384,128]{1,0:T(8,128)S(1)} %get-tuple-element.63.inner_ref, ...), custom_call_target="tpu_custom_call" | custom-call | bytes 2506756 | tf_op jit(solution)/shard_map/second/pallas_call | solution.py:578
  90.2 6.9 %all-to-all-start.3 = ((f32[32,8,128]{2,1,0:T(8,128)}), f32[32,8,128]{2,1,0:T(8,128)S(1)}, u32[]{:S(2)}, u32[]{:S(2)}) async-start(f32[32,8,128]{2,1,0:T(8,128)} %get-tuple-element.67), calls=%async_computation.3 | async-start | bytes 262144 | tf_op jit(solution)/shard_map/all_to_all | solution.py:695
  97.1 2.5 %collective-permute-start.6 = (f32[640,128]{1,0:T(8,128)}, f32[640,128]{1,0:T(8,128)S(1)}, u32[]{:S(2)}, u32[]{:S(2)}) collective-permute-start(f32[640,128]{1,0:T(8,128)} %get-tuple-element.73), channel_id=1, source_target_pairs={{0,3},{1,0},{2,1},{3,2},{4,7},{5,4},{6,5},{7,6},{8,11},{9,8},{10,9... | collective-permute-start | bytes 983048 | tf_op jit(solution)/shard_map/ppermute | solution.py:646
  99.6 0.6 collective-permute-start.7
  100.2 0.6 collective-permute-start.8
  100.8 5.8 %all-to-all-done.3 = f32[32,8,128]{2,1,0:T(8,128)S(1)} async-done(((f32[32,8,128]{2,1,0:T(8,128)}), f32[32,8,128]{2,1,0:T(8,128)S(1)}, u32[]{:S(2)}, u32[]{:S(2)}) %all-to-all-start.3) | async-done | bytes 131104 | tf_op jit(solution)/shard_map/all_to_all | solution.py:695
  106.6 9.7 %all_to_all.31.gram_ref = f32[8,32,128]{2,1,0:T(8,128)S(1)} all-to-all(f32[8,32,128]{2,1,0:T(8,128)S(1)} %sum.1), channel_id=1, replica_groups=mesh['px'=8,'py'=8,'case'=4] {'px'}, dimensions={0} | all-to-all | bytes 262144 | tf_op jit(solution)/shard_map/all_to_all | solution.py:709
  116.3 4.3 %solve.1 = (f32[64,8,128]{2,1,0:T(8,128)S(1)}, f32[32,256]{1,0:T(8,128)S(1)}) custom-call(s32[1]{0:T(128)} %bitcast.case_ref.rest_0_, f32[8,32,128]{2,1,0:T(8,128)S(1)} %all_to_all.31.gram_ref), custom_call_target="tpu_custom_call" | custom-call | bytes 131076 | tf_op jit(solution)/shard_map/solve/pallas_call | solution.py:578
  120.6 0.0 collective-permute-done.6.refs_9_.refs_1_
  120.7 0.0 collective-permute-done.8.refs_11_.refs_3_
  120.7 1.1 bubble.1
  121.8 3.4 %all-to-all-start.5 = ((f32[4,128,128]{2,1,0:T(8,128)}), f32[4,128,128]{2,1,0:T(8,128)S(1)}, u32[]{:S(2)}, u32[]{:S(2)}) async-start(f32[4,128,128]{2,1,0:T(8,128)} %bubble.1), calls=%async_computation.5 | async-start | bytes 524288 | tf_op jit(solution)/shard_map/all_to_all | solution.py:720
  125.2 0.0 copy-start.10
  125.2 0.9 copy-done.10
  126.1 2.9 %ports.1 = (f32[384,128]{1,0:T(8,128)}, f32[384,128]{1,0:T(8,128)}) custom-call(f32[64,8,128]{2,1,0:T(8,128)S(1)} %get-tuple-element.68.coef, f32[384,128]{1,0:T(8,128)S(1)} %copy-done, f32[384,128]{1,0:T(8,128)S(1)} %collective-permute-done.refs_1_, f32[384,128]{1,0:T(8,128)S(1)} %collective-permute-done.1.refs_2_, ...), custom_call_target="tpu_custom_call" | custom-call | flops 1000000000 | bytes 3014656 | tf_op jit(solution)/shard_map/ports/pallas_call | solution.py:578
  129.0 1.7 %all-to-all-done.5 = f32[4,128,128]{2,1,0:T(8,128)S(1)} async-done(((f32[4,128,128]{2,1,0:T(8,128)}), f32[4,128,128]{2,1,0:T(8,128)S(1)}, u32[]{:S(2)}, u32[]{:S(2)}) %all-to-all-start.5) | async-done | bytes 262176 | tf_op jit(solution)/shard_map/all_to_all | solution.py:720
  130.7 0.7 join.1
  (31 shorter events, 0.1 us)
Async XLA Ops:
  4.0 26.4 %copy-start.6 = (f32[48,8,128]{2,1,0:T(8,128)S(1)}, f32[48,8,128]{2,1,0:T(8,128)}, u32[]{:S(2)}) copy-start(f32[48,8,128]{2,1,0:T(8,128)} %param.16) | copy-start | bytes 589828
  4.0 26.4 %copy-start.7 = (f32[384,128]{1,0:T(8,128)S(1)}, f32[384,128]{1,0:T(8,128)}, u32[]{:S(2)}) copy-start(f32[384,128]{1,0:T(8,128)} %get-tuple-element.43.near_sum_ref) | copy-start | bytes 589828
  30.4 12.7 %copy-start.9 = (f32[8,96,96]{2,1,0:T(8,128)S(1)}, f32[8,96,96]{2,1,0:T(8,128)}, u32[]{:S(2)}) copy-start(f32[8,96,96]{2,1,0:T(8,128)} %block_ref.1) | copy-start | bytes 884740
  31.8 6.3 %copy-start = (f32[384,128]{1,0:T(8,128)S(1)}, f32[384,128]{1,0:T(8,128)}, u32[]{:S(2)}) copy-start(f32[384,128]{1,0:T(8,128)} %get-tuple-element.46.refs_0_.field_ref) | copy-start | bytes 589828
  31.8 11.3 %copy-start.3 = (f32[64,8,128]{2,1,0:T(8,128)S(1)}, f32[64,8,128]{2,1,0:T(8,128)}, u32[]{:S(2)}) copy-start(f32[64,8,128]{2,1,0:T(8,128)} %param.15) | copy-start | bytes 786436
  31.8 11.3 %copy-start.4 = (f32[8,64,64]{2,1,0:T(8,128)S(1)}, f32[8,64,64]{2,1,0:T(8,128)}, u32[]{:S(2)}) copy-start(f32[8,64,64]{2,1,0:T(8,128)} %inverse_ref.1) | copy-start | bytes 393220
  31.8 11.3 %copy-start.5 = (f32[8,96,64]{1,2,0:T(8,128)S(1)}, f32[8,96,64]{1,2,0:T(8,128)}, u32[]{:S(2)}) copy-start(f32[8,96,64]{1,2,0:T(8,128)} %param.18) | copy-start | bytes 589828
  31.8 24.9 %all-to-all-start.1 = ((f32[64,1,2304]{2,1,0:T(1,128)}), f32[64,1,2304]{2,1,0:T(1,128)S(1)}, u32[]{:S(2)}, u32[]{:S(2)}) async-start(f32[64,1,2304]{2,1,0:T(1,128)} %bitcast.11), calls=%async_computation.1 | async-start | bytes 1179648 | tf_op jit(solution)/shard_map/all_to_all | solution.py:594
  38.2 9.2 %collective-permute-start.2 = (f32[384,128]{1,0:T(8,128)S(1)}, f32[384,128]{1,0:T(8,128)S(1)}, u32[]{:S(2)}, u32[]{:S(2)}) collective-permute-start(f32[384,128]{1,0:T(8,128)S(1)} %copy-done), channel_id=1, source_target_pairs={{0,1},{1,2},{2,3},{3,0},{4,5},{5,6},{6,7},{7,4},{8,9},{9,10},{10,1... | collective-permute-start | bytes 589832 | tf_op jit(solution)/shard_map/ppermute | solution.py:646
  39.5 11.2 %collective-permute-start.1 = (f32[384,128]{1,0:T(8,128)S(1)}, f32[384,128]{1,0:T(8,128)S(1)}, u32[]{:S(2)}, u32[]{:S(2)}) collective-permute-start(f32[384,128]{1,0:T(8,128)S(1)} %copy-done), channel_id=1, source_target_pairs={{0,2},{1,3},{2,0},{3,1},{4,6},{5,7},{6,4},{7,5},{8,10},{9,11},{10,... | collective-permute-start | bytes 589832 | tf_op jit(solution)/shard_map/ppermute | solution.py:646
  41.9 8.8 %collective-permute-start = (f32[384,128]{1,0:T(8,128)S(1)}, f32[384,128]{1,0:T(8,128)S(1)}, u32[]{:S(2)}, u32[]{:S(2)}) collective-permute-start(f32[384,128]{1,0:T(8,128)S(1)} %copy-done), channel_id=1, source_target_pairs={{0,3},{1,0},{2,1},{3,2},{4,7},{5,4},{6,5},{7,6},{8,11},{9,8},{10,9... | collective-permute-start | bytes 589832 | tf_op jit(solution)/shard_map/ppermute | solution.py:646
  45.7 1.7 %copy-start.13 = (bf16[384,144]{1,0:T(8,128)(2,1)}, bf16[384,144]{1,0:T(8,128)(2,1)S(1)}, u32[]{:S(2)}) copy-start(bf16[384,144]{1,0:T(8,128)(2,1)S(1)} %get-tuple-element.51.far_far) | copy-start | bytes 331780
  47.3 4.9 %copy-start.15 = (f32[384,128]{1,0:T(8,128)}, f32[384,128]{1,0:T(8,128)S(1)}, u32[]{:S(2)}) copy-start(f32[384,128]{1,0:T(8,128)S(1)} %get-tuple-element.56.near_values) | copy-start | bytes 589828
  59.4 11.6 %copy-start.14 = (bf16[384,144]{1,0:T(8,128)(2,1)S(1)}, bf16[384,144]{1,0:T(8,128)(2,1)}, u32[]{:S(2)}) copy-start(bf16[384,144]{1,0:T(8,128)(2,1)} %copy-done.13) | copy-start | bytes 331780
  59.4 25.5 %all-to-all-start.2 = ((f32[64,1,2304]{2,1,0:T(1,128)}), f32[64,1,2304]{2,1,0:T(1,128)S(1)}, u32[]{:S(2)}, u32[]{:S(2)}) async-start(f32[64,1,2304]{2,1,0:T(1,128)} %bitcast.13), calls=%async_computation.2 | async-start | bytes 1179648 | tf_op jit(solution)/shard_map/all_to_all | solution.py:594
  66.3 18.6 %collective-permute-start.5 = (f32[384,128]{1,0:T(8,128)S(1)}, f32[384,128]{1,0:T(8,128)S(1)}, u32[]{:S(2)}, u32[]{:S(2)}) collective-permute-start(f32[384,128]{1,0:T(8,128)S(1)} %get-tuple-element.60.field_ref.refs_4_.rest_5_), channel_id=1, source_target_pairs={{0,1},{1,2},{2,3},{3,0},{4,5},{5,6},{6,7},{7,4},{8,9},{9,10},{10,1... | collective-permute-start | bytes 589832 | tf_op jit(solution)/shard_map/ppermute | solution.py:646
  67.5 17.4 %collective-permute-start.4 = (f32[384,128]{1,0:T(8,128)S(1)}, f32[384,128]{1,0:T(8,128)S(1)}, u32[]{:S(2)}, u32[]{:S(2)}) collective-permute-start(f32[384,128]{1,0:T(8,128)S(1)} %get-tuple-element.60.field_ref.refs_4_.rest_5_), channel_id=1, source_target_pairs={{0,2},{1,3},{2,0},{3,1},{4,6},{5,7},{6,4},{7,5},{8,10},{9,11},{10,... | collective-permute-start | bytes 589832 | tf_op jit(solution)/shard_map/ppermute | solution.py:646
  69.8 15.1 %collective-permute-start.3 = (f32[384,128]{1,0:T(8,128)S(1)}, f32[384,128]{1,0:T(8,128)S(1)}, u32[]{:S(2)}, u32[]{:S(2)}) collective-permute-start(f32[384,128]{1,0:T(8,128)S(1)} %get-tuple-element.60.field_ref.refs_4_.rest_5_), channel_id=1, source_target_pairs={{0,3},{1,0},{2,1},{3,2},{4,7},{5,4},{6,5},{7,6},{8,11},{9,8},{10,9... | collective-permute-start | bytes 589832 | tf_op jit(solution)/shard_map/ppermute | solution.py:646
  72.7 1.5 %copy-start.12 = (bf16[512,144]{1,0:T(8,128)(2,1)S(1)}, bf16[512,144]{1,0:T(8,128)(2,1)}, u32[]{:S(2)}) copy-start(bf16[512,144]{1,0:T(8,128)(2,1)} %get-tuple-element.58.turned_near) | copy-start | bytes 442372
  74.2 1.2 copy-start.2
  74.2 1.2 copy-start.11
  74.2 1.2 copy-start.16
  90.2 16.3 %all-to-all-start.3 = ((f32[32,8,128]{2,1,0:T(8,128)}), f32[32,8,128]{2,1,0:T(8,128)S(1)}, u32[]{:S(2)}, u32[]{:S(2)}) async-start(f32[32,8,128]{2,1,0:T(8,128)} %get-tuple-element.67), calls=%async_computation.3 | async-start | bytes 262144 | tf_op jit(solution)/shard_map/all_to_all | solution.py:695
  97.1 23.5 %collective-permute-start.6 = (f32[640,128]{1,0:T(8,128)}, f32[640,128]{1,0:T(8,128)S(1)}, u32[]{:S(2)}, u32[]{:S(2)}) collective-permute-start(f32[640,128]{1,0:T(8,128)} %get-tuple-element.73), channel_id=1, source_target_pairs={{0,3},{1,0},{2,1},{3,2},{4,7},{5,4},{6,5},{7,6},{8,11},{9,8},{10,9... | collective-permute-start | bytes 983048 | tf_op jit(solution)/shard_map/ppermute | solution.py:646
  99.6 21.0 %collective-permute-start.7 = (f32[640,128]{1,0:T(8,128)}, f32[640,128]{1,0:T(8,128)S(1)}, u32[]{:S(2)}, u32[]{:S(2)}) collective-permute-start(f32[640,128]{1,0:T(8,128)} %get-tuple-element.74), channel_id=1, source_target_pairs={{0,2},{1,3},{2,0},{3,1},{4,6},{5,7},{6,4},{7,5},{8,10},{9,11},{10,... | collective-permute-start | bytes 983048 | tf_op jit(solution)/shard_map/ppermute | solution.py:646
  100.2 20.5 %collective-permute-start.8 = (f32[640,128]{1,0:T(8,128)}, f32[640,128]{1,0:T(8,128)S(1)}, u32[]{:S(2)}, u32[]{:S(2)}) collective-permute-start(f32[640,128]{1,0:T(8,128)} %get-tuple-element.75), channel_id=1, source_target_pairs={{0,1},{1,2},{2,3},{3,0},{4,5},{5,6},{6,7},{7,4},{8,9},{9,10},{10,1... | collective-permute-start | bytes 983048 | tf_op jit(solution)/shard_map/ppermute | solution.py:646
  116.3 4.4 %copy-start.8 = (f32[256,128]{1,0:T(8,128)S(1)}, f32[256,128]{1,0:T(8,128)}, u32[]{:S(2)}) copy-start(f32[256,128]{1,0:T(8,128)} %get-tuple-element.80.refs_0_) | copy-start | bytes 393220
  121.8 8.9 %all-to-all-start.5 = ((f32[4,128,128]{2,1,0:T(8,128)}), f32[4,128,128]{2,1,0:T(8,128)S(1)}, u32[]{:S(2)}, u32[]{:S(2)}) async-start(f32[4,128,128]{2,1,0:T(8,128)} %bubble.1), calls=%async_computation.5 | async-start | bytes 524288 | tf_op jit(solution)/shard_map/all_to_all | solution.py:720
  125.2 0.9 copy-start.10
  126.1 4.6 %copy-start.1 = (f32[512,128]{1,0:T(8,128)S(1)}, f32[512,128]{1,0:T(8,128)}, u32[]{:S(2)}) copy-start(f32[512,128]{1,0:T(8,128)} %get-tuple-element.78.bubble_ref) | copy-start | bytes 786436

commit v11 on v10

--- a/solution.py
+++ b/solution.py
@@ -505,10 +505,10 @@
                     coef[h * n + j] = jnp.broadcast_to(mine[:, j : j + 1], (CASES, LANES))
 
 
-def bubble_kernel(groups, rows, case_ref, coef_ref, *refs):
-    turned, out_ref = refs[:groups], refs[groups]
+def bubble_kernel(groups, rows, coef_ref, *refs):
+    turned, outs = refs[:groups], refs[groups:]
     n = groups * CASES
-    part = out_ref.shape[1]
+    part = outs[0].shape[0]
     firsts = [0] + [rows] * (groups - 1)
     left = stacked_table(jnp.concatenate([coef_ref[:, :n], coef_ref[:, LANES : LANES + n]], axis=1))
     for m in range(0, part // CASES, 2):
@@ -526,7 +526,7 @@
         result = dot(left, stacked_values(jnp.concatenate(values, axis=1)))
         for i in range(2):
             for h in range(groups):
-                out_ref[lax.rem(case_ref[0] + h, groups), (m + i) * CASES : (m + i + 1) * CASES, :] = result[
+                outs[h][(m + i) * CASES : (m + i + 1) * CASES, :] = result[
                     h * CASES : (h + 1) * CASES, i * LANES : (i + 1) * LANES
                 ]
 
@@ -559,8 +559,12 @@
     lax.fori_loop(0, dofs // wide, ports, 0)
 
 
-def join_kernel(bubble_ref, sums_ref, out_ref):
-    out_ref[...] = bubble_ref[...] - sums_ref[...]
+def join_kernel(groups, case_ref, bubble_ref, *refs):
+    parts, out_ref = refs[:groups], refs[groups]
+    part = parts[0].shape[0]
+    for h in range(groups):
+        at = pl.ds(pl.multiple_of(lax.rem(case_ref[0] + h, groups) * part, part), part)
+        out_ref[at, :] = bubble_ref[at, :] - parts[h][...]
 
 
 def call(kernel, outs, scratch=(), name=None, flops=0, smem=(), hbm=(), anywhere=(), sems=0, limit=12):
@@ -714,14 +718,16 @@
         "solve",
         smem=(0,),
     )(case, copies)
-    (sums,) = call(
-        functools.partial(bubble_kernel, groups, rows), [((groups, part, comps), F32, False)], name="bubble", smem=(0,)
-    )(case, coef_rows, turned_own, *both1)
-    sums = lax.all_to_all(sums, "case", split_axis=0, concat_axis=0)
+    own, *messages = call(
+        functools.partial(bubble_kernel, groups, rows), [((part, comps), F32, False)] * groups, name="bubble"
+    )(coef_rows, turned_own, *both1)
+    back = to_cases(messages)
     x, residual = call(
         functools.partial(ports_kernel, groups), [field_of, field_of], name="ports", flops=10**9
     )(coef, base, *base_all, image, *image_all, second, *both1)
-    (bubble,) = call(join_kernel, [bubble_of], name="join")(bubble_base, sums.reshape(bubbles, comps))
+    (bubble,) = call(functools.partial(join_kernel, groups), [bubble_of], name="join", smem=(0,))(
+        case, bubble_base, own, *back
+    )
     return (
         x.reshape(port_load.shape),
         residual.reshape(port_load.shape),

time: 132 us -> 129 us (0.977)
    all_to_all x1 -> x0, starting transfers between devices: 3.41 us -> none  [local(): sums = lax.all_to_all(sums, 'case', split_axis=0, concat_axis=0)]
    ppermute x9 -> x12, starting transfers between devices: 13.2 us -> 15.5 us  [to_cases(): lax.ppermute(message, 'case', [(k, (k + h) % groups) for k in range(group...]
    all_to_all x1 -> x0, waiting for transfers between devices: 1.69 us -> none  [local(): sums = lax.all_to_all(sums, 'case', split_axis=0, concat_axis=0)]
    ppermute x9 -> x12, waiting for transfers between devices: 3.34 us -> 4.9 us  [to_cases(): lax.ppermute(message, 'case', [(k, (k + h) % groups) for k in range(group...]
  transfers between devices with their start and end apart: 13 -> 15, of which waited for: 5 -> 6; matrix products, arithmetic and copies ran while one was open for 0% -> 0% of each run, Pallas kernels for 14% -> 15%
where the time goes in v11:
time: 129 us
  blocking collectives  36.1 us (28%)
  starting transfers between devices  35.6 us (28%)
  Pallas kernels  32.7 us (25%)
  waiting for transfers between devices  23.2 us (18%)
    pallas_call x16, Pallas kernels, run(): pl.pallas_call(kernel, out_shape=results, in_specs=specs, out_specs=[vmem...  32.7 us
    all_to_all x1, blocking collectives, exchange(): lax.all_to_all(rows.reshape(parts, 1, -1), PLANE, split_axis=0, concat_ax...  26.4 us
    ppermute x12, starting transfers between devices, to_cases(): lax.ppermute(message, 'case', [(k, (k + h) % groups) for k in range(group...  15.5 us
    all_to_all x2, starting transfers between devices, exchange(): lax.all_to_all(rows.reshape(parts, 1, -1), PLANE, split_axis=0, concat_ax...  13.2 us
    all_to_all x2, waiting for transfers between devices, exchange(): lax.all_to_all(rows.reshape(parts, 1, -1), PLANE, split_axis=0, concat_ax...  12.6 us
    all_to_all x1, blocking collectives, local(): copies = lax.all_to_all(copies, 'px', split_axis=0, concat_axis=0)  9.74 us
    all_to_all x1, starting transfers between devices, local(): copies = lax.all_to_all(copies, ('py', 'case'), split_axis=0, concat_axis=0)  6.89 us
    all_to_all x1, waiting for transfers between devices, local(): copies = lax.all_to_all(copies, ('py', 'case'), split_axis=0, concat_axis=0)  5.76 us
  transfers between devices with their start and end apart: 15, of which 6 were waited for; matrix products, arithmetic and copies ran while one was open for 0% of the time, Pallas kernels for 15%

profile of v11, /device:TPU:1, one launch (start us, length us, event | category | flops | bytes accessed | tf_op | source)
XLA Modules:
  0.0 128.5 jit_solution(4557392521988885655)
XLA Ops:
  0.6 3.4 %condense.1 = (f32[640,128]{1,0:T(8,128)S(1)}, f32[384,128]{1,0:T(8,128)}, f32[64,128]{1,0:T(8,128)S(1)}, f32[8,128]{1,0:T(8,128)S(1)}) custom-call(s32[1,128]{1,0:T(1,128)} %bitcast.30, f32[1,128]{1,0:T(1,128)} %bitcast.31, s32[1,128]{1,0:T(1,128)} %bitcast.32, s32[1,128]{1,0:T(1,128)} %bitcast.33, s32[1,128]{1,0:T(1,128)} %bitcast.34, ...), custom_call_target="tpu_custom_call" | custom-call | bytes 592384 | tf_op jit(solution)/shard_map/condense/pallas_call | solution.py:582
  4.0 0.0 copy-start.6
  4.0 0.0 copy-start.7
  4.0 26.4 %all_to_all.25 = f32[64,1,1280]{2,1,0:T(1,128)S(1)} all-to-all(f32[64,1,1280]{2,1,0:T(1,128)S(1)} %bitcast.23), channel_id=1, replica_groups=mesh['px'=8,'py'=8,'case'=4] {'px','py'}, dimensions={0} | all-to-all | bytes 655360 | tf_op jit(solution)/shard_map/all_to_all | solution.py:598
  30.4 1.4 %rhs.1 = (f32[384,128]{1,0:T(8,128)}, f32[1152,128]{1,0:T(8,128)}, f32[64,128]{1,0:T(8,128)S(1)}) custom-call(f32[640,128]{1,0:T(8,128)S(1)} %bitcast.21, f32[384,128]{1,0:T(8,128)S(1)} %copy-done.7, f32[384,128]{1,0:T(8,128)S(1)} %bitcast.28, f32[64,128]{1,0:T(8,128)S(1)} %get-tuple-element.48.meta_ref.rest_0_), custom_call_target="tpu_custom_call" | custom-call | bytes 753664 | tf_op jit(solution)/shard_map/rhs/pallas_call | solution.py:582
  31.8 6.3 %all-to-all-start.1 = ((f32[64,1,2304]{2,1,0:T(1,128)}), f32[64,1,2304]{2,1,0:T(1,128)S(1)}, u32[]{:S(2)}, u32[]{:S(2)}) async-start(f32[64,1,2304]{2,1,0:T(1,128)} %bitcast.11), calls=%async_computation.1 | async-start | bytes 1179648 | tf_op jit(solution)/shard_map/all_to_all | solution.py:598
  38.2 1.3 %collective-permute-start.2 = (f32[384,128]{1,0:T(8,128)S(1)}, f32[384,128]{1,0:T(8,128)S(1)}, u32[]{:S(2)}, u32[]{:S(2)}) collective-permute-start(f32[384,128]{1,0:T(8,128)S(1)} %copy-done), channel_id=1, source_target_pairs={{0,1},{1,2},{2,3},{3,0},{4,5},{5,6},{6,7},{7,4},{8,9},{9,10},{10,1... | collective-permute-start | bytes 589832 | tf_op jit(solution)/shard_map/ppermute | solution.py:650
  39.5 2.4 %collective-permute-start.1 = (f32[384,128]{1,0:T(8,128)S(1)}, f32[384,128]{1,0:T(8,128)S(1)}, u32[]{:S(2)}, u32[]{:S(2)}) collective-permute-start(f32[384,128]{1,0:T(8,128)S(1)} %copy-done), channel_id=1, source_target_pairs={{0,2},{1,3},{2,0},{3,1},{4,6},{5,7},{6,4},{7,5},{8,10},{9,11},{10,... | collective-permute-start | bytes 589832 | tf_op jit(solution)/shard_map/ppermute | solution.py:650
  41.9 1.2 collective-permute-start
  43.1 2.6 %tables.1 = (bf16[384,144]{1,0:T(8,128)(2,1)S(1)}, bf16[384,144]{1,0:T(8,128)(2,1)S(1)}, bf16[384,144]{1,0:T(8,128)(2,1)S(1)}, bf16[384,144]{1,0:T(8,128)(2,1)S(...) custom-call(f32[8,128]{1,0:T(8,128)S(1)} %get-tuple-element.53.where_ref, ...), custom_call_target="tpu_custom_call" | custom-call | flops 1000000000 | bytes 888832 | tf_op jit(solution)/shard_map/tables/pallas_call | solution.py:582
  45.7 1.6 %inner.2 = (f32[384,128]{1,0:T(8,128)S(1)}, f32[384,128]{1,0:T(8,128)S(1)}) custom-call(f32[384,128]{1,0:T(8,128)S(1)} %copy-done, f32[64,128]{1,0:T(8,128)S(1)} %get-tuple-element.52.asked_ref, f32[8,128]{1,0:T(8,128)S(1)} %get-tuple-element.53.where_ref, bf16[384,144]{1,0:T(8,128)(2,1)S(1)} %get-tuple-element.54.near_near, ...), custom_call_target="tpu_custom_call" | custom-call | flops 1000000000 | bytes 454656 | tf_op jit(solution)/shard_map/inner/pallas_call | solution.py:582
  47.4 0.0 collective-permute-done.2.refs_3_
  47.4 3.3 %collective-permute-done.1.refs_2_ = f32[384,128]{1,0:T(8,128)S(1)} collective-permute-done((f32[384,128]{1,0:T(8,128)S(1)}, f32[384,128]{1,0:T(8,128)S(1)}, u32[]{:S(2)}, u32[]{:S(2)}) %collective-permute-start.1) | collective-permute-done | bytes 196640 | tf_op jit(solution)/shard_map/ppermute | solution.py:650
  50.7 1.5 %base_gram.1.gram_ref = f32[8,128]{1,0:T(8,128)S(1)} custom-call(s32[1]{0:T(128)} %bitcast.case_ref.rest_0_, f32[384,128]{1,0:T(8,128)S(1)} %copy-done, f32[384,128]{1,0:T(8,128)S(1)} %collective-permute-done.refs_1_, f32[384,128]{1,0:T(8,128)S(1)} %collective-permute-done.1.refs_2_, f32[384,128]{1,0:T(8,128)S(1)} %collective-permute-done.2.refs_3_), custom_call_target="tpu_custom_call" | custom-call | bytes 786436 | tf_op jit(solution)/shard_map/base_gram/pallas_call | solution.py:582
  52.2 4.5 %all-to-all-done.1 = f32[64,1,2304]{2,1,0:T(1,128)S(1)} async-done(((f32[64,1,2304]{2,1,0:T(1,128)}), f32[64,1,2304]{2,1,0:T(1,128)S(1)}, u32[]{:S(2)}, u32[]{:S(2)}) %all-to-all-start.1) | async-done | bytes 589856 | tf_op jit(solution)/shard_map/all_to_all | solution.py:598
  56.7 2.7 %image.1 = (f32[384,128]{1,0:T(8,128)S(1)}, f32[384,128]{1,0:T(8,128)}, f32[1152,128]{1,0:T(8,128)}) custom-call(f32[1152,128]{1,0:T(8,128)S(1)} %bitcast.19, f32[384,128]{1,0:T(8,128)S(1)} %get-tuple-element.56.inner_ref, f32[64,128]{1,0:T(8,128)S(1)} %get-tuple-element.52.asked_ref, f32[8,128]{1,0:T(8,128)S(1)} %get-tuple-element.53.where_ref, ...), custom_call_target="tpu_custom_call" | custom-call | bytes 1077248 | tf_op jit(solution)/shard_map/image/pallas_call | solution.py:582
  59.4 6.9 %all-to-all-start.2 = ((f32[64,1,2304]{2,1,0:T(1,128)}), f32[64,1,2304]{2,1,0:T(1,128)S(1)}, u32[]{:S(2)}, u32[]{:S(2)}) async-start(f32[64,1,2304]{2,1,0:T(1,128)} %bitcast.13), calls=%async_computation.2 | async-start | bytes 1179648 | tf_op jit(solution)/shard_map/all_to_all | solution.py:598
  66.3 1.1 collective-permute-start.5
  67.5 2.4 %collective-permute-start.4 = (f32[384,128]{1,0:T(8,128)S(1)}, f32[384,128]{1,0:T(8,128)S(1)}, u32[]{:S(2)}, u32[]{:S(2)}) collective-permute-start(f32[384,128]{1,0:T(8,128)S(1)} %get-tuple-element.64.field_ref.refs_4_.rest_5_), channel_id=1, source_target_pairs={{0,2},{1,3},{2,0},{3,1},{4,6},{5,7},{6,4},{7,5},{8,10},{9,11},{10,... | collective-permute-start | bytes 589832 | tf_op jit(solution)/shard_map/ppermute | solution.py:650
  69.8 1.2 collective-permute-start.3
  71.0 1.6 %inner.3 = (f32[384,128]{1,0:T(8,128)S(1)}, f32[384,128]{1,0:T(8,128)S(1)}) custom-call(f32[384,128]{1,0:T(8,128)S(1)} %get-tuple-element.64.field_ref.refs_4_.rest_5_, f32[64,128]{1,0:T(8,128)S(1)} %get-tuple-element.52.asked_ref, f32[8,128]{1,0:T(8,128)S(1)} %get-tuple-element.53.where_ref, bf16[384,144]{1,0:T(8,128)(2,1)S(1)} %get-tuple-element.54.near_near, ...), custom_call_target="tpu_custom_call" | custom-call | flops 1000000000 | bytes 454656 | tf_op jit(solution)/shard_map/inner/pallas_call | solution.py:582
  72.7 0.0 copy-start.12
  72.7 1.5 %gram.1.rest_1_ = f32[8,128]{1,0:T(8,128)S(1)} custom-call(s32[1]{0:T(128)} %bitcast.case_ref.rest_0_, f32[8,128]{1,0:T(8,128)S(1)} %base_gram.1.gram_ref, f32[384,128]{1,0:T(8,128)S(1)} %copy-done, f32[384,128]{1,0:T(8,128)S(1)} %collective-permute-done.refs_1_, f32[384,128]{1,0:T(8,128)S(1)} %collective-permute-done.1.refs_2_, ...), custom_call_target="tpu_custom_call" | custom-call | bytes 987140 | tf_op jit(solution)/shard_map/gram/pallas_call | solution.py:582
  74.2 0.0 copy-start.11
  74.2 1.2 turned_near.1.rest_4_
  75.4 1.4 %turned.1.rest_3_ = f32[512,128]{1,0:T(8,128)} custom-call(f32[384,128]{1,0:T(8,128)S(1)} %copy-done.16, f32[384,128]{1,0:T(8,128)S(1)} %copy-done.11, f32[8,128]{1,0:T(8,128)S(1)} %get-tuple-element.53.where_ref, bf16[512,144]{1,0:T(8,128)(2,1)S(1)} %copy-done.12, bf16[512,144]{1,0:T(8,128)(2,1)S(1)} %copy-done.1), custom_call_target="tpu_custom_call" | custom-call | flops 1000000000 | bytes 692224 | tf_op jit(solution)/shard_map/turned/pallas_call | solution.py:582
  76.8 8.1 %all-to-all-done.2 = f32[64,1,2304]{2,1,0:T(1,128)S(1)} async-done(((f32[64,1,2304]{2,1,0:T(1,128)}), f32[64,1,2304]{2,1,0:T(1,128)S(1)}, u32[]{:S(2)}, u32[]{:S(2)}) %all-to-all-start.2) | async-done | bytes 589856 | tf_op jit(solution)/shard_map/all_to_all | solution.py:598
  84.9 0.0 collective-permute-done.5.rest_8_.refs_7_
  84.9 0.0 collective-permute-done.4.rest_7_.refs_6_
  84.9 0.0 collective-permute-done.3.rest_6_.refs_5_
  84.9 5.3 %second.1 = (f32[384,128]{1,0:T(8,128)}, f32[32,8,128]{2,1,0:T(8,128)}, f32[256,128]{1,0:T(8,128)}, f32[640,128]{1,0:T(8,128)}, f32[640,128]{1,0:T(8,128)}, /*index=5*/f32[640,128]{1,0:T(8,128)}) custom-call(f32[1152,128]{1,0:T(8,128)S(1)} %bitcast.20, f32[384,128]{1,0:T(8,128)S(1)} %get-tuple-element.67.inner_ref, ...), custom_call_target="tpu_custom_call" | custom-call | bytes 2506756 | tf_op jit(solution)/shard_map/second/pallas_call | solution.py:582
  90.2 6.9 %all-to-all-start.3 = ((f32[32,8,128]{2,1,0:T(8,128)}), f32[32,8,128]{2,1,0:T(8,128)S(1)}, u32[]{:S(2)}, u32[]{:S(2)}) async-start(f32[32,8,128]{2,1,0:T(8,128)} %get-tuple-element.71), calls=%async_computation.3 | async-start | bytes 262144 | tf_op jit(solution)/shard_map/all_to_all | solution.py:699
  97.1 2.5 %collective-permute-start.6 = (f32[640,128]{1,0:T(8,128)}, f32[640,128]{1,0:T(8,128)S(1)}, u32[]{:S(2)}, u32[]{:S(2)}) collective-permute-start(f32[640,128]{1,0:T(8,128)} %get-tuple-element.77), channel_id=1, source_target_pairs={{0,3},{1,0},{2,1},{3,2},{4,7},{5,4},{6,5},{7,6},{8,11},{9,8},{10,9... | collective-permute-start | bytes 983048 | tf_op jit(solution)/shard_map/ppermute | solution.py:650
  99.6 0.6 collective-permute-start.7
  100.2 0.6 collective-permute-start.8
  100.8 5.8 %all-to-all-done.3 = f32[32,8,128]{2,1,0:T(8,128)S(1)} async-done(((f32[32,8,128]{2,1,0:T(8,128)}), f32[32,8,128]{2,1,0:T(8,128)S(1)}, u32[]{:S(2)}, u32[]{:S(2)}) %all-to-all-start.3) | async-done | bytes 131104 | tf_op jit(solution)/shard_map/all_to_all | solution.py:699
  106.6 9.7 %all_to_all.26.gram_ref = f32[8,32,128]{2,1,0:T(8,128)S(1)} all-to-all(f32[8,32,128]{2,1,0:T(8,128)S(1)} %sum.1), channel_id=1, replica_groups=mesh['px'=8,'py'=8,'case'=4] {'px'}, dimensions={0} | all-to-all | bytes 262144 | tf_op jit(solution)/shard_map/all_to_all | solution.py:713
  116.3 4.3 %solve.1 = (f32[64,8,128]{2,1,0:T(8,128)S(1)}, f32[32,256]{1,0:T(8,128)S(1)}) custom-call(s32[1]{0:T(128)} %bitcast.case_ref.rest_0_, f32[8,32,128]{2,1,0:T(8,128)S(1)} %all_to_all.26.gram_ref), custom_call_target="tpu_custom_call" | custom-call | bytes 131076 | tf_op jit(solution)/shard_map/solve/pallas_call | solution.py:582
  120.6 0.0 collective-permute-done.7.refs_10_.refs_2_
  120.7 0.0 copy-start.10
  120.7 0.4 bubble.1
  121.0 1.5 %collective-permute-start.9 = (f32[128,128]{1,0:T(8,128)S(1)}, f32[128,128]{1,0:T(8,128)S(1)}, u32[]{:S(2)}, u32[]{:S(2)}) collective-permute-start(f32[128,128]{1,0:T(8,128)S(1)} %get-tuple-element.86), channel_id=1, source_target_pairs={{0,3},{1,0},{2,1},{3,2},{4,7},{5,4},{6,5},{7,6},{8,11},{9,8},{10,9... | collective-permute-start | bytes 196616 | tf_op jit(solution)/shard_map/ppermute | solution.py:650
  122.6 0.2 collective-permute-start.10
  122.8 0.5 collective-permute-start.11
  123.3 2.9 %ports.1 = (f32[384,128]{1,0:T(8,128)}, f32[384,128]{1,0:T(8,128)}) custom-call(f32[64,8,128]{2,1,0:T(8,128)S(1)} %get-tuple-element.72.coef, f32[384,128]{1,0:T(8,128)S(1)} %copy-done, f32[384,128]{1,0:T(8,128)S(1)} %collective-permute-done.refs_1_, f32[384,128]{1,0:T(8,128)S(1)} %collective-permute-done.1.refs_2_, ...), custom_call_target="tpu_custom_call" | custom-call | flops 1000000000 | bytes 3014656 | tf_op jit(solution)/shard_map/ports/pallas_call | solution.py:582
  126.2 1.1 collective-permute-done.10.refs_2_
  127.3 0.5 collective-permute-done.11.refs_3_
  127.8 0.7 join.1
  (35 shorter events, 0.1 us)
Async XLA Ops:
  4.0 26.4 %copy-start.6 = (f32[48,8,128]{2,1,0:T(8,128)S(1)}, f32[48,8,128]{2,1,0:T(8,128)}, u32[]{:S(2)}) copy-start(f32[48,8,128]{2,1,0:T(8,128)} %param.16) | copy-start | bytes 589828
  4.0 26.4 %copy-start.7 = (f32[384,128]{1,0:T(8,128)S(1)}, f32[384,128]{1,0:T(8,128)}, u32[]{:S(2)}) copy-start(f32[384,128]{1,0:T(8,128)} %get-tuple-element.47.near_sum_ref) | copy-start | bytes 589828
  30.4 12.7 %copy-start.9 = (f32[8,96,96]{2,1,0:T(8,128)S(1)}, f32[8,96,96]{2,1,0:T(8,128)}, u32[]{:S(2)}) copy-start(f32[8,96,96]{2,1,0:T(8,128)} %block_ref.1) | copy-start | bytes 884740
  31.8 6.3 %copy-start = (f32[384,128]{1,0:T(8,128)S(1)}, f32[384,128]{1,0:T(8,128)}, u32[]{:S(2)}) copy-start(f32[384,128]{1,0:T(8,128)} %get-tuple-element.50.refs_0_.field_ref) | copy-start | bytes 589828
  31.8 11.3 %copy-start.2 = (f32[64,8,128]{2,1,0:T(8,128)S(1)}, f32[64,8,128]{2,1,0:T(8,128)}, u32[]{:S(2)}) copy-start(f32[64,8,128]{2,1,0:T(8,128)} %param.15) | copy-start | bytes 786436
  31.8 11.3 %copy-start.3 = (f32[8,64,64]{2,1,0:T(8,128)S(1)}, f32[8,64,64]{2,1,0:T(8,128)}, u32[]{:S(2)}) copy-start(f32[8,64,64]{2,1,0:T(8,128)} %inverse_ref.1) | copy-start | bytes 393220
  31.8 11.3 %copy-start.4 = (f32[8,96,64]{1,2,0:T(8,128)S(1)}, f32[8,96,64]{1,2,0:T(8,128)}, u32[]{:S(2)}) copy-start(f32[8,96,64]{1,2,0:T(8,128)} %param.18) | copy-start | bytes 589828
  31.8 24.9 %all-to-all-start.1 = ((f32[64,1,2304]{2,1,0:T(1,128)}), f32[64,1,2304]{2,1,0:T(1,128)S(1)}, u32[]{:S(2)}, u32[]{:S(2)}) async-start(f32[64,1,2304]{2,1,0:T(1,128)} %bitcast.11), calls=%async_computation.1 | async-start | bytes 1179648 | tf_op jit(solution)/shard_map/all_to_all | solution.py:598
  38.2 9.2 %collective-permute-start.2 = (f32[384,128]{1,0:T(8,128)S(1)}, f32[384,128]{1,0:T(8,128)S(1)}, u32[]{:S(2)}, u32[]{:S(2)}) collective-permute-start(f32[384,128]{1,0:T(8,128)S(1)} %copy-done), channel_id=1, source_target_pairs={{0,1},{1,2},{2,3},{3,0},{4,5},{5,6},{6,7},{7,4},{8,9},{9,10},{10,1... | collective-permute-start | bytes 589832 | tf_op jit(solution)/shard_map/ppermute | solution.py:650
  39.5 11.2 %collective-permute-start.1 = (f32[384,128]{1,0:T(8,128)S(1)}, f32[384,128]{1,0:T(8,128)S(1)}, u32[]{:S(2)}, u32[]{:S(2)}) collective-permute-start(f32[384,128]{1,0:T(8,128)S(1)} %copy-done), channel_id=1, source_target_pairs={{0,2},{1,3},{2,0},{3,1},{4,6},{5,7},{6,4},{7,5},{8,10},{9,11},{10,... | collective-permute-start | bytes 589832 | tf_op jit(solution)/shard_map/ppermute | solution.py:650
  41.9 8.8 %collective-permute-start = (f32[384,128]{1,0:T(8,128)S(1)}, f32[384,128]{1,0:T(8,128)S(1)}, u32[]{:S(2)}, u32[]{:S(2)}) collective-permute-start(f32[384,128]{1,0:T(8,128)S(1)} %copy-done), channel_id=1, source_target_pairs={{0,3},{1,0},{2,1},{3,2},{4,7},{5,4},{6,5},{7,6},{8,11},{9,8},{10,9... | collective-permute-start | bytes 589832 | tf_op jit(solution)/shard_map/ppermute | solution.py:650
  45.7 1.7 %copy-start.13 = (bf16[384,144]{1,0:T(8,128)(2,1)}, bf16[384,144]{1,0:T(8,128)(2,1)S(1)}, u32[]{:S(2)}) copy-start(bf16[384,144]{1,0:T(8,128)(2,1)S(1)} %get-tuple-element.55.far_far) | copy-start | bytes 331780
  47.4 4.9 %copy-start.15 = (f32[384,128]{1,0:T(8,128)}, f32[384,128]{1,0:T(8,128)S(1)}, u32[]{:S(2)}) copy-start(f32[384,128]{1,0:T(8,128)S(1)} %get-tuple-element.60.near_values) | copy-start | bytes 589828
  59.4 11.6 %copy-start.14 = (bf16[384,144]{1,0:T(8,128)(2,1)S(1)}, bf16[384,144]{1,0:T(8,128)(2,1)}, u32[]{:S(2)}) copy-start(bf16[384,144]{1,0:T(8,128)(2,1)} %copy-done.13) | copy-start | bytes 331780
  59.4 25.5 %all-to-all-start.2 = ((f32[64,1,2304]{2,1,0:T(1,128)}), f32[64,1,2304]{2,1,0:T(1,128)S(1)}, u32[]{:S(2)}, u32[]{:S(2)}) async-start(f32[64,1,2304]{2,1,0:T(1,128)} %bitcast.13), calls=%async_computation.2 | async-start | bytes 1179648 | tf_op jit(solution)/shard_map/all_to_all | solution.py:598
  66.3 18.6 %collective-permute-start.5 = (f32[384,128]{1,0:T(8,128)S(1)}, f32[384,128]{1,0:T(8,128)S(1)}, u32[]{:S(2)}, u32[]{:S(2)}) collective-permute-start(f32[384,128]{1,0:T(8,128)S(1)} %get-tuple-element.64.field_ref.refs_4_.rest_5_), channel_id=1, source_target_pairs={{0,1},{1,2},{2,3},{3,0},{4,5},{5,6},{6,7},{7,4},{8,9},{9,10},{10,1... | collective-permute-start | bytes 589832 | tf_op jit(solution)/shard_map/ppermute | solution.py:650
  67.5 17.4 %collective-permute-start.4 = (f32[384,128]{1,0:T(8,128)S(1)}, f32[384,128]{1,0:T(8,128)S(1)}, u32[]{:S(2)}, u32[]{:S(2)}) collective-permute-start(f32[384,128]{1,0:T(8,128)S(1)} %get-tuple-element.64.field_ref.refs_4_.rest_5_), channel_id=1, source_target_pairs={{0,2},{1,3},{2,0},{3,1},{4,6},{5,7},{6,4},{7,5},{8,10},{9,11},{10,... | collective-permute-start | bytes 589832 | tf_op jit(solution)/shard_map/ppermute | solution.py:650
  69.8 15.1 %collective-permute-start.3 = (f32[384,128]{1,0:T(8,128)S(1)}, f32[384,128]{1,0:T(8,128)S(1)}, u32[]{:S(2)}, u32[]{:S(2)}) collective-permute-start(f32[384,128]{1,0:T(8,128)S(1)} %get-tuple-element.64.field_ref.refs_4_.rest_5_), channel_id=1, source_target_pairs={{0,3},{1,0},{2,1},{3,2},{4,7},{5,4},{6,5},{7,6},{8,11},{9,8},{10,9... | collective-permute-start | bytes 589832 | tf_op jit(solution)/shard_map/ppermute | solution.py:650
  72.7 1.5 %copy-start.12 = (bf16[512,144]{1,0:T(8,128)(2,1)S(1)}, bf16[512,144]{1,0:T(8,128)(2,1)}, u32[]{:S(2)}) copy-start(bf16[512,144]{1,0:T(8,128)(2,1)} %get-tuple-element.62.turned_near) | copy-start | bytes 442372
  74.2 1.2 copy-start.1
  74.2 1.2 copy-start.11
  74.2 1.2 copy-start.16
  90.2 16.3 %all-to-all-start.3 = ((f32[32,8,128]{2,1,0:T(8,128)}), f32[32,8,128]{2,1,0:T(8,128)S(1)}, u32[]{:S(2)}, u32[]{:S(2)}) async-start(f32[32,8,128]{2,1,0:T(8,128)} %get-tuple-element.71), calls=%async_computation.3 | async-start | bytes 262144 | tf_op jit(solution)/shard_map/all_to_all | solution.py:699
  97.1 23.5 %collective-permute-start.6 = (f32[640,128]{1,0:T(8,128)}, f32[640,128]{1,0:T(8,128)S(1)}, u32[]{:S(2)}, u32[]{:S(2)}) collective-permute-start(f32[640,128]{1,0:T(8,128)} %get-tuple-element.77), channel_id=1, source_target_pairs={{0,3},{1,0},{2,1},{3,2},{4,7},{5,4},{6,5},{7,6},{8,11},{9,8},{10,9... | collective-permute-start | bytes 983048 | tf_op jit(solution)/shard_map/ppermute | solution.py:650
  99.6 21.0 %collective-permute-start.7 = (f32[640,128]{1,0:T(8,128)}, f32[640,128]{1,0:T(8,128)S(1)}, u32[]{:S(2)}, u32[]{:S(2)}) collective-permute-start(f32[640,128]{1,0:T(8,128)} %get-tuple-element.78), channel_id=1, source_target_pairs={{0,2},{1,3},{2,0},{3,1},{4,6},{5,7},{6,4},{7,5},{8,10},{9,11},{10,... | collective-permute-start | bytes 983048 | tf_op jit(solution)/shard_map/ppermute | solution.py:650
  100.2 20.5 %collective-permute-start.8 = (f32[640,128]{1,0:T(8,128)}, f32[640,128]{1,0:T(8,128)S(1)}, u32[]{:S(2)}, u32[]{:S(2)}) collective-permute-start(f32[640,128]{1,0:T(8,128)} %get-tuple-element.79), channel_id=1, source_target_pairs={{0,1},{1,2},{2,3},{3,0},{4,5},{5,6},{6,7},{7,4},{8,9},{9,10},{10,1... | collective-permute-start | bytes 983048 | tf_op jit(solution)/shard_map/ppermute | solution.py:650
  116.3 4.4 %copy-start.8 = (f32[256,128]{1,0:T(8,128)S(1)}, f32[256,128]{1,0:T(8,128)}, u32[]{:S(2)}) copy-start(f32[256,128]{1,0:T(8,128)} %get-tuple-element.84.refs_0_) | copy-start | bytes 393220
  120.7 2.6 %copy-start.10 = (f32[384,128]{1,0:T(8,128)S(1)}, f32[384,128]{1,0:T(8,128)}, u32[]{:S(2)}) copy-start(f32[384,128]{1,0:T(8,128)} %get-tuple-element.73.refs_8_) | copy-start | bytes 589828
  121.0 5.2 %collective-permute-start.9 = (f32[128,128]{1,0:T(8,128)S(1)}, f32[128,128]{1,0:T(8,128)S(1)}, u32[]{:S(2)}, u32[]{:S(2)}) collective-permute-start(f32[128,128]{1,0:T(8,128)S(1)} %get-tuple-element.86), channel_id=1, source_target_pairs={{0,3},{1,0},{2,1},{3,2},{4,7},{5,4},{6,5},{7,6},{8,11},{9,8},{10,9... | collective-permute-start | bytes 196616 | tf_op jit(solution)/shard_map/ppermute | solution.py:650
  122.6 4.7 %collective-permute-start.10 = (f32[128,128]{1,0:T(8,128)S(1)}, f32[128,128]{1,0:T(8,128)S(1)}, u32[]{:S(2)}, u32[]{:S(2)}) collective-permute-start(f32[128,128]{1,0:T(8,128)S(1)} %get-tuple-element.87), channel_id=1, source_target_pairs={{0,2},{1,3},{2,0},{3,1},{4,6},{5,7},{6,4},{7,5},{8,10},{9,11},{10,... | collective-permute-start | bytes 196616 | tf_op jit(solution)/shard_map/ppermute | solution.py:650
  122.8 5.0 %collective-permute-start.11 = (f32[128,128]{1,0:T(8,128)S(1)}, f32[128,128]{1,0:T(8,128)S(1)}, u32[]{:S(2)}, u32[]{:S(2)}) collective-permute-start(f32[128,128]{1,0:T(8,128)S(1)} %get-tuple-element.88), channel_id=1, source_target_pairs={{0,1},{1,2},{2,3},{3,0},{4,5},{5,6},{6,7},{7,4},{8,9},{9,10},{10,1... | collective-permute-start | bytes 196616 | tf_op jit(solution)/shard_map/ppermute | solution.py:650
  123.3 4.5 %copy-start.5 = (f32[512,128]{1,0:T(8,128)S(1)}, f32[512,128]{1,0:T(8,128)}, u32[]{:S(2)}) copy-start(f32[512,128]{1,0:T(8,128)} %get-tuple-element.82.bubble_ref) | copy-start | bytes 786436

commit v12 on v11

--- a/solution.py
+++ b/solution.py
@@ -348,7 +348,7 @@
     if last:
         total = groups * CASES
         gram = add_products(
-            LANES, images, [images[0], image_ref], [2 * total, 3 * total], case_ref[0], gram_ref[...]
+            LANES, images, [image_ref], [3 * total], case_ref[0], gram_ref[...]
         )
         for p in range(copies_ref.shape[0]):
             copies_ref[p] = gram
@@ -431,6 +431,11 @@
 def gram_kernel(groups, case_ref, gram_ref, *refs):
     base, image_ref, out_ref = refs[:groups], refs[groups], refs[groups + 1]
     out_ref[...] = add_products(LANES, base, [image_ref], [groups * CASES], case_ref[0], gram_ref[...])
+
+
+def image_gram_kernel(groups, case_ref, gram_ref, *refs):
+    image, out_ref = refs[:groups], refs[groups]
+    out_ref[...] = add_products(LANES, image, [image[0]], [2 * groups * CASES], case_ref[0], gram_ref[...])
 
 
 def sum_kernel(in_ref, out_ref):
@@ -681,7 +686,10 @@
     (gram,) = call(functools.partial(gram_kernel, groups), gram_of, name="gram", smem=(0,))(
         case, gram, base, *base_all, image
     )
-    arrived, turned0, turned1 = lax.optimization_barrier((arrived, turned0, turned1))
+    (gram,) = call(functools.partial(image_gram_kernel, groups), gram_of, name="image_gram", smem=(0,))(
+        case, gram, image, *image_all
+    )
+    arrived, turned0, turned1, gram = lax.optimization_barrier((arrived, turned0, turned1, gram))
     minor = lax.axis_size("py")
     second, copies, turned_own, *messages = call(
         functools.partial(image_kernel, parts, groups, True),

time: 129 us -> 128 us (level)
  waiting for transfers between devices: 23.2 us -> 21.7 us
    all_to_all x2, waiting for transfers between devices: 12.6 us -> 9.26 us  [exchange(): lax.all_to_all(rows.reshape(parts, 1, -1), PLANE, split_axis=0, concat_ax...]
    ppermute x12, waiting for transfers between devices: 4.9 us -> 6.73 us  [to_cases(): lax.ppermute(message, 'case', [(k, (k + h) % groups) for k in range(group...]
    pallas_call x16 -> x17, Pallas kernels: 32.7 us -> 33.6 us  [run(): pl.pallas_call(kernel, out_shape=results, in_specs=specs, out_specs=[vmem...]
  transfers between devices with their start and end apart: 15 -> 15, of which waited for: 6 -> 7; matrix products, arithmetic and copies ran while one was open for 0% -> 0% of each run, Pallas kernels for 15% -> 16%
where the time goes in v12:
time: 128 us
  blocking collectives  36.1 us (28%)
  starting transfers between devices  35.6 us (28%)
  Pallas kernels  33.6 us (26%)
  waiting for transfers between devices  21.7 us (17%)
    pallas_call x17, Pallas kernels, run(): pl.pallas_call(kernel, out_shape=results, in_specs=specs, out_specs=[vmem...  33.6 us
    all_to_all x1, blocking collectives, exchange(): lax.all_to_all(rows.reshape(parts, 1, -1), PLANE, split_axis=0, concat_ax...  26.4 us
    ppermute x12, starting transfers between devices, to_cases(): lax.ppermute(message, 'case', [(k, (k + h) % groups) for k in range(group...  15.5 us
    all_to_all x2, starting transfers between devices, exchange(): lax.all_to_all(rows.reshape(parts, 1, -1), PLANE, split_axis=0, concat_ax...  13.2 us
    all_to_all x1, blocking collectives, local(): copies = lax.all_to_all(copies, 'px', split_axis=0, concat_axis=0)  9.74 us
    all_to_all x2, waiting for transfers between devices, exchange(): lax.all_to_all(rows.reshape(parts, 1, -1), PLANE, split_axis=0, concat_ax...  9.26 us
    all_to_all x1, starting transfers between devices, local(): copies = lax.all_to_all(copies, ('py', 'case'), split_axis=0, concat_axis=0)  6.89 us
    ppermute x12, waiting for transfers between devices, to_cases(): lax.ppermute(message, 'case', [(k, (k + h) % groups) for k in range(group...  6.73 us
  transfers between devices with their start and end apart: 15, of which 7 were waited for; matrix products, arithmetic and copies ran while one was open for 0% of the time, Pallas kernels for 16%

profile of v12, /device:TPU:1, one launch (start us, length us, event | category | flops | bytes accessed | tf_op | source)
XLA Modules:
  0.0 127.9 jit_solution(13213655991025618292)
XLA Ops:
  0.6 3.4 %condense.1 = (f32[640,128]{1,0:T(8,128)S(1)}, f32[384,128]{1,0:T(8,128)}, f32[64,128]{1,0:T(8,128)S(1)}, f32[8,128]{1,0:T(8,128)S(1)}) custom-call(s32[1,128]{1,0:T(1,128)} %bitcast.30, f32[1,128]{1,0:T(1,128)} %bitcast.31, s32[1,128]{1,0:T(1,128)} %bitcast.32, s32[1,128]{1,0:T(1,128)} %bitcast.33, s32[1,128]{1,0:T(1,128)} %bitcast.34, ...), custom_call_target="tpu_custom_call" | custom-call | bytes 592384 | tf_op jit(solution)/shard_map/condense/pallas_call | solution.py:587
  4.0 0.0 copy-start.6
  4.0 0.0 copy-start.7
  4.0 26.4 %all_to_all.25 = f32[64,1,1280]{2,1,0:T(1,128)S(1)} all-to-all(f32[64,1,1280]{2,1,0:T(1,128)S(1)} %bitcast.23), channel_id=1, replica_groups=mesh['px'=8,'py'=8,'case'=4] {'px','py'}, dimensions={0} | all-to-all | bytes 655360 | tf_op jit(solution)/shard_map/all_to_all | solution.py:603
  30.4 1.4 %rhs.1 = (f32[384,128]{1,0:T(8,128)}, f32[1152,128]{1,0:T(8,128)}, f32[64,128]{1,0:T(8,128)S(1)}) custom-call(f32[640,128]{1,0:T(8,128)S(1)} %bitcast.21, f32[384,128]{1,0:T(8,128)S(1)} %copy-done.7, f32[384,128]{1,0:T(8,128)S(1)} %bitcast.28, f32[64,128]{1,0:T(8,128)S(1)} %get-tuple-element.49.meta_ref.rest_0_), custom_call_target="tpu_custom_call" | custom-call | bytes 753664 | tf_op jit(solution)/shard_map/rhs/pallas_call | solution.py:587
  31.8 6.3 %all-to-all-start.1 = ((f32[64,1,2304]{2,1,0:T(1,128)}), f32[64,1,2304]{2,1,0:T(1,128)S(1)}, u32[]{:S(2)}, u32[]{:S(2)}) async-start(f32[64,1,2304]{2,1,0:T(1,128)} %bitcast.11), calls=%async_computation.1 | async-start | bytes 1179648 | tf_op jit(solution)/shard_map/all_to_all | solution.py:603
  38.2 1.3 %collective-permute-start.2 = (f32[384,128]{1,0:T(8,128)S(1)}, f32[384,128]{1,0:T(8,128)S(1)}, u32[]{:S(2)}, u32[]{:S(2)}) collective-permute-start(f32[384,128]{1,0:T(8,128)S(1)} %copy-done), channel_id=1, source_target_pairs={{0,1},{1,2},{2,3},{3,0},{4,5},{5,6},{6,7},{7,4},{8,9},{9,10},{10,1... | collective-permute-start | bytes 589832 | tf_op jit(solution)/shard_map/ppermute | solution.py:655
  39.4 2.4 %collective-permute-start.1 = (f32[384,128]{1,0:T(8,128)S(1)}, f32[384,128]{1,0:T(8,128)S(1)}, u32[]{:S(2)}, u32[]{:S(2)}) collective-permute-start(f32[384,128]{1,0:T(8,128)S(1)} %copy-done), channel_id=1, source_target_pairs={{0,2},{1,3},{2,0},{3,1},{4,6},{5,7},{6,4},{7,5},{8,10},{9,11},{10,... | collective-permute-start | bytes 589832 | tf_op jit(solution)/shard_map/ppermute | solution.py:655
  41.9 1.2 collective-permute-start
  43.1 2.6 %tables.1 = (bf16[384,144]{1,0:T(8,128)(2,1)S(1)}, bf16[384,144]{1,0:T(8,128)(2,1)S(1)}, bf16[384,144]{1,0:T(8,128)(2,1)S(1)}, bf16[384,144]{1,0:T(8,128)(2,1)S(...) custom-call(f32[8,128]{1,0:T(8,128)S(1)} %get-tuple-element.54.where_ref, ...), custom_call_target="tpu_custom_call" | custom-call | flops 1000000000 | bytes 888832 | tf_op jit(solution)/shard_map/tables/pallas_call | solution.py:587
  45.7 1.6 %inner.2 = (f32[384,128]{1,0:T(8,128)S(1)}, f32[384,128]{1,0:T(8,128)S(1)}) custom-call(f32[384,128]{1,0:T(8,128)S(1)} %copy-done, f32[64,128]{1,0:T(8,128)S(1)} %get-tuple-element.53.asked_ref, f32[8,128]{1,0:T(8,128)S(1)} %get-tuple-element.54.where_ref, bf16[384,144]{1,0:T(8,128)(2,1)S(1)} %get-tuple-element.55.near_near, ...), custom_call_target="tpu_custom_call" | custom-call | flops 1000000000 | bytes 454656 | tf_op jit(solution)/shard_map/inner/pallas_call | solution.py:587
  47.3 0.0 collective-permute-done.2.refs_3_
  47.3 3.3 %collective-permute-done.1.refs_2_ = f32[384,128]{1,0:T(8,128)S(1)} collective-permute-done((f32[384,128]{1,0:T(8,128)S(1)}, f32[384,128]{1,0:T(8,128)S(1)}, u32[]{:S(2)}, u32[]{:S(2)}) %collective-permute-start.1) | collective-permute-done | bytes 196640 | tf_op jit(solution)/shard_map/ppermute | solution.py:655
  50.7 1.5 %base_gram.1.gram_ref = f32[8,128]{1,0:T(8,128)S(1)} custom-call(s32[1]{0:T(128)} %bitcast.case_ref.rest_0_, f32[384,128]{1,0:T(8,128)S(1)} %copy-done, f32[384,128]{1,0:T(8,128)S(1)} %collective-permute-done.refs_1_, f32[384,128]{1,0:T(8,128)S(1)} %collective-permute-done.1.refs_2_, f32[384,128]{1,0:T(8,128)S(1)} %collective-permute-done.2.refs_3_), custom_call_target="tpu_custom_call" | custom-call | bytes 786436 | tf_op jit(solution)/shard_map/base_gram/pallas_call | solution.py:587
  52.2 4.5 %all-to-all-done.1 = f32[64,1,2304]{2,1,0:T(1,128)S(1)} async-done(((f32[64,1,2304]{2,1,0:T(1,128)}), f32[64,1,2304]{2,1,0:T(1,128)S(1)}, u32[]{:S(2)}, u32[]{:S(2)}) %all-to-all-start.1) | async-done | bytes 589856 | tf_op jit(solution)/shard_map/all_to_all | solution.py:603
  56.7 2.7 %image.1 = (f32[384,128]{1,0:T(8,128)S(1)}, f32[384,128]{1,0:T(8,128)}, f32[1152,128]{1,0:T(8,128)}) custom-call(f32[1152,128]{1,0:T(8,128)S(1)} %bitcast.19, f32[384,128]{1,0:T(8,128)S(1)} %get-tuple-element.57.inner_ref, f32[64,128]{1,0:T(8,128)S(1)} %get-tuple-element.53.asked_ref, f32[8,128]{1,0:T(8,128)S(1)} %get-tuple-element.54.where_ref, ...), custom_call_target="tpu_custom_call" | custom-call | bytes 1077248 | tf_op jit(solution)/shard_map/image/pallas_call | solution.py:587
  59.4 6.9 %all-to-all-start.2 = ((f32[64,1,2304]{2,1,0:T(1,128)}), f32[64,1,2304]{2,1,0:T(1,128)S(1)}, u32[]{:S(2)}, u32[]{:S(2)}) async-start(f32[64,1,2304]{2,1,0:T(1,128)} %bitcast.13), calls=%async_computation.2 | async-start | bytes 1179648 | tf_op jit(solution)/shard_map/all_to_all | solution.py:603
  66.3 1.1 collective-permute-start.5
  67.4 2.4 %collective-permute-start.4 = (f32[384,128]{1,0:T(8,128)S(1)}, f32[384,128]{1,0:T(8,128)S(1)}, u32[]{:S(2)}, u32[]{:S(2)}) collective-permute-start(f32[384,128]{1,0:T(8,128)S(1)} %get-tuple-element.65.field_ref.refs_4_.refs_0_.rest_5_), channel_id=1, source_target_pairs={{0,2},{1,3},{2,0},{3,1},{4,6},{5,7},{6,4},{7,5},{8,10},{9,11},{10,... | collective-permute-start | bytes 589832 | tf_op jit(solution)/shard_map/ppermute | solution.py:655
  69.8 1.2 collective-permute-start.3
  71.0 1.7 %inner.3 = (f32[384,128]{1,0:T(8,128)S(1)}, f32[384,128]{1,0:T(8,128)S(1)}) custom-call(f32[384,128]{1,0:T(8,128)S(1)} %get-tuple-element.65.field_ref.refs_4_.refs_0_.rest_5_, f32[64,128]{1,0:T(8,128)S(1)} %get-tuple-element.53.asked_ref, f32[8,128]{1,0:T(8,128)S(1)} %get-tuple-element.54.where_ref, bf16[384,144]{1,0:T(8,128)(2,1)S(1)} %copy-done.14, ...), custom_call_target="tpu_custom_call" | custom-call | flops 1000000000 | bytes 454656 | tf_op jit(solution)/shard_map/inner/pallas_call | solution.py:587
  72.6 0.0 copy-start.12
  72.6 1.5 %gram.1.gram_ref = f32[8,128]{1,0:T(8,128)S(1)} custom-call(s32[1]{0:T(128)} %bitcast.case_ref.rest_0_, f32[8,128]{1,0:T(8,128)S(1)} %base_gram.1.gram_ref, f32[384,128]{1,0:T(8,128)S(1)} %copy-done, f32[384,128]{1,0:T(8,128)S(1)} %collective-permute-done.refs_1_, f32[384,128]{1,0:T(8,128)S(1)} %collective-permute-done.1.refs_2_, ...), custom_call_target="tpu_custom_call" | custom-call | bytes 987140 | tf_op jit(solution)/shard_map/gram/pallas_call | solution.py:587
  74.2 0.0 copy-start.11
  74.2 1.2 turned_near.1.rest_4_
  75.3 1.4 %turned.1.rest_3_ = f32[512,128]{1,0:T(8,128)} custom-call(f32[384,128]{1,0:T(8,128)S(1)} %get-tuple-element.61.near_values, f32[384,128]{1,0:T(8,128)S(1)} %copy-done.11, f32[8,128]{1,0:T(8,128)S(1)} %get-tuple-element.54.where_ref, bf16[512,144]{1,0:T(8,128)(2,1)S(1)} %copy-done.12, bf16[512,144]{1,0:T(8,128)(2,1)S(1)} %copy-done.1), custom_call_target="tpu_custom_call" | custom-call | flops 1000000000 | bytes 692224 | tf_op jit(solution)/shard_map/turned/pallas_call | solution.py:587
  76.7 0.0 collective-permute-done.5.refs_3_.rest_8_.refs_7_
  76.7 1.8 %collective-permute-done.4.refs_2_.rest_7_.refs_6_ = f32[384,128]{1,0:T(8,128)S(1)} collective-permute-done((f32[384,128]{1,0:T(8,128)S(1)}, f32[384,128]{1,0:T(8,128)S(1)}, u32[]{:S(2)}, u32[]{:S(2)}) %collective-permute-start.4) | collective-permute-done | bytes 196640 | tf_op jit(solution)/shard_map/ppermute | solution.py:655
  78.6 1.5 %image_gram.1.rest_1_ = f32[8,128]{1,0:T(8,128)S(1)} custom-call(s32[1]{0:T(128)} %bitcast.case_ref.rest_0_, f32[8,128]{1,0:T(8,128)S(1)} %gram.1.gram_ref, f32[384,128]{1,0:T(8,128)S(1)} %get-tuple-element.65.field_ref.refs_4_.refs_0_.rest_5_, f32[384,128]{1,0:T(8,128)S(1)} %collective-permute-done.3.refs_1_.rest_6_.refs_5_, ...), custom_call_target="tpu_custom_call" | custom-call | bytes 790532 | tf_op jit(solution)/shard_map/image_gram/pallas_call | solution.py:587
  80.1 4.7 %all-to-all-done.2 = f32[64,1,2304]{2,1,0:T(1,128)S(1)} async-done(((f32[64,1,2304]{2,1,0:T(1,128)}), f32[64,1,2304]{2,1,0:T(1,128)S(1)}, u32[]{:S(2)}, u32[]{:S(2)}) %all-to-all-start.2) | async-done | bytes 589856 | tf_op jit(solution)/shard_map/all_to_all | solution.py:603
  84.8 4.7 %second.1 = (f32[384,128]{1,0:T(8,128)}, f32[32,8,128]{2,1,0:T(8,128)}, f32[256,128]{1,0:T(8,128)}, f32[640,128]{1,0:T(8,128)}, f32[640,128]{1,0:T(8,128)}, /*index=5*/f32[640,128]{1,0:T(8,128)}) custom-call(f32[1152,128]{1,0:T(8,128)S(1)} %bitcast.20, f32[384,128]{1,0:T(8,128)S(1)} %get-tuple-element.69.inner_ref, ...), custom_call_target="tpu_custom_call" | custom-call | bytes 2506756 | tf_op jit(solution)/shard_map/second/pallas_call | solution.py:587
  89.6 6.9 %all-to-all-start.3 = ((f32[32,8,128]{2,1,0:T(8,128)}), f32[32,8,128]{2,1,0:T(8,128)S(1)}, u32[]{:S(2)}, u32[]{:S(2)}) async-start(f32[32,8,128]{2,1,0:T(8,128)} %get-tuple-element.73), calls=%async_computation.3 | async-start | bytes 262144 | tf_op jit(solution)/shard_map/all_to_all | solution.py:707
  96.5 2.5 %collective-permute-start.6 = (f32[640,128]{1,0:T(8,128)}, f32[640,128]{1,0:T(8,128)S(1)}, u32[]{:S(2)}, u32[]{:S(2)}) collective-permute-start(f32[640,128]{1,0:T(8,128)} %get-tuple-element.79), channel_id=1, source_target_pairs={{0,3},{1,0},{2,1},{3,2},{4,7},{5,4},{6,5},{7,6},{8,11},{9,8},{10,9... | collective-permute-start | bytes 983048 | tf_op jit(solution)/shard_map/ppermute | solution.py:655
  99.0 0.6 collective-permute-start.7
  99.6 0.6 collective-permute-start.8
  100.2 5.8 %all-to-all-done.3 = f32[32,8,128]{2,1,0:T(8,128)S(1)} async-done(((f32[32,8,128]{2,1,0:T(8,128)}), f32[32,8,128]{2,1,0:T(8,128)S(1)}, u32[]{:S(2)}, u32[]{:S(2)}) %all-to-all-start.3) | async-done | bytes 131104 | tf_op jit(solution)/shard_map/all_to_all | solution.py:707
  105.9 9.7 %all_to_all.26.gram_ref = f32[8,32,128]{2,1,0:T(8,128)S(1)} all-to-all(f32[8,32,128]{2,1,0:T(8,128)S(1)} %sum.1), channel_id=1, replica_groups=mesh['px'=8,'py'=8,'case'=4] {'px'}, dimensions={0} | all-to-all | bytes 262144 | tf_op jit(solution)/shard_map/all_to_all | solution.py:721
  115.7 4.3 %solve.1 = (f32[64,8,128]{2,1,0:T(8,128)S(1)}, f32[32,256]{1,0:T(8,128)S(1)}) custom-call(s32[1]{0:T(128)} %bitcast.case_ref.rest_0_, f32[8,32,128]{2,1,0:T(8,128)S(1)} %all_to_all.26.gram_ref), custom_call_target="tpu_custom_call" | custom-call | bytes 131076 | tf_op jit(solution)/shard_map/solve/pallas_call | solution.py:587
  120.0 0.0 collective-permute-done.7.refs_10_.refs_2_
  120.1 0.0 copy-start.10
  120.1 0.4 bubble.1
  120.4 1.5 %collective-permute-start.9 = (f32[128,128]{1,0:T(8,128)S(1)}, f32[128,128]{1,0:T(8,128)S(1)}, u32[]{:S(2)}, u32[]{:S(2)}) collective-permute-start(f32[128,128]{1,0:T(8,128)S(1)} %get-tuple-element.88), channel_id=1, source_target_pairs={{0,3},{1,0},{2,1},{3,2},{4,7},{5,4},{6,5},{7,6},{8,11},{9,8},{10,9... | collective-permute-start | bytes 196616 | tf_op jit(solution)/shard_map/ppermute | solution.py:655
  122.0 0.2 collective-permute-start.10
  122.1 0.5 collective-permute-start.11
  122.7 2.9 %ports.1 = (f32[384,128]{1,0:T(8,128)}, f32[384,128]{1,0:T(8,128)}) custom-call(f32[64,8,128]{2,1,0:T(8,128)S(1)} %get-tuple-element.74.coef, f32[384,128]{1,0:T(8,128)S(1)} %copy-done, f32[384,128]{1,0:T(8,128)S(1)} %collective-permute-done.refs_1_, f32[384,128]{1,0:T(8,128)S(1)} %collective-permute-done.1.refs_2_, ...), custom_call_target="tpu_custom_call" | custom-call | flops 1000000000 | bytes 3014656 | tf_op jit(solution)/shard_map/ports/pallas_call | solution.py:587
  125.6 1.1 collective-permute-done.10.refs_2_
  126.7 0.5 collective-permute-done.11.refs_3_
  127.2 0.7 join.1
  (36 shorter events, 0.1 us)
Async XLA Ops:
  4.0 26.4 %copy-start.6 = (f32[48,8,128]{2,1,0:T(8,128)S(1)}, f32[48,8,128]{2,1,0:T(8,128)}, u32[]{:S(2)}) copy-start(f32[48,8,128]{2,1,0:T(8,128)} %param.16) | copy-start | bytes 589828
  4.0 26.4 %copy-start.7 = (f32[384,128]{1,0:T(8,128)S(1)}, f32[384,128]{1,0:T(8,128)}, u32[]{:S(2)}) copy-start(f32[384,128]{1,0:T(8,128)} %get-tuple-element.48.near_sum_ref) | copy-start | bytes 589828
  30.4 12.7 %copy-start.9 = (f32[8,96,96]{2,1,0:T(8,128)S(1)}, f32[8,96,96]{2,1,0:T(8,128)}, u32[]{:S(2)}) copy-start(f32[8,96,96]{2,1,0:T(8,128)} %block_ref.1) | copy-start | bytes 884740
  31.8 6.3 %copy-start = (f32[384,128]{1,0:T(8,128)S(1)}, f32[384,128]{1,0:T(8,128)}, u32[]{:S(2)}) copy-start(f32[384,128]{1,0:T(8,128)} %get-tuple-element.51.refs_0_.field_ref) | copy-start | bytes 589828
  31.8 11.3 %copy-start.2 = (f32[64,8,128]{2,1,0:T(8,128)S(1)}, f32[64,8,128]{2,1,0:T(8,128)}, u32[]{:S(2)}) copy-start(f32[64,8,128]{2,1,0:T(8,128)} %param.15) | copy-start | bytes 786436
  31.8 11.3 %copy-start.3 = (f32[8,64,64]{2,1,0:T(8,128)S(1)}, f32[8,64,64]{2,1,0:T(8,128)}, u32[]{:S(2)}) copy-start(f32[8,64,64]{2,1,0:T(8,128)} %inverse_ref.1) | copy-start | bytes 393220
  31.8 11.3 %copy-start.4 = (f32[8,96,64]{1,2,0:T(8,128)S(1)}, f32[8,96,64]{1,2,0:T(8,128)}, u32[]{:S(2)}) copy-start(f32[8,96,64]{1,2,0:T(8,128)} %param.18) | copy-start | bytes 589828
  31.8 24.9 %all-to-all-start.1 = ((f32[64,1,2304]{2,1,0:T(1,128)}), f32[64,1,2304]{2,1,0:T(1,128)S(1)}, u32[]{:S(2)}, u32[]{:S(2)}) async-start(f32[64,1,2304]{2,1,0:T(1,128)} %bitcast.11), calls=%async_computation.1 | async-start | bytes 1179648 | tf_op jit(solution)/shard_map/all_to_all | solution.py:603
  38.2 9.2 %collective-permute-start.2 = (f32[384,128]{1,0:T(8,128)S(1)}, f32[384,128]{1,0:T(8,128)S(1)}, u32[]{:S(2)}, u32[]{:S(2)}) collective-permute-start(f32[384,128]{1,0:T(8,128)S(1)} %copy-done), channel_id=1, source_target_pairs={{0,1},{1,2},{2,3},{3,0},{4,5},{5,6},{6,7},{7,4},{8,9},{9,10},{10,1... | collective-permute-start | bytes 589832 | tf_op jit(solution)/shard_map/ppermute | solution.py:655
  39.4 11.2 %collective-permute-start.1 = (f32[384,128]{1,0:T(8,128)S(1)}, f32[384,128]{1,0:T(8,128)S(1)}, u32[]{:S(2)}, u32[]{:S(2)}) collective-permute-start(f32[384,128]{1,0:T(8,128)S(1)} %copy-done), channel_id=1, source_target_pairs={{0,2},{1,3},{2,0},{3,1},{4,6},{5,7},{6,4},{7,5},{8,10},{9,11},{10,... | collective-permute-start | bytes 589832 | tf_op jit(solution)/shard_map/ppermute | solution.py:655
  41.9 8.8 %collective-permute-start = (f32[384,128]{1,0:T(8,128)S(1)}, f32[384,128]{1,0:T(8,128)S(1)}, u32[]{:S(2)}, u32[]{:S(2)}) collective-permute-start(f32[384,128]{1,0:T(8,128)S(1)} %copy-done), channel_id=1, source_target_pairs={{0,3},{1,0},{2,1},{3,2},{4,7},{5,4},{6,5},{7,6},{8,11},{9,8},{10,9... | collective-permute-start | bytes 589832 | tf_op jit(solution)/shard_map/ppermute | solution.py:655
  45.7 1.7 %copy-start.13 = (bf16[384,144]{1,0:T(8,128)(2,1)}, bf16[384,144]{1,0:T(8,128)(2,1)S(1)}, u32[]{:S(2)}) copy-start(bf16[384,144]{1,0:T(8,128)(2,1)S(1)} %get-tuple-element.55.near_near) | copy-start | bytes 331780
  45.7 1.7 %copy-start.15 = (bf16[384,144]{1,0:T(8,128)(2,1)}, bf16[384,144]{1,0:T(8,128)(2,1)S(1)}, u32[]{:S(2)}) copy-start(bf16[384,144]{1,0:T(8,128)(2,1)S(1)} %get-tuple-element.56.far_far) | copy-start | bytes 331780
  59.4 11.6 %copy-start.14 = (bf16[384,144]{1,0:T(8,128)(2,1)S(1)}, bf16[384,144]{1,0:T(8,128)(2,1)}, u32[]{:S(2)}) copy-start(bf16[384,144]{1,0:T(8,128)(2,1)} %copy-done.13) | copy-start | bytes 331780
  59.4 11.6 %copy-start.16 = (bf16[384,144]{1,0:T(8,128)(2,1)S(1)}, bf16[384,144]{1,0:T(8,128)(2,1)}, u32[]{:S(2)}) copy-start(bf16[384,144]{1,0:T(8,128)(2,1)} %copy-done.15) | copy-start | bytes 331780
  59.4 25.4 %all-to-all-start.2 = ((f32[64,1,2304]{2,1,0:T(1,128)}), f32[64,1,2304]{2,1,0:T(1,128)S(1)}, u32[]{:S(2)}, u32[]{:S(2)}) async-start(f32[64,1,2304]{2,1,0:T(1,128)} %bitcast.13), calls=%async_computation.2 | async-start | bytes 1179648 | tf_op jit(solution)/shard_map/all_to_all | solution.py:603
  66.3 10.5 %collective-permute-start.5 = (f32[384,128]{1,0:T(8,128)S(1)}, f32[384,128]{1,0:T(8,128)S(1)}, u32[]{:S(2)}, u32[]{:S(2)}) collective-permute-start(f32[384,128]{1,0:T(8,128)S(1)} %get-tuple-element.65.field_ref.refs_4_.refs_0_.rest_5_), channel_id=1, source_target_pairs={{0,1},{1,2},{2,3},{3,0},{4,5},{5,6},{6,7},{7,4},{8,9},{9,10},{10,1... | collective-permute-start | bytes 589832 | tf_op jit(solution)/shard_map/ppermute | solution.py:655
  67.4 11.1 %collective-permute-start.4 = (f32[384,128]{1,0:T(8,128)S(1)}, f32[384,128]{1,0:T(8,128)S(1)}, u32[]{:S(2)}, u32[]{:S(2)}) collective-permute-start(f32[384,128]{1,0:T(8,128)S(1)} %get-tuple-element.65.field_ref.refs_4_.refs_0_.rest_5_), channel_id=1, source_target_pairs={{0,2},{1,3},{2,0},{3,1},{4,6},{5,7},{6,4},{7,5},{8,10},{9,11},{10,... | collective-permute-start | bytes 589832 | tf_op jit(solution)/shard_map/ppermute | solution.py:655
  69.8 8.8 %collective-permute-start.3 = (f32[384,128]{1,0:T(8,128)S(1)}, f32[384,128]{1,0:T(8,128)S(1)}, u32[]{:S(2)}, u32[]{:S(2)}) collective-permute-start(f32[384,128]{1,0:T(8,128)S(1)} %get-tuple-element.65.field_ref.refs_4_.refs_0_.rest_5_), channel_id=1, source_target_pairs={{0,3},{1,0},{2,1},{3,2},{4,7},{5,4},{6,5},{7,6},{8,11},{9,8},{10,9... | collective-permute-start | bytes 589832 | tf_op jit(solution)/shard_map/ppermute | solution.py:655
  72.6 1.5 %copy-start.12 = (bf16[512,144]{1,0:T(8,128)(2,1)S(1)}, bf16[512,144]{1,0:T(8,128)(2,1)}, u32[]{:S(2)}) copy-start(bf16[512,144]{1,0:T(8,128)(2,1)} %get-tuple-element.63.turned_near) | copy-start | bytes 442372
  74.2 1.2 copy-start.1
  74.2 1.2 copy-start.11
  89.6 16.3 %all-to-all-start.3 = ((f32[32,8,128]{2,1,0:T(8,128)}), f32[32,8,128]{2,1,0:T(8,128)S(1)}, u32[]{:S(2)}, u32[]{:S(2)}) async-start(f32[32,8,128]{2,1,0:T(8,128)} %get-tuple-element.73), calls=%async_computation.3 | async-start | bytes 262144 | tf_op jit(solution)/shard_map/all_to_all | solution.py:707
  96.5 23.5 %collective-permute-start.6 = (f32[640,128]{1,0:T(8,128)}, f32[640,128]{1,0:T(8,128)S(1)}, u32[]{:S(2)}, u32[]{:S(2)}) collective-permute-start(f32[640,128]{1,0:T(8,128)} %get-tuple-element.79), channel_id=1, source_target_pairs={{0,3},{1,0},{2,1},{3,2},{4,7},{5,4},{6,5},{7,6},{8,11},{9,8},{10,9... | collective-permute-start | bytes 983048 | tf_op jit(solution)/shard_map/ppermute | solution.py:655
  99.0 21.0 %collective-permute-start.7 = (f32[640,128]{1,0:T(8,128)}, f32[640,128]{1,0:T(8,128)S(1)}, u32[]{:S(2)}, u32[]{:S(2)}) collective-permute-start(f32[640,128]{1,0:T(8,128)} %get-tuple-element.80), channel_id=1, source_target_pairs={{0,2},{1,3},{2,0},{3,1},{4,6},{5,7},{6,4},{7,5},{8,10},{9,11},{10,... | collective-permute-start | bytes 983048 | tf_op jit(solution)/shard_map/ppermute | solution.py:655
  99.6 20.5 %collective-permute-start.8 = (f32[640,128]{1,0:T(8,128)}, f32[640,128]{1,0:T(8,128)S(1)}, u32[]{:S(2)}, u32[]{:S(2)}) collective-permute-start(f32[640,128]{1,0:T(8,128)} %get-tuple-element.81), channel_id=1, source_target_pairs={{0,1},{1,2},{2,3},{3,0},{4,5},{5,6},{6,7},{7,4},{8,9},{9,10},{10,1... | collective-permute-start | bytes 983048 | tf_op jit(solution)/shard_map/ppermute | solution.py:655
  115.7 4.4 %copy-start.8 = (f32[256,128]{1,0:T(8,128)S(1)}, f32[256,128]{1,0:T(8,128)}, u32[]{:S(2)}) copy-start(f32[256,128]{1,0:T(8,128)} %get-tuple-element.86.refs_0_) | copy-start | bytes 393220
  120.1 2.6 %copy-start.10 = (f32[384,128]{1,0:T(8,128)S(1)}, f32[384,128]{1,0:T(8,128)}, u32[]{:S(2)}) copy-start(f32[384,128]{1,0:T(8,128)} %get-tuple-element.75.refs_8_) | copy-start | bytes 589828
  120.4 5.2 %collective-permute-start.9 = (f32[128,128]{1,0:T(8,128)S(1)}, f32[128,128]{1,0:T(8,128)S(1)}, u32[]{:S(2)}, u32[]{:S(2)}) collective-permute-start(f32[128,128]{1,0:T(8,128)S(1)} %get-tuple-element.88), channel_id=1, source_target_pairs={{0,3},{1,0},{2,1},{3,2},{4,7},{5,4},{6,5},{7,6},{8,11},{9,8},{10,9... | collective-permute-start | bytes 196616 | tf_op jit(solution)/shard_map/ppermute | solution.py:655
  122.0 4.7 %collective-permute-start.10 = (f32[128,128]{1,0:T(8,128)S(1)}, f32[128,128]{1,0:T(8,128)S(1)}, u32[]{:S(2)}, u32[]{:S(2)}) collective-permute-start(f32[128,128]{1,0:T(8,128)S(1)} %get-tuple-element.89), channel_id=1, source_target_pairs={{0,2},{1,3},{2,0},{3,1},{4,6},{5,7},{6,4},{7,5},{8,10},{9,11},{10,... | collective-permute-start | bytes 196616 | tf_op jit(solution)/shard_map/ppermute | solution.py:655
  122.1 5.0 %collective-permute-start.11 = (f32[128,128]{1,0:T(8,128)S(1)}, f32[128,128]{1,0:T(8,128)S(1)}, u32[]{:S(2)}, u32[]{:S(2)}) collective-permute-start(f32[128,128]{1,0:T(8,128)S(1)} %get-tuple-element.90), channel_id=1, source_target_pairs={{0,1},{1,2},{2,3},{3,0},{4,5},{5,6},{6,7},{7,4},{8,9},{9,10},{10,1... | collective-permute-start | bytes 196616 | tf_op jit(solution)/shard_map/ppermute | solution.py:655
  122.7 4.5 %copy-start.5 = (f32[512,128]{1,0:T(8,128)S(1)}, f32[512,128]{1,0:T(8,128)}, u32[]{:S(2)}) copy-start(f32[512,128]{1,0:T(8,128)} %get-tuple-element.84.bubble_ref) | copy-start | bytes 786436
